TPU v7x, 32 devices: a whole 2x2x4 slice. The times are simulated.
32 devices in a mesh: samp: 4 (over z), pix: 8 (over y, x, core).
Axes of the slice: x: 2, y: 2, z: 4, core: 2. Of those that a mesh axis runs over, the one named last changes fastest.
Arguments:
- stamps: bfloat16 [2048, 16384], P(('samp', 'pix')), may hold values from -6 to 6
- start_panel: float32 [16384, 32], P('pix'), may hold values from -0.046875 to 0.046875
Outputs:
- eigen_psfs: float32 [16384, 32], P('pix')
All inputs are finite; a program needn't handle non-finite values.
Results may differ from a plain program's by a relative error of at most 0.025.
Values may be sent and summed in bfloat16 or wider, within the bound.
No kernel may reach another device: no remote copies, remote signals or barrier semaphores. Data moves between devices by JAX's collectives and lax.ppermute only.
A program may use at most 64 MiB of HBM per device.

v0:
```python
import math

import jax
import jax.numpy as jnp
from jax import lax
from jax.sharding import PartitionSpec as P

PIX = 16384
ITERS = 10


def orthonormal(back, gram):
    lower = jnp.linalg.cholesky(gram)
    return lax.linalg.triangular_solve(lower, back, left_side=False, lower=True, transpose_a=True)


def gram_local(back):
    return jnp.dot(back.T, back, precision=lax.Precision.HIGHEST)


def local(stamps, start_panel):
    block = lax.all_to_all(stamps, "pix", split_axis=1, concat_axis=0, tiled=True)

    def sweep(step, panel):
        partial_value = jnp.dot(
            block, panel.astype(jnp.bfloat16), preferred_element_type=jnp.float32
        )
        proj = lax.psum(partial_value.astype(jnp.bfloat16), "pix")
        back = lax.dot_general(
            block, proj, (((0,), (0,)), ((), ())), preferred_element_type=jnp.float32
        )
        summed = lax.psum(back.astype(jnp.bfloat16), "samp").astype(jnp.float32)
        gram = lax.psum(gram_local(summed), "pix")
        return orthonormal(summed, gram)

    panel = lax.fori_loop(0, ITERS, sweep, start_panel)
    return panel * math.sqrt(PIX)


def solution(mesh):
    return jax.shard_map(
        local,
        mesh=mesh,
        in_specs=(P(("samp", "pix"), None), P("pix", None)),
        out_specs=P("pix", None),
        check_vma=False,
    )
```

profile of v0, /device:TPU:0, one launch (start us, length us, event | category | flops | bytes accessed | tf_op | source)
XLA Modules:
  0.0 957.0 jit_solution(1826507982793259952)
XLA Ops:
  6.5 3.2 copy.9
  9.7 5.3 all-to-all-start
  15.1 26.6 %all-to-all-done = bf16[64,8,2048]{2,0,1:T(8,128)(2,1)S(1)} async-done(((bf16[64,8,2048]{2,0,1:T(8,128)(2,1)}), bf16[64,8,2048]{2,0,1:T(8,128)(2,1)S(1)}, u32[]{:S(2)}, u32[]{:S(2)}) %all-to-all-start) | async-done | bytes 2097184 | tf_op jit(solution)/shard_map/all_to_all | solution.py:22
  41.7 907.7 %while.10 = (s32[]{:T(128)}, f32[2048,32]{0,1:T(8,128)S(1)}, bf16[512,2048]{1,0:T(8,128)(2,1)S(1)}, s32[]{:T(128)}) while((s32[]{:T(128)}, f32[2048,32]{0,1:T(8,128)S(1)}, bf16[512,2048]{1,0:T(8,128)(2,1)S(1)}, s32[]{:T(128)}) %tuple.24), condition=%wide.region_6.7_spmd, body=%wide.region_0.6_spmd.sunk | while | flops 163817504 | bytes 6078815 | solution.py:36
  42.4 23.6 %psum.24 = bf16[512,32]{1,0:T(8,128)(2,1)S(1)} all-reduce(bf16[512,32]{1,0:T(8,128)(2,1)S(1)} %convolution_convert_fusion.3), channel_id=1, replica_groups=mesh['samp'=4,'pix'=8] {'pix'}, use_global_device_ids=true, to_apply=%region_1.0 | all-reduce | flops 16384 | bytes 65536 | tf_op jit(solution)/shard_map/while/body/eval_jaxpr/psum | solution.py:28
  67.2 35.1 %all-reduce.2.cloned.1.call-done = bf16[2048,32]{0,1:T(8,128)(2,1)} async-done(((bf16[2048,32]{0,1:T(8,128)(2,1)}), bf16[2048,32]{0,1:T(8,128)(2,1)}) %all-reduce.2.cloned.1.call-update) | async-done | bytes 131088 | tf_op jit(solution)/shard_map/while/body/eval_jaxpr/psum | solution.py:32
  103.4 22.3 %psum.26 = f32[32,32]{0,1:T(8,128)S(1)} all-reduce(f32[32,32]{0,1:T(8,128)S(1)} %fusion.35), channel_id=1, replica_groups=mesh['samp'=4,'pix'=8] {'pix'}, use_global_device_ids=true, to_apply=%region_3.0 | all-reduce | flops 1024 | bytes 8192 | tf_op jit(solution)/shard_map/while/body/eval_jaxpr/psum | solution.py:33
  125.8 2.9 cholesky.58
  130.0 2.4 custom-call.7
  134.5 23.6 %psum.24 = bf16[512,32]{1,0:T(8,128)(2,1)S(1)} all-reduce(bf16[512,32]{1,0:T(8,128)(2,1)S(1)} %convolution_convert_fusion.3), channel_id=1, replica_groups=mesh['samp'=4,'pix'=8] {'pix'}, use_global_device_ids=true, to_apply=%region_1.0 | all-reduce | flops 16384 | bytes 65536 | tf_op jit(solution)/shard_map/while/body/eval_jaxpr/psum | solution.py:28
  159.3 33.6 %all-reduce.2.cloned.1.call-done = bf16[2048,32]{0,1:T(8,128)(2,1)} async-done(((bf16[2048,32]{0,1:T(8,128)(2,1)}), bf16[2048,32]{0,1:T(8,128)(2,1)}) %all-reduce.2.cloned.1.call-update) | async-done | bytes 131088 | tf_op jit(solution)/shard_map/while/body/eval_jaxpr/psum | solution.py:32
  194.0 22.3 %psum.26 = f32[32,32]{0,1:T(8,128)S(1)} all-reduce(f32[32,32]{0,1:T(8,128)S(1)} %fusion.35), channel_id=1, replica_groups=mesh['samp'=4,'pix'=8] {'pix'}, use_global_device_ids=true, to_apply=%region_3.0 | all-reduce | flops 1024 | bytes 8192 | tf_op jit(solution)/shard_map/while/body/eval_jaxpr/psum | solution.py:33
  216.4 2.9 cholesky.58
  225.1 23.6 %psum.24 = bf16[512,32]{1,0:T(8,128)(2,1)S(1)} all-reduce(bf16[512,32]{1,0:T(8,128)(2,1)S(1)} %convolution_convert_fusion.3), channel_id=1, replica_groups=mesh['samp'=4,'pix'=8] {'pix'}, use_global_device_ids=true, to_apply=%region_1.0 | all-reduce | flops 16384 | bytes 65536 | tf_op jit(solution)/shard_map/while/body/eval_jaxpr/psum | solution.py:28
  249.9 33.6 %all-reduce.2.cloned.1.call-done = bf16[2048,32]{0,1:T(8,128)(2,1)} async-done(((bf16[2048,32]{0,1:T(8,128)(2,1)}), bf16[2048,32]{0,1:T(8,128)(2,1)}) %all-reduce.2.cloned.1.call-update) | async-done | bytes 131088 | tf_op jit(solution)/shard_map/while/body/eval_jaxpr/psum | solution.py:32
  284.6 22.3 %psum.26 = f32[32,32]{0,1:T(8,128)S(1)} all-reduce(f32[32,32]{0,1:T(8,128)S(1)} %fusion.35), channel_id=1, replica_groups=mesh['samp'=4,'pix'=8] {'pix'}, use_global_device_ids=true, to_apply=%region_3.0 | all-reduce | flops 1024 | bytes 8192 | tf_op jit(solution)/shard_map/while/body/eval_jaxpr/psum | solution.py:33
  307.0 2.9 cholesky.58
  311.3 2.4 custom-call.7
  315.8 23.6 %psum.24 = bf16[512,32]{1,0:T(8,128)(2,1)S(1)} all-reduce(bf16[512,32]{1,0:T(8,128)(2,1)S(1)} %convolution_convert_fusion.3), channel_id=1, replica_groups=mesh['samp'=4,'pix'=8] {'pix'}, use_global_device_ids=true, to_apply=%region_1.0 | all-reduce | flops 16384 | bytes 65536 | tf_op jit(solution)/shard_map/while/body/eval_jaxpr/psum | solution.py:28
  340.5 33.6 %all-reduce.2.cloned.1.call-done = bf16[2048,32]{0,1:T(8,128)(2,1)} async-done(((bf16[2048,32]{0,1:T(8,128)(2,1)}), bf16[2048,32]{0,1:T(8,128)(2,1)}) %all-reduce.2.cloned.1.call-update) | async-done | bytes 131088 | tf_op jit(solution)/shard_map/while/body/eval_jaxpr/psum | solution.py:32
  375.3 22.3 %psum.26 = f32[32,32]{0,1:T(8,128)S(1)} all-reduce(f32[32,32]{0,1:T(8,128)S(1)} %fusion.35), channel_id=1, replica_groups=mesh['samp'=4,'pix'=8] {'pix'}, use_global_device_ids=true, to_apply=%region_3.0 | all-reduce | flops 1024 | bytes 8192 | tf_op jit(solution)/shard_map/while/body/eval_jaxpr/psum | solution.py:33
  397.7 2.9 cholesky.58
  406.4 23.6 %psum.24 = bf16[512,32]{1,0:T(8,128)(2,1)S(1)} all-reduce(bf16[512,32]{1,0:T(8,128)(2,1)S(1)} %convolution_convert_fusion.3), channel_id=1, replica_groups=mesh['samp'=4,'pix'=8] {'pix'}, use_global_device_ids=true, to_apply=%region_1.0 | all-reduce | flops 16384 | bytes 65536 | tf_op jit(solution)/shard_map/while/body/eval_jaxpr/psum | solution.py:28
  431.2 33.6 %all-reduce.2.cloned.1.call-done = bf16[2048,32]{0,1:T(8,128)(2,1)} async-done(((bf16[2048,32]{0,1:T(8,128)(2,1)}), bf16[2048,32]{0,1:T(8,128)(2,1)}) %all-reduce.2.cloned.1.call-update) | async-done | bytes 131088 | tf_op jit(solution)/shard_map/while/body/eval_jaxpr/psum | solution.py:32
  465.9 22.3 %psum.26 = f32[32,32]{0,1:T(8,128)S(1)} all-reduce(f32[32,32]{0,1:T(8,128)S(1)} %fusion.35), channel_id=1, replica_groups=mesh['samp'=4,'pix'=8] {'pix'}, use_global_device_ids=true, to_apply=%region_3.0 | all-reduce | flops 1024 | bytes 8192 | tf_op jit(solution)/shard_map/while/body/eval_jaxpr/psum | solution.py:33
  488.3 2.9 cholesky.58
  492.6 2.4 custom-call.7
  497.0 23.6 %psum.24 = bf16[512,32]{1,0:T(8,128)(2,1)S(1)} all-reduce(bf16[512,32]{1,0:T(8,128)(2,1)S(1)} %convolution_convert_fusion.3), channel_id=1, replica_groups=mesh['samp'=4,'pix'=8] {'pix'}, use_global_device_ids=true, to_apply=%region_1.0 | all-reduce | flops 16384 | bytes 65536 | tf_op jit(solution)/shard_map/while/body/eval_jaxpr/psum | solution.py:28
  521.8 33.6 %all-reduce.2.cloned.1.call-done = bf16[2048,32]{0,1:T(8,128)(2,1)} async-done(((bf16[2048,32]{0,1:T(8,128)(2,1)}), bf16[2048,32]{0,1:T(8,128)(2,1)}) %all-reduce.2.cloned.1.call-update) | async-done | bytes 131088 | tf_op jit(solution)/shard_map/while/body/eval_jaxpr/psum | solution.py:32
  556.5 22.3 %psum.26 = f32[32,32]{0,1:T(8,128)S(1)} all-reduce(f32[32,32]{0,1:T(8,128)S(1)} %fusion.35), channel_id=1, replica_groups=mesh['samp'=4,'pix'=8] {'pix'}, use_global_device_ids=true, to_apply=%region_3.0 | all-reduce | flops 1024 | bytes 8192 | tf_op jit(solution)/shard_map/while/body/eval_jaxpr/psum | solution.py:33
  578.9 2.9 cholesky.58
  587.6 23.6 %psum.24 = bf16[512,32]{1,0:T(8,128)(2,1)S(1)} all-reduce(bf16[512,32]{1,0:T(8,128)(2,1)S(1)} %convolution_convert_fusion.3), channel_id=1, replica_groups=mesh['samp'=4,'pix'=8] {'pix'}, use_global_device_ids=true, to_apply=%region_1.0 | all-reduce | flops 16384 | bytes 65536 | tf_op jit(solution)/shard_map/while/body/eval_jaxpr/psum | solution.py:28
  612.4 33.6 %all-reduce.2.cloned.1.call-done = bf16[2048,32]{0,1:T(8,128)(2,1)} async-done(((bf16[2048,32]{0,1:T(8,128)(2,1)}), bf16[2048,32]{0,1:T(8,128)(2,1)}) %all-reduce.2.cloned.1.call-update) | async-done | bytes 131088 | tf_op jit(solution)/shard_map/while/body/eval_jaxpr/psum | solution.py:32
  647.2 22.3 %psum.26 = f32[32,32]{0,1:T(8,128)S(1)} all-reduce(f32[32,32]{0,1:T(8,128)S(1)} %fusion.35), channel_id=1, replica_groups=mesh['samp'=4,'pix'=8] {'pix'}, use_global_device_ids=true, to_apply=%region_3.0 | all-reduce | flops 1024 | bytes 8192 | tf_op jit(solution)/shard_map/while/body/eval_jaxpr/psum | solution.py:33
  669.6 2.9 cholesky.58
  678.3 23.6 %psum.24 = bf16[512,32]{1,0:T(8,128)(2,1)S(1)} all-reduce(bf16[512,32]{1,0:T(8,128)(2,1)S(1)} %convolution_convert_fusion.3), channel_id=1, replica_groups=mesh['samp'=4,'pix'=8] {'pix'}, use_global_device_ids=true, to_apply=%region_1.0 | all-reduce | flops 16384 | bytes 65536 | tf_op jit(solution)/shard_map/while/body/eval_jaxpr/psum | solution.py:28
  703.0 33.6 %all-reduce.2.cloned.1.call-done = bf16[2048,32]{0,1:T(8,128)(2,1)} async-done(((bf16[2048,32]{0,1:T(8,128)(2,1)}), bf16[2048,32]{0,1:T(8,128)(2,1)}) %all-reduce.2.cloned.1.call-update) | async-done | bytes 131088 | tf_op jit(solution)/shard_map/while/body/eval_jaxpr/psum | solution.py:32
  737.8 22.3 %psum.26 = f32[32,32]{0,1:T(8,128)S(1)} all-reduce(f32[32,32]{0,1:T(8,128)S(1)} %fusion.35), channel_id=1, replica_groups=mesh['samp'=4,'pix'=8] {'pix'}, use_global_device_ids=true, to_apply=%region_3.0 | all-reduce | flops 1024 | bytes 8192 | tf_op jit(solution)/shard_map/while/body/eval_jaxpr/psum | solution.py:33
  760.2 2.9 cholesky.58
  764.4 2.4 custom-call.7
  768.9 23.6 %psum.24 = bf16[512,32]{1,0:T(8,128)(2,1)S(1)} all-reduce(bf16[512,32]{1,0:T(8,128)(2,1)S(1)} %convolution_convert_fusion.3), channel_id=1, replica_groups=mesh['samp'=4,'pix'=8] {'pix'}, use_global_device_ids=true, to_apply=%region_1.0 | all-reduce | flops 16384 | bytes 65536 | tf_op jit(solution)/shard_map/while/body/eval_jaxpr/psum | solution.py:28
  793.7 33.6 %all-reduce.2.cloned.1.call-done = bf16[2048,32]{0,1:T(8,128)(2,1)} async-done(((bf16[2048,32]{0,1:T(8,128)(2,1)}), bf16[2048,32]{0,1:T(8,128)(2,1)}) %all-reduce.2.cloned.1.call-update) | async-done | bytes 131088 | tf_op jit(solution)/shard_map/while/body/eval_jaxpr/psum | solution.py:32
  828.4 22.3 %psum.26 = f32[32,32]{0,1:T(8,128)S(1)} all-reduce(f32[32,32]{0,1:T(8,128)S(1)} %fusion.35), channel_id=1, replica_groups=mesh['samp'=4,'pix'=8] {'pix'}, use_global_device_ids=true, to_apply=%region_3.0 | all-reduce | flops 1024 | bytes 8192 | tf_op jit(solution)/shard_map/while/body/eval_jaxpr/psum | solution.py:33
  850.8 2.9 cholesky.58
  859.5 23.6 %psum.24 = bf16[512,32]{1,0:T(8,128)(2,1)S(1)} all-reduce(bf16[512,32]{1,0:T(8,128)(2,1)S(1)} %convolution_convert_fusion.3), channel_id=1, replica_groups=mesh['samp'=4,'pix'=8] {'pix'}, use_global_device_ids=true, to_apply=%region_1.0 | all-reduce | flops 16384 | bytes 65536 | tf_op jit(solution)/shard_map/while/body/eval_jaxpr/psum | solution.py:28
  884.3 33.6 %all-reduce.2.cloned.1.call-done = bf16[2048,32]{0,1:T(8,128)(2,1)} async-done(((bf16[2048,32]{0,1:T(8,128)(2,1)}), bf16[2048,32]{0,1:T(8,128)(2,1)}) %all-reduce.2.cloned.1.call-update) | async-done | bytes 131088 | tf_op jit(solution)/shard_map/while/body/eval_jaxpr/psum | solution.py:32
  919.0 22.3 %psum.26 = f32[32,32]{0,1:T(8,128)S(1)} all-reduce(f32[32,32]{0,1:T(8,128)S(1)} %fusion.35), channel_id=1, replica_groups=mesh['samp'=4,'pix'=8] {'pix'}, use_global_device_ids=true, to_apply=%region_3.0 | all-reduce | flops 1024 | bytes 8192 | tf_op jit(solution)/shard_map/while/body/eval_jaxpr/psum | solution.py:33
  941.4 2.9 cholesky.58
  (119 shorter events, 72.1 us)
Async XLA Ops:
  9.7 31.9 %copy-start = (f32[2048,32]{0,1:T(8,128)S(1)}, f32[2048,32]{0,1:T(8,128)}, u32[]{:S(2)}) copy-start(f32[2048,32]{0,1:T(8,128)} %param.5) | copy-start | bytes 786436
  9.7 31.9 %all-to-all-start = ((bf16[64,8,2048]{2,0,1:T(8,128)(2,1)}), bf16[64,8,2048]{2,0,1:T(8,128)(2,1)S(1)}, u32[]{:S(2)}, u32[]{:S(2)}) async-start(bf16[64,8,2048]{2,0,1:T(8,128)(2,1)} %bitcast.45), calls=%async_computation | async-start | bytes 4194304 | tf_op jit(solution)/shard_map/all_to_all | solution.py:22
  41.7 60.6 %all-reduce.2.cloned.1.call-start = ((), (), s32[]{:S(2)}) async-start(), calls=%async_computation.1 | async-start | bytes 262144 | tf_op jit(solution)/shard_map/while/body/eval_jaxpr/psum | solution.py:32
  133.8 59.1 %all-reduce.2.cloned.1.call-start = ((), (), s32[]{:S(2)}) async-start(), calls=%async_computation.1 | async-start | bytes 262144 | tf_op jit(solution)/shard_map/while/body/eval_jaxpr/psum | solution.py:32
  224.4 59.1 %all-reduce.2.cloned.1.call-start = ((), (), s32[]{:S(2)}) async-start(), calls=%async_computation.1 | async-start | bytes 262144 | tf_op jit(solution)/shard_map/while/body/eval_jaxpr/psum | solution.py:32
  315.0 59.1 %all-reduce.2.cloned.1.call-start = ((), (), s32[]{:S(2)}) async-start(), calls=%async_computation.1 | async-start | bytes 262144 | tf_op jit(solution)/shard_map/while/body/eval_jaxpr/psum | solution.py:32
  405.6 59.1 %all-reduce.2.cloned.1.call-start = ((), (), s32[]{:S(2)}) async-start(), calls=%async_computation.1 | async-start | bytes 262144 | tf_op jit(solution)/shard_map/while/body/eval_jaxpr/psum | solution.py:32
  496.3 59.1 %all-reduce.2.cloned.1.call-start = ((), (), s32[]{:S(2)}) async-start(), calls=%async_computation.1 | async-start | bytes 262144 | tf_op jit(solution)/shard_map/while/body/eval_jaxpr/psum | solution.py:32
  586.9 59.1 %all-reduce.2.cloned.1.call-start = ((), (), s32[]{:S(2)}) async-start(), calls=%async_computation.1 | async-start | bytes 262144 | tf_op jit(solution)/shard_map/while/body/eval_jaxpr/psum | solution.py:32
  677.5 59.1 %all-reduce.2.cloned.1.call-start = ((), (), s32[]{:S(2)}) async-start(), calls=%async_computation.1 | async-start | bytes 262144 | tf_op jit(solution)/shard_map/while/body/eval_jaxpr/psum | solution.py:32
  768.1 59.1 %all-reduce.2.cloned.1.call-start = ((), (), s32[]{:S(2)}) async-start(), calls=%async_computation.1 | async-start | bytes 262144 | tf_op jit(solution)/shard_map/while/body/eval_jaxpr/psum | solution.py:32
  858.8 59.1 %all-reduce.2.cloned.1.call-start = ((), (), s32[]{:S(2)}) async-start(), calls=%async_computation.1 | async-start | bytes 262144 | tf_op jit(solution)/shard_map/while/body/eval_jaxpr/psum | solution.py:32
Sparse Core Ops, SparseCore 0:
  67.3 34.8 all-reduce.1
  159.4 33.4 all-reduce.1
  250.0 33.4 all-reduce.1
  340.7 33.4 all-reduce.1
  431.3 33.4 all-reduce.1
  521.9 33.4 all-reduce.1
  612.5 33.4 all-reduce.1
  703.2 33.4 all-reduce.1
  793.8 33.4 all-reduce.1
  884.4 33.4 all-reduce.1
where the time goes:
time: 958 us; the launch traced here: 957 us
  blocking collectives  459 us (48%)
  waiting for transfers between devices  364 us (38%)
  other arithmetic  67.6 us (7%)
  matrix products  42.2 us (4%)
  between operations  13.4 us (1%)
    psum x10, waiting for transfers between devices, sweep(): summed = lax.psum(back.astype(jnp.bfloat16), 'samp').astype(jnp.float32)  337 us
    psum x10, blocking collectives, sweep(): proj = lax.psum(partial_value.astype(jnp.bfloat16), 'pix')  236 us
    psum x10, blocking collectives, sweep(): gram = lax.psum(gram_local(summed), 'pix')  223 us
    another operation x30, other arithmetic, orthonormal(): lower = jnp.linalg.cholesky(gram)  35.9 us
    another operation x20, other arithmetic, orthonormal(): lax.linalg.triangular_solve(lower, back, left_side=False, lower=True, tra...  30.9 us
    all_to_all x1, waiting for transfers between devices, local(): lax.all_to_all(stamps, 'pix', split_axis=1, concat_axis=0, tiled=True)  26.6 us
  transfers between devices with their start and end apart: 11, of which 11 were waited for; matrix products, arithmetic and copies ran while one was open for 0% of the time, Pallas kernels for 0%

commit v1 on v0

v1 whole, which is shorter than its diff:
```python
import functools
import math

import jax
import jax.numpy as jnp
from jax import lax
from jax.experimental import pallas as pl
from jax.experimental.pallas import tpu as pltpu
from jax.sharding import PartitionSpec as P

ITERS = 10
LANES = 128
SAMPLE_SPACE_LIMIT = 4096
INTERPRET = False
F32 = jnp.float32
BF16 = jnp.bfloat16

NN = (((1,), (0,)), ((), ()))
NT = (((1,), (1,)), ((), ()))
TN = (((0,), (0,)), ((), ()))


def orthonormal(back, gram):
    lower = jnp.linalg.cholesky(gram)
    return lax.linalg.triangular_solve(lower, back, left_side=False, lower=True, transpose_a=True)


def pixel_space(stamps, start_panel):
    block = lax.all_to_all(stamps, "pix", split_axis=1, concat_axis=0, tiled=True)

    def sweep(step, panel):
        partial_value = jnp.dot(block, panel.astype(BF16), preferred_element_type=F32)
        proj = lax.psum(partial_value.astype(BF16), "pix")
        back = lax.dot_general(block, proj, TN, preferred_element_type=F32)
        summed = lax.psum(back.astype(BF16), "samp").astype(F32)
        gram = lax.psum(jnp.dot(summed.T, summed, precision=lax.Precision.HIGHEST), "pix")
        return orthonormal(summed, gram)

    panel = lax.fori_loop(0, ITERS, sweep, start_panel)
    return panel * math.sqrt(start_panel.shape[0] * lax.axis_size("pix"))


def dot(a, b, dims):
    return lax.dot_general(a, b, dims, preferred_element_type=F32)


def split3(x):
    hi = x.astype(BF16)
    rest = x - hi.astype(F32)
    mid = rest.astype(BF16)
    lo = (rest - mid.astype(F32)).astype(BF16)
    return hi, mid, lo


def kernel_call(body, out_shape, **kw):
    return pl.pallas_call(body, out_shape=out_shape, interpret=INTERPRET, **kw)


def vmem(n=1):
    return [pl.BlockSpec(memory_space=pltpu.VMEM)] * n


def smem():
    return pl.BlockSpec(memory_space=pltpu.SMEM)


def inverse_lower(gram):
    k = gram.shape[0]
    lane = lax.broadcasted_iota(jnp.int32, gram.shape, 1)
    row = lax.broadcasted_iota(jnp.int32, gram.shape, 0)
    m = jnp.where(lane < k, gram, jnp.where(lane == row + k, 1.0, 0.0))
    for j in range(k):
        col = jnp.broadcast_to(m[:, j : j + 1], m.shape)
        scale = lax.rsqrt(jnp.broadcast_to(col[j : j + 1, :], m.shape))
        pivot = jnp.broadcast_to(m[j : j + 1, :], m.shape) * scale
        m = jnp.where(row > j, m - (col * scale) * pivot, jnp.where(row == j, pivot, m))
    return pltpu.roll(m, LANES - k, 1)


def lane_sum3(x, k):
    return x + pltpu.roll(x, LANES - k, 1) + pltpu.roll(x, LANES - 2 * k, 1)


def gram_of(left, parts, zeros):
    k = left.shape[0]
    stack = jnp.concatenate(list(parts) + [zeros], axis=0)
    return lane_sum3(dot(left, stack, NT), k)


def apply_lower(inv, parts, zeros):
    k = inv.shape[0]
    lane = lax.broadcasted_iota(jnp.int32, inv.shape, 1)
    inv = jnp.where(lane < k, inv, 0.0)
    inv = inv + pltpu.roll(inv, k, 1)
    inv = inv + pltpu.roll(inv, 2 * k, 1)
    h1, h2, h3 = [h.astype(F32) for h in split3(inv)]
    first = jnp.where(lane < 3 * k, h1, h2)
    second = jnp.where(lane < k, h2, jnp.where(lane < 2 * k, h3, 0.0))
    left = jnp.concatenate([first, second], axis=1).astype(BF16)
    y1, y2, y3 = parts
    right = jnp.concatenate([y1, y2, y3, y1, y2, y1, zeros, zeros], axis=0)
    return dot(left, right, NN)


def basis_kernel(p0_ref, q_ref):
    p0 = p0_ref[...]
    zeros = jnp.zeros_like(p0)
    gram = gram_of(p0, (p0, zeros, zeros), zeros)
    q_ref[...] = apply_lower(inverse_lower(gram), (p0, zeros, zeros), zeros)


def weighted_rows(q, m, w):
    return w - 0.5 * m


def form_kernel(core_ref, own_ref, other_ref, q_ref, out_ref, own_ext, other_ext, left, right):
    n = own_ref.shape[0]
    k = q_ref.shape[0]
    rows, width = out_ref.shape
    width -= LANES
    bs = width - n // 2
    core = core_ref[0]
    q = q_ref[...]
    zeros = jnp.zeros(q.shape, BF16)

    own_ext[:n] = own_ref[...]
    own_ext[n:] = own_ref[: n // 2]
    other_ext[:n] = other_ref[...]
    other_ext[n:] = other_ref[: n // 2]

    q3 = split3(q)
    qs = jnp.concatenate(q3, axis=0)
    w = jnp.zeros(q.shape, F32)
    m = jnp.zeros((k, LANES), F32)
    for ref in (own_ref, other_ref):
        t3 = dot(qs, ref[...], NN)
        t = t3[:k] + t3[k : 2 * k] + t3[2 * k :]
        ts = split3(t)
        w3 = dot(jnp.concatenate(ts, axis=0), ref[...], NT)
        w += w3[:k] + w3[k : 2 * k] + w3[2 * k :]
    ws = split3(w)
    wst = jnp.concatenate(list(ws) + [zeros], axis=0)
    q1, q2, q3_ = q3
    m = lane_sum3(dot(q1, wst, NT) + dot(q2, wst, NT) + dot(q3_, wst, NT), k)
    w = w - 0.5 * apply_lower(m, q3, zeros)
    w1, w2, w3 = split3(w)

    u1 = jnp.concatenate([q1, w1], axis=0)
    u2 = jnp.concatenate([q2, w2], axis=0)
    u3 = jnp.concatenate([q3_, w3], axis=0)
    v1 = jnp.concatenate([w1, q1], axis=0)
    v2 = jnp.concatenate([w2, q2], axis=0)
    v3 = jnp.concatenate([w3, q3_], axis=0)
    left[...] = jnp.concatenate([u1, u1, u1, u2, u2, u3], axis=0)
    vs = jnp.concatenate([v1, v2, v3, v1, v2, v1], axis=0)
    right[:, :n] = vs
    right[:, n:] = vs[:, : n // 2]
    wt = jnp.concatenate([w1, w2, w3, zeros], axis=0).astype(F32)
    del wt

    def step(i, _):
        at = pl.multiple_of(core * rows + i * bs, bs)
        to = pl.multiple_of(i * bs, bs)
        s = dot(own_ext[pl.ds(at, bs), :], own_ext[pl.ds(at, width), :], NT)
        s += dot(other_ext[pl.ds(at, bs), :], other_ext[pl.ds(at, width), :], NT)
        s -= dot(left[:, pl.ds(at, bs)], right[:, pl.ds(at, width)], TN)
        out_ref[pl.ds(to, bs), :width] = s.astype(BF16)
        wb = jnp.concatenate(
            [
                right[:k, pl.ds(at, bs)],
                right[2 * k : 3 * k, pl.ds(at, bs)],
                right[4 * k : 5 * k, pl.ds(at, bs)],
                jnp.zeros((LANES - 3 * k, bs), BF16),
            ],
            axis=0,
        ).astype(F32)
        out_ref[pl.ds(to, bs), width:] = wb.T.astype(BF16)
        return 0

    lax.fori_loop(0, rows // bs, step, 0)


def add_kernel(k, a_ref, b_ref, o_ref):
    width = a_ref.shape[1] - LANES
    o_ref[:, :width] = (a_ref[:, :width].astype(F32) + b_ref[:, :width].astype(F32)).astype(BF16)
    x = lane_sum3(a_ref[:, width:].astype(F32), k) + lane_sum3(b_ref[:, width:].astype(F32), k)
    lane = lax.broadcasted_iota(jnp.int32, x.shape, 1)
    h1, h2, h3 = [h.astype(F32) for h in split3(x)]
    packed = jnp.where(
        lane < k,
        h1,
        jnp.where(
            lane < 2 * k,
            pltpu.roll(h2, k, 1),
            jnp.where(lane < 3 * k, pltpu.roll(h3, 2 * k, 1), 0.0),
        ),
    )
    o_ref[:, width:] = packed.astype(BF16)


def add_shares(a, b, k):
    return kernel_call(
        functools.partial(add_kernel, k),
        jax.ShapeDtypeStruct(a.shape, BF16),
        in_specs=vmem(2),
        out_specs=vmem()[0],
    )(a, b)


def iterate_kernel(index_ref, share_ref, q_ref, p0_ref, p_ref, inv_ref, full, u, v):
    n = share_ref.shape[0]
    k = q_ref.shape[0]
    width = share_ref.shape[1] - LANES
    bs = width - n // 2
    nb = n // bs

    def unpack(r, _):
        i = index_ref[r]
        frm = pl.multiple_of(r * bs, bs)
        to = pl.multiple_of(i * bs, bs)
        for d in range(nb // 2 + 1):
            part = share_ref[pl.ds(frm, bs), d * bs : (d + 1) * bs]
            at = pl.multiple_of(lax.rem(i + d, nb) * bs, bs)
            full[pl.ds(to, bs), pl.ds(at, bs)] = part
            if 0 < d < nb // 2:
                full[pl.ds(at, bs), pl.ds(to, bs)] = part.T
        wb = share_ref[pl.ds(frm, bs), width:].astype(F32).T
        w = wb[:k] + wb[k : 2 * k] + wb[2 * k : 3 * k]
        q = q_ref[:, pl.ds(to, bs)]
        us = split3(jnp.concatenate([w, q], axis=0))
        vs = split3(jnp.concatenate([q, w], axis=0))
        u[:, pl.ds(to, bs)] = jnp.concatenate(list(us) + [jnp.zeros((2 * k, bs), BF16)], axis=0)
        v1, v2, v3 = vs
        v[:, pl.ds(to, bs)] = jnp.concatenate([v1, v2, v3, v1, v2, v1], axis=0)
        return 0

    lax.fori_loop(0, nb, unpack, 0)

    zeros = jnp.zeros((k, n), BF16)
    lane = lax.broadcasted_iota(jnp.int32, (k, LANES), 1)

    def product(p):
        t = dot(p, u[...], NT)
        t = t[:, :LANES] + t[:, LANES:]
        t = t + pltpu.roll(t, 2 * k, 1)
        h1, h2, h3 = [h.astype(F32) for h in split3(t)]
        low = lane < 2 * k
        ts = jnp.concatenate([h1, jnp.where(low, h1, h2), jnp.where(low, h2, h3)], axis=1).astype(BF16)
        y = dot(p, full[...], NN) + dot(ts, v[...], NN)
        return split3(y)

    def sweep(step, p):
        parts = product(p)
        inv = inverse_lower(gram_of(p, parts, zeros))
        return apply_lower(inv, parts, zeros).astype(BF16)

    p = lax.fori_loop(0, ITERS - 1, sweep, p0_ref[...])
    p_ref[...] = p
    inv_ref[...] = inverse_lower(gram_of(p, product(p), zeros))


def finish_kernel(scale, p_ref, inv_ref, block_ref, o_ref):
    k, n = p_ref.shape
    back = dot(p_ref[...], block_ref[...], NN)
    zeros = jnp.zeros(back.shape, BF16)
    o_ref[...] = apply_lower(inv_ref[...], split3(back), zeros) * scale


def flip(x, axes, perm):
    return lax.ppermute(x, axes, perm)


def ordered(own, recv, bit, axis=0):
    return jnp.where(
        bit == 0,
        jnp.concatenate([own, recv], axis=axis),
        jnp.concatenate([recv, own], axis=axis),
    )


def halves(x, bit):
    h = x.shape[0] // 2
    keep = lax.dynamic_slice_in_dim(x, bit * h, h, 0)
    send = lax.dynamic_slice_in_dim(x, (1 - bit) * h, h, 0)
    return keep, send


def sample_space(stamps, start_panel):
    pix = lax.axis_size("pix")
    samp = lax.axis_size("samp")
    n = stamps.shape[0] * pix * samp
    k = start_panel.shape[1]
    scale = math.sqrt(start_panel.shape[0] * pix)
    p = lax.axis_index("pix")
    s = lax.axis_index("samp")
    xor_pix = lambda b: [(i, i ^ b) for i in range(pix)]
    xor_samp = lambda b: [(i, i ^ b) for i in range(samp)]

    block = lax.all_to_all(stamps, ("pix", "samp"), split_axis=1, concat_axis=0, tiled=True)

    low = start_panel.astype(BF16).T
    for b in (1, 2, 4):
        low = ordered(low, flip(low, "pix", xor_pix(b)), p & b, axis=1)
    proj = dot(low, stamps, NT).astype(BF16)
    for b in (1, 2):
        proj = ordered(proj, flip(proj, "samp", xor_samp(b)), s & b, axis=1)
    for b in (1, 2, 4):
        proj = ordered(proj, flip(proj, "pix", xor_pix(b)), p & b, axis=1)
    q = kernel_call(
        basis_kernel, jax.ShapeDtypeStruct((k, n), F32), in_specs=vmem(), out_specs=vmem()[0]
    )(proj)

    core = p & 1
    x, y = (p >> 1) & 1, (p >> 2) & 1
    other = flip(block, "pix", xor_pix(1))
    bs = 2 * stamps.shape[0]
    width = n // 2 + bs
    px = block.shape[1]
    share = kernel_call(
        form_kernel,
        jax.ShapeDtypeStruct((n // 2, width + LANES), BF16),
        in_specs=[smem()] + vmem(3),
        out_specs=vmem()[0],
        scratch_shapes=[
            pltpu.VMEM((n + n // 2, px), BF16),
            pltpu.VMEM((n + n // 2, px), BF16),
            pltpu.VMEM((12 * k, n), BF16),
            pltpu.VMEM((12 * k, n + n // 2), BF16),
        ],
    )(core[None], block, other, q)

    first = [(i, i ^ (2 if i % 2 == 0 else 4)) for i in range(pix)]
    second = [(i, i ^ (4 if i % 2 == 0 else 2)) for i in range(pix)]
    bit_a = jnp.where(core == 0, x, y)
    bit_b = jnp.where(core == 0, y, x)
    z0, z1 = s & 1, (s >> 1) & 1
    stages = (
        ("pix", first, bit_a),
        ("pix", second, bit_b),
        ("samp", xor_samp(1), z0),
        ("samp", xor_samp(2), z1),
    )
    for axis, perm, bit in stages:
        keep, send = halves(share, bit)
        share = add_shares(keep, flip(send, axis, perm), k)

    share = ordered(share, flip(share, "samp", xor_samp(2)), z1)
    for axis, perm in (("samp", xor_samp(1)), ("pix", second), ("pix", first), ("pix", xor_pix(1))):
        share = jnp.concatenate([share, flip(share, axis, perm)], axis=0)
    at = jnp.arange(n // bs, dtype=jnp.int32)
    c_of = core ^ ((at >> 3) & 1)
    a_of = jnp.where(c_of == 0, x, y) ^ ((at >> 2) & 1)
    b_of = jnp.where(c_of == 0, y, x) ^ ((at >> 1) & 1)
    index = c_of * 8 + a_of * 4 + b_of * 2 + (z0 ^ (at & 1))

    proj, inv = kernel_call(
        iterate_kernel,
        (jax.ShapeDtypeStruct((k, n), BF16), jax.ShapeDtypeStruct((k, LANES), F32)),
        in_specs=[smem()] + vmem(3),
        out_specs=tuple(vmem(2)),
        scratch_shapes=[
            pltpu.VMEM((n, n), BF16),
            pltpu.VMEM((8 * k, n), BF16),
            pltpu.VMEM((12 * k, n), BF16),
        ],
    )(index, share, q, proj)

    mine = kernel_call(
        functools.partial(finish_kernel, scale),
        jax.ShapeDtypeStruct((k, px), F32),
        in_specs=vmem(3),
        out_specs=vmem()[0],
    )(proj, inv, block)
    for b in (1, 2):
        mine = ordered(mine, flip(mine, "samp", xor_samp(b)), s & b, axis=1)
    return mine.T


def solution(mesh):
    pix, samp = mesh.shape["pix"], mesh.shape["samp"]

    def local(stamps, start_panel):
        n = stamps.shape[0] * pix * samp
        k = start_panel.shape[1]
        if n <= SAMPLE_SPACE_LIMIT and (pix, samp) == (8, 4) and 4 * k == LANES:
            return sample_space(stamps, start_panel)
        return pixel_space(stamps, start_panel)

    return jax.shard_map(
        local,
        mesh=mesh,
        in_specs=(P(("samp", "pix"), None), P("pix", None)),
        out_specs=P("pix", None),
        check_vma=False,
    )
```

time: 958 us -> 340 us (0.35)
  blocking collectives: 459 us -> 0 us
  waiting for transfers between devices: 364 us -> 168 us
  Pallas kernels: 0 us -> 115 us
  other arithmetic: 67.6 us -> 5.4 us
  matrix products: 42.2 us -> 2.26 us
  starting transfers between devices: 5.7 us -> 29.1 us
  local copies, waits for them, and re-layouts: 3.93 us -> 19.7 us
  between operations: 13.4 us -> 0.12 us
    psum x20 -> x0, blocking collectives: 459 us -> none  [the longest x10 236 us: sweep(): proj = lax.psum(partial_value.astype(jnp.bfloat16), 'pix')]
    psum x10 -> x0, waiting for transfers between devices: 337 us -> none  [sweep(): summed = lax.psum(back.astype(jnp.bfloat16), 'samp').astype(jnp.float32)]
    ppermute x0 -> x20, waiting for transfers between devices: none -> 124 us  [flip(): return lax.ppermute(x, axes, perm)]
    pallas_call x0 -> x8, Pallas kernels: none -> 115 us  [the longest x1 79.8 us: sample_space(): kernel_call(iterate_kernel, (jax.ShapeDtypeStruct((k, n), BF16), jax.Shap...]
    another operation x50 -> x0, other arithmetic: 66.8 us -> none  [the longest x30 35.9 us: orthonormal(): lower = jnp.linalg.cholesky(gram)]
    dot_general x30 -> x1, matrix products: 29.7 us -> 2.26 us  [dot(): return lax.dot_general(a, b, dims, preferred_element_type=F32)]
    ppermute x0 -> x20, starting transfers between devices: none -> 21.8 us  [flip(): return lax.ppermute(x, axes, perm)]
    all_to_all x1, waiting for transfers between devices: 26.6 us -> 43.4 us  [sample_space(): lax.all_to_all(stamps, ('pix', 'samp'), split_axis=1, concat_axis=0, tile...]
  transfers between devices with their start and end apart: 11 -> 21, of which waited for: 11 -> 19; matrix products, arithmetic and copies ran while one was open for 0% -> 2% of each run, Pallas kernels for 0% -> 2%
where the time goes in v1:
time: 340 us
  waiting for transfers between devices  168 us (49%)
  Pallas kernels  115 us (34%)
  starting transfers between devices  29.1 us (9%)
  local copies, waits for them, and re-layouts  19.7 us (6%)
  other arithmetic  5.4 us (2%)
    ppermute x20, waiting for transfers between devices, flip(): return lax.ppermute(x, axes, perm)  124 us
    pallas_call x1, Pallas kernels, sample_space(): kernel_call(iterate_kernel, (jax.ShapeDtypeStruct((k, n), BF16), jax.Shap...  79.8 us
    all_to_all x1, waiting for transfers between devices, sample_space(): lax.all_to_all(stamps, ('pix', 'samp'), split_axis=1, concat_axis=0, tile...  43.4 us
    ppermute x20, starting transfers between devices, flip(): return lax.ppermute(x, axes, perm)  21.8 us
    pallas_call x1, Pallas kernels, sample_space(): kernel_call(form_kernel, jax.ShapeDtypeStruct((n // 2, width + LANES), BF...  16 us
    pallas_call x4, Pallas kernels, add_shares(): kernel_call(functools.partial(add_kernel, k), jax.ShapeDtypeStruct(a.shap...  10.2 us
    dynamic_slice x4, local copies, waits for them, and re-layouts, halves(): send = lax.dynamic_slice_in_dim(x, (1 - bit) * h, h, 0)  8.68 us
    all_to_all x1, starting transfers between devices, sample_space(): lax.all_to_all(stamps, ('pix', 'samp'), split_axis=1, concat_axis=0, tile...  7.33 us
  transfers between devices with their start and end apart: 21, of which 19 were waited for; matrix products, arithmetic and copies ran while one was open for 2% of the time, Pallas kernels for 2%

profile of v1, /device:TPU:0, one launch (start us, length us, event | category | flops | bytes accessed | tf_op | source)
XLA Modules:
  0.0 339.5 jit_solution(13753560688188519695)
XLA Ops:
  0.0 3.2 copy.6
  3.2 7.3 %all-to-all-start = ((bf16[64,32,512]{2,0,1:T(8,128)(2,1)}), bf16[64,32,512]{2,0,1:T(8,128)(2,1)S(1)}, u32[]{:S(2)}, u32[]{:S(2)}) async-start(bf16[64,32,512]{2,0,1:T(8,128)(2,1)} %bitcast.16), calls=%async_computation | async-start | bytes 4194304 | tf_op jit(solution)/shard_map/all_to_all | solution.py:299
  10.9 1.1 collective-permute-done.1
  12.1 1.8 collective-permute-start.2
  13.9 43.4 %all-to-all-done = bf16[64,32,512]{2,0,1:T(8,128)(2,1)S(1)} async-done(((bf16[64,32,512]{2,0,1:T(8,128)(2,1)}), bf16[64,32,512]{2,0,1:T(8,128)(2,1)S(1)}, u32[]{:S(2)}, u32[]{:S(2)}) %all-to-all-start) | async-done | bytes 2097184 | tf_op jit(solution)/shard_map/all_to_all | solution.py:299
  57.3 1.8 collective-permute-start
  59.3 1.6 collective-permute-start.3
  60.8 12.3 %collective-permute-done.3 = bf16[32,8192]{1,0:T(8,128)(2,1)S(1)} collective-permute-done((bf16[32,8192]{1,0:T(8,128)(2,1)S(1)}, bf16[32,8192]{1,0:T(8,128)(2,1)S(1)}, u32[]{:S(2)}, u32[]{:S(2)}) %collective-permute-start.3) | collective-permute-done | bytes 524320 | tf_op jit(solution)/shard_map/ppermute | solution.py:270
  73.2 2.3 convolution_convert_fusion
  75.4 2.5 collective-permute-start.4
  77.9 1.6 collective-permute-done.4
  79.7 1.1 collective-permute-start.5
  80.7 3.5 %collective-permute-done.5 = bf16[32,128]{1,0:T(8,128)(2,1)S(1)} collective-permute-done((bf16[32,128]{1,0:T(8,128)(2,1)S(1)}, bf16[32,128]{1,0:T(8,128)(2,1)S(1)}, u32[]{:S(2)}, u32[]{:S(2)}) %collective-permute-start.5) | collective-permute-done | bytes 8224 | tf_op jit(solution)/shard_map/ppermute | solution.py:270
  84.2 1.2 collective-permute-done.6
  85.4 1.2 collective-permute-start.7
  86.6 2.8 collective-permute-done.7
  89.4 1.1 collective-permute-start.8
  90.5 3.2 collective-permute-done.8
  94.4 6.4 %shard_map.28.q_ref = f32[32,2048]{1,0:T(8,128)} custom-call(bf16[32,2048]{1,0:T(8,128)(2,1)} %maximum_select_fusion.6.p0_ref), custom_call_target="tpu_custom_call" | custom-call | tf_op jit(solution)/shard_map/pallas_call | solution.py:309
  100.8 16.0 %shard_map.29 = bf16[1024,1280]{1,0:T(8,128)(2,1)} custom-call(s32[1]{0:T(128)} %bitcast.core_ref, bf16[2048,512]{1,0:T(8,128)(2,1)} %bitcast.14, bf16[2048,512]{1,0:T(8,128)(2,1)} %collective-permute-done.other_ref, f32[32,2048]{1,0:T(8,128)} %shard_map.28.q_ref), custom_call_target="tpu_custom_call" | custom-call | tf_op jit(solution)/shard_map/pallas_call | solution.py:319
  116.8 3.0 constant_dynamic-slice_fusion.6
  119.8 1.1 collective-permute-start.9
  120.9 16.5 %collective-permute-done.9.b_ref = bf16[512,1280]{1,0:T(8,128)(2,1)S(1)} collective-permute-done((bf16[512,1280]{1,0:T(8,128)(2,1)S(1)}, bf16[512,1280]{1,0:T(8,128)(2,1)S(1)}, u32[]{:S(2)}, u32[]{:S(2)}) %collective-permute-start.9) | collective-permute-done | bytes 1310752 | tf_op jit(solution)/shard_map/ppermute | solution.py:270
  138.5 3.7 %shard_map.30 = bf16[512,1280]{1,0:T(8,128)(2,1)} custom-call(bf16[512,1280]{1,0:T(8,128)(2,1)} %get-tuple-element.12.a_ref, bf16[512,1280]{1,0:T(8,128)(2,1)} %copy-done.1), custom_call_target="tpu_custom_call" | custom-call | tf_op jit(solution)/shard_map/pallas_call | solution.py:202
  142.2 2.2 constant_dynamic-slice_fusion.4
  145.4 9.5 %collective-permute-done.10.b_ref = bf16[256,1280]{1,0:T(8,128)(2,1)S(1)} collective-permute-done((bf16[256,1280]{1,0:T(8,128)(2,1)S(1)}, bf16[256,1280]{1,0:T(8,128)(2,1)S(1)}, u32[]{:S(2)}, u32[]{:S(2)}) %collective-permute-start.10) | collective-permute-done | bytes 655392 | tf_op jit(solution)/shard_map/ppermute | solution.py:270
  155.8 2.6 shard_map.31
  158.4 1.8 constant_dynamic-slice_fusion.2
  160.3 2.0 collective-permute-start.11
  162.3 5.1 %collective-permute-done.11.b_ref = bf16[128,1280]{1,0:T(8,128)(2,1)S(1)} collective-permute-done((bf16[128,1280]{1,0:T(8,128)(2,1)S(1)}, bf16[128,1280]{1,0:T(8,128)(2,1)S(1)}, u32[]{:S(2)}, u32[]{:S(2)}) %collective-permute-start.11) | collective-permute-done | bytes 327712 | tf_op jit(solution)/shard_map/ppermute | solution.py:270
  168.1 2.0 shard_map.32
  170.1 1.7 constant_dynamic-slice_fusion
  172.9 8.8 %collective-permute-done.12.b_ref = bf16[64,1280]{1,0:T(8,128)(2,1)S(1)} collective-permute-done((bf16[64,1280]{1,0:T(8,128)(2,1)S(1)}, bf16[64,1280]{1,0:T(8,128)(2,1)S(1)}, u32[]{:S(2)}, u32[]{:S(2)}) %collective-permute-start.12) | collective-permute-done | bytes 163872 | tf_op jit(solution)/shard_map/ppermute | solution.py:270
  182.3 1.8 shard_map.33
  184.2 7.7 %collective-permute-done.13 = bf16[64,1280]{1,0:T(8,128)(2,1)S(1)} collective-permute-done((bf16[64,1280]{1,0:T(8,128)(2,1)}, bf16[64,1280]{1,0:T(8,128)(2,1)S(1)}, u32[]{:S(2)}, u32[]{:S(2)}) %collective-permute-start.13) | collective-permute-done | bytes 163872 | tf_op jit(solution)/shard_map/ppermute | solution.py:270
  191.8 1.8 constant_dynamic-update-slice_fusion.4
  193.6 7.1 %collective-permute-done.14 = bf16[128,1280]{1,0:T(8,128)(2,1)S(1)} collective-permute-done((bf16[128,1280]{1,0:T(8,128)(2,1)S(1)}, bf16[128,1280]{1,0:T(8,128)(2,1)S(1)}, u32[]{:S(2)}, u32[]{:S(2)}) %collective-permute-start.14) | collective-permute-done | bytes 327712 | tf_op jit(solution)/shard_map/ppermute | solution.py:270
  200.7 1.8 collective-permute-start.15
  202.6 15.3 %collective-permute-done.15 = bf16[256,1280]{1,0:T(8,128)(2,1)S(1)} collective-permute-done((bf16[256,1280]{1,0:T(8,128)(2,1)S(1)}, bf16[256,1280]{1,0:T(8,128)(2,1)S(1)}, u32[]{:S(2)}, u32[]{:S(2)}) %collective-permute-start.15) | collective-permute-done | bytes 655392 | tf_op jit(solution)/shard_map/ppermute | solution.py:270
  218.0 2.3 collective-permute-start.16
  220.3 15.6 %collective-permute-done.16 = bf16[512,1280]{1,0:T(8,128)(2,1)S(1)} collective-permute-done((bf16[512,1280]{1,0:T(8,128)(2,1)S(1)}, bf16[512,1280]{1,0:T(8,128)(2,1)S(1)}, u32[]{:S(2)}, u32[]{:S(2)}) %collective-permute-start.16) | collective-permute-done | bytes 1310752 | tf_op jit(solution)/shard_map/ppermute | solution.py:270
  238.5 1.2 constant_dynamic-update-slice_fusion.1
  239.6 1.5 collective-permute-done.17
  241.1 1.7 constant_dynamic-update-slice_fusion.share_ref
  242.8 79.8 %shard_map.34 = (bf16[32,2048]{1,0:T(8,128)(2,1)}, f32[32,128]{1,0:T(8,128)}) custom-call(s32[16]{0:T(128)} %xor_add_fusion.index_ref, bf16[2048,1280]{1,0:T(8,128)(2,1)} %constant_dynamic-update-slice_fusion.share_ref, f32[32,2048]{1,0:T(8,128)} %shard_map.28.q_ref, bf16[32,2048]{1,0:T(8,128)(2,1)} %maximum_select_fusion.6.p0_ref), custom_call_target="tpu_custom_call" | custom-call | tf_op jit(solution)/shard_map/pallas_call | solution.py:356
  322.6 2.9 shard_map.35
  325.7 4.3 %collective-permute-done.18 = f32[32,512]{1,0:T(8,128)S(1)} collective-permute-done((f32[32,512]{1,0:T(8,128)}, f32[32,512]{1,0:T(8,128)S(1)}, u32[]{:S(2)}, u32[]{:S(2)}) %collective-permute-start.18) | collective-permute-done | bytes 65568 | tf_op jit(solution)/shard_map/ppermute | solution.py:270
  331.6 7.2 %collective-permute-done.19 = f32[32,1024]{1,0:T(8,128)S(1)} collective-permute-done((f32[32,1024]{1,0:T(8,128)S(1)}, f32[32,1024]{1,0:T(8,128)S(1)}, u32[]{:S(2)}, u32[]{:S(2)}) %collective-permute-start.19) | collective-permute-done | bytes 131104 | tf_op jit(solution)/shard_map/ppermute | solution.py:270
  (39 shorter events, 11.9 us)
Async XLA Ops:
  3.2 7.3 %copy-start.4 = (f32[2048,32]{0,1:T(8,128)S(1)}, f32[2048,32]{0,1:T(8,128)}, u32[]{:S(2)}) copy-start(f32[2048,32]{0,1:T(8,128)} %param.3) | copy-start | bytes 786436
  3.2 54.1 %all-to-all-start = ((bf16[64,32,512]{2,0,1:T(8,128)(2,1)}), bf16[64,32,512]{2,0,1:T(8,128)(2,1)S(1)}, u32[]{:S(2)}, u32[]{:S(2)}) async-start(bf16[64,32,512]{2,0,1:T(8,128)(2,1)} %bitcast.16), calls=%async_computation | async-start | bytes 4194304 | tf_op jit(solution)/shard_map/all_to_all | solution.py:299
  10.6 1.4 collective-permute-start.1
  12.1 47.0 %collective-permute-start.2 = (bf16[32,4096]{1,0:T(8,128)(2,1)S(1)}, bf16[32,4096]{1,0:T(8,128)(2,1)S(1)}, u32[]{:S(2)}, u32[]{:S(2)}) collective-permute-start(bf16[32,4096]{1,0:T(8,128)(2,1)S(1)} %maximum_select_fusion.4), channel_id=1, source_target_pairs={{0,2},{1,3},{2,0},{3,1},{4,6},{5,7},{6,4},{7,5},{8,10},{9,11},{10,... | collective-permute-start | bytes 786440 | tf_op jit(solution)/shard_map/ppermute | solution.py:270
  57.3 18.1 %copy-start = (bf16[64,32,512]{2,0,1:T(8,128)(2,1)}, bf16[64,32,512]{2,0,1:T(8,128)(2,1)S(1)}, u32[]{:S(2)}) copy-start(bf16[64,32,512]{2,0,1:T(8,128)(2,1)S(1)} %all-to-all-done) | copy-start | bytes 6291460
  57.3 43.5 %collective-permute-start = (bf16[2048,512]{1,0:T(8,128)(2,1)S(1)}, bf16[2048,512]{1,0:T(8,128)(2,1)}, u32[]{:S(2)}, u32[]{:S(2)}) collective-permute-start(bf16[2048,512]{1,0:T(8,128)(2,1)S(1)} %bitcast.13), channel_id=1, source_target_pairs={{0,1},{1,0},{2,3},{3,2},{4,5},{5,4},{6,7},{7,6},{8,9},{9,8},{10,11... | collective-permute-start | bytes 6291464 | tf_op jit(solution)/shard_map/ppermute | solution.py:270
  59.3 13.9 %collective-permute-start.3 = (bf16[32,8192]{1,0:T(8,128)(2,1)S(1)}, bf16[32,8192]{1,0:T(8,128)(2,1)S(1)}, u32[]{:S(2)}, u32[]{:S(2)}) collective-permute-start(bf16[32,8192]{1,0:T(8,128)(2,1)S(1)} %maximum_select_fusion.2), channel_id=1, source_target_pairs={{0,4},{1,5},{2,6},{3,7},{4,0},{5,1},{6,2},{7,3},{8,12},{9,13},{10,... | collective-permute-start | bytes 1572872 | tf_op jit(solution)/shard_map/ppermute | solution.py:270
  75.4 4.1 %collective-permute-start.4 = (bf16[32,64]{1,0:T(8,128)(2,1)S(1)}, bf16[32,64]{1,0:T(8,128)(2,1)S(1)}, u32[]{:S(2)}, u32[]{:S(2)}) collective-permute-start(bf16[32,64]{1,0:T(8,128)(2,1)S(1)} %convolution_convert_fusion), channel_id=1, source_target_pairs={{0,8},{8,0},{16,24},{24,16},{1,9},{9,1},{17,25},{25,17},{2,10},{10... | collective-permute-start | bytes 12296 | tf_op jit(solution)/shard_map/ppermute | solution.py:270
  79.7 4.6 %collective-permute-start.5 = (bf16[32,128]{1,0:T(8,128)(2,1)S(1)}, bf16[32,128]{1,0:T(8,128)(2,1)S(1)}, u32[]{:S(2)}, u32[]{:S(2)}) collective-permute-start(bf16[32,128]{1,0:T(8,128)(2,1)S(1)} %maximum_select_fusion.11), channel_id=1, source_target_pairs={{0,16},{8,24},{16,0},{24,8},{1,17},{9,25},{17,1},{25,9},{2,18},{10... | collective-permute-start | bytes 24584 | tf_op jit(solution)/shard_map/ppermute | solution.py:270
  84.2 1.2 collective-permute-start.6
  85.4 4.0 %collective-permute-start.7 = (bf16[32,512]{1,0:T(8,128)(2,1)S(1)}, bf16[32,512]{1,0:T(8,128)(2,1)S(1)}, u32[]{:S(2)}, u32[]{:S(2)}) collective-permute-start(bf16[32,512]{1,0:T(8,128)(2,1)S(1)} %maximum_select_fusion.9), channel_id=1, source_target_pairs={{0,2},{1,3},{2,0},{3,1},{4,6},{5,7},{6,4},{7,5},{8,10},{9,11},{10,... | collective-permute-start | bytes 98312 | tf_op jit(solution)/shard_map/ppermute | solution.py:270
  89.4 4.3 %collective-permute-start.8 = (bf16[32,1024]{1,0:T(8,128)(2,1)S(1)}, bf16[32,1024]{1,0:T(8,128)(2,1)S(1)}, u32[]{:S(2)}, u32[]{:S(2)}) collective-permute-start(bf16[32,1024]{1,0:T(8,128)(2,1)S(1)} %maximum_select_fusion.8), channel_id=1, source_target_pairs={{0,4},{1,5},{2,6},{3,7},{4,0},{5,1},{6,2},{7,3},{8,12},{9,13},{10,... | collective-permute-start | bytes 196616 | tf_op jit(solution)/shard_map/ppermute | solution.py:270
  119.8 17.6 %collective-permute-start.9 = (bf16[512,1280]{1,0:T(8,128)(2,1)S(1)}, bf16[512,1280]{1,0:T(8,128)(2,1)S(1)}, u32[]{:S(2)}, u32[]{:S(2)}) collective-permute-start(bf16[512,1280]{1,0:T(8,128)(2,1)S(1)} %get-tuple-element.11), channel_id=1, source_target_pairs={{0,2},{1,5},{2,0},{3,7},{4,6},{5,1},{6,4},{7,3},{8,10},{9,13},{10,... | collective-permute-start | bytes 3932168 | tf_op jit(solution)/shard_map/ppermute | solution.py:270
  137.4 1.1 copy-start.1
  144.4 10.6 %collective-permute-start.10 = (bf16[256,1280]{1,0:T(8,128)(2,1)S(1)}, bf16[256,1280]{1,0:T(8,128)(2,1)S(1)}, u32[]{:S(2)}, u32[]{:S(2)}) collective-permute-start(bf16[256,1280]{1,0:T(8,128)(2,1)S(1)} %get-tuple-element.13), channel_id=1, source_target_pairs={{0,4},{1,3},{2,6},{3,1},{4,0},{5,7},{6,2},{7,5},{8,12},{9,11},{10,... | collective-permute-start | bytes 1966088 | tf_op jit(solution)/shard_map/ppermute | solution.py:270
  155.0 0.8 copy-start.2
  160.3 7.1 %collective-permute-start.11 = (bf16[128,1280]{1,0:T(8,128)(2,1)S(1)}, bf16[128,1280]{1,0:T(8,128)(2,1)S(1)}, u32[]{:S(2)}, u32[]{:S(2)}) collective-permute-start(bf16[128,1280]{1,0:T(8,128)(2,1)S(1)} %get-tuple-element.15), channel_id=1, source_target_pairs={{0,8},{8,0},{16,24},{24,16},{1,9},{9,1},{17,25},{25,17},{2,10},{10... | collective-permute-start | bytes 983048 | tf_op jit(solution)/shard_map/ppermute | solution.py:270
  167.4 0.7 copy-start.3
  171.8 9.9 %collective-permute-start.12 = (bf16[64,1280]{1,0:T(8,128)(2,1)S(1)}, bf16[64,1280]{1,0:T(8,128)(2,1)S(1)}, u32[]{:S(2)}, u32[]{:S(2)}) collective-permute-start(bf16[64,1280]{1,0:T(8,128)(2,1)S(1)} %get-tuple-element.17), channel_id=1, source_target_pairs={{0,16},{8,24},{16,0},{24,8},{1,17},{9,25},{17,1},{25,9},{2,18},{10... | collective-permute-start | bytes 491528 | tf_op jit(solution)/shard_map/ppermute | solution.py:270
  181.7 0.7 copy-start.5
  184.2 7.7 %collective-permute-start.13 = (bf16[64,1280]{1,0:T(8,128)(2,1)}, bf16[64,1280]{1,0:T(8,128)(2,1)S(1)}, u32[]{:S(2)}, u32[]{:S(2)}) collective-permute-start(bf16[64,1280]{1,0:T(8,128)(2,1)} %shard_map.33), channel_id=1, source_target_pairs={{0,16},{8,24},{16,0},{24,8},{1,17},{9,25},{17,1},{25,9},{2,18},{10... | collective-permute-start | bytes 491528 | tf_op jit(solution)/shard_map/ppermute | solution.py:270
  193.6 7.1 %collective-permute-start.14 = (bf16[128,1280]{1,0:T(8,128)(2,1)S(1)}, bf16[128,1280]{1,0:T(8,128)(2,1)S(1)}, u32[]{:S(2)}, u32[]{:S(2)}) collective-permute-start(bf16[128,1280]{1,0:T(8,128)(2,1)S(1)} %get-tuple-element.10), channel_id=1, source_target_pairs={{0,8},{8,0},{16,24},{24,16},{1,9},{9,1},{17,25},{25,17},{2,10},{10... | collective-permute-start | bytes 983048 | tf_op jit(solution)/shard_map/ppermute | solution.py:270
  200.7 17.2 %collective-permute-start.15 = (bf16[256,1280]{1,0:T(8,128)(2,1)S(1)}, bf16[256,1280]{1,0:T(8,128)(2,1)S(1)}, u32[]{:S(2)}, u32[]{:S(2)}) collective-permute-start(bf16[256,1280]{1,0:T(8,128)(2,1)S(1)} %pad_maximum_fusion.2), channel_id=1, source_target_pairs={{0,4},{1,3},{2,6},{3,1},{4,0},{5,7},{6,2},{7,5},{8,12},{9,11},{10,... | collective-permute-start | bytes 1966088 | tf_op jit(solution)/shard_map/ppermute | solution.py:270
  218.0 17.9 %collective-permute-start.16 = (bf16[512,1280]{1,0:T(8,128)(2,1)S(1)}, bf16[512,1280]{1,0:T(8,128)(2,1)S(1)}, u32[]{:S(2)}, u32[]{:S(2)}) collective-permute-start(bf16[512,1280]{1,0:T(8,128)(2,1)S(1)} %pad_maximum_fusion.1), channel_id=1, source_target_pairs={{0,2},{1,5},{2,0},{3,7},{4,6},{5,1},{6,4},{7,3},{8,10},{9,13},{10,... | collective-permute-start | bytes 3932168 | tf_op jit(solution)/shard_map/ppermute | solution.py:270
  236.1 5.0 %collective-permute-start.17 = (bf16[1024,1280]{1,0:T(8,128)(2,1)S(1)}, bf16[1024,1280]{1,0:T(8,128)(2,1)S(1)}, u32[]{:S(2)}, u32[]{:S(2)}) collective-permute-start(bf16[1024,1280]{1,0:T(8,128)(2,1)S(1)} %pad_maximum_fusion), channel_id=1, source_target_pairs={{0,1},{1,0},{2,3},{3,2},{4,5},{5,4},{6,7},{7,6},{8,9},{9,8},{10,11... | collective-permute-start | bytes 7864328 | tf_op jit(solution)/shard_map/ppermute | solution.py:270
  325.5 4.5 %collective-permute-start.18 = (f32[32,512]{1,0:T(8,128)}, f32[32,512]{1,0:T(8,128)S(1)}, u32[]{:S(2)}, u32[]{:S(2)}) collective-permute-start(f32[32,512]{1,0:T(8,128)} %shard_map.35), channel_id=1, source_target_pairs={{0,8},{8,0},{16,24},{24,16},{1,9},{9,1},{17,25},{25,17},{2,10},{10... | collective-permute-start | bytes 196616 | tf_op jit(solution)/shard_map/ppermute | solution.py:270
  330.9 7.9 %collective-permute-start.19 = (f32[32,1024]{1,0:T(8,128)S(1)}, f32[32,1024]{1,0:T(8,128)S(1)}, u32[]{:S(2)}, u32[]{:S(2)}) collective-permute-start(f32[32,1024]{1,0:T(8,128)S(1)} %maximum_select_fusion.7), channel_id=1, source_target_pairs={{0,16},{8,24},{16,0},{24,8},{1,17},{9,25},{17,1},{25,9},{2,18},{10... | collective-permute-start | bytes 393224 | tf_op jit(solution)/shard_map/ppermute | solution.py:270

commit v2 on v1

v2 whole, which is shorter than its diff:
```python
import functools
import math

import jax
import jax.numpy as jnp
from jax import lax
from jax.experimental import pallas as pl
from jax.experimental.pallas import tpu as pltpu
from jax.sharding import PartitionSpec as P


ITERS = 10
LANES = 128
PANEL = 16
GROUP = 40
SAMPLE_SPACE_LIMIT = 4096
INTERPRET = False
F32 = jnp.float32
BF16 = jnp.bfloat16

NN = (((1,), (0,)), ((), ()))
NT = (((1,), (1,)), ((), ()))
TN = (((0,), (0,)), ((), ()))


def orthonormal(back, gram):
    lower = jnp.linalg.cholesky(gram)
    return lax.linalg.triangular_solve(lower, back, left_side=False, lower=True, transpose_a=True)


def pixel_space(stamps, start_panel):
    block = lax.all_to_all(stamps, "pix", split_axis=1, concat_axis=0, tiled=True)

    def sweep(step, panel):
        partial_value = jnp.dot(block, panel.astype(BF16), preferred_element_type=F32)
        proj = lax.psum(partial_value.astype(BF16), "pix")
        back = lax.dot_general(block, proj, TN, preferred_element_type=F32)
        summed = lax.psum(back.astype(BF16), "samp").astype(F32)
        gram = lax.psum(jnp.dot(summed.T, summed, precision=lax.Precision.HIGHEST), "pix")
        return orthonormal(summed, gram)

    panel = lax.fori_loop(0, ITERS, sweep, start_panel)
    return panel * math.sqrt(start_panel.shape[0] * lax.axis_size("pix"))


def dot(a, b, dims):
    return lax.dot_general(a, b, dims, preferred_element_type=F32)


def split3(x):
    hi = x.astype(BF16)
    rest = x - hi.astype(F32)
    mid = rest.astype(BF16)
    lo = (rest - mid.astype(F32)).astype(BF16)
    return hi, mid, lo


def kernel_call(body, out_shape, **kw):
    return pl.pallas_call(body, out_shape=out_shape, interpret=INTERPRET, **kw)


def vmem(n=1):
    return [pl.BlockSpec(memory_space=pltpu.VMEM)] * n


def smem():
    return pl.BlockSpec(memory_space=pltpu.SMEM)


def inverse_lower(gram):
    k = gram.shape[0]
    lane = lax.broadcasted_iota(jnp.int32, gram.shape, 1)
    row = lax.broadcasted_iota(jnp.int32, gram.shape, 0)
    m = jnp.where(lane < k, gram, jnp.where(lane == row + k, 1.0, 0.0))
    pivots = jnp.ones(gram.shape, F32)
    for start in range(0, k, PANEL):
        cols = [jnp.broadcast_to(m[:, j : j + 1], m.shape) for j in range(start, start + PANEL)]
        for t in range(PANEL):
            j = start + t
            pivot = cols[t][j : j + 1, :]
            factor = jnp.where(row > j, cols[t] * (1.0 / pivot), 0.0)
            pivots = jnp.where(row == j, pivot, pivots)
            for later in range(t + 1, PANEL):
                cols[later] = cols[later] - factor * cols[later][j : j + 1, :]
            m = m - factor * m[j : j + 1, :]
    return pltpu.roll(m * lax.rsqrt(pivots), LANES - k, 1)


def lane_sum3(x, k):
    return x + pltpu.roll(x, LANES - k, 1) + pltpu.roll(x, LANES - 2 * k, 1)


def gram_of(left, parts, zeros):
    k = left.shape[0]
    stack = jnp.concatenate(list(parts) + [zeros], axis=0)
    return lane_sum3(dot(left, stack, NT), k)


def apply_lower(inv, parts, zeros):
    k = inv.shape[0]
    lane = lax.broadcasted_iota(jnp.int32, inv.shape, 1)
    inv = jnp.where(lane < k, inv, 0.0)
    inv = inv + pltpu.roll(inv, k, 1)
    inv = inv + pltpu.roll(inv, 2 * k, 1)
    h1, h2, h3 = [h.astype(F32) for h in split3(inv)]
    first = jnp.where(lane < 3 * k, h1, h2)
    second = jnp.where(lane < k, h2, jnp.where(lane < 2 * k, h3, 0.0))
    left = jnp.concatenate([first, second], axis=1).astype(BF16)
    y1, y2, y3 = parts
    right = jnp.concatenate([y1, y2, y3, y1, y2, y1, zeros, zeros], axis=0)
    return dot(left, right, NN)


def basis_kernel(p0_ref, q_ref):
    p0 = p0_ref[...]
    zeros = jnp.zeros_like(p0)
    gram = gram_of(p0, (p0, zeros, zeros), zeros)
    q_ref[...] = apply_lower(inverse_lower(gram), (p0, zeros, zeros), zeros)


def split_off(own_ref, other_ref, q_ref, left, right):
    k = q_ref.shape[0]
    q = q_ref[...]
    zeros = jnp.zeros(q.shape, BF16)
    q1, q2, q3 = split3(q)
    qs = jnp.concatenate([q1, q2, q3], axis=0)
    w = jnp.zeros(q.shape, F32)
    for ref in (own_ref, other_ref):
        t3 = dot(qs, ref[...], NN)
        ts = split3(t3[:k] + t3[k : 2 * k] + t3[2 * k :])
        w3 = dot(jnp.concatenate(ts, axis=0), ref[...], NT)
        w += w3[:k] + w3[k : 2 * k] + w3[2 * k :]
    ws = jnp.concatenate(list(split3(w)) + [zeros], axis=0)
    m = lane_sum3(dot(q1, ws, NT) + dot(q2, ws, NT) + dot(q3, ws, NT), k)
    w1, w2, w3 = split3(w - 0.5 * apply_lower(m, (q1, q2, q3), zeros))
    left[...] = jnp.concatenate([q1, w1, q1, w1, q1, w1, q2, w2, q2, w2, q3, w3], axis=0)
    right[...] = jnp.concatenate([w1, q1, w2, q2, w3, q3, w1, q1, w2, q2, w1, q1], axis=0)


def form_rows(k, first, own_ref, other_ref, left, right, out_ref, own_win, other_win, right_win):
    n = own_ref.shape[0]
    rows, width = out_ref.shape
    width -= LANES
    bs = width - n // 2
    nb = n // bs
    for b in range(own_win.shape[0] // bs):
        at = pl.multiple_of(lax.rem(first + b, nb) * bs, bs)
        own_win[b * bs : (b + 1) * bs, :] = own_ref[pl.ds(at, bs), :]
        other_win[b * bs : (b + 1) * bs, :] = other_ref[pl.ds(at, bs), :]
        right_win[:, b * bs : (b + 1) * bs] = right[:, pl.ds(at, bs)]
    eye = lax.broadcasted_iota(jnp.int32, (bs, bs), 0) == lax.broadcasted_iota(jnp.int32, (bs, bs), 1)
    for i in range(rows // bs):
        at = pl.multiple_of((first + i) * bs, bs)
        to, end = i * bs, i * bs + width
        s = dot(own_win[to : to + bs, :], own_win[to:end, :], NT)
        s += dot(other_win[to : to + bs, :], other_win[to:end, :], NT)
        s -= dot(left[:, pl.ds(at, bs)], right_win[:, to:end], TN)
        corner = s[:, :bs]
        diagonal = jnp.sum(jnp.where(eye, corner, 0.0), axis=0, keepdims=True)
        out_ref[to : to + bs, :bs] = jnp.where(eye, 0.0, corner).astype(BF16)
        out_ref[to : to + bs, bs:width] = s[:, bs:].astype(BF16)
        side = []
        for g, d in enumerate(split3(diagonal)):
            side.append(right_win[2 * g * k : (2 * g + 1) * k, to : to + bs].astype(F32))
            side.append(jnp.broadcast_to(d.astype(F32), (GROUP - k, bs)))
        side.append(jnp.zeros((LANES - 3 * GROUP, bs), F32))
        out_ref[to : to + bs, width:] = jnp.concatenate(side, axis=0).T.astype(BF16)


def form_first_kernel(at_ref, own_ref, other_ref, q_ref, out_ref, left, right, *wins):
    split_off(own_ref, other_ref, q_ref, left, right)
    form_rows(q_ref.shape[0], at_ref[0], own_ref, other_ref, left, right, out_ref, *wins)


def form_second_kernel(k, at_ref, own_ref, other_ref, left, right, out_ref, *wins):
    form_rows(k, at_ref[0], own_ref, other_ref, left, right, out_ref, *wins)


def add_kernel(half_ref, a_ref, b_ref, o_ref):
    h = o_ref.shape[0]
    width = a_ref.shape[1] - LANES
    at = pl.multiple_of(half_ref[0] * h, h)
    a, b = a_ref[pl.ds(at, h), :], b_ref[pl.ds(at, h), :]
    o_ref[:, :width] = (a[:, :width].astype(F32) + b[:, :width].astype(F32)).astype(BF16)
    x = lane_sum3(a[:, width:].astype(F32), GROUP) + lane_sum3(b[:, width:].astype(F32), GROUP)
    lane = lax.broadcasted_iota(jnp.int32, x.shape, 1)
    h1, h2, h3 = [part.astype(F32) for part in split3(x)]
    packed = jnp.where(lane < 2 * GROUP, pltpu.roll(h2, GROUP, 1), pltpu.roll(h3, 2 * GROUP, 1))
    packed = jnp.where(lane < GROUP, h1, packed)
    o_ref[:, width:] = jnp.where(lane < 3 * GROUP, packed, 0.0).astype(BF16)


def add_shares(a, b, half=None):
    rows = a.shape[0] // (1 if half is None else 2)
    half = jnp.zeros((1,), jnp.int32) if half is None else half[None]
    return kernel_call(
        add_kernel,
        jax.ShapeDtypeStruct((rows, a.shape[1]), BF16),
        in_specs=[smem()] + vmem(2),
        out_specs=vmem()[0],
    )(half, a, b)


def iterate_kernel(index_ref, near_ref, far_ref, q_ref, p0_ref, p_ref, inv_ref, full, u, v, diag):
    k, n = q_ref.shape
    width = near_ref.shape[1] - LANES
    bs = width - n // 2
    nb = n // bs

    def unpack(share_ref, offset):
        def one(r, _):
            i = index_ref[r + offset]
            frm = pl.multiple_of(r * bs, bs)
            to = pl.multiple_of(i * bs, bs)
            for d in range(nb // 2 + 1):
                part = share_ref[pl.ds(frm, bs), d * bs : (d + 1) * bs]
                at = pl.multiple_of(lax.rem(i + d, nb) * bs, bs)
                full[pl.ds(to, bs), pl.ds(at, bs)] = part
                if 0 < d < nb // 2:
                    full[pl.ds(at, bs), pl.ds(to, bs)] = part.T
            side = share_ref[pl.ds(frm, bs), width:].astype(F32).T
            side = side[:GROUP] + side[GROUP : 2 * GROUP] + side[2 * GROUP : 3 * GROUP]
            w = side[:k]
            diag[:, pl.ds(to, bs)] = side[k : k + 8]
            q = q_ref[:, pl.ds(to, bs)]
            us = split3(jnp.concatenate([w, q], axis=0))
            v1, v2, v3 = split3(jnp.concatenate([q, w], axis=0))
            u[:, pl.ds(to, bs)] = jnp.concatenate(list(us) + [jnp.zeros((2 * k, bs), BF16)], axis=0)
            v[:, pl.ds(to, bs)] = jnp.concatenate([v1, v2, v3, v1, v2, v1], axis=0)
            return 0

        lax.fori_loop(0, nb // 2, one, 0)

    unpack(near_ref, 0)
    unpack(far_ref, nb // 2)

    zeros = jnp.zeros((k, n), BF16)
    lane = lax.broadcasted_iota(jnp.int32, (k, LANES), 1)

    def product(p):
        t = dot(p, u[...], NT)
        t = t[:, :LANES] + t[:, LANES:]
        t = t + pltpu.roll(t, 2 * k, 1)
        h1, h2, h3 = [h.astype(F32) for h in split3(t)]
        low = lane < 2 * k
        ts = jnp.concatenate([h1, jnp.where(low, h1, h2), jnp.where(low, h2, h3)], axis=1).astype(BF16)
        y = dot(p, full[...], NN) + dot(ts, v[...], NN) + p.astype(F32) * diag[0:1, :]
        return split3(y)

    def sweep(step, p):
        parts = product(p)
        inv = inverse_lower(gram_of(p, parts, zeros))
        return apply_lower(inv, parts, zeros).astype(BF16)

    p = lax.fori_loop(0, ITERS - 1, sweep, p0_ref[...])
    p_ref[...] = p
    inv_ref[...] = inverse_lower(gram_of(p, product(p), zeros))


def finish_kernel(scale, p_ref, inv_ref, block_ref, o_ref):
    back = dot(p_ref[...], block_ref[...], NN)
    zeros = jnp.zeros(back.shape, BF16)
    o_ref[...] = apply_lower(inv_ref[...], split3(back), zeros) * scale


def flip(x, axes, perm):
    return lax.ppermute(x, axes, perm)


def ordered(own, recv, bit, axis=0):
    return jnp.where(
        bit == 0,
        jnp.concatenate([own, recv], axis=axis),
        jnp.concatenate([recv, own], axis=axis),
    )


def sample_space(stamps, start_panel):
    pix = lax.axis_size("pix")
    samp = lax.axis_size("samp")
    n = stamps.shape[0] * pix * samp
    k = start_panel.shape[1]
    scale = math.sqrt(start_panel.shape[0] * pix)
    p = lax.axis_index("pix")
    s = lax.axis_index("samp")
    xor_pix = lambda b: [(i, i ^ b) for i in range(pix)]
    xor_samp = lambda b: [(i, i ^ b) for i in range(samp)]

    core = p & 1
    x, y = (p >> 1) & 1, (p >> 2) & 1
    z0, z1 = s & 1, (s >> 1) & 1

    low = start_panel.astype(BF16).T
    for b in (1, 2, 4):
        low = ordered(low, flip(low, "pix", xor_pix(b)), p & b, axis=1)

    block = lax.all_to_all(stamps, ("pix", "samp"), split_axis=1, concat_axis=0, tiled=True)

    proj = dot(low, stamps, NT).astype(BF16)
    for b in (1, 2):
        proj = ordered(proj, flip(proj, "samp", xor_samp(b)), s & b, axis=1)
    for b in (1, 2, 4):
        proj = ordered(proj, flip(proj, "pix", xor_pix(b)), p & b, axis=1)
    q = kernel_call(
        basis_kernel, jax.ShapeDtypeStruct((k, n), F32), in_specs=vmem(), out_specs=vmem()[0]
    )(proj)

    first = [(i, i ^ (2 if i % 2 == 0 else 4)) for i in range(pix)]
    second = [(i, i ^ (4 if i % 2 == 0 else 2)) for i in range(pix)]
    bit_a = jnp.where(core == 0, x, y)
    bit_b = jnp.where(core == 0, y, x)

    other = flip(block, "pix", xor_pix(1))
    bs = 2 * stamps.shape[0]
    nb = n // bs
    px = block.shape[1]
    width = n // 2 + bs
    rows = n // 4
    window = rows - bs + width
    piece = jax.ShapeDtypeStruct((rows, width + LANES), BF16)
    stack = jax.ShapeDtypeStruct((12 * k, n), BF16)
    wins = [
        pltpu.VMEM((window, px), BF16),
        pltpu.VMEM((window, px), BF16),
        pltpu.VMEM((12 * k, window), BF16),
    ]
    blocks = rows // bs
    at = core * 2 * blocks
    send, left, right = kernel_call(
        form_first_kernel,
        (piece, stack, stack),
        in_specs=[smem()] + vmem(3),
        out_specs=tuple(vmem(3)),
        scratch_shapes=wins,
    )((at + (1 - bit_a) * blocks)[None], block, other, q)
    recv = flip(send, "pix", first)
    keep = kernel_call(
        functools.partial(form_second_kernel, k),
        piece,
        in_specs=[smem()] + vmem(4),
        out_specs=vmem()[0],
        scratch_shapes=wins,
    )((at + bit_a * blocks)[None], block, other, left, right)
    for axis, perm, bit in (
        ("pix", second, bit_b),
        ("samp", xor_samp(1), z0),
        ("samp", xor_samp(2), z1),
    ):
        send = add_shares(keep, recv, 1 - bit)
        keep = add_shares(keep, recv, bit)
        recv = flip(send, axis, perm)
    share = add_shares(keep, recv)

    share = ordered(share, flip(share, "samp", xor_samp(2)), z1)
    for axis, perm in (("samp", xor_samp(1)), ("pix", second), ("pix", first)):
        share = jnp.concatenate([share, flip(share, axis, perm)], axis=0)
    far = flip(share, "pix", xor_pix(1))
    at = jnp.arange(nb, dtype=jnp.int32)
    c_of = core ^ ((at >> 3) & 1)
    a_of = jnp.where(c_of == 0, x, y) ^ ((at >> 2) & 1)
    b_of = jnp.where(c_of == 0, y, x) ^ ((at >> 1) & 1)
    index = c_of * 8 + a_of * 4 + b_of * 2 + (z0 ^ (at & 1))

    proj, inv = kernel_call(
        iterate_kernel,
        (jax.ShapeDtypeStruct((k, n), BF16), jax.ShapeDtypeStruct((k, LANES), F32)),
        in_specs=[smem()] + vmem(4),
        out_specs=tuple(vmem(2)),
        scratch_shapes=[
            pltpu.VMEM((n, n), BF16),
            pltpu.VMEM((8 * k, n), BF16),
            pltpu.VMEM((12 * k, n), BF16),
            pltpu.VMEM((8, n), F32),
        ],
    )(index, share, far, q, proj)

    mine = kernel_call(
        functools.partial(finish_kernel, scale),
        jax.ShapeDtypeStruct((k, px), F32),
        in_specs=vmem(3),
        out_specs=vmem()[0],
    )(proj, inv, block)
    for b in (2, 1):
        mine = jnp.concatenate([mine, flip(mine, "samp", xor_samp(b))], axis=1)
    parts = [mine[:, i * px : (i + 1) * px] for i in range(samp)]
    by_distance = {0: parts[0], 2: parts[1], 1: parts[2], 3: parts[3]}
    swap0 = [jnp.where(z0 == 0, by_distance[i], by_distance[i ^ 1]) for i in range(samp)]
    swap1 = [jnp.where(z1 == 0, swap0[i], swap0[i ^ 2]) for i in range(samp)]
    return jnp.concatenate(swap1, axis=1).T


def solution(mesh):
    pix, samp = mesh.shape["pix"], mesh.shape["samp"]

    def local(stamps, start_panel):
        n = stamps.shape[0] * pix * samp
        k = start_panel.shape[1]
        if n <= SAMPLE_SPACE_LIMIT and (pix, samp) == (8, 4) and 4 * k == LANES:
            return sample_space(stamps, start_panel)
        return pixel_space(stamps, start_panel)

    return jax.shard_map(
        local,
        mesh=mesh,
        in_specs=(P(("samp", "pix"), None), P("pix", None)),
        out_specs=P("pix", None),
        check_vma=False,
    )
```

time: 340 us -> 287 us (0.84)
  Pallas kernels: 115 us -> 87.2 us
  waiting for transfers between devices: 168 us -> 149 us
  local copies, waits for them, and re-layouts: 19.7 us -> 6.53 us
  starting transfers between devices: 29.1 us -> 35.7 us
    pallas_call x1, Pallas kernels: 79.8 us -> 45.9 us  [sample_space(): kernel_call(iterate_kernel, (jax.ShapeDtypeStruct((k, n), BF16), jax.Shap...]
    ppermute x20, waiting for transfers between devices: 124 us -> 105 us  [flip(): return lax.ppermute(x, axes, perm)]
    pallas_call x5 -> x9, Pallas kernels: 26.2 us -> 35.4 us  [the longest x7 16.2 us: add_shares(): kernel_call(add_kernel, jax.ShapeDtypeStruct((rows, a.shape[1]), BF16), i...]
    dynamic_slice x4 -> x0, local copies, waits for them, and re-layouts: 8.68 us -> none  [halves(): send = lax.dynamic_slice_in_dim(x, (1 - bit) * h, h, 0)]
    ppermute x20, starting transfers between devices: 21.8 us -> 28.4 us  [flip(): return lax.ppermute(x, axes, perm)]
  transfers between devices with their start and end apart: 21 -> 21, of which waited for: 19 -> 19; matrix products, arithmetic and copies ran while one was open for 2% -> 1% of each run, Pallas kernels for 2% -> 6%
where the time goes in v2:
time: 287 us; the launch traced here: 286 us
  waiting for transfers between devices  149 us (52%)
  Pallas kernels  87.2 us (30%)
  starting transfers between devices  35.7 us (12%)
  local copies, waits for them, and re-layouts  6.53 us (2%)
  other arithmetic  5.77 us (2%)
    ppermute x20, waiting for transfers between devices, flip(): return lax.ppermute(x, axes, perm)  105 us
    pallas_call x1, Pallas kernels, sample_space(): kernel_call(iterate_kernel, (jax.ShapeDtypeStruct((k, n), BF16), jax.Shap...  45.9 us
    all_to_all x1, waiting for transfers between devices, sample_space(): lax.all_to_all(stamps, ('pix', 'samp'), split_axis=1, concat_axis=0, tile...  43.4 us
    ppermute x20, starting transfers between devices, flip(): return lax.ppermute(x, axes, perm)  28.4 us
    pallas_call x7, Pallas kernels, add_shares(): kernel_call(add_kernel, jax.ShapeDtypeStruct((rows, a.shape[1]), BF16), i...  16.2 us
    pallas_call x1, Pallas kernels, sample_space(): kernel_call(form_first_kernel, (piece, stack, stack), in_specs=[smem()] +...  11 us
    pallas_call x1, Pallas kernels, sample_space(): kernel_call(functools.partial(form_second_kernel, k), piece, in_specs=[sm...  8.16 us
    all_to_all x1, starting transfers between devices, sample_space(): lax.all_to_all(stamps, ('pix', 'samp'), split_axis=1, concat_axis=0, tile...  7.33 us
  transfers between devices with their start and end apart: 21, of which 19 were waited for; matrix products, arithmetic and copies ran while one was open for 1% of the time, Pallas kernels for 6%

profile of v2, /device:TPU:0, one launch (start us, length us, event | category | flops | bytes accessed | tf_op | source)
XLA Modules:
  0.0 286.5 jit_solution(347795181579253131)
XLA Ops:
  0.0 3.2 %copy.6 = bf16[8,32,8,512]{3,2,0,1:T(8,128)(2,1)} copy(bf16[8,32,8,512]{3,2,1,0:T(8,128)(2,1)} %bitcast.25) | data formatting | bytes 4194304 | tf_op jit(solution)/shard_map/all_to_all | solution.py:297
  3.2 7.3 %all-to-all-start = ((bf16[64,32,512]{2,0,1:T(8,128)(2,1)}), bf16[64,32,512]{2,0,1:T(8,128)(2,1)S(1)}, u32[]{:S(2)}, u32[]{:S(2)}) async-start(bf16[64,32,512]{2,0,1:T(8,128)(2,1)} %bitcast.24), calls=%async_computation | async-start | bytes 4194304 | tf_op jit(solution)/shard_map/all_to_all | solution.py:297
  10.9 1.1 collective-permute-done.1
  12.1 1.8 collective-permute-start.2
  13.9 43.4 %all-to-all-done = bf16[64,32,512]{2,0,1:T(8,128)(2,1)S(1)} async-done(((bf16[64,32,512]{2,0,1:T(8,128)(2,1)}), bf16[64,32,512]{2,0,1:T(8,128)(2,1)S(1)}, u32[]{:S(2)}, u32[]{:S(2)}) %all-to-all-start) | async-done | bytes 2097184 | tf_op jit(solution)/shard_map/all_to_all | solution.py:297
  57.3 1.8 collective-permute-start
  59.2 1.6 collective-permute-start.3
  60.8 12.3 %collective-permute-done.3 = bf16[32,8192]{1,0:T(8,128)(2,1)S(1)} collective-permute-done((bf16[32,8192]{1,0:T(8,128)(2,1)S(1)}, bf16[32,8192]{1,0:T(8,128)(2,1)S(1)}, u32[]{:S(2)}, u32[]{:S(2)}) %collective-permute-start.3) | collective-permute-done | bytes 524320 | tf_op jit(solution)/shard_map/ppermute | solution.py:267
  73.2 2.3 convolution_convert_fusion
  75.4 2.5 collective-permute-start.4
  77.9 1.6 collective-permute-done.4
  79.6 1.1 collective-permute-start.5
  80.7 3.5 %collective-permute-done.5 = bf16[32,128]{1,0:T(8,128)(2,1)S(1)} collective-permute-done((bf16[32,128]{1,0:T(8,128)(2,1)S(1)}, bf16[32,128]{1,0:T(8,128)(2,1)S(1)}, u32[]{:S(2)}, u32[]{:S(2)}) %collective-permute-start.5) | collective-permute-done | bytes 8224 | tf_op jit(solution)/shard_map/ppermute | solution.py:267
  84.2 1.2 collective-permute-done.6
  85.4 1.2 collective-permute-start.7
  86.6 2.8 collective-permute-done.7
  89.4 1.1 collective-permute-start.8
  90.5 3.2 %collective-permute-done.8 = bf16[32,1024]{1,0:T(8,128)(2,1)S(1)} collective-permute-done((bf16[32,1024]{1,0:T(8,128)(2,1)S(1)}, bf16[32,1024]{1,0:T(8,128)(2,1)S(1)}, u32[]{:S(2)}, u32[]{:S(2)}) %collective-permute-start.8) | collective-permute-done | bytes 65568 | tf_op jit(solution)/shard_map/ppermute | solution.py:267
  94.4 3.0 %shard_map.28.q_ref = f32[32,2048]{1,0:T(8,128)} custom-call(bf16[32,2048]{1,0:T(8,128)(2,1)} %maximum_select_fusion.5.p0_ref), custom_call_target="tpu_custom_call" | custom-call | tf_op jit(solution)/shard_map/pallas_call | solution.py:304
  97.4 11.0 %shard_map.29 = (bf16[512,1280]{1,0:T(8,128)(2,1)}, bf16[384,2048]{1,0:T(8,128)(2,1)}, bf16[384,2048]{1,0:T(8,128)(2,1)}) custom-call(s32[1]{0:T(128)} %bitcast.7.at_ref, bf16[2048,512]{1,0:T(8,128)(2,1)} %bitcast.21, bf16[2048,512]{1,0:T(8,128)(2,1)} %collective-permute-done.other_ref, f32[32,2048]{1,0:T(8,128)} %shard_map.28.q_ref), custom_call_target="tpu_custom_call" | custom-call | tf_op jit(solution)/shard_map/pallas_call | solution.py:329
  108.4 1.1 collective-permute-start.9
  109.5 8.2 %shard_map.30.a_ref = bf16[512,1280]{1,0:T(8,128)(2,1)} custom-call(s32[1]{0:T(128)} %bitcast.3.at_ref, bf16[2048,512]{1,0:T(8,128)(2,1)} %bitcast.22, bf16[2048,512]{1,0:T(8,128)(2,1)} %collective-permute-done.other_ref, bf16[384,2048]{1,0:T(8,128)(2,1)} %get-tuple-element.10.left, bf16[384,2048]{1,0:T(8,128)(2,1)} %get-tuple-element.11.right), custom_call_target="tpu_custom_call" | custom-call | tf_op jit(solution)/shard_map/pallas_call | solution.py:337
  117.7 8.5 %collective-permute-done.9.b_ref = bf16[512,1280]{1,0:T(8,128)(2,1)S(1)} collective-permute-done((bf16[512,1280]{1,0:T(8,128)(2,1)}, bf16[512,1280]{1,0:T(8,128)(2,1)S(1)}, u32[]{:S(2)}, u32[]{:S(2)}) %collective-permute-start.9) | collective-permute-done | bytes 1310752 | tf_op jit(solution)/shard_map/ppermute | solution.py:267
  126.3 1.1 copy-done.2
  127.3 3.0 %shard_map.32 = bf16[256,1280]{1,0:T(8,128)(2,1)} custom-call(s32[1]{0:T(128)} %bitcast.9.half_ref, bf16[512,1280]{1,0:T(8,128)(2,1)} %shard_map.30.a_ref, bf16[512,1280]{1,0:T(8,128)(2,1)} %copy-done.2), custom_call_target="tpu_custom_call" | custom-call | tf_op jit(solution)/shard_map/pallas_call | solution.py:196
  130.4 1.1 collective-permute-start.10
  131.4 3.0 %shard_map.31.a_ref = bf16[256,1280]{1,0:T(8,128)(2,1)} custom-call(s32[1]{0:T(128)} %bitcast.2.half_ref, bf16[512,1280]{1,0:T(8,128)(2,1)} %shard_map.30.a_ref, bf16[512,1280]{1,0:T(8,128)(2,1)} %copy-done.2), custom_call_target="tpu_custom_call" | custom-call | tf_op jit(solution)/shard_map/pallas_call | solution.py:196
  134.5 6.7 %collective-permute-done.10.b_ref = bf16[256,1280]{1,0:T(8,128)(2,1)S(1)} collective-permute-done((bf16[256,1280]{1,0:T(8,128)(2,1)}, bf16[256,1280]{1,0:T(8,128)(2,1)S(1)}, u32[]{:S(2)}, u32[]{:S(2)}) %collective-permute-start.10) | collective-permute-done | bytes 655392 | tf_op jit(solution)/shard_map/ppermute | solution.py:267
  142.0 2.2 shard_map.34
  144.2 2.0 collective-permute-start.11
  146.3 2.2 shard_map.33.a_ref
  148.5 3.2 %collective-permute-done.11.b_ref = bf16[128,1280]{1,0:T(8,128)(2,1)S(1)} collective-permute-done((bf16[128,1280]{1,0:T(8,128)(2,1)}, bf16[128,1280]{1,0:T(8,128)(2,1)S(1)}, u32[]{:S(2)}, u32[]{:S(2)}) %collective-permute-start.11) | collective-permute-done | bytes 327712 | tf_op jit(solution)/shard_map/ppermute | solution.py:267
  152.4 1.9 shard_map.36
  155.2 1.9 shard_map.35.a_ref
  157.1 3.6 %collective-permute-done.12.b_ref = bf16[64,1280]{1,0:T(8,128)(2,1)S(1)} collective-permute-done((bf16[64,1280]{1,0:T(8,128)(2,1)}, bf16[64,1280]{1,0:T(8,128)(2,1)S(1)}, u32[]{:S(2)}, u32[]{:S(2)}) %collective-permute-start.12) | collective-permute-done | bytes 163872 | tf_op jit(solution)/shard_map/ppermute | solution.py:267
  161.4 1.8 shard_map.37
  164.2 5.4 %collective-permute-done.13 = bf16[64,1280]{1,0:T(8,128)(2,1)S(1)} collective-permute-done((bf16[64,1280]{1,0:T(8,128)(2,1)}, bf16[64,1280]{1,0:T(8,128)(2,1)S(1)}, u32[]{:S(2)}, u32[]{:S(2)}) %collective-permute-start.13) | collective-permute-done | bytes 163872 | tf_op jit(solution)/shard_map/ppermute | solution.py:267
  170.7 5.1 %collective-permute-start.14 = (bf16[128,1280]{1,0:T(8,128)(2,1)S(1)}, bf16[128,1280]{1,0:T(8,128)(2,1)S(1)}, u32[]{:S(2)}, u32[]{:S(2)}) collective-permute-start(bf16[128,1280]{1,0:T(8,128)(2,1)S(1)} %maximum_select_fusion.3), channel_id=1, source_target_pairs={{0,8},{8,0},{16,24},{24,16},{1,9},{9,1},{17,25},{25,17},{2,10},{10... | collective-permute-start | bytes 983048 | tf_op jit(solution)/shard_map/ppermute | solution.py:267
  175.8 5.1 %collective-permute-done.14 = bf16[128,1280]{1,0:T(8,128)(2,1)S(1)} collective-permute-done((bf16[128,1280]{1,0:T(8,128)(2,1)S(1)}, bf16[128,1280]{1,0:T(8,128)(2,1)S(1)}, u32[]{:S(2)}, u32[]{:S(2)}) %collective-permute-start.14) | collective-permute-done | bytes 327712 | tf_op jit(solution)/shard_map/ppermute | solution.py:267
  180.9 3.4 %collective-permute-start.15 = (bf16[256,1280]{1,0:T(8,128)(2,1)S(1)}, bf16[256,1280]{1,0:T(8,128)(2,1)S(1)}, u32[]{:S(2)}, u32[]{:S(2)}) collective-permute-start(bf16[256,1280]{1,0:T(8,128)(2,1)S(1)} %pad_maximum_fusion.2), channel_id=1, source_target_pairs={{0,4},{1,3},{2,6},{3,1},{4,0},{5,7},{6,2},{7,5},{8,12},{9,11},{10,... | collective-permute-start | bytes 1966088 | tf_op jit(solution)/shard_map/ppermute | solution.py:267
  184.4 15.4 %collective-permute-done.15 = bf16[256,1280]{1,0:T(8,128)(2,1)S(1)} collective-permute-done((bf16[256,1280]{1,0:T(8,128)(2,1)S(1)}, bf16[256,1280]{1,0:T(8,128)(2,1)S(1)}, u32[]{:S(2)}, u32[]{:S(2)}) %collective-permute-start.15) | collective-permute-done | bytes 655392 | tf_op jit(solution)/shard_map/ppermute | solution.py:267
  200.1 2.2 collective-permute-start.16
  202.3 15.6 %collective-permute-done.16 = bf16[512,1280]{1,0:T(8,128)(2,1)S(1)} collective-permute-done((bf16[512,1280]{1,0:T(8,128)(2,1)S(1)}, bf16[512,1280]{1,0:T(8,128)(2,1)S(1)}, u32[]{:S(2)}, u32[]{:S(2)}) %collective-permute-start.16) | collective-permute-done | bytes 1310752 | tf_op jit(solution)/shard_map/ppermute | solution.py:267
  218.9 4.3 %collective-permute-done.17.far_ref = bf16[1024,1280]{1,0:T(8,128)(2,1)} collective-permute-done((bf16[1024,1280]{1,0:T(8,128)(2,1)S(1)}, bf16[1024,1280]{1,0:T(8,128)(2,1)}, u32[]{:S(2)}, u32[]{:S(2)}) %collective-permute-start.17) | collective-permute-done | bytes 2621472 | tf_op jit(solution)/shard_map/ppermute | solution.py:267
  223.2 45.9 %shard_map.38 = (bf16[32,2048]{1,0:T(8,128)(2,1)}, f32[32,128]{1,0:T(8,128)}) custom-call(s32[16]{0:T(128)} %xor_add_fusion.index_ref, bf16[1024,1280]{1,0:T(8,128)(2,1)} %copy-done.1, bf16[1024,1280]{1,0:T(8,128)(2,1)} %collective-permute-done.17.far_ref, f32[32,2048]{1,0:T(8,128)} %shard_map.28.q_ref, bf16[32,2048]{1,0:T(8,128)(2,1)} %maximum_select_fusion.5.p0_ref), custom_call_target="tpu_custom_call" | custom-call | tf_op jit(solution)/shard_map/pallas_call | solution.py:364
  269.2 2.9 %shard_map.39 = f32[32,512]{1,0:T(8,128)} custom-call(bf16[32,2048]{1,0:T(8,128)(2,1)} %get-tuple-element.13.p_ref, f32[32,128]{1,0:T(8,128)} %get-tuple-element.14.inv_ref, bf16[2048,512]{1,0:T(8,128)(2,1)} %bitcast.23), custom_call_target="tpu_custom_call" | custom-call | tf_op jit(solution)/shard_map/pallas_call | solution.py:377
  272.1 6.5 %collective-permute-done.18 = f32[32,512]{1,0:T(8,128)S(1)} collective-permute-done((f32[32,512]{1,0:T(8,128)}, f32[32,512]{1,0:T(8,128)S(1)}, u32[]{:S(2)}, u32[]{:S(2)}) %collective-permute-start.18) | collective-permute-done | bytes 65568 | tf_op jit(solution)/shard_map/ppermute | solution.py:267
  279.5 5.4 %collective-permute-done.19 = f32[32,1024]{1,0:T(8,128)S(1)} collective-permute-done((f32[32,1024]{1,0:T(8,128)S(1)}, f32[32,1024]{1,0:T(8,128)S(1)}, u32[]{:S(2)}, u32[]{:S(2)}) %collective-permute-start.19) | collective-permute-done | bytes 131104 | tf_op jit(solution)/shard_map/ppermute | solution.py:267
  (38 shorter events, 10.3 us)
Async XLA Ops:
  3.2 7.3 %copy-start.5 = (f32[2048,32]{0,1:T(8,128)S(1)}, f32[2048,32]{0,1:T(8,128)}, u32[]{:S(2)}) copy-start(f32[2048,32]{0,1:T(8,128)} %param.3) | copy-start | bytes 786436
  3.2 54.1 %all-to-all-start = ((bf16[64,32,512]{2,0,1:T(8,128)(2,1)}), bf16[64,32,512]{2,0,1:T(8,128)(2,1)S(1)}, u32[]{:S(2)}, u32[]{:S(2)}) async-start(bf16[64,32,512]{2,0,1:T(8,128)(2,1)} %bitcast.24), calls=%async_computation | async-start | bytes 4194304 | tf_op jit(solution)/shard_map/all_to_all | solution.py:297
  10.6 1.4 collective-permute-start.1
  12.1 47.0 %collective-permute-start.2 = (bf16[32,4096]{1,0:T(8,128)(2,1)S(1)}, bf16[32,4096]{1,0:T(8,128)(2,1)S(1)}, u32[]{:S(2)}, u32[]{:S(2)}) collective-permute-start(bf16[32,4096]{1,0:T(8,128)(2,1)S(1)} %maximum_select_fusion.4), channel_id=1, source_target_pairs={{0,2},{1,3},{2,0},{3,1},{4,6},{5,7},{6,4},{7,5},{8,10},{9,11},{10,... | collective-permute-start | bytes 786440 | tf_op jit(solution)/shard_map/ppermute | solution.py:267
  57.3 18.1 %copy-start = (bf16[64,32,512]{2,0,1:T(8,128)(2,1)}, bf16[64,32,512]{2,0,1:T(8,128)(2,1)S(1)}, u32[]{:S(2)}) copy-start(bf16[64,32,512]{2,0,1:T(8,128)(2,1)S(1)} %all-to-all-done) | copy-start | bytes 6291460
  57.3 40.1 %collective-permute-start = (bf16[2048,512]{1,0:T(8,128)(2,1)S(1)}, bf16[2048,512]{1,0:T(8,128)(2,1)}, u32[]{:S(2)}, u32[]{:S(2)}) collective-permute-start(bf16[2048,512]{1,0:T(8,128)(2,1)S(1)} %bitcast.20), channel_id=1, source_target_pairs={{0,1},{1,0},{2,3},{3,2},{4,5},{5,4},{6,7},{7,6},{8,9},{9,8},{10,11... | collective-permute-start | bytes 6291464 | tf_op jit(solution)/shard_map/ppermute | solution.py:267
  59.2 13.9 %collective-permute-start.3 = (bf16[32,8192]{1,0:T(8,128)(2,1)S(1)}, bf16[32,8192]{1,0:T(8,128)(2,1)S(1)}, u32[]{:S(2)}, u32[]{:S(2)}) collective-permute-start(bf16[32,8192]{1,0:T(8,128)(2,1)S(1)} %maximum_select_fusion.2), channel_id=1, source_target_pairs={{0,4},{1,5},{2,6},{3,7},{4,0},{5,1},{6,2},{7,3},{8,12},{9,13},{10,... | collective-permute-start | bytes 1572872 | tf_op jit(solution)/shard_map/ppermute | solution.py:267
  75.4 4.1 %collective-permute-start.4 = (bf16[32,64]{1,0:T(8,128)(2,1)S(1)}, bf16[32,64]{1,0:T(8,128)(2,1)S(1)}, u32[]{:S(2)}, u32[]{:S(2)}) collective-permute-start(bf16[32,64]{1,0:T(8,128)(2,1)S(1)} %convolution_convert_fusion), channel_id=1, source_target_pairs={{0,8},{8,0},{16,24},{24,16},{1,9},{9,1},{17,25},{25,17},{2,10},{10... | collective-permute-start | bytes 12296 | tf_op jit(solution)/shard_map/ppermute | solution.py:267
  79.6 4.6 %collective-permute-start.5 = (bf16[32,128]{1,0:T(8,128)(2,1)S(1)}, bf16[32,128]{1,0:T(8,128)(2,1)S(1)}, u32[]{:S(2)}, u32[]{:S(2)}) collective-permute-start(bf16[32,128]{1,0:T(8,128)(2,1)S(1)} %maximum_select_fusion.9), channel_id=1, source_target_pairs={{0,16},{8,24},{16,0},{24,8},{1,17},{9,25},{17,1},{25,9},{2,18},{10... | collective-permute-start | bytes 24584 | tf_op jit(solution)/shard_map/ppermute | solution.py:267
  84.2 1.2 collective-permute-start.6
  85.4 4.0 %collective-permute-start.7 = (bf16[32,512]{1,0:T(8,128)(2,1)S(1)}, bf16[32,512]{1,0:T(8,128)(2,1)S(1)}, u32[]{:S(2)}, u32[]{:S(2)}) collective-permute-start(bf16[32,512]{1,0:T(8,128)(2,1)S(1)} %maximum_select_fusion.7), channel_id=1, source_target_pairs={{0,2},{1,3},{2,0},{3,1},{4,6},{5,7},{6,4},{7,5},{8,10},{9,11},{10,... | collective-permute-start | bytes 98312 | tf_op jit(solution)/shard_map/ppermute | solution.py:267
  89.4 4.3 %collective-permute-start.8 = (bf16[32,1024]{1,0:T(8,128)(2,1)S(1)}, bf16[32,1024]{1,0:T(8,128)(2,1)S(1)}, u32[]{:S(2)}, u32[]{:S(2)}) collective-permute-start(bf16[32,1024]{1,0:T(8,128)(2,1)S(1)} %maximum_select_fusion.6), channel_id=1, source_target_pairs={{0,4},{1,5},{2,6},{3,7},{4,0},{5,1},{6,2},{7,3},{8,12},{9,13},{10,... | collective-permute-start | bytes 196616 | tf_op jit(solution)/shard_map/ppermute | solution.py:267
  108.4 17.8 %collective-permute-start.9 = (bf16[512,1280]{1,0:T(8,128)(2,1)}, bf16[512,1280]{1,0:T(8,128)(2,1)S(1)}, u32[]{:S(2)}, u32[]{:S(2)}) collective-permute-start(bf16[512,1280]{1,0:T(8,128)(2,1)} %get-tuple-element.12), channel_id=1, source_target_pairs={{0,2},{1,5},{2,0},{3,7},{4,6},{5,1},{6,4},{7,3},{8,10},{9,13},{10,... | collective-permute-start | bytes 3932168 | tf_op jit(solution)/shard_map/ppermute | solution.py:267
  126.3 1.1 copy-start.2
  130.4 10.8 %collective-permute-start.10 = (bf16[256,1280]{1,0:T(8,128)(2,1)}, bf16[256,1280]{1,0:T(8,128)(2,1)S(1)}, u32[]{:S(2)}, u32[]{:S(2)}) collective-permute-start(bf16[256,1280]{1,0:T(8,128)(2,1)} %shard_map.32), channel_id=1, source_target_pairs={{0,4},{1,3},{2,6},{3,1},{4,0},{5,7},{6,2},{7,5},{8,12},{9,11},{10,... | collective-permute-start | bytes 1966088 | tf_op jit(solution)/shard_map/ppermute | solution.py:267
  141.2 0.8 copy-start.3
  144.2 7.5 %collective-permute-start.11 = (bf16[128,1280]{1,0:T(8,128)(2,1)}, bf16[128,1280]{1,0:T(8,128)(2,1)S(1)}, u32[]{:S(2)}, u32[]{:S(2)}) collective-permute-start(bf16[128,1280]{1,0:T(8,128)(2,1)} %shard_map.34), channel_id=1, source_target_pairs={{0,8},{8,0},{16,24},{24,16},{1,9},{9,1},{17,25},{25,17},{2,10},{10... | collective-permute-start | bytes 983048 | tf_op jit(solution)/shard_map/ppermute | solution.py:267
  151.7 0.7 copy-start.4
  154.3 6.4 %collective-permute-start.12 = (bf16[64,1280]{1,0:T(8,128)(2,1)}, bf16[64,1280]{1,0:T(8,128)(2,1)S(1)}, u32[]{:S(2)}, u32[]{:S(2)}) collective-permute-start(bf16[64,1280]{1,0:T(8,128)(2,1)} %shard_map.36), channel_id=1, source_target_pairs={{0,16},{8,24},{16,0},{24,8},{1,17},{9,25},{17,1},{25,9},{2,18},{10... | collective-permute-start | bytes 491528 | tf_op jit(solution)/shard_map/ppermute | solution.py:267
  160.8 0.7 copy-start.6
  163.3 6.4 %collective-permute-start.13 = (bf16[64,1280]{1,0:T(8,128)(2,1)}, bf16[64,1280]{1,0:T(8,128)(2,1)S(1)}, u32[]{:S(2)}, u32[]{:S(2)}) collective-permute-start(bf16[64,1280]{1,0:T(8,128)(2,1)} %shard_map.37), channel_id=1, source_target_pairs={{0,16},{8,24},{16,0},{24,8},{1,17},{9,25},{17,1},{25,9},{2,18},{10... | collective-permute-start | bytes 491528 | tf_op jit(solution)/shard_map/ppermute | solution.py:267
  170.7 10.2 %collective-permute-start.14 = (bf16[128,1280]{1,0:T(8,128)(2,1)S(1)}, bf16[128,1280]{1,0:T(8,128)(2,1)S(1)}, u32[]{:S(2)}, u32[]{:S(2)}) collective-permute-start(bf16[128,1280]{1,0:T(8,128)(2,1)S(1)} %maximum_select_fusion.3), channel_id=1, source_target_pairs={{0,8},{8,0},{16,24},{24,16},{1,9},{9,1},{17,25},{25,17},{2,10},{10... | collective-permute-start | bytes 983048 | tf_op jit(solution)/shard_map/ppermute | solution.py:267
  180.9 18.9 %collective-permute-start.15 = (bf16[256,1280]{1,0:T(8,128)(2,1)S(1)}, bf16[256,1280]{1,0:T(8,128)(2,1)S(1)}, u32[]{:S(2)}, u32[]{:S(2)}) collective-permute-start(bf16[256,1280]{1,0:T(8,128)(2,1)S(1)} %pad_maximum_fusion.2), channel_id=1, source_target_pairs={{0,4},{1,3},{2,6},{3,1},{4,0},{5,7},{6,2},{7,5},{8,12},{9,11},{10,... | collective-permute-start | bytes 1966088 | tf_op jit(solution)/shard_map/ppermute | solution.py:267
  200.1 17.8 %collective-permute-start.16 = (bf16[512,1280]{1,0:T(8,128)(2,1)S(1)}, bf16[512,1280]{1,0:T(8,128)(2,1)S(1)}, u32[]{:S(2)}, u32[]{:S(2)}) collective-permute-start(bf16[512,1280]{1,0:T(8,128)(2,1)S(1)} %pad_maximum_fusion.1), channel_id=1, source_target_pairs={{0,2},{1,5},{2,0},{3,7},{4,6},{5,1},{6,4},{7,3},{8,10},{9,13},{10,... | collective-permute-start | bytes 3932168 | tf_op jit(solution)/shard_map/ppermute | solution.py:267
  218.1 5.1 %copy-start.1 = (bf16[1024,1280]{1,0:T(8,128)(2,1)}, bf16[1024,1280]{1,0:T(8,128)(2,1)S(1)}, u32[]{:S(2)}) copy-start(bf16[1024,1280]{1,0:T(8,128)(2,1)S(1)} %pad_maximum_fusion.near_ref) | copy-start | bytes 7864324
  218.1 5.1 %collective-permute-start.17 = (bf16[1024,1280]{1,0:T(8,128)(2,1)S(1)}, bf16[1024,1280]{1,0:T(8,128)(2,1)}, u32[]{:S(2)}, u32[]{:S(2)}) collective-permute-start(bf16[1024,1280]{1,0:T(8,128)(2,1)S(1)} %pad_maximum_fusion.near_ref), channel_id=1, source_target_pairs={{0,1},{1,0},{2,3},{3,2},{4,5},{5,4},{6,7},{7,6},{8,9},{9,8},{10,11... | collective-permute-start | bytes 7864328 | tf_op jit(solution)/shard_map/ppermute | solution.py:267
  272.1 6.5 %collective-permute-start.18 = (f32[32,512]{1,0:T(8,128)}, f32[32,512]{1,0:T(8,128)S(1)}, u32[]{:S(2)}, u32[]{:S(2)}) collective-permute-start(f32[32,512]{1,0:T(8,128)} %shard_map.39), channel_id=1, source_target_pairs={{0,16},{8,24},{16,0},{24,8},{1,17},{9,25},{17,1},{25,9},{2,18},{10... | collective-permute-start | bytes 196616 | tf_op jit(solution)/shard_map/ppermute | solution.py:267
  279.4 5.4 %collective-permute-start.19 = (f32[32,1024]{1,0:T(8,128)S(1)}, f32[32,1024]{1,0:T(8,128)S(1)}, u32[]{:S(2)}, u32[]{:S(2)}) collective-permute-start(f32[32,1024]{1,0:T(8,128)S(1)} %pad_maximum_fusion.3), channel_id=1, source_target_pairs={{0,8},{8,0},{16,24},{24,16},{1,9},{9,1},{17,25},{25,17},{2,10},{10... | collective-permute-start | bytes 393224 | tf_op jit(solution)/shard_map/ppermute | solution.py:267

commit v3 on v2

--- a/solution.py
+++ b/solution.py
@@ -14,7 +14,6 @@
 PANEL = 16
 GROUP = 40
 SAMPLE_SPACE_LIMIT = 4096
-INTERPRET = False
 F32 = jnp.float32
 BF16 = jnp.bfloat16
 
@@ -55,8 +54,23 @@
     return hi, mid, lo
 
 
-def kernel_call(body, out_shape, **kw):
-    return pl.pallas_call(body, out_shape=out_shape, interpret=INTERPRET, **kw)
+def kernel_call(body, out_shape, in_specs=(), scratch_mib=8, **kw):
+    single = not isinstance(out_shape, tuple)
+    outs = tuple(pltpu.VMEM(o.shape, o.dtype) for o in ((out_shape,) if single else out_shape))
+    call = pl.pallas_call(
+        body,
+        out_shape=outs[0] if single else outs,
+        in_specs=in_specs,
+        compiler_params=pltpu.CompilerParams(vmem_limit_bytes=scratch_mib << 20),
+        **kw,
+    )
+
+    def place(x, spec):
+        if spec.memory_space != pltpu.VMEM:
+            return x
+        return pltpu.with_memory_space_constraint(x, pltpu.VMEM)
+
+    return lambda *args: call(*map(place, args, in_specs))
 
 
 def vmem(n=1):
@@ -167,13 +181,9 @@
         out_ref[to : to + bs, width:] = jnp.concatenate(side, axis=0).T.astype(BF16)
 
 
-def form_first_kernel(at_ref, own_ref, other_ref, q_ref, out_ref, left, right, *wins):
+def form_kernel(at_ref, own_ref, other_ref, q_ref, out_ref, left, right, *wins):
     split_off(own_ref, other_ref, q_ref, left, right)
     form_rows(q_ref.shape[0], at_ref[0], own_ref, other_ref, left, right, out_ref, *wins)
-
-
-def form_second_kernel(k, at_ref, own_ref, other_ref, left, right, out_ref, *wins):
-    form_rows(k, at_ref[0], own_ref, other_ref, left, right, out_ref, *wins)
 
 
 def add_kernel(half_ref, a_ref, b_ref, o_ref):
@@ -318,29 +328,25 @@
     rows = n // 4
     window = rows - bs + width
     piece = jax.ShapeDtypeStruct((rows, width + LANES), BF16)
-    stack = jax.ShapeDtypeStruct((12 * k, n), BF16)
-    wins = [
-        pltpu.VMEM((window, px), BF16),
-        pltpu.VMEM((window, px), BF16),
-        pltpu.VMEM((12 * k, window), BF16),
-    ]
+    form = kernel_call(
+        form_kernel,
+        piece,
+        in_specs=[smem()] + vmem(3),
+        out_specs=vmem()[0],
+        scratch_mib=20,
+        scratch_shapes=[
+            pltpu.VMEM((12 * k, n), BF16),
+            pltpu.VMEM((12 * k, n), BF16),
+            pltpu.VMEM((window, px), BF16),
+            pltpu.VMEM((window, px), BF16),
+            pltpu.VMEM((12 * k, window), BF16),
+        ],
+    )
     blocks = rows // bs
     at = core * 2 * blocks
-    send, left, right = kernel_call(
-        form_first_kernel,
-        (piece, stack, stack),
-        in_specs=[smem()] + vmem(3),
-        out_specs=tuple(vmem(3)),
-        scratch_shapes=wins,
-    )((at + (1 - bit_a) * blocks)[None], block, other, q)
+    send = form((at + (1 - bit_a) * blocks)[None], block, other, q)
     recv = flip(send, "pix", first)
-    keep = kernel_call(
-        functools.partial(form_second_kernel, k),
-        piece,
-        in_specs=[smem()] + vmem(4),
-        out_specs=vmem()[0],
-        scratch_shapes=wins,
-    )((at + bit_a * blocks)[None], block, other, left, right)
+    keep = form((at + bit_a * blocks)[None], block, other, q)
     for axis, perm, bit in (
         ("pix", second, bit_b),
         ("samp", xor_samp(1), z0),
@@ -366,6 +372,7 @@
         (jax.ShapeDtypeStruct((k, n), BF16), jax.ShapeDtypeStruct((k, LANES), F32)),
         in_specs=[smem()] + vmem(4),
         out_specs=tuple(vmem(2)),
+        scratch_mib=24,
         scratch_shapes=[
             pltpu.VMEM((n, n), BF16),
             pltpu.VMEM((8 * k, n), BF16),

time: 287 us -> 269 us (0.937)
  Pallas kernels: 87.2 us -> 72 us
  waiting for transfers between devices: 149 us -> 160 us
  starting transfers between devices: 35.7 us -> 26.9 us
  other arithmetic: 5.77 us -> 1.55 us
    pallas_call x12, Pallas kernels: 87.2 us -> 72 us  [kernel_call(): return lambda *args: call(*map(place, args, in_specs))]
    ppermute x20, waiting for transfers between devices: 105 us -> 116 us  [flip(): return lax.ppermute(x, axes, perm)]
    ppermute x20, starting transfers between devices: 28.4 us -> 19.6 us  [flip(): return lax.ppermute(x, axes, perm)]
  transfers between devices with their start and end apart: 21 -> 21, of which waited for: 19 -> 19; matrix products, arithmetic and copies ran while one was open for 1% -> 1% of each run, Pallas kernels for 6% -> 5%
where the time goes in v3:
time: 269 us
  waiting for transfers between devices  160 us (59%)
  Pallas kernels  72 us (27%)
  starting transfers between devices  26.9 us (10%)
  local copies, waits for them, and re-layouts  6.13 us (2%)
    ppermute x20, waiting for transfers between devices, flip(): return lax.ppermute(x, axes, perm)  116 us
    pallas_call x12, Pallas kernels, kernel_call(): return lambda *args: call(*map(place, args, in_specs))  72 us
    all_to_all x1, waiting for transfers between devices, sample_space(): lax.all_to_all(stamps, ('pix', 'samp'), split_axis=1, concat_axis=0, tile...  43.4 us
    ppermute x20, starting transfers between devices, flip(): return lax.ppermute(x, axes, perm)  19.6 us
    all_to_all x1, starting transfers between devices, sample_space(): lax.all_to_all(stamps, ('pix', 'samp'), split_axis=1, concat_axis=0, tile...  7.33 us
  transfers between devices with their start and end apart: 21, of which 19 were waited for; matrix products, arithmetic and copies ran while one was open for 1% of the time, Pallas kernels for 5%

profile of v3, /device:TPU:0, one launch (start us, length us, event | category | flops | bytes accessed | tf_op | source)
XLA Modules:
  0.0 268.8 jit_solution(7024214909400585572)
XLA Ops:
  0.0 3.2 %copy.6 = bf16[8,32,8,512]{3,2,0,1:T(8,128)(2,1)} copy(bf16[8,32,8,512]{3,2,1,0:T(8,128)(2,1)} %bitcast.25) | data formatting | bytes 4194304 | tf_op jit(solution)/shard_map/all_to_all | solution.py:307
  3.2 7.3 %all-to-all-start = ((bf16[64,32,512]{2,0,1:T(8,128)(2,1)}), bf16[64,32,512]{2,0,1:T(8,128)(2,1)S(1)}, u32[]{:S(2)}, u32[]{:S(2)}) async-start(bf16[64,32,512]{2,0,1:T(8,128)(2,1)} %bitcast.24), calls=%async_computation | async-start | bytes 4194304 | tf_op jit(solution)/shard_map/all_to_all | solution.py:307
  10.9 1.1 collective-permute-done.1
  12.1 1.8 collective-permute-start.2
  13.9 43.4 %all-to-all-done = bf16[64,32,512]{2,0,1:T(8,128)(2,1)S(1)} async-done(((bf16[64,32,512]{2,0,1:T(8,128)(2,1)}), bf16[64,32,512]{2,0,1:T(8,128)(2,1)S(1)}, u32[]{:S(2)}, u32[]{:S(2)}) %all-to-all-start) | async-done | bytes 2097184 | tf_op jit(solution)/shard_map/all_to_all | solution.py:307
  57.3 1.8 collective-permute-start
  59.2 1.6 collective-permute-start.3
  60.8 12.3 %collective-permute-done.3 = bf16[32,8192]{1,0:T(8,128)(2,1)S(1)} collective-permute-done((bf16[32,8192]{1,0:T(8,128)(2,1)S(1)}, bf16[32,8192]{1,0:T(8,128)(2,1)S(1)}, u32[]{:S(2)}, u32[]{:S(2)}) %collective-permute-start.3) | collective-permute-done | bytes 524320 | tf_op jit(solution)/shard_map/ppermute | solution.py:277
  73.1 2.3 convolution_convert_fusion
  75.4 2.5 collective-permute-start.4
  77.9 1.6 collective-permute-done.4
  79.6 1.1 collective-permute-start.5
  80.6 3.5 %collective-permute-done.5 = bf16[32,128]{1,0:T(8,128)(2,1)S(1)} collective-permute-done((bf16[32,128]{1,0:T(8,128)(2,1)S(1)}, bf16[32,128]{1,0:T(8,128)(2,1)S(1)}, u32[]{:S(2)}, u32[]{:S(2)}) %collective-permute-start.5) | collective-permute-done | bytes 8224 | tf_op jit(solution)/shard_map/ppermute | solution.py:277
  84.1 1.2 collective-permute-done.6
  85.3 1.2 collective-permute-start.7
  86.5 2.8 %collective-permute-done.7 = bf16[32,512]{1,0:T(8,128)(2,1)S(1)} collective-permute-done((bf16[32,512]{1,0:T(8,128)(2,1)S(1)}, bf16[32,512]{1,0:T(8,128)(2,1)S(1)}, u32[]{:S(2)}, u32[]{:S(2)}) %collective-permute-start.7) | collective-permute-done | bytes 32800 | tf_op jit(solution)/shard_map/ppermute | solution.py:277
  89.3 1.1 collective-permute-start.8
  90.5 3.2 %collective-permute-done.8 = bf16[32,1024]{1,0:T(8,128)(2,1)S(1)} collective-permute-done((bf16[32,1024]{1,0:T(8,128)(2,1)S(1)}, bf16[32,1024]{1,0:T(8,128)(2,1)S(1)}, u32[]{:S(2)}, u32[]{:S(2)}) %collective-permute-start.8) | collective-permute-done | bytes 65568 | tf_op jit(solution)/shard_map/ppermute | solution.py:277
  93.7 1.4 shard_map.28.q_ref
  95.1 9.9 %shard_map.30 = bf16[512,1280]{1,0:T(8,128)(2,1)} custom-call(s32[1]{0:T(128)} %bitcast.8.at_ref, bf16[2048,512]{1,0:T(8,128)(2,1)S(1)} %bitcast.21, bf16[2048,512]{1,0:T(8,128)(2,1)} %collective-permute-done.other_ref, f32[32,2048]{1,0:T(8,128)S(1)} %shard_map.28.q_ref), custom_call_target="tpu_custom_call" | custom-call | tf_op jit(solution)/shard_map/pallas_call | solution.py:73
  105.0 1.1 collective-permute-start.9
  106.1 0.9 copy-done.3
  107.1 8.8 %shard_map.29.a_ref = bf16[512,1280]{1,0:T(8,128)(2,1)S(1)} custom-call(s32[1]{0:T(128)} %bitcast.3.at_ref, bf16[2048,512]{1,0:T(8,128)(2,1)S(1)} %bitcast.22, bf16[2048,512]{1,0:T(8,128)(2,1)} %collective-permute-done.other_ref, f32[32,2048]{1,0:T(8,128)S(1)} %copy-done.3), custom_call_target="tpu_custom_call" | custom-call | tf_op jit(solution)/shard_map/pallas_call | solution.py:73
  115.9 7.1 %collective-permute-done.9.b_ref = bf16[512,1280]{1,0:T(8,128)(2,1)} collective-permute-done((bf16[512,1280]{1,0:T(8,128)(2,1)}, bf16[512,1280]{1,0:T(8,128)(2,1)}, u32[]{:S(2)}, u32[]{:S(2)}) %collective-permute-start.9) | collective-permute-done | bytes 1310752 | tf_op jit(solution)/shard_map/ppermute | solution.py:277
  122.9 2.7 shard_map.32
  125.6 1.1 collective-permute-start.10
  126.7 2.0 shard_map.31.a_ref
  128.7 7.8 %collective-permute-done.10.b_ref = bf16[256,1280]{1,0:T(8,128)(2,1)} collective-permute-done((bf16[256,1280]{1,0:T(8,128)(2,1)}, bf16[256,1280]{1,0:T(8,128)(2,1)}, u32[]{:S(2)}, u32[]{:S(2)}) %collective-permute-start.10) | collective-permute-done | bytes 655392 | tf_op jit(solution)/shard_map/ppermute | solution.py:277
  136.5 1.4 shard_map.34
  137.9 0.9 copy-done
  138.8 2.0 collective-permute-start.11
  140.8 1.1 copy-done.1
  141.9 1.4 shard_map.33.a_ref
  143.3 4.1 %collective-permute-done.11.b_ref = bf16[128,1280]{1,0:T(8,128)(2,1)S(1)} collective-permute-done((bf16[128,1280]{1,0:T(8,128)(2,1)S(1)}, bf16[128,1280]{1,0:T(8,128)(2,1)S(1)}, u32[]{:S(2)}, u32[]{:S(2)}) %collective-permute-start.11) | collective-permute-done | bytes 327712 | tf_op jit(solution)/shard_map/ppermute | solution.py:277
  147.9 10.9 %collective-permute-done.12.b_ref = bf16[64,1280]{1,0:T(8,128)(2,1)S(1)} collective-permute-done((bf16[64,1280]{1,0:T(8,128)(2,1)S(1)}, bf16[64,1280]{1,0:T(8,128)(2,1)S(1)}, u32[]{:S(2)}, u32[]{:S(2)}) %collective-permute-start.12) | collective-permute-done | bytes 163872 | tf_op jit(solution)/shard_map/ppermute | solution.py:277
  159.1 7.2 %collective-permute-done.13 = bf16[64,1280]{1,0:T(8,128)(2,1)S(1)} collective-permute-done((bf16[64,1280]{1,0:T(8,128)(2,1)S(1)}, bf16[64,1280]{1,0:T(8,128)(2,1)S(1)}, u32[]{:S(2)}, u32[]{:S(2)}) %collective-permute-start.13) | collective-permute-done | bytes 163872 | tf_op jit(solution)/shard_map/ppermute | solution.py:277
  166.5 7.1 %collective-permute-done.14 = bf16[128,1280]{1,0:T(8,128)(2,1)S(1)} collective-permute-done((bf16[128,1280]{1,0:T(8,128)(2,1)S(1)}, bf16[128,1280]{1,0:T(8,128)(2,1)S(1)}, u32[]{:S(2)}, u32[]{:S(2)}) %collective-permute-start.14) | collective-permute-done | bytes 327712 | tf_op jit(solution)/shard_map/ppermute | solution.py:277
  173.6 0.8 collective-permute-start.15
  174.4 15.0 %collective-permute-done.15 = bf16[256,1280]{1,0:T(8,128)(2,1)S(1)} collective-permute-done((bf16[256,1280]{1,0:T(8,128)(2,1)S(1)}, bf16[256,1280]{1,0:T(8,128)(2,1)S(1)}, u32[]{:S(2)}, u32[]{:S(2)}) %collective-permute-start.15) | collective-permute-done | bytes 655392 | tf_op jit(solution)/shard_map/ppermute | solution.py:277
  189.5 1.6 collective-permute-start.16
  191.1 16.1 %collective-permute-done.16 = bf16[512,1280]{1,0:T(8,128)(2,1)S(1)} collective-permute-done((bf16[512,1280]{1,0:T(8,128)(2,1)S(1)}, bf16[512,1280]{1,0:T(8,128)(2,1)S(1)}, u32[]{:S(2)}, u32[]{:S(2)}) %collective-permute-start.16) | collective-permute-done | bytes 1310752 | tf_op jit(solution)/shard_map/ppermute | solution.py:277
  207.5 4.9 %collective-permute-done.17.far_ref = bf16[1024,1280]{1,0:T(8,128)(2,1)S(1)} collective-permute-done((bf16[1024,1280]{1,0:T(8,128)(2,1)S(1)}, bf16[1024,1280]{1,0:T(8,128)(2,1)S(1)}, u32[]{:S(2)}, u32[]{:S(2)}) %collective-permute-start.17) | collective-permute-done | bytes 2621472 | tf_op jit(solution)/shard_map/ppermute | solution.py:277
  212.4 43.3 %shard_map.38 = (bf16[32,2048]{1,0:T(8,128)(2,1)S(1)}, f32[32,128]{1,0:T(8,128)S(1)}) custom-call(s32[16]{0:T(128)S(1)} %xor_add_fusion.index_ref, bf16[1024,1280]{1,0:T(8,128)(2,1)S(1)} %pad_maximum_fusion.near_ref, bf16[1024,1280]{1,0:T(8,128)(2,1)S(1)} %collective-permute-done.17.far_ref, f32[32,2048]{1,0:T(8,128)S(1)} %copy-done.4, ...), custom_call_target="tpu_custom_call" | custom-call | tf_op jit(solution)/shard_map/pallas_call | solution.py:73
  255.7 0.6 shard_map.39
  256.3 1.3 collective-permute-start.18
  257.6 4.9 %collective-permute-done.18 = f32[32,512]{1,0:T(8,128)S(1)} collective-permute-done((f32[32,512]{1,0:T(8,128)S(1)}, f32[32,512]{1,0:T(8,128)S(1)}, u32[]{:S(2)}, u32[]{:S(2)}) %collective-permute-start.18) | collective-permute-done | bytes 65568 | tf_op jit(solution)/shard_map/ppermute | solution.py:277
  262.6 5.4 %collective-permute-done.19 = f32[32,1024]{1,0:T(8,128)S(1)} collective-permute-done((f32[32,1024]{1,0:T(8,128)S(1)}, f32[32,1024]{1,0:T(8,128)S(1)}, u32[]{:S(2)}, u32[]{:S(2)}) %collective-permute-start.19) | collective-permute-done | bytes 131104 | tf_op jit(solution)/shard_map/ppermute | solution.py:277
  268.0 0.7 maximum_bitcast_fusion
  (36 shorter events, 2.1 us)
Async XLA Ops:
  3.2 7.3 %copy-start.5 = (f32[2048,32]{0,1:T(8,128)S(1)}, f32[2048,32]{0,1:T(8,128)}, u32[]{:S(2)}) copy-start(f32[2048,32]{0,1:T(8,128)} %param.3) | copy-start | bytes 786436
  3.2 54.1 %all-to-all-start = ((bf16[64,32,512]{2,0,1:T(8,128)(2,1)}), bf16[64,32,512]{2,0,1:T(8,128)(2,1)S(1)}, u32[]{:S(2)}, u32[]{:S(2)}) async-start(bf16[64,32,512]{2,0,1:T(8,128)(2,1)} %bitcast.24), calls=%async_computation | async-start | bytes 4194304 | tf_op jit(solution)/shard_map/all_to_all | solution.py:307
  10.6 1.4 collective-permute-start.1
  12.1 47.0 %collective-permute-start.2 = (bf16[32,4096]{1,0:T(8,128)(2,1)S(1)}, bf16[32,4096]{1,0:T(8,128)(2,1)S(1)}, u32[]{:S(2)}, u32[]{:S(2)}) collective-permute-start(bf16[32,4096]{1,0:T(8,128)(2,1)S(1)} %maximum_select_fusion.4), channel_id=1, source_target_pairs={{0,2},{1,3},{2,0},{3,1},{4,6},{5,7},{6,4},{7,5},{8,10},{9,11},{10,... | collective-permute-start | bytes 786440 | tf_op jit(solution)/shard_map/ppermute | solution.py:277
  57.3 37.8 %collective-permute-start = (bf16[2048,512]{1,0:T(8,128)(2,1)S(1)}, bf16[2048,512]{1,0:T(8,128)(2,1)}, u32[]{:S(2)}, u32[]{:S(2)}) collective-permute-start(bf16[2048,512]{1,0:T(8,128)(2,1)S(1)} %bitcast.20), channel_id=1, source_target_pairs={{0,1},{1,0},{2,3},{3,2},{4,5},{5,4},{6,7},{7,6},{8,9},{9,8},{10,11... | collective-permute-start | bytes 6291464 | tf_op jit(solution)/shard_map/ppermute | solution.py:277
  59.2 13.9 %collective-permute-start.3 = (bf16[32,8192]{1,0:T(8,128)(2,1)S(1)}, bf16[32,8192]{1,0:T(8,128)(2,1)S(1)}, u32[]{:S(2)}, u32[]{:S(2)}) collective-permute-start(bf16[32,8192]{1,0:T(8,128)(2,1)S(1)} %maximum_select_fusion.2), channel_id=1, source_target_pairs={{0,4},{1,5},{2,6},{3,7},{4,0},{5,1},{6,2},{7,3},{8,12},{9,13},{10,... | collective-permute-start | bytes 1572872 | tf_op jit(solution)/shard_map/ppermute | solution.py:277
  75.4 4.1 %collective-permute-start.4 = (bf16[32,64]{1,0:T(8,128)(2,1)S(1)}, bf16[32,64]{1,0:T(8,128)(2,1)S(1)}, u32[]{:S(2)}, u32[]{:S(2)}) collective-permute-start(bf16[32,64]{1,0:T(8,128)(2,1)S(1)} %convolution_convert_fusion), channel_id=1, source_target_pairs={{0,8},{8,0},{16,24},{24,16},{1,9},{9,1},{17,25},{25,17},{2,10},{10... | collective-permute-start | bytes 12296 | tf_op jit(solution)/shard_map/ppermute | solution.py:277
  79.6 4.6 %collective-permute-start.5 = (bf16[32,128]{1,0:T(8,128)(2,1)S(1)}, bf16[32,128]{1,0:T(8,128)(2,1)S(1)}, u32[]{:S(2)}, u32[]{:S(2)}) collective-permute-start(bf16[32,128]{1,0:T(8,128)(2,1)S(1)} %maximum_select_fusion.9), channel_id=1, source_target_pairs={{0,16},{8,24},{16,0},{24,8},{1,17},{9,25},{17,1},{25,9},{2,18},{10... | collective-permute-start | bytes 24584 | tf_op jit(solution)/shard_map/ppermute | solution.py:277
  84.1 1.2 collective-permute-start.6
  85.3 4.0 %collective-permute-start.7 = (bf16[32,512]{1,0:T(8,128)(2,1)S(1)}, bf16[32,512]{1,0:T(8,128)(2,1)S(1)}, u32[]{:S(2)}, u32[]{:S(2)}) collective-permute-start(bf16[32,512]{1,0:T(8,128)(2,1)S(1)} %maximum_select_fusion.7), channel_id=1, source_target_pairs={{0,2},{1,3},{2,0},{3,1},{4,6},{5,7},{6,4},{7,5},{8,10},{9,11},{10,... | collective-permute-start | bytes 98312 | tf_op jit(solution)/shard_map/ppermute | solution.py:277
  89.3 4.3 %collective-permute-start.8 = (bf16[32,1024]{1,0:T(8,128)(2,1)S(1)}, bf16[32,1024]{1,0:T(8,128)(2,1)S(1)}, u32[]{:S(2)}, u32[]{:S(2)}) collective-permute-start(bf16[32,1024]{1,0:T(8,128)(2,1)S(1)} %maximum_select_fusion.6), channel_id=1, source_target_pairs={{0,4},{1,5},{2,6},{3,7},{4,0},{5,1},{6,2},{7,3},{8,12},{9,13},{10,... | collective-permute-start | bytes 196616 | tf_op jit(solution)/shard_map/ppermute | solution.py:277
  95.1 10.0 %copy-start.2 = (f32[32,2048]{1,0:T(8,128)}, f32[32,2048]{1,0:T(8,128)S(1)}, u32[]{:S(2)}) copy-start(f32[32,2048]{1,0:T(8,128)S(1)} %shard_map.28.q_ref) | copy-start | bytes 786436
  105.0 17.9 %collective-permute-start.9 = (bf16[512,1280]{1,0:T(8,128)(2,1)}, bf16[512,1280]{1,0:T(8,128)(2,1)}, u32[]{:S(2)}, u32[]{:S(2)}) collective-permute-start(bf16[512,1280]{1,0:T(8,128)(2,1)} %shard_map.30), channel_id=1, source_target_pairs={{0,2},{1,5},{2,0},{3,7},{4,6},{5,1},{6,4},{7,3},{8,10},{9,13},{10,... | collective-permute-start | bytes 3932168 | tf_op jit(solution)/shard_map/ppermute | solution.py:277
  106.1 0.9 copy-start.3
  125.6 10.9 %collective-permute-start.10 = (bf16[256,1280]{1,0:T(8,128)(2,1)}, bf16[256,1280]{1,0:T(8,128)(2,1)}, u32[]{:S(2)}, u32[]{:S(2)}) collective-permute-start(bf16[256,1280]{1,0:T(8,128)(2,1)} %shard_map.32), channel_id=1, source_target_pairs={{0,4},{1,3},{2,6},{3,1},{4,0},{5,7},{6,2},{7,5},{8,12},{9,11},{10,... | collective-permute-start | bytes 1966088 | tf_op jit(solution)/shard_map/ppermute | solution.py:277
  137.9 0.9 copy-start
  138.8 8.6 %collective-permute-start.11 = (bf16[128,1280]{1,0:T(8,128)(2,1)S(1)}, bf16[128,1280]{1,0:T(8,128)(2,1)S(1)}, u32[]{:S(2)}, u32[]{:S(2)}) collective-permute-start(bf16[128,1280]{1,0:T(8,128)(2,1)S(1)} %shard_map.34), channel_id=1, source_target_pairs={{0,8},{8,0},{16,24},{24,16},{1,9},{9,1},{17,25},{25,17},{2,10},{10... | collective-permute-start | bytes 983048 | tf_op jit(solution)/shard_map/ppermute | solution.py:277
  140.8 1.1 copy-start.1
  147.6 11.2 %collective-permute-start.12 = (bf16[64,1280]{1,0:T(8,128)(2,1)S(1)}, bf16[64,1280]{1,0:T(8,128)(2,1)S(1)}, u32[]{:S(2)}, u32[]{:S(2)}) collective-permute-start(bf16[64,1280]{1,0:T(8,128)(2,1)S(1)} %shard_map.36), channel_id=1, source_target_pairs={{0,16},{8,24},{16,0},{24,8},{1,17},{9,25},{17,1},{25,9},{2,18},{10... | collective-permute-start | bytes 491528 | tf_op jit(solution)/shard_map/ppermute | solution.py:277
  159.0 7.3 %collective-permute-start.13 = (bf16[64,1280]{1,0:T(8,128)(2,1)S(1)}, bf16[64,1280]{1,0:T(8,128)(2,1)S(1)}, u32[]{:S(2)}, u32[]{:S(2)}) collective-permute-start(bf16[64,1280]{1,0:T(8,128)(2,1)S(1)} %shard_map.37), channel_id=1, source_target_pairs={{0,16},{8,24},{16,0},{24,8},{1,17},{9,25},{17,1},{25,9},{2,18},{10... | collective-permute-start | bytes 491528 | tf_op jit(solution)/shard_map/ppermute | solution.py:277
  166.4 7.1 %collective-permute-start.14 = (bf16[128,1280]{1,0:T(8,128)(2,1)S(1)}, bf16[128,1280]{1,0:T(8,128)(2,1)S(1)}, u32[]{:S(2)}, u32[]{:S(2)}) collective-permute-start(bf16[128,1280]{1,0:T(8,128)(2,1)S(1)} %maximum_select_fusion.3), channel_id=1, source_target_pairs={{0,8},{8,0},{16,24},{24,16},{1,9},{9,1},{17,25},{25,17},{2,10},{10... | collective-permute-start | bytes 983048 | tf_op jit(solution)/shard_map/ppermute | solution.py:277
  173.6 15.8 %collective-permute-start.15 = (bf16[256,1280]{1,0:T(8,128)(2,1)S(1)}, bf16[256,1280]{1,0:T(8,128)(2,1)S(1)}, u32[]{:S(2)}, u32[]{:S(2)}) collective-permute-start(bf16[256,1280]{1,0:T(8,128)(2,1)S(1)} %pad_maximum_fusion.2), channel_id=1, source_target_pairs={{0,4},{1,3},{2,6},{3,1},{4,0},{5,7},{6,2},{7,5},{8,12},{9,11},{10,... | collective-permute-start | bytes 1966088 | tf_op jit(solution)/shard_map/ppermute | solution.py:277
  189.5 22.9 %copy-start.4 = (f32[32,2048]{1,0:T(8,128)S(1)}, f32[32,2048]{1,0:T(8,128)}, u32[]{:S(2)}) copy-start(f32[32,2048]{1,0:T(8,128)} %copy-done.2) | copy-start | bytes 786436
  189.5 17.7 %collective-permute-start.16 = (bf16[512,1280]{1,0:T(8,128)(2,1)S(1)}, bf16[512,1280]{1,0:T(8,128)(2,1)S(1)}, u32[]{:S(2)}, u32[]{:S(2)}) collective-permute-start(bf16[512,1280]{1,0:T(8,128)(2,1)S(1)} %pad_maximum_fusion.1), channel_id=1, source_target_pairs={{0,2},{1,5},{2,0},{3,7},{4,6},{5,1},{6,4},{7,3},{8,10},{9,13},{10,... | collective-permute-start | bytes 3932168 | tf_op jit(solution)/shard_map/ppermute | solution.py:277
  207.4 5.0 %collective-permute-start.17 = (bf16[1024,1280]{1,0:T(8,128)(2,1)S(1)}, bf16[1024,1280]{1,0:T(8,128)(2,1)S(1)}, u32[]{:S(2)}, u32[]{:S(2)}) collective-permute-start(bf16[1024,1280]{1,0:T(8,128)(2,1)S(1)} %pad_maximum_fusion.near_ref), channel_id=1, source_target_pairs={{0,1},{1,0},{2,3},{3,2},{4,5},{5,4},{6,7},{7,6},{8,9},{9,8},{10,11... | collective-permute-start | bytes 7864328 | tf_op jit(solution)/shard_map/ppermute | solution.py:277
  256.3 6.2 %collective-permute-start.18 = (f32[32,512]{1,0:T(8,128)S(1)}, f32[32,512]{1,0:T(8,128)S(1)}, u32[]{:S(2)}, u32[]{:S(2)}) collective-permute-start(f32[32,512]{1,0:T(8,128)S(1)} %shard_map.39), channel_id=1, source_target_pairs={{0,16},{8,24},{16,0},{24,8},{1,17},{9,25},{17,1},{25,9},{2,18},{10... | collective-permute-start | bytes 196616 | tf_op jit(solution)/shard_map/ppermute | solution.py:277
  262.5 5.5 %collective-permute-start.19 = (f32[32,1024]{1,0:T(8,128)S(1)}, f32[32,1024]{1,0:T(8,128)S(1)}, u32[]{:S(2)}, u32[]{:S(2)}) collective-permute-start(f32[32,1024]{1,0:T(8,128)S(1)} %pad_maximum_fusion.3), channel_id=1, source_target_pairs={{0,8},{8,0},{16,24},{24,16},{1,9},{9,1},{17,25},{25,17},{2,10},{10... | collective-permute-start | bytes 393224 | tf_op jit(solution)/shard_map/ppermute | solution.py:277

commit v4 on v3

--- a/solution.py
+++ b/solution.py
@@ -125,8 +125,32 @@
     return dot(left, right, NN)
 
 
-def basis_kernel(p0_ref, q_ref):
-    p0 = p0_ref[...]
+def rows_kernel(index_ref, near_ref, far_ref, stamps_ref, o_ref):
+    m = near_ref.shape[1] * 2 // index_ref.shape[0]
+    total = jnp.zeros(o_ref.shape, F32)
+    for j in range(index_ref.shape[0]):
+        ref = near_ref if j * m < near_ref.shape[1] else far_ref
+        at = j * m % near_ref.shape[1]
+        stamps = stamps_ref[:, pl.ds(pl.multiple_of(index_ref[j] * m, LANES), m)]
+        total += dot(ref[:, at : at + m], stamps, NT)
+    o_ref[...] = total.astype(BF16)
+
+
+def basis_kernel(pix, samp, p0_ref, p_ref, q_ref):
+    k, n = p0_ref.shape
+    m = n // (pix * samp)
+    per = LANES // m
+    lane = lax.broadcasted_iota(jnp.int32, (k, LANES), 1)
+    for to in range(n // LANES):
+        block = jnp.zeros((k, LANES), F32)
+        for j in range(per):
+            p, s = divmod(to * per + j, samp)
+            group, slot = divmod(s * pix + p, per)
+            part = p0_ref[:, group * LANES : (group + 1) * LANES].astype(F32)
+            part = pltpu.roll(part, (j - slot) * m % LANES, 1) if j != slot else part
+            block = jnp.where(lane // m == j, part, block)
+        p_ref[:, to * LANES : (to + 1) * LANES] = block.astype(BF16)
+    p0 = p_ref[...]
     zeros = jnp.zeros_like(p0)
     gram = gram_of(p0, (p0, zeros, zeros), zeros)
     q_ref[...] = apply_lower(inverse_lower(gram), (p0, zeros, zeros), zeros)
@@ -270,7 +294,7 @@
 def finish_kernel(scale, p_ref, inv_ref, block_ref, o_ref):
     back = dot(p_ref[...], block_ref[...], NN)
     zeros = jnp.zeros(back.shape, BF16)
-    o_ref[...] = apply_lower(inv_ref[...], split3(back), zeros) * scale
+    o_ref[...] = (apply_lower(inv_ref[...], split3(back), zeros) * scale).astype(BF16)
 
 
 def flip(x, axes, perm):
@@ -301,18 +325,29 @@
     z0, z1 = s & 1, (s >> 1) & 1
 
     low = start_panel.astype(BF16).T
+    for b in (2, 4):
+        low = jnp.concatenate([low, flip(low, "pix", xor_pix(b))], axis=1)
+    far = flip(low, "pix", xor_pix(1))
+    at = jnp.arange(pix, dtype=jnp.int32)
+    index = p ^ (((at & 1) << 1) | ((at & 2) << 1) | (at >> 2))
+
+    block = lax.all_to_all(stamps, ("pix", "samp"), split_axis=1, concat_axis=0, tiled=True)
+
+    proj = kernel_call(
+        rows_kernel,
+        jax.ShapeDtypeStruct((k, stamps.shape[0]), BF16),
+        in_specs=[smem()] + vmem(3),
+        out_specs=vmem()[0],
+    )(index, low, far, stamps)
     for b in (1, 2, 4):
-        low = ordered(low, flip(low, "pix", xor_pix(b)), p & b, axis=1)
-
-    block = lax.all_to_all(stamps, ("pix", "samp"), split_axis=1, concat_axis=0, tiled=True)
-
-    proj = dot(low, stamps, NT).astype(BF16)
+        proj = ordered(proj, flip(proj, "pix", xor_pix(b)), p & b, axis=1)
     for b in (1, 2):
         proj = ordered(proj, flip(proj, "samp", xor_samp(b)), s & b, axis=1)
-    for b in (1, 2, 4):
-        proj = ordered(proj, flip(proj, "pix", xor_pix(b)), p & b, axis=1)
-    q = kernel_call(
-        basis_kernel, jax.ShapeDtypeStruct((k, n), F32), in_specs=vmem(), out_specs=vmem()[0]
+    proj, q = kernel_call(
+        functools.partial(basis_kernel, pix, samp),
+        (jax.ShapeDtypeStruct((k, n), BF16), jax.ShapeDtypeStruct((k, n), F32)),
+        in_specs=vmem(),
+        out_specs=tuple(vmem(2)),
     )(proj)
 
     first = [(i, i ^ (2 if i % 2 == 0 else 4)) for i in range(pix)]
@@ -383,7 +418,7 @@
 
     mine = kernel_call(
         functools.partial(finish_kernel, scale),
-        jax.ShapeDtypeStruct((k, px), F32),
+        jax.ShapeDtypeStruct((k, px), BF16),
         in_specs=vmem(3),
         out_specs=vmem()[0],
     )(proj, inv, block)
@@ -393,7 +428,7 @@
     by_distance = {0: parts[0], 2: parts[1], 1: parts[2], 3: parts[3]}
     swap0 = [jnp.where(z0 == 0, by_distance[i], by_distance[i ^ 1]) for i in range(samp)]
     swap1 = [jnp.where(z1 == 0, swap0[i], swap0[i ^ 2]) for i in range(samp)]
-    return jnp.concatenate(swap1, axis=1).T
+    return jnp.concatenate(swap1, axis=1).astype(F32).T
 
 
 def solution(mesh):

time: 269 us -> 257 us (0.955)
  waiting for transfers between devices: 160 us -> 141 us
  starting transfers between devices: 26.9 us -> 32.5 us
    all_to_all x1, waiting for transfers between devices: 43.4 us -> 26 us  [sample_space(): lax.all_to_all(stamps, ('pix', 'samp'), split_axis=1, concat_axis=0, tile...]
    ppermute x20, starting transfers between devices: 19.6 us -> 25.2 us  [flip(): return lax.ppermute(x, axes, perm)]
    pallas_call x12 -> x13, Pallas kernels: 72 us -> 73.3 us  [kernel_call(): return lambda *args: call(*map(place, args, in_specs))]
  transfers between devices with their start and end apart: 21 -> 21, of which waited for: 19 -> 19; matrix products, arithmetic and copies ran while one was open for 1% -> 0% of each run, Pallas kernels for 5% -> 6%
where the time goes in v4:
time: 257 us; the launch traced here: 256 us
  waiting for transfers between devices  141 us (55%)
  Pallas kernels  73.3 us (29%)
  starting transfers between devices  32.5 us (13%)
  local copies, waits for them, and re-layouts  7.74 us (3%)
    ppermute x20, waiting for transfers between devices, flip(): return lax.ppermute(x, axes, perm)  115 us
    pallas_call x13, Pallas kernels, kernel_call(): return lambda *args: call(*map(place, args, in_specs))  73.3 us
    all_to_all x1, waiting for transfers between devices, sample_space(): lax.all_to_all(stamps, ('pix', 'samp'), split_axis=1, concat_axis=0, tile...  26 us
    ppermute x20, starting transfers between devices, flip(): return lax.ppermute(x, axes, perm)  25.2 us
    all_to_all x1, starting transfers between devices, sample_space(): lax.all_to_all(stamps, ('pix', 'samp'), split_axis=1, concat_axis=0, tile...  7.33 us
  transfers between devices with their start and end apart: 21, of which 19 were waited for; matrix products, arithmetic and copies ran while one was open for 0% of the time, Pallas kernels for 6%

profile of v4, /device:TPU:0, one launch (start us, length us, event | category | flops | bytes accessed | tf_op | source)
XLA Modules:
  0.0 256.4 jit_solution(3056991719840743435)
XLA Ops:
  0.0 3.2 %copy.6 = bf16[8,32,8,512]{3,2,0,1:T(8,128)(2,1)} copy(bf16[8,32,8,512]{3,2,1,0:T(8,128)(2,1)} %bitcast.23) | data formatting | bytes 4194304 | tf_op jit(solution)/shard_map/all_to_all | solution.py:334
  3.2 7.3 %all-to-all-start = ((bf16[64,32,512]{2,0,1:T(8,128)(2,1)}), bf16[64,32,512]{2,0,1:T(8,128)(2,1)S(1)}, u32[]{:S(2)}, u32[]{:S(2)}) async-start(bf16[64,32,512]{2,0,1:T(8,128)(2,1)} %bitcast.24), calls=%async_computation | async-start | bytes 4194304 | tf_op jit(solution)/shard_map/all_to_all | solution.py:334
  10.6 1.8 collective-permute-start.1
  12.4 17.3 %collective-permute-done.1 = bf16[32,2048]{1,0:T(8,128)(2,1)S(1)} collective-permute-done((bf16[32,2048]{1,0:T(8,128)(2,1)S(1)}, bf16[32,2048]{1,0:T(8,128)(2,1)S(1)}, u32[]{:S(2)}, u32[]{:S(2)}) %collective-permute-start.1) | collective-permute-done | bytes 131104 | tf_op jit(solution)/shard_map/ppermute | solution.py:301
  29.8 1.5 collective-permute-start.2
  31.3 26.0 %all-to-all-done = bf16[64,32,512]{2,0,1:T(8,128)(2,1)S(1)} async-done(((bf16[64,32,512]{2,0,1:T(8,128)(2,1)}), bf16[64,32,512]{2,0,1:T(8,128)(2,1)S(1)}, u32[]{:S(2)}, u32[]{:S(2)}) %all-to-all-start) | async-done | bytes 2097184 | tf_op jit(solution)/shard_map/all_to_all | solution.py:334
  57.3 1.8 collective-permute-start
  59.3 4.4 %collective-permute-done.3.far_ref = bf16[32,8192]{1,0:T(8,128)(2,1)S(1)} collective-permute-done((bf16[32,8192]{1,0:T(8,128)(2,1)S(1)}, bf16[32,8192]{1,0:T(8,128)(2,1)S(1)}, u32[]{:S(2)}, u32[]{:S(2)}) %collective-permute-start.3) | collective-permute-done | bytes 524320 | tf_op jit(solution)/shard_map/ppermute | solution.py:301
  63.7 1.6 copy-done
  65.2 1.2 shard_map.28
  66.8 0.8 collective-permute-done.4
  67.8 1.5 collective-permute-start.5
  69.3 2.1 collective-permute-done.5
  71.4 1.5 collective-permute-start.6
  72.9 2.2 collective-permute-done.6
  75.2 2.4 collective-permute-start.7
  77.5 1.9 collective-permute-done.7
  79.4 1.2 collective-permute-start.8
  80.6 4.0 %collective-permute-done.8 = bf16[32,1024]{1,0:T(8,128)(2,1)S(1)} collective-permute-done((bf16[32,1024]{1,0:T(8,128)(2,1)S(1)}, bf16[32,1024]{1,0:T(8,128)(2,1)S(1)}, u32[]{:S(2)}, u32[]{:S(2)}) %collective-permute-start.8) | collective-permute-done | bytes 65568 | tf_op jit(solution)/shard_map/ppermute | solution.py:301
  84.7 1.4 shard_map.29
  86.2 10.0 %shard_map.31 = bf16[512,1280]{1,0:T(8,128)(2,1)} custom-call(s32[1]{0:T(128)} %bitcast.8.at_ref, bf16[2048,512]{1,0:T(8,128)(2,1)S(1)} %bitcast.20, bf16[2048,512]{1,0:T(8,128)(2,1)} %collective-permute-done.other_ref, f32[32,2048]{1,0:T(8,128)S(1)} %get-tuple-element.9.q_ref), custom_call_target="tpu_custom_call" | custom-call | tf_op jit(solution)/shard_map/pallas_call | solution.py:73
  96.1 2.0 collective-permute-start.9
  98.1 0.9 copy-done.4
  99.0 8.8 %shard_map.30.a_ref = bf16[512,1280]{1,0:T(8,128)(2,1)S(1)} custom-call(s32[1]{0:T(128)} %bitcast.3.at_ref, bf16[2048,512]{1,0:T(8,128)(2,1)S(1)} %bitcast.21, bf16[2048,512]{1,0:T(8,128)(2,1)} %collective-permute-done.other_ref, f32[32,2048]{1,0:T(8,128)S(1)} %copy-done.4), custom_call_target="tpu_custom_call" | custom-call | tf_op jit(solution)/shard_map/pallas_call | solution.py:73
  107.8 6.2 %collective-permute-done.9.b_ref = bf16[512,1280]{1,0:T(8,128)(2,1)} collective-permute-done((bf16[512,1280]{1,0:T(8,128)(2,1)}, bf16[512,1280]{1,0:T(8,128)(2,1)}, u32[]{:S(2)}, u32[]{:S(2)}) %collective-permute-start.9) | collective-permute-done | bytes 1310752 | tf_op jit(solution)/shard_map/ppermute | solution.py:301
  114.0 2.7 %shard_map.33 = bf16[256,1280]{1,0:T(8,128)(2,1)} custom-call(s32[1]{0:T(128)} %bitcast.9.half_ref, bf16[512,1280]{1,0:T(8,128)(2,1)S(1)} %shard_map.30.a_ref, bf16[512,1280]{1,0:T(8,128)(2,1)} %collective-permute-done.9.b_ref), custom_call_target="tpu_custom_call" | custom-call | tf_op jit(solution)/shard_map/pallas_call | solution.py:73
  116.7 1.2 collective-permute-start.10
  117.9 2.0 shard_map.32.a_ref
  119.9 7.7 %collective-permute-done.10.b_ref = bf16[256,1280]{1,0:T(8,128)(2,1)} collective-permute-done((bf16[256,1280]{1,0:T(8,128)(2,1)}, bf16[256,1280]{1,0:T(8,128)(2,1)}, u32[]{:S(2)}, u32[]{:S(2)}) %collective-permute-start.10) | collective-permute-done | bytes 655392 | tf_op jit(solution)/shard_map/ppermute | solution.py:301
  127.6 1.4 shard_map.35
  129.0 0.9 copy-done.1
  129.9 2.0 collective-permute-start.11
  131.9 1.1 copy-done.2
  133.0 1.4 shard_map.34.a_ref
  134.4 4.3 %collective-permute-done.11.b_ref = bf16[128,1280]{1,0:T(8,128)(2,1)S(1)} collective-permute-done((bf16[128,1280]{1,0:T(8,128)(2,1)S(1)}, bf16[128,1280]{1,0:T(8,128)(2,1)S(1)}, u32[]{:S(2)}, u32[]{:S(2)}) %collective-permute-start.11) | collective-permute-done | bytes 327712 | tf_op jit(solution)/shard_map/ppermute | solution.py:301
  138.9 1.3 collective-permute-start.12
  140.4 6.9 %collective-permute-done.12.b_ref = bf16[64,1280]{1,0:T(8,128)(2,1)S(1)} collective-permute-done((bf16[64,1280]{1,0:T(8,128)(2,1)S(1)}, bf16[64,1280]{1,0:T(8,128)(2,1)S(1)}, u32[]{:S(2)}, u32[]{:S(2)}) %collective-permute-start.12) | collective-permute-done | bytes 163872 | tf_op jit(solution)/shard_map/ppermute | solution.py:301
  147.6 6.9 %collective-permute-done.13 = bf16[64,1280]{1,0:T(8,128)(2,1)S(1)} collective-permute-done((bf16[64,1280]{1,0:T(8,128)(2,1)S(1)}, bf16[64,1280]{1,0:T(8,128)(2,1)S(1)}, u32[]{:S(2)}, u32[]{:S(2)}) %collective-permute-start.13) | collective-permute-done | bytes 163872 | tf_op jit(solution)/shard_map/ppermute | solution.py:301
  154.7 7.1 %collective-permute-done.14 = bf16[128,1280]{1,0:T(8,128)(2,1)S(1)} collective-permute-done((bf16[128,1280]{1,0:T(8,128)(2,1)S(1)}, bf16[128,1280]{1,0:T(8,128)(2,1)S(1)}, u32[]{:S(2)}, u32[]{:S(2)}) %collective-permute-start.14) | collective-permute-done | bytes 327712 | tf_op jit(solution)/shard_map/ppermute | solution.py:301
  161.8 2.7 %collective-permute-start.15 = (bf16[256,1280]{1,0:T(8,128)(2,1)S(1)}, bf16[256,1280]{1,0:T(8,128)(2,1)S(1)}, u32[]{:S(2)}, u32[]{:S(2)}) collective-permute-start(bf16[256,1280]{1,0:T(8,128)(2,1)S(1)} %pad_maximum_fusion.2), channel_id=1, source_target_pairs={{0,4},{1,3},{2,6},{3,1},{4,0},{5,7},{6,2},{7,5},{8,12},{9,11},{10,... | collective-permute-start | bytes 1966088 | tf_op jit(solution)/shard_map/ppermute | solution.py:301
  164.5 13.8 %collective-permute-done.15 = bf16[256,1280]{1,0:T(8,128)(2,1)S(1)} collective-permute-done((bf16[256,1280]{1,0:T(8,128)(2,1)S(1)}, bf16[256,1280]{1,0:T(8,128)(2,1)S(1)}, u32[]{:S(2)}, u32[]{:S(2)}) %collective-permute-start.15) | collective-permute-done | bytes 655392 | tf_op jit(solution)/shard_map/ppermute | solution.py:301
  178.4 3.4 %collective-permute-start.16 = (bf16[512,1280]{1,0:T(8,128)(2,1)S(1)}, bf16[512,1280]{1,0:T(8,128)(2,1)S(1)}, u32[]{:S(2)}, u32[]{:S(2)}) collective-permute-start(bf16[512,1280]{1,0:T(8,128)(2,1)S(1)} %pad_maximum_fusion.1), channel_id=1, source_target_pairs={{0,2},{1,5},{2,0},{3,7},{4,6},{5,1},{6,4},{7,3},{8,10},{9,13},{10,... | collective-permute-start | bytes 3932168 | tf_op jit(solution)/shard_map/ppermute | solution.py:301
  181.8 15.6 %collective-permute-done.16 = bf16[512,1280]{1,0:T(8,128)(2,1)S(1)} collective-permute-done((bf16[512,1280]{1,0:T(8,128)(2,1)S(1)}, bf16[512,1280]{1,0:T(8,128)(2,1)S(1)}, u32[]{:S(2)}, u32[]{:S(2)}) %collective-permute-start.16) | collective-permute-done | bytes 1310752 | tf_op jit(solution)/shard_map/ppermute | solution.py:301
  197.7 4.9 %collective-permute-done.17.far_ref = bf16[1024,1280]{1,0:T(8,128)(2,1)S(1)} collective-permute-done((bf16[1024,1280]{1,0:T(8,128)(2,1)S(1)}, bf16[1024,1280]{1,0:T(8,128)(2,1)S(1)}, u32[]{:S(2)}, u32[]{:S(2)}) %collective-permute-start.17) | collective-permute-done | bytes 2621472 | tf_op jit(solution)/shard_map/ppermute | solution.py:301
  202.6 43.3 %shard_map.39 = (bf16[32,2048]{1,0:T(8,128)(2,1)S(1)}, f32[32,128]{1,0:T(8,128)S(1)}) custom-call(s32[16]{0:T(128)S(1)} %xor_add_fusion.index_ref, bf16[1024,1280]{1,0:T(8,128)(2,1)S(1)} %pad_maximum_fusion.near_ref, bf16[1024,1280]{1,0:T(8,128)(2,1)S(1)} %collective-permute-done.17.far_ref, f32[32,2048]{1,0:T(8,128)S(1)} %copy-done.5, ...), custom_call_target="tpu_custom_call" | custom-call | tf_op jit(solution)/shard_map/pallas_call | solution.py:73
  246.7 4.7 %collective-permute-done.18 = bf16[32,512]{1,0:T(8,128)(2,1)S(1)} collective-permute-done((bf16[32,512]{1,0:T(8,128)(2,1)S(1)}, bf16[32,512]{1,0:T(8,128)(2,1)S(1)}, u32[]{:S(2)}, u32[]{:S(2)}) %collective-permute-start.18) | collective-permute-done | bytes 32800 | tf_op jit(solution)/shard_map/ppermute | solution.py:301
  251.4 4.3 %collective-permute-done.19 = bf16[32,1024]{1,0:T(8,128)(2,1)S(1)} collective-permute-done((bf16[32,1024]{1,0:T(8,128)(2,1)S(1)}, bf16[32,1024]{1,0:T(8,128)(2,1)S(1)}, u32[]{:S(2)}, u32[]{:S(2)}) %collective-permute-start.19) | collective-permute-done | bytes 65568 | tf_op jit(solution)/shard_map/ppermute | solution.py:301
  255.6 0.7 convert_bitcast_fusion
  (39 shorter events, 2.8 us)
Async XLA Ops:
  3.2 7.3 %copy-start.6 = (f32[2048,32]{0,1:T(8,128)S(1)}, f32[2048,32]{0,1:T(8,128)}, u32[]{:S(2)}) copy-start(f32[2048,32]{0,1:T(8,128)} %param.3) | copy-start | bytes 786436
  3.2 54.1 %all-to-all-start = ((bf16[64,32,512]{2,0,1:T(8,128)(2,1)}), bf16[64,32,512]{2,0,1:T(8,128)(2,1)S(1)}, u32[]{:S(2)}, u32[]{:S(2)}) async-start(bf16[64,32,512]{2,0,1:T(8,128)(2,1)} %bitcast.24), calls=%async_computation | async-start | bytes 4194304 | tf_op jit(solution)/shard_map/all_to_all | solution.py:334
  10.6 19.1 %collective-permute-start.1 = (bf16[32,2048]{1,0:T(8,128)(2,1)S(1)}, bf16[32,2048]{1,0:T(8,128)(2,1)S(1)}, u32[]{:S(2)}, u32[]{:S(2)}) collective-permute-start(bf16[32,2048]{1,0:T(8,128)(2,1)S(1)} %convert_bitcast_fusion.1), channel_id=1, source_target_pairs={{0,2},{1,3},{2,0},{3,1},{4,6},{5,7},{6,4},{7,5},{8,10},{9,11},{10,... | collective-permute-start | bytes 393224 | tf_op jit(solution)/shard_map/ppermute | solution.py:301
  29.8 29.4 %collective-permute-start.2 = (bf16[32,4096]{1,0:T(8,128)(2,1)S(1)}, bf16[32,4096]{1,0:T(8,128)(2,1)S(1)}, u32[]{:S(2)}, u32[]{:S(2)}) collective-permute-start(bf16[32,4096]{1,0:T(8,128)(2,1)S(1)} %pad_maximum_fusion.4), channel_id=1, source_target_pairs={{0,4},{1,5},{2,6},{3,7},{4,0},{5,1},{6,2},{7,3},{8,12},{9,13},{10,... | collective-permute-start | bytes 786440 | tf_op jit(solution)/shard_map/ppermute | solution.py:301
  57.3 28.9 %collective-permute-start = (bf16[2048,512]{1,0:T(8,128)(2,1)S(1)}, bf16[2048,512]{1,0:T(8,128)(2,1)}, u32[]{:S(2)}, u32[]{:S(2)}) collective-permute-start(bf16[2048,512]{1,0:T(8,128)(2,1)S(1)} %bitcast.19), channel_id=1, source_target_pairs={{0,1},{1,0},{2,3},{3,2},{4,5},{5,4},{6,7},{7,6},{8,9},{9,8},{10,11... | collective-permute-start | bytes 6291464 | tf_op jit(solution)/shard_map/ppermute | solution.py:301
  59.2 4.5 %collective-permute-start.3 = (bf16[32,8192]{1,0:T(8,128)(2,1)S(1)}, bf16[32,8192]{1,0:T(8,128)(2,1)S(1)}, u32[]{:S(2)}, u32[]{:S(2)}) collective-permute-start(bf16[32,8192]{1,0:T(8,128)(2,1)S(1)} %pad_maximum_fusion.3.near_ref), channel_id=1, source_target_pairs={{0,1},{1,0},{2,3},{3,2},{4,5},{5,4},{6,7},{7,6},{8,9},{9,8},{10,11... | collective-permute-start | bytes 1572872 | tf_op jit(solution)/shard_map/ppermute | solution.py:301
  63.7 1.6 copy-start
  66.5 1.2 collective-permute-start.4
  67.8 3.7 %collective-permute-start.5 = (bf16[32,128]{1,0:T(8,128)(2,1)S(1)}, bf16[32,128]{1,0:T(8,128)(2,1)S(1)}, u32[]{:S(2)}, u32[]{:S(2)}) collective-permute-start(bf16[32,128]{1,0:T(8,128)(2,1)S(1)} %maximum_select_fusion.5), channel_id=1, source_target_pairs={{0,2},{1,3},{2,0},{3,1},{4,6},{5,7},{6,4},{7,5},{8,10},{9,11},{10,... | collective-permute-start | bytes 24584 | tf_op jit(solution)/shard_map/ppermute | solution.py:301
  71.4 3.7 %collective-permute-start.6 = (bf16[32,256]{1,0:T(8,128)(2,1)S(1)}, bf16[32,256]{1,0:T(8,128)(2,1)S(1)}, u32[]{:S(2)}, u32[]{:S(2)}) collective-permute-start(bf16[32,256]{1,0:T(8,128)(2,1)S(1)} %maximum_select_fusion.4), channel_id=1, source_target_pairs={{0,4},{1,5},{2,6},{3,7},{4,0},{5,1},{6,2},{7,3},{8,12},{9,13},{10,... | collective-permute-start | bytes 49160 | tf_op jit(solution)/shard_map/ppermute | solution.py:301
  75.2 4.2 %collective-permute-start.7 = (bf16[32,512]{1,0:T(8,128)(2,1)S(1)}, bf16[32,512]{1,0:T(8,128)(2,1)S(1)}, u32[]{:S(2)}, u32[]{:S(2)}) collective-permute-start(bf16[32,512]{1,0:T(8,128)(2,1)S(1)} %maximum_select_fusion.3), channel_id=1, source_target_pairs={{0,8},{8,0},{16,24},{24,16},{1,9},{9,1},{17,25},{25,17},{2,10},{10... | collective-permute-start | bytes 98312 | tf_op jit(solution)/shard_map/ppermute | solution.py:301
  79.4 5.2 %collective-permute-start.8 = (bf16[32,1024]{1,0:T(8,128)(2,1)S(1)}, bf16[32,1024]{1,0:T(8,128)(2,1)S(1)}, u32[]{:S(2)}, u32[]{:S(2)}) collective-permute-start(bf16[32,1024]{1,0:T(8,128)(2,1)S(1)} %maximum_select_fusion.2), channel_id=1, source_target_pairs={{0,16},{8,24},{16,0},{24,8},{1,17},{9,25},{17,1},{25,9},{2,18},{10... | collective-permute-start | bytes 196616 | tf_op jit(solution)/shard_map/ppermute | solution.py:301
  86.1 10.0 %copy-start.3 = (f32[32,2048]{1,0:T(8,128)}, f32[32,2048]{1,0:T(8,128)S(1)}, u32[]{:S(2)}) copy-start(f32[32,2048]{1,0:T(8,128)S(1)} %get-tuple-element.9.q_ref) | copy-start | bytes 786436
  96.1 17.9 %collective-permute-start.9 = (bf16[512,1280]{1,0:T(8,128)(2,1)}, bf16[512,1280]{1,0:T(8,128)(2,1)}, u32[]{:S(2)}, u32[]{:S(2)}) collective-permute-start(bf16[512,1280]{1,0:T(8,128)(2,1)} %shard_map.31), channel_id=1, source_target_pairs={{0,2},{1,5},{2,0},{3,7},{4,6},{5,1},{6,4},{7,3},{8,10},{9,13},{10,... | collective-permute-start | bytes 3932168 | tf_op jit(solution)/shard_map/ppermute | solution.py:301
  98.1 0.9 copy-start.4
  116.7 10.9 %collective-permute-start.10 = (bf16[256,1280]{1,0:T(8,128)(2,1)}, bf16[256,1280]{1,0:T(8,128)(2,1)}, u32[]{:S(2)}, u32[]{:S(2)}) collective-permute-start(bf16[256,1280]{1,0:T(8,128)(2,1)} %shard_map.33), channel_id=1, source_target_pairs={{0,4},{1,3},{2,6},{3,1},{4,0},{5,7},{6,2},{7,5},{8,12},{9,11},{10,... | collective-permute-start | bytes 1966088 | tf_op jit(solution)/shard_map/ppermute | solution.py:301
  129.0 0.9 copy-start.1
  129.9 8.8 %collective-permute-start.11 = (bf16[128,1280]{1,0:T(8,128)(2,1)S(1)}, bf16[128,1280]{1,0:T(8,128)(2,1)S(1)}, u32[]{:S(2)}, u32[]{:S(2)}) collective-permute-start(bf16[128,1280]{1,0:T(8,128)(2,1)S(1)} %shard_map.35), channel_id=1, source_target_pairs={{0,8},{8,0},{16,24},{24,16},{1,9},{9,1},{17,25},{25,17},{2,10},{10... | collective-permute-start | bytes 983048 | tf_op jit(solution)/shard_map/ppermute | solution.py:301
  131.9 1.1 copy-start.2
  138.9 8.4 %collective-permute-start.12 = (bf16[64,1280]{1,0:T(8,128)(2,1)S(1)}, bf16[64,1280]{1,0:T(8,128)(2,1)S(1)}, u32[]{:S(2)}, u32[]{:S(2)}) collective-permute-start(bf16[64,1280]{1,0:T(8,128)(2,1)S(1)} %shard_map.37), channel_id=1, source_target_pairs={{0,16},{8,24},{16,0},{24,8},{1,17},{9,25},{17,1},{25,9},{2,18},{10... | collective-permute-start | bytes 491528 | tf_op jit(solution)/shard_map/ppermute | solution.py:301
  147.6 7.0 %collective-permute-start.13 = (bf16[64,1280]{1,0:T(8,128)(2,1)S(1)}, bf16[64,1280]{1,0:T(8,128)(2,1)S(1)}, u32[]{:S(2)}, u32[]{:S(2)}) collective-permute-start(bf16[64,1280]{1,0:T(8,128)(2,1)S(1)} %shard_map.38), channel_id=1, source_target_pairs={{0,16},{8,24},{16,0},{24,8},{1,17},{9,25},{17,1},{25,9},{2,18},{10... | collective-permute-start | bytes 491528 | tf_op jit(solution)/shard_map/ppermute | solution.py:301
  154.6 7.1 %collective-permute-start.14 = (bf16[128,1280]{1,0:T(8,128)(2,1)S(1)}, bf16[128,1280]{1,0:T(8,128)(2,1)S(1)}, u32[]{:S(2)}, u32[]{:S(2)}) collective-permute-start(bf16[128,1280]{1,0:T(8,128)(2,1)S(1)} %maximum_select_fusion), channel_id=1, source_target_pairs={{0,8},{8,0},{16,24},{24,16},{1,9},{9,1},{17,25},{25,17},{2,10},{10... | collective-permute-start | bytes 983048 | tf_op jit(solution)/shard_map/ppermute | solution.py:301
  161.8 16.5 %collective-permute-start.15 = (bf16[256,1280]{1,0:T(8,128)(2,1)S(1)}, bf16[256,1280]{1,0:T(8,128)(2,1)S(1)}, u32[]{:S(2)}, u32[]{:S(2)}) collective-permute-start(bf16[256,1280]{1,0:T(8,128)(2,1)S(1)} %pad_maximum_fusion.2), channel_id=1, source_target_pairs={{0,4},{1,3},{2,6},{3,1},{4,0},{5,7},{6,2},{7,5},{8,12},{9,11},{10,... | collective-permute-start | bytes 1966088 | tf_op jit(solution)/shard_map/ppermute | solution.py:301
  178.4 24.2 %copy-start.5 = (f32[32,2048]{1,0:T(8,128)S(1)}, f32[32,2048]{1,0:T(8,128)}, u32[]{:S(2)}) copy-start(f32[32,2048]{1,0:T(8,128)} %copy-done.3) | copy-start | bytes 786436
  178.4 19.0 %collective-permute-start.16 = (bf16[512,1280]{1,0:T(8,128)(2,1)S(1)}, bf16[512,1280]{1,0:T(8,128)(2,1)S(1)}, u32[]{:S(2)}, u32[]{:S(2)}) collective-permute-start(bf16[512,1280]{1,0:T(8,128)(2,1)S(1)} %pad_maximum_fusion.1), channel_id=1, source_target_pairs={{0,2},{1,5},{2,0},{3,7},{4,6},{5,1},{6,4},{7,3},{8,10},{9,13},{10,... | collective-permute-start | bytes 3932168 | tf_op jit(solution)/shard_map/ppermute | solution.py:301
  197.6 5.0 %collective-permute-start.17 = (bf16[1024,1280]{1,0:T(8,128)(2,1)S(1)}, bf16[1024,1280]{1,0:T(8,128)(2,1)S(1)}, u32[]{:S(2)}, u32[]{:S(2)}) collective-permute-start(bf16[1024,1280]{1,0:T(8,128)(2,1)S(1)} %pad_maximum_fusion.near_ref), channel_id=1, source_target_pairs={{0,1},{1,0},{2,3},{3,2},{4,5},{5,4},{6,7},{7,6},{8,9},{9,8},{10,11... | collective-permute-start | bytes 7864328 | tf_op jit(solution)/shard_map/ppermute | solution.py:301
  246.5 4.8 %collective-permute-start.18 = (bf16[32,512]{1,0:T(8,128)(2,1)S(1)}, bf16[32,512]{1,0:T(8,128)(2,1)S(1)}, u32[]{:S(2)}, u32[]{:S(2)}) collective-permute-start(bf16[32,512]{1,0:T(8,128)(2,1)S(1)} %shard_map.40), channel_id=1, source_target_pairs={{0,16},{8,24},{16,0},{24,8},{1,17},{9,25},{17,1},{25,9},{2,18},{10... | collective-permute-start | bytes 98312 | tf_op jit(solution)/shard_map/ppermute | solution.py:301
  251.4 4.3 %collective-permute-start.19 = (bf16[32,1024]{1,0:T(8,128)(2,1)S(1)}, bf16[32,1024]{1,0:T(8,128)(2,1)S(1)}, u32[]{:S(2)}, u32[]{:S(2)}) collective-permute-start(bf16[32,1024]{1,0:T(8,128)(2,1)S(1)} %pad_maximum_fusion.5), channel_id=1, source_target_pairs={{0,8},{8,0},{16,24},{24,16},{1,9},{9,1},{17,25},{25,17},{2,10},{10... | collective-permute-start | bytes 196616 | tf_op jit(solution)/shard_map/ppermute | solution.py:301

commit v5 on v4

--- a/solution.py
+++ b/solution.py
@@ -13,6 +13,7 @@
 LANES = 128
 PANEL = 16
 GROUP = 40
+STEP = 2
 SAMPLE_SPACE_LIMIT = 4096
 F32 = jnp.float32
 BF16 = jnp.bfloat16
@@ -85,7 +86,7 @@
     k = gram.shape[0]
     lane = lax.broadcasted_iota(jnp.int32, gram.shape, 1)
     row = lax.broadcasted_iota(jnp.int32, gram.shape, 0)
-    m = jnp.where(lane < k, gram, jnp.where(lane == row + k, 1.0, 0.0))
+    m = jnp.where(lane < k, gram, jnp.where(lane % k == row, 1.0, 0.0))
     pivots = jnp.ones(gram.shape, F32)
     for start in range(0, k, PANEL):
         cols = [jnp.broadcast_to(m[:, j : j + 1], m.shape) for j in range(start, start + PANEL)]
@@ -97,32 +98,30 @@
             for later in range(t + 1, PANEL):
                 cols[later] = cols[later] - factor * cols[later][j : j + 1, :]
             m = m - factor * m[j : j + 1, :]
-    return pltpu.roll(m * lax.rsqrt(pivots), LANES - k, 1)
+    return m * lax.rsqrt(pivots)
 
 
 def lane_sum3(x, k):
     return x + pltpu.roll(x, LANES - k, 1) + pltpu.roll(x, LANES - 2 * k, 1)
 
 
-def gram_of(left, parts, zeros):
-    k = left.shape[0]
-    stack = jnp.concatenate(list(parts) + [zeros], axis=0)
-    return lane_sum3(dot(left, stack, NT), k)
-
-
-def apply_lower(inv, parts, zeros):
+def gram_of(parts, right):
+    k = right.shape[0]
+    wide = jnp.concatenate([right, jnp.zeros((3 * k, right.shape[1]), right.dtype)], axis=0)
+    g = dot(jnp.concatenate(parts, axis=0), wide, NT)
+    return g[:k] + g[k : 2 * k] + g[2 * k :]
+
+
+def apply_lower(inv, parts):
     k = inv.shape[0]
     lane = lax.broadcasted_iota(jnp.int32, inv.shape, 1)
-    inv = jnp.where(lane < k, inv, 0.0)
-    inv = inv + pltpu.roll(inv, k, 1)
-    inv = inv + pltpu.roll(inv, 2 * k, 1)
     h1, h2, h3 = [h.astype(F32) for h in split3(inv)]
-    first = jnp.where(lane < 3 * k, h1, h2)
-    second = jnp.where(lane < k, h2, jnp.where(lane < 2 * k, h3, 0.0))
+    first = jnp.where(lane < k, 0.0, h1)
+    second = jnp.where(lane < k, 0.0, jnp.where(lane < 3 * k, h2, h3))
     left = jnp.concatenate([first, second], axis=1).astype(BF16)
     y1, y2, y3 = parts
-    right = jnp.concatenate([y1, y2, y3, y1, y2, y1, zeros, zeros], axis=0)
-    return dot(left, right, NN)
+    zeros = jnp.zeros_like(y1)
+    return dot(left, jnp.concatenate([zeros, y1, y2, y3, zeros, y1, y2, y1], axis=0), NN)
 
 
 def rows_kernel(index_ref, near_ref, far_ref, stamps_ref, o_ref):
@@ -151,9 +150,8 @@
             block = jnp.where(lane // m == j, part, block)
         p_ref[:, to * LANES : (to + 1) * LANES] = block.astype(BF16)
     p0 = p_ref[...]
-    zeros = jnp.zeros_like(p0)
-    gram = gram_of(p0, (p0, zeros, zeros), zeros)
-    q_ref[...] = apply_lower(inverse_lower(gram), (p0, zeros, zeros), zeros)
+    parts = (p0, jnp.zeros_like(p0), jnp.zeros_like(p0))
+    q_ref[...] = apply_lower(inverse_lower(gram_of(parts, p0)), parts)
 
 
 def split_off(own_ref, other_ref, q_ref, left, right):
@@ -170,29 +168,35 @@
         w += w3[:k] + w3[k : 2 * k] + w3[2 * k :]
     ws = jnp.concatenate(list(split3(w)) + [zeros], axis=0)
     m = lane_sum3(dot(q1, ws, NT) + dot(q2, ws, NT) + dot(q3, ws, NT), k)
-    w1, w2, w3 = split3(w - 0.5 * apply_lower(m, (q1, q2, q3), zeros))
+    m = jnp.where(lax.broadcasted_iota(jnp.int32, m.shape, 1) < k, m, 0.0)
+    m = pltpu.roll(m, k, 1) + pltpu.roll(m, 2 * k, 1) + pltpu.roll(m, 3 * k, 1)
+    w1, w2, w3 = split3(w - 0.5 * apply_lower(m, (q1, q2, q3)))
     left[...] = jnp.concatenate([q1, w1, q1, w1, q1, w1, q2, w2, q2, w2, q3, w3], axis=0)
     right[...] = jnp.concatenate([w1, q1, w2, q2, w3, q3, w1, q1, w2, q2, w1, q1], axis=0)
 
 
-def form_rows(k, first, own_ref, other_ref, left, right, out_ref, own_win, other_win, right_win):
-    n = own_ref.shape[0]
+def form_rows(k, first, own_ref, other_ref, left, right, out_ref, window, right_win):
+    n, px = own_ref.shape
     rows, width = out_ref.shape
     width -= LANES
     bs = width - n // 2
     nb = n // bs
-    for b in range(own_win.shape[0] // bs):
+    for b in range(window.shape[0] // bs):
         at = pl.multiple_of(lax.rem(first + b, nb) * bs, bs)
-        own_win[b * bs : (b + 1) * bs, :] = own_ref[pl.ds(at, bs), :]
-        other_win[b * bs : (b + 1) * bs, :] = other_ref[pl.ds(at, bs), :]
+        window[b * bs : (b + 1) * bs, :px] = own_ref[pl.ds(at, bs), :]
+        window[b * bs : (b + 1) * bs, px:] = other_ref[pl.ds(at, bs), :]
         right_win[:, b * bs : (b + 1) * bs] = right[:, pl.ds(at, bs)]
     eye = lax.broadcasted_iota(jnp.int32, (bs, bs), 0) == lax.broadcasted_iota(jnp.int32, (bs, bs), 1)
+    step = STEP * bs
     for i in range(rows // bs):
-        at = pl.multiple_of((first + i) * bs, bs)
-        to, end = i * bs, i * bs + width
-        s = dot(own_win[to : to + bs, :], own_win[to:end, :], NT)
-        s += dot(other_win[to : to + bs, :], other_win[to:end, :], NT)
-        s -= dot(left[:, pl.ds(at, bs)], right_win[:, to:end], TN)
+        if i % STEP == 0:
+            at = pl.multiple_of((first + i) * bs, bs)
+            lo, end = i * bs, i * bs + step - bs + width
+            wide = dot(window[lo : lo + step, :], window[lo:end, :], NT)
+            wide -= dot(left[:, pl.ds(at, step)], right_win[:, lo:end], TN)
+        off = i % STEP * bs
+        to = i * bs
+        s = wide[off : off + bs, off : off + width]
         corner = s[:, :bs]
         diagonal = jnp.sum(jnp.where(eye, corner, 0.0), axis=0, keepdims=True)
         out_ref[to : to + bs, :bs] = jnp.where(eye, 0.0, corner).astype(BF16)
@@ -210,29 +214,29 @@
     form_rows(q_ref.shape[0], at_ref[0], own_ref, other_ref, left, right, out_ref, *wins)
 
 
-def add_kernel(half_ref, a_ref, b_ref, o_ref):
-    h = o_ref.shape[0]
+def add_kernel(at_ref, a_ref, b_ref, *o_refs):
     width = a_ref.shape[1] - LANES
-    at = pl.multiple_of(half_ref[0] * h, h)
-    a, b = a_ref[pl.ds(at, h), :], b_ref[pl.ds(at, h), :]
-    o_ref[:, :width] = (a[:, :width].astype(F32) + b[:, :width].astype(F32)).astype(BF16)
-    x = lane_sum3(a[:, width:].astype(F32), GROUP) + lane_sum3(b[:, width:].astype(F32), GROUP)
-    lane = lax.broadcasted_iota(jnp.int32, x.shape, 1)
-    h1, h2, h3 = [part.astype(F32) for part in split3(x)]
-    packed = jnp.where(lane < 2 * GROUP, pltpu.roll(h2, GROUP, 1), pltpu.roll(h3, 2 * GROUP, 1))
-    packed = jnp.where(lane < GROUP, h1, packed)
-    o_ref[:, width:] = jnp.where(lane < 3 * GROUP, packed, 0.0).astype(BF16)
-
-
-def add_shares(a, b, half=None):
-    rows = a.shape[0] // (1 if half is None else 2)
-    half = jnp.zeros((1,), jnp.int32) if half is None else half[None]
+    for i, o_ref in enumerate(o_refs):
+        h = o_ref.shape[0]
+        at = pl.multiple_of(at_ref[i] * h, h)
+        a, b = a_ref[pl.ds(at, h), :], b_ref[pl.ds(at, h), :]
+        o_ref[:, :width] = (a[:, :width].astype(F32) + b[:, :width].astype(F32)).astype(BF16)
+        x = lane_sum3(a[:, width:].astype(F32), GROUP) + lane_sum3(b[:, width:].astype(F32), GROUP)
+        lane = lax.broadcasted_iota(jnp.int32, x.shape, 1)
+        h1, h2, h3 = [part.astype(F32) for part in split3(x)]
+        packed = jnp.where(lane < 2 * GROUP, pltpu.roll(h2, GROUP, 1), pltpu.roll(h3, 2 * GROUP, 1))
+        packed = jnp.where(lane < GROUP, h1, packed)
+        o_ref[:, width:] = jnp.where(lane < 3 * GROUP, packed, 0.0).astype(BF16)
+
+
+def add_shares(a, b, pieces, of=2):
+    shape = jax.ShapeDtypeStruct((a.shape[0] // of, a.shape[1]), BF16)
     return kernel_call(
         add_kernel,
-        jax.ShapeDtypeStruct((rows, a.shape[1]), BF16),
+        (shape,) * len(pieces),
         in_specs=[smem()] + vmem(2),
-        out_specs=vmem()[0],
-    )(half, a, b)
+        out_specs=tuple(vmem(len(pieces))),
+    )(jnp.stack(pieces).astype(jnp.int32), a, b)
 
 
 def iterate_kernel(index_ref, near_ref, far_ref, q_ref, p0_ref, p_ref, inv_ref, full, u, v, diag):
@@ -257,9 +261,11 @@
             w = side[:k]
             diag[:, pl.ds(to, bs)] = side[k : k + 8]
             q = q_ref[:, pl.ds(to, bs)]
-            us = split3(jnp.concatenate([w, q], axis=0))
+            us = [part.astype(F32) for part in split3(jnp.concatenate([w, q], axis=0))]
             v1, v2, v3 = split3(jnp.concatenate([q, w], axis=0))
-            u[:, pl.ds(to, bs)] = jnp.concatenate(list(us) + [jnp.zeros((2 * k, bs), BF16)], axis=0)
+            u[pl.ds(to, bs), :LANES] = jnp.concatenate(us[:2], axis=0).T.astype(BF16)
+            tail = jnp.concatenate([us[2], jnp.zeros((2 * k, bs), F32)], axis=0)
+            u[pl.ds(to, bs), LANES:] = tail.T.astype(BF16)
             v[:, pl.ds(to, bs)] = jnp.concatenate([v1, v2, v3, v1, v2, v1], axis=0)
             return 0
 
@@ -268,11 +274,10 @@
     unpack(near_ref, 0)
     unpack(far_ref, nb // 2)
 
-    zeros = jnp.zeros((k, n), BF16)
     lane = lax.broadcasted_iota(jnp.int32, (k, LANES), 1)
 
     def product(p):
-        t = dot(p, u[...], NT)
+        t = dot(p, u[...], NN)
         t = t[:, :LANES] + t[:, LANES:]
         t = t + pltpu.roll(t, 2 * k, 1)
         h1, h2, h3 = [h.astype(F32) for h in split3(t)]
@@ -283,18 +288,16 @@
 
     def sweep(step, p):
         parts = product(p)
-        inv = inverse_lower(gram_of(p, parts, zeros))
-        return apply_lower(inv, parts, zeros).astype(BF16)
+        return apply_lower(inverse_lower(gram_of(parts, p)), parts).astype(BF16)
 
     p = lax.fori_loop(0, ITERS - 1, sweep, p0_ref[...])
     p_ref[...] = p
-    inv_ref[...] = inverse_lower(gram_of(p, product(p), zeros))
+    inv_ref[...] = inverse_lower(gram_of(product(p), p))
 
 
 def finish_kernel(scale, p_ref, inv_ref, block_ref, o_ref):
     back = dot(p_ref[...], block_ref[...], NN)
-    zeros = jnp.zeros(back.shape, BF16)
-    o_ref[...] = (apply_lower(inv_ref[...], split3(back), zeros) * scale).astype(BF16)
+    o_ref[...] = (apply_lower(inv_ref[...], split3(back)) * scale).astype(BF16)
 
 
 def flip(x, axes, perm):
@@ -372,8 +375,7 @@
         scratch_shapes=[
             pltpu.VMEM((12 * k, n), BF16),
             pltpu.VMEM((12 * k, n), BF16),
-            pltpu.VMEM((window, px), BF16),
-            pltpu.VMEM((window, px), BF16),
+            pltpu.VMEM((window, 2 * px), BF16),
             pltpu.VMEM((12 * k, window), BF16),
         ],
     )
@@ -382,15 +384,13 @@
     send = form((at + (1 - bit_a) * blocks)[None], block, other, q)
     recv = flip(send, "pix", first)
     keep = form((at + bit_a * blocks)[None], block, other, q)
-    for axis, perm, bit in (
-        ("pix", second, bit_b),
-        ("samp", xor_samp(1), z0),
-        ("samp", xor_samp(2), z1),
-    ):
-        send = add_shares(keep, recv, 1 - bit)
-        keep = add_shares(keep, recv, bit)
-        recv = flip(send, axis, perm)
-    share = add_shares(keep, recv)
+    (send,) = add_shares(keep, recv, [1 - bit_b])
+    (keep,) = add_shares(keep, recv, [bit_b])
+    recv = flip(send, "pix", second)
+    for b, bit in ((1, z0), (2, z1)):
+        send, keep = add_shares(keep, recv, [1 - bit, bit])
+        recv = flip(send, "samp", xor_samp(b))
+    (share,) = add_shares(keep, recv, [jnp.int32(0)], of=1)
 
     share = ordered(share, flip(share, "samp", xor_samp(2)), z1)
     for axis, perm in (("samp", xor_samp(1)), ("pix", second), ("pix", first)):
@@ -410,7 +410,7 @@
         scratch_mib=24,
         scratch_shapes=[
             pltpu.VMEM((n, n), BF16),
-            pltpu.VMEM((8 * k, n), BF16),
+            pltpu.VMEM((n, 8 * k), BF16),
             pltpu.VMEM((12 * k, n), BF16),
             pltpu.VMEM((8, n), F32),
         ],

time: 257 us -> 251 us (0.977)
  Pallas kernels: 73.3 us -> 64.8 us
  waiting for transfers between devices: 141 us -> 145 us
    pallas_call x13 -> x11, Pallas kernels: 73.3 us -> 64.8 us  [kernel_call(): return lambda *args: call(*map(place, args, in_specs))]
    ppermute x20, waiting for transfers between devices: 115 us -> 119 us  [flip(): return lax.ppermute(x, axes, perm)]
  transfers between devices with their start and end apart: 21 -> 21, of which waited for: 19 -> 19; matrix products, arithmetic and copies ran while one was open for 0% -> 0% of each run, Pallas kernels for 6% -> 5%
where the time goes in v5:
time: 251 us
  waiting for transfers between devices  145 us (58%)
  Pallas kernels  64.8 us (26%)
  starting transfers between devices  33 us (13%)
  local copies, waits for them, and re-layouts  5.77 us (2%)
    ppermute x20, waiting for transfers between devices, flip(): return lax.ppermute(x, axes, perm)  119 us
    pallas_call x11, Pallas kernels, kernel_call(): return lambda *args: call(*map(place, args, in_specs))  64.8 us
    all_to_all x1, waiting for transfers between devices, sample_space(): lax.all_to_all(stamps, ('pix', 'samp'), split_axis=1, concat_axis=0, tile...  26 us
    ppermute x20, starting transfers between devices, flip(): return lax.ppermute(x, axes, perm)  25.6 us
    all_to_all x1, starting transfers between devices, sample_space(): lax.all_to_all(stamps, ('pix', 'samp'), split_axis=1, concat_axis=0, tile...  7.33 us
  transfers between devices with their start and end apart: 21, of which 19 were waited for; matrix products, arithmetic and copies ran while one was open for 0% of the time, Pallas kernels for 5%

profile of v5, /device:TPU:0, one launch (start us, length us, event | category | flops | bytes accessed | tf_op | source)
XLA Modules:
  0.0 250.6 jit_solution(6475352427462958776)
XLA Ops:
  0.0 3.2 %copy.6 = bf16[8,32,8,512]{3,2,0,1:T(8,128)(2,1)} copy(bf16[8,32,8,512]{3,2,1,0:T(8,128)(2,1)} %bitcast.23) | data formatting | bytes 4194304 | tf_op jit(solution)/shard_map/all_to_all | solution.py:337
  3.2 7.3 %all-to-all-start = ((bf16[64,32,512]{2,0,1:T(8,128)(2,1)}), bf16[64,32,512]{2,0,1:T(8,128)(2,1)S(1)}, u32[]{:S(2)}, u32[]{:S(2)}) async-start(bf16[64,32,512]{2,0,1:T(8,128)(2,1)} %bitcast.24), calls=%async_computation | async-start | bytes 4194304 | tf_op jit(solution)/shard_map/all_to_all | solution.py:337
  10.6 1.8 collective-permute-start.1
  12.4 17.3 %collective-permute-done.1 = bf16[32,2048]{1,0:T(8,128)(2,1)S(1)} collective-permute-done((bf16[32,2048]{1,0:T(8,128)(2,1)S(1)}, bf16[32,2048]{1,0:T(8,128)(2,1)S(1)}, u32[]{:S(2)}, u32[]{:S(2)}) %collective-permute-start.1) | collective-permute-done | bytes 131104 | tf_op jit(solution)/shard_map/ppermute | solution.py:304
  29.8 1.5 collective-permute-start.2
  31.3 26.0 %all-to-all-done = bf16[64,32,512]{2,0,1:T(8,128)(2,1)S(1)} async-done(((bf16[64,32,512]{2,0,1:T(8,128)(2,1)}), bf16[64,32,512]{2,0,1:T(8,128)(2,1)S(1)}, u32[]{:S(2)}, u32[]{:S(2)}) %all-to-all-start) | async-done | bytes 2097184 | tf_op jit(solution)/shard_map/all_to_all | solution.py:337
  57.3 1.8 collective-permute-start
  59.3 4.4 %collective-permute-done.3.far_ref = bf16[32,8192]{1,0:T(8,128)(2,1)S(1)} collective-permute-done((bf16[32,8192]{1,0:T(8,128)(2,1)S(1)}, bf16[32,8192]{1,0:T(8,128)(2,1)S(1)}, u32[]{:S(2)}, u32[]{:S(2)}) %collective-permute-start.3) | collective-permute-done | bytes 524320 | tf_op jit(solution)/shard_map/ppermute | solution.py:304
  63.7 1.6 copy-done
  65.2 1.2 shard_map.28
  66.5 0.4 collective-permute-start.4
  66.8 0.8 collective-permute-done.4
  67.8 1.5 collective-permute-start.5
  69.3 2.1 collective-permute-done.5
  71.4 1.5 collective-permute-start.6
  72.9 2.2 collective-permute-done.6
  75.2 2.4 collective-permute-start.7
  77.5 1.9 collective-permute-done.7
  79.4 1.2 collective-permute-start.8
  80.6 4.0 %collective-permute-done.8 = bf16[32,1024]{1,0:T(8,128)(2,1)S(1)} collective-permute-done((bf16[32,1024]{1,0:T(8,128)(2,1)S(1)}, bf16[32,1024]{1,0:T(8,128)(2,1)S(1)}, u32[]{:S(2)}, u32[]{:S(2)}) %collective-permute-start.8) | collective-permute-done | bytes 65568 | tf_op jit(solution)/shard_map/ppermute | solution.py:304
  84.7 1.4 shard_map.29
  86.1 8.6 %shard_map.31 = bf16[512,1280]{1,0:T(8,128)(2,1)} custom-call(s32[1]{0:T(128)} %bitcast.10.at_ref, bf16[2048,512]{1,0:T(8,128)(2,1)S(1)} %bitcast.20, bf16[2048,512]{1,0:T(8,128)(2,1)} %collective-permute-done.other_ref, f32[32,2048]{1,0:T(8,128)S(1)} %get-tuple-element.13.q_ref), custom_call_target="tpu_custom_call" | custom-call | tf_op jit(solution)/shard_map/pallas_call | solution.py:74
  94.7 2.0 collective-permute-start.9
  96.7 0.9 copy-done.2
  97.6 7.4 %shard_map.30.a_ref = bf16[512,1280]{1,0:T(8,128)(2,1)S(1)} custom-call(s32[1]{0:T(128)} %bitcast.5.at_ref, bf16[2048,512]{1,0:T(8,128)(2,1)S(1)} %bitcast.21, bf16[2048,512]{1,0:T(8,128)(2,1)} %collective-permute-done.other_ref, f32[32,2048]{1,0:T(8,128)S(1)} %copy-done.2), custom_call_target="tpu_custom_call" | custom-call | tf_op jit(solution)/shard_map/pallas_call | solution.py:74
  105.0 7.6 %collective-permute-done.9.b_ref = bf16[512,1280]{1,0:T(8,128)(2,1)} collective-permute-done((bf16[512,1280]{1,0:T(8,128)(2,1)}, bf16[512,1280]{1,0:T(8,128)(2,1)}, u32[]{:S(2)}, u32[]{:S(2)}) %collective-permute-start.9) | collective-permute-done | bytes 1310752 | tf_op jit(solution)/shard_map/ppermute | solution.py:304
  112.6 2.6 %shard_map.33 = bf16[256,1280]{1,0:T(8,128)(2,1)} custom-call(s32[1]{0:T(128)} %bitcast.11.at_ref, bf16[512,1280]{1,0:T(8,128)(2,1)S(1)} %shard_map.30.a_ref, bf16[512,1280]{1,0:T(8,128)(2,1)} %collective-permute-done.9.b_ref), custom_call_target="tpu_custom_call" | custom-call | tf_op jit(solution)/shard_map/pallas_call | solution.py:74
  115.2 1.2 collective-permute-start.10
  116.5 1.8 shard_map.32.a_ref
  118.4 7.8 %collective-permute-done.10.b_ref = bf16[256,1280]{1,0:T(8,128)(2,1)} collective-permute-done((bf16[256,1280]{1,0:T(8,128)(2,1)}, bf16[256,1280]{1,0:T(8,128)(2,1)}, u32[]{:S(2)}, u32[]{:S(2)}) %collective-permute-start.10) | collective-permute-done | bytes 655392 | tf_op jit(solution)/shard_map/ppermute | solution.py:304
  126.1 1.5 shard_map.34
  127.7 2.1 collective-permute-start.11
  129.8 6.7 %collective-permute-done.11.b_ref = bf16[128,1280]{1,0:T(8,128)(2,1)S(1)} collective-permute-done((bf16[128,1280]{1,0:T(8,128)(2,1)S(1)}, bf16[128,1280]{1,0:T(8,128)(2,1)S(1)}, u32[]{:S(2)}, u32[]{:S(2)}) %collective-permute-start.11) | collective-permute-done | bytes 327712 | tf_op jit(solution)/shard_map/ppermute | solution.py:304
  136.6 0.8 shard_map.35
  137.4 1.5 collective-permute-start.12
  138.9 7.1 %collective-permute-done.12.b_ref = bf16[64,1280]{1,0:T(8,128)(2,1)S(1)} collective-permute-done((bf16[64,1280]{1,0:T(8,128)(2,1)S(1)}, bf16[64,1280]{1,0:T(8,128)(2,1)S(1)}, u32[]{:S(2)}, u32[]{:S(2)}) %collective-permute-start.12) | collective-permute-done | bytes 163872 | tf_op jit(solution)/shard_map/ppermute | solution.py:304
  146.3 6.9 %collective-permute-done.13 = bf16[64,1280]{1,0:T(8,128)(2,1)S(1)} collective-permute-done((bf16[64,1280]{1,0:T(8,128)(2,1)S(1)}, bf16[64,1280]{1,0:T(8,128)(2,1)S(1)}, u32[]{:S(2)}, u32[]{:S(2)}) %collective-permute-start.13) | collective-permute-done | bytes 163872 | tf_op jit(solution)/shard_map/ppermute | solution.py:304
  153.3 7.1 %collective-permute-done.14 = bf16[128,1280]{1,0:T(8,128)(2,1)S(1)} collective-permute-done((bf16[128,1280]{1,0:T(8,128)(2,1)S(1)}, bf16[128,1280]{1,0:T(8,128)(2,1)S(1)}, u32[]{:S(2)}, u32[]{:S(2)}) %collective-permute-start.14) | collective-permute-done | bytes 327712 | tf_op jit(solution)/shard_map/ppermute | solution.py:304
  160.4 2.7 %collective-permute-start.15 = (bf16[256,1280]{1,0:T(8,128)(2,1)S(1)}, bf16[256,1280]{1,0:T(8,128)(2,1)S(1)}, u32[]{:S(2)}, u32[]{:S(2)}) collective-permute-start(bf16[256,1280]{1,0:T(8,128)(2,1)S(1)} %pad_maximum_fusion.2), channel_id=1, source_target_pairs={{0,4},{1,3},{2,6},{3,1},{4,0},{5,7},{6,2},{7,5},{8,12},{9,11},{10,... | collective-permute-start | bytes 1966088 | tf_op jit(solution)/shard_map/ppermute | solution.py:304
  163.2 13.8 %collective-permute-done.15 = bf16[256,1280]{1,0:T(8,128)(2,1)S(1)} collective-permute-done((bf16[256,1280]{1,0:T(8,128)(2,1)S(1)}, bf16[256,1280]{1,0:T(8,128)(2,1)S(1)}, u32[]{:S(2)}, u32[]{:S(2)}) %collective-permute-start.15) | collective-permute-done | bytes 655392 | tf_op jit(solution)/shard_map/ppermute | solution.py:304
  177.0 3.7 %collective-permute-start.16 = (bf16[512,1280]{1,0:T(8,128)(2,1)S(1)}, bf16[512,1280]{1,0:T(8,128)(2,1)S(1)}, u32[]{:S(2)}, u32[]{:S(2)}) collective-permute-start(bf16[512,1280]{1,0:T(8,128)(2,1)S(1)} %pad_maximum_fusion.1), channel_id=1, source_target_pairs={{0,2},{1,5},{2,0},{3,7},{4,6},{5,1},{6,4},{7,3},{8,10},{9,13},{10,... | collective-permute-start | bytes 3932168 | tf_op jit(solution)/shard_map/ppermute | solution.py:304
  180.7 15.6 %collective-permute-done.16 = bf16[512,1280]{1,0:T(8,128)(2,1)S(1)} collective-permute-done((bf16[512,1280]{1,0:T(8,128)(2,1)S(1)}, bf16[512,1280]{1,0:T(8,128)(2,1)S(1)}, u32[]{:S(2)}, u32[]{:S(2)}) %collective-permute-start.16) | collective-permute-done | bytes 1310752 | tf_op jit(solution)/shard_map/ppermute | solution.py:304
  196.7 4.9 %collective-permute-done.17.far_ref = bf16[1024,1280]{1,0:T(8,128)(2,1)S(1)} collective-permute-done((bf16[1024,1280]{1,0:T(8,128)(2,1)S(1)}, bf16[1024,1280]{1,0:T(8,128)(2,1)S(1)}, u32[]{:S(2)}, u32[]{:S(2)}) %collective-permute-start.17) | collective-permute-done | bytes 2621472 | tf_op jit(solution)/shard_map/ppermute | solution.py:304
  201.6 38.6 %shard_map.37 = (bf16[32,2048]{1,0:T(8,128)(2,1)S(1)}, f32[32,128]{1,0:T(8,128)S(1)}) custom-call(s32[16]{0:T(128)S(1)} %xor_add_fusion.index_ref, bf16[1024,1280]{1,0:T(8,128)(2,1)S(1)} %pad_maximum_fusion.near_ref, bf16[1024,1280]{1,0:T(8,128)(2,1)S(1)} %collective-permute-done.17.far_ref, f32[32,2048]{1,0:T(8,128)S(1)} %copy-done.3, ...), custom_call_target="tpu_custom_call" | custom-call | tf_op jit(solution)/shard_map/pallas_call | solution.py:74
  240.2 0.6 shard_map.38
  240.8 4.8 %collective-permute-done.18 = bf16[32,512]{1,0:T(8,128)(2,1)S(1)} collective-permute-done((bf16[32,512]{1,0:T(8,128)(2,1)S(1)}, bf16[32,512]{1,0:T(8,128)(2,1)S(1)}, u32[]{:S(2)}, u32[]{:S(2)}) %collective-permute-start.18) | collective-permute-done | bytes 32800 | tf_op jit(solution)/shard_map/ppermute | solution.py:304
  245.6 4.3 %collective-permute-done.19 = bf16[32,1024]{1,0:T(8,128)(2,1)S(1)} collective-permute-done((bf16[32,1024]{1,0:T(8,128)(2,1)S(1)}, bf16[32,1024]{1,0:T(8,128)(2,1)S(1)}, u32[]{:S(2)}, u32[]{:S(2)}) %collective-permute-start.19) | collective-permute-done | bytes 65568 | tf_op jit(solution)/shard_map/ppermute | solution.py:304
  249.9 0.7 convert_bitcast_fusion
  (35 shorter events, 1.4 us)
Async XLA Ops:
  3.2 7.3 %copy-start.4 = (f32[2048,32]{0,1:T(8,128)S(1)}, f32[2048,32]{0,1:T(8,128)}, u32[]{:S(2)}) copy-start(f32[2048,32]{0,1:T(8,128)} %param.3) | copy-start | bytes 786436
  3.2 54.1 %all-to-all-start = ((bf16[64,32,512]{2,0,1:T(8,128)(2,1)}), bf16[64,32,512]{2,0,1:T(8,128)(2,1)S(1)}, u32[]{:S(2)}, u32[]{:S(2)}) async-start(bf16[64,32,512]{2,0,1:T(8,128)(2,1)} %bitcast.24), calls=%async_computation | async-start | bytes 4194304 | tf_op jit(solution)/shard_map/all_to_all | solution.py:337
  10.6 19.1 %collective-permute-start.1 = (bf16[32,2048]{1,0:T(8,128)(2,1)S(1)}, bf16[32,2048]{1,0:T(8,128)(2,1)S(1)}, u32[]{:S(2)}, u32[]{:S(2)}) collective-permute-start(bf16[32,2048]{1,0:T(8,128)(2,1)S(1)} %convert_bitcast_fusion.1), channel_id=1, source_target_pairs={{0,2},{1,3},{2,0},{3,1},{4,6},{5,7},{6,4},{7,5},{8,10},{9,11},{10,... | collective-permute-start | bytes 393224 | tf_op jit(solution)/shard_map/ppermute | solution.py:304
  29.8 29.4 %collective-permute-start.2 = (bf16[32,4096]{1,0:T(8,128)(2,1)S(1)}, bf16[32,4096]{1,0:T(8,128)(2,1)S(1)}, u32[]{:S(2)}, u32[]{:S(2)}) collective-permute-start(bf16[32,4096]{1,0:T(8,128)(2,1)S(1)} %pad_maximum_fusion.4), channel_id=1, source_target_pairs={{0,4},{1,5},{2,6},{3,7},{4,0},{5,1},{6,2},{7,3},{8,12},{9,13},{10,... | collective-permute-start | bytes 786440 | tf_op jit(solution)/shard_map/ppermute | solution.py:304
  57.3 28.8 %collective-permute-start = (bf16[2048,512]{1,0:T(8,128)(2,1)S(1)}, bf16[2048,512]{1,0:T(8,128)(2,1)}, u32[]{:S(2)}, u32[]{:S(2)}) collective-permute-start(bf16[2048,512]{1,0:T(8,128)(2,1)S(1)} %bitcast.19), channel_id=1, source_target_pairs={{0,1},{1,0},{2,3},{3,2},{4,5},{5,4},{6,7},{7,6},{8,9},{9,8},{10,11... | collective-permute-start | bytes 6291464 | tf_op jit(solution)/shard_map/ppermute | solution.py:304
  59.2 4.5 %collective-permute-start.3 = (bf16[32,8192]{1,0:T(8,128)(2,1)S(1)}, bf16[32,8192]{1,0:T(8,128)(2,1)S(1)}, u32[]{:S(2)}, u32[]{:S(2)}) collective-permute-start(bf16[32,8192]{1,0:T(8,128)(2,1)S(1)} %pad_maximum_fusion.3.near_ref), channel_id=1, source_target_pairs={{0,1},{1,0},{2,3},{3,2},{4,5},{5,4},{6,7},{7,6},{8,9},{9,8},{10,11... | collective-permute-start | bytes 1572872 | tf_op jit(solution)/shard_map/ppermute | solution.py:304
  63.7 1.6 copy-start
  66.5 1.2 collective-permute-start.4
  67.8 3.7 %collective-permute-start.5 = (bf16[32,128]{1,0:T(8,128)(2,1)S(1)}, bf16[32,128]{1,0:T(8,128)(2,1)S(1)}, u32[]{:S(2)}, u32[]{:S(2)}) collective-permute-start(bf16[32,128]{1,0:T(8,128)(2,1)S(1)} %maximum_select_fusion.5), channel_id=1, source_target_pairs={{0,2},{1,3},{2,0},{3,1},{4,6},{5,7},{6,4},{7,5},{8,10},{9,11},{10,... | collective-permute-start | bytes 24584 | tf_op jit(solution)/shard_map/ppermute | solution.py:304
  71.4 3.7 %collective-permute-start.6 = (bf16[32,256]{1,0:T(8,128)(2,1)S(1)}, bf16[32,256]{1,0:T(8,128)(2,1)S(1)}, u32[]{:S(2)}, u32[]{:S(2)}) collective-permute-start(bf16[32,256]{1,0:T(8,128)(2,1)S(1)} %maximum_select_fusion.4), channel_id=1, source_target_pairs={{0,4},{1,5},{2,6},{3,7},{4,0},{5,1},{6,2},{7,3},{8,12},{9,13},{10,... | collective-permute-start | bytes 49160 | tf_op jit(solution)/shard_map/ppermute | solution.py:304
  75.2 4.2 %collective-permute-start.7 = (bf16[32,512]{1,0:T(8,128)(2,1)S(1)}, bf16[32,512]{1,0:T(8,128)(2,1)S(1)}, u32[]{:S(2)}, u32[]{:S(2)}) collective-permute-start(bf16[32,512]{1,0:T(8,128)(2,1)S(1)} %maximum_select_fusion.3), channel_id=1, source_target_pairs={{0,8},{8,0},{16,24},{24,16},{1,9},{9,1},{17,25},{25,17},{2,10},{10... | collective-permute-start | bytes 98312 | tf_op jit(solution)/shard_map/ppermute | solution.py:304
  79.4 5.2 %collective-permute-start.8 = (bf16[32,1024]{1,0:T(8,128)(2,1)S(1)}, bf16[32,1024]{1,0:T(8,128)(2,1)S(1)}, u32[]{:S(2)}, u32[]{:S(2)}) collective-permute-start(bf16[32,1024]{1,0:T(8,128)(2,1)S(1)} %maximum_select_fusion.2), channel_id=1, source_target_pairs={{0,16},{8,24},{16,0},{24,8},{1,17},{9,25},{17,1},{25,9},{2,18},{10... | collective-permute-start | bytes 196616 | tf_op jit(solution)/shard_map/ppermute | solution.py:304
  86.1 8.6 %copy-start.1 = (f32[32,2048]{1,0:T(8,128)}, f32[32,2048]{1,0:T(8,128)S(1)}, u32[]{:S(2)}) copy-start(f32[32,2048]{1,0:T(8,128)S(1)} %get-tuple-element.13.q_ref) | copy-start | bytes 786436
  94.7 17.9 %collective-permute-start.9 = (bf16[512,1280]{1,0:T(8,128)(2,1)}, bf16[512,1280]{1,0:T(8,128)(2,1)}, u32[]{:S(2)}, u32[]{:S(2)}) collective-permute-start(bf16[512,1280]{1,0:T(8,128)(2,1)} %shard_map.31), channel_id=1, source_target_pairs={{0,2},{1,5},{2,0},{3,7},{4,6},{5,1},{6,4},{7,3},{8,10},{9,13},{10,... | collective-permute-start | bytes 3932168 | tf_op jit(solution)/shard_map/ppermute | solution.py:304
  96.7 0.9 copy-start.2
  115.2 10.9 %collective-permute-start.10 = (bf16[256,1280]{1,0:T(8,128)(2,1)}, bf16[256,1280]{1,0:T(8,128)(2,1)}, u32[]{:S(2)}, u32[]{:S(2)}) collective-permute-start(bf16[256,1280]{1,0:T(8,128)(2,1)} %shard_map.33), channel_id=1, source_target_pairs={{0,4},{1,3},{2,6},{3,1},{4,0},{5,7},{6,2},{7,5},{8,12},{9,11},{10,... | collective-permute-start | bytes 1966088 | tf_op jit(solution)/shard_map/ppermute | solution.py:304
  127.7 8.9 %collective-permute-start.11 = (bf16[128,1280]{1,0:T(8,128)(2,1)S(1)}, bf16[128,1280]{1,0:T(8,128)(2,1)S(1)}, u32[]{:S(2)}, u32[]{:S(2)}) collective-permute-start(bf16[128,1280]{1,0:T(8,128)(2,1)S(1)} %get-tuple-element.15), channel_id=1, source_target_pairs={{0,8},{8,0},{16,24},{24,16},{1,9},{9,1},{17,25},{25,17},{2,10},{10... | collective-permute-start | bytes 983048 | tf_op jit(solution)/shard_map/ppermute | solution.py:304
  137.4 8.6 %collective-permute-start.12 = (bf16[64,1280]{1,0:T(8,128)(2,1)S(1)}, bf16[64,1280]{1,0:T(8,128)(2,1)S(1)}, u32[]{:S(2)}, u32[]{:S(2)}) collective-permute-start(bf16[64,1280]{1,0:T(8,128)(2,1)S(1)} %get-tuple-element.17), channel_id=1, source_target_pairs={{0,16},{8,24},{16,0},{24,8},{1,17},{9,25},{17,1},{25,9},{2,18},{10... | collective-permute-start | bytes 491528 | tf_op jit(solution)/shard_map/ppermute | solution.py:304
  146.2 7.0 %collective-permute-start.13 = (bf16[64,1280]{1,0:T(8,128)(2,1)S(1)}, bf16[64,1280]{1,0:T(8,128)(2,1)S(1)}, u32[]{:S(2)}, u32[]{:S(2)}) collective-permute-start(bf16[64,1280]{1,0:T(8,128)(2,1)S(1)} %shard_map.36), channel_id=1, source_target_pairs={{0,16},{8,24},{16,0},{24,8},{1,17},{9,25},{17,1},{25,9},{2,18},{10... | collective-permute-start | bytes 491528 | tf_op jit(solution)/shard_map/ppermute | solution.py:304
  153.3 7.1 %collective-permute-start.14 = (bf16[128,1280]{1,0:T(8,128)(2,1)S(1)}, bf16[128,1280]{1,0:T(8,128)(2,1)S(1)}, u32[]{:S(2)}, u32[]{:S(2)}) collective-permute-start(bf16[128,1280]{1,0:T(8,128)(2,1)S(1)} %maximum_select_fusion), channel_id=1, source_target_pairs={{0,8},{8,0},{16,24},{24,16},{1,9},{9,1},{17,25},{25,17},{2,10},{10... | collective-permute-start | bytes 983048 | tf_op jit(solution)/shard_map/ppermute | solution.py:304
  160.4 16.5 %collective-permute-start.15 = (bf16[256,1280]{1,0:T(8,128)(2,1)S(1)}, bf16[256,1280]{1,0:T(8,128)(2,1)S(1)}, u32[]{:S(2)}, u32[]{:S(2)}) collective-permute-start(bf16[256,1280]{1,0:T(8,128)(2,1)S(1)} %pad_maximum_fusion.2), channel_id=1, source_target_pairs={{0,4},{1,3},{2,6},{3,1},{4,0},{5,7},{6,2},{7,5},{8,12},{9,11},{10,... | collective-permute-start | bytes 1966088 | tf_op jit(solution)/shard_map/ppermute | solution.py:304
  177.0 24.5 %copy-start.3 = (f32[32,2048]{1,0:T(8,128)S(1)}, f32[32,2048]{1,0:T(8,128)}, u32[]{:S(2)}) copy-start(f32[32,2048]{1,0:T(8,128)} %copy-done.1) | copy-start | bytes 786436
  177.0 19.3 %collective-permute-start.16 = (bf16[512,1280]{1,0:T(8,128)(2,1)S(1)}, bf16[512,1280]{1,0:T(8,128)(2,1)S(1)}, u32[]{:S(2)}, u32[]{:S(2)}) collective-permute-start(bf16[512,1280]{1,0:T(8,128)(2,1)S(1)} %pad_maximum_fusion.1), channel_id=1, source_target_pairs={{0,2},{1,5},{2,0},{3,7},{4,6},{5,1},{6,4},{7,3},{8,10},{9,13},{10,... | collective-permute-start | bytes 3932168 | tf_op jit(solution)/shard_map/ppermute | solution.py:304
  196.6 5.0 %collective-permute-start.17 = (bf16[1024,1280]{1,0:T(8,128)(2,1)S(1)}, bf16[1024,1280]{1,0:T(8,128)(2,1)S(1)}, u32[]{:S(2)}, u32[]{:S(2)}) collective-permute-start(bf16[1024,1280]{1,0:T(8,128)(2,1)S(1)} %pad_maximum_fusion.near_ref), channel_id=1, source_target_pairs={{0,1},{1,0},{2,3},{3,2},{4,5},{5,4},{6,7},{7,6},{8,9},{9,8},{10,11... | collective-permute-start | bytes 7864328 | tf_op jit(solution)/shard_map/ppermute | solution.py:304
  240.8 4.8 %collective-permute-start.18 = (bf16[32,512]{1,0:T(8,128)(2,1)S(1)}, bf16[32,512]{1,0:T(8,128)(2,1)S(1)}, u32[]{:S(2)}, u32[]{:S(2)}) collective-permute-start(bf16[32,512]{1,0:T(8,128)(2,1)S(1)} %shard_map.38), channel_id=1, source_target_pairs={{0,16},{8,24},{16,0},{24,8},{1,17},{9,25},{17,1},{25,9},{2,18},{10... | collective-permute-start | bytes 98312 | tf_op jit(solution)/shard_map/ppermute | solution.py:304
  245.6 4.3 %collective-permute-start.19 = (bf16[32,1024]{1,0:T(8,128)(2,1)S(1)}, bf16[32,1024]{1,0:T(8,128)(2,1)S(1)}, u32[]{:S(2)}, u32[]{:S(2)}) collective-permute-start(bf16[32,1024]{1,0:T(8,128)(2,1)S(1)} %pad_maximum_fusion.5), channel_id=1, source_target_pairs={{0,8},{8,0},{16,24},{24,16},{1,9},{9,1},{17,25},{25,17},{2,10},{10... | collective-permute-start | bytes 196616 | tf_op jit(solution)/shard_map/ppermute | solution.py:304

commit v6 on v5

--- a/solution.py
+++ b/solution.py
@@ -14,6 +14,7 @@
 PANEL = 16
 GROUP = 40
 STEP = 2
+SEND, KEEP, PLACE, BLOCKS = 0, 1, 8, 16
 SAMPLE_SPACE_LIMIT = 4096
 F32 = jnp.float32
 BF16 = jnp.bfloat16
@@ -125,12 +126,13 @@
 
 
 def rows_kernel(index_ref, near_ref, far_ref, stamps_ref, o_ref):
-    m = near_ref.shape[1] * 2 // index_ref.shape[0]
     total = jnp.zeros(o_ref.shape, F32)
-    for j in range(index_ref.shape[0]):
+    pix = BLOCKS - PLACE
+    m = near_ref.shape[1] * 2 // pix
+    for j in range(pix):
         ref = near_ref if j * m < near_ref.shape[1] else far_ref
         at = j * m % near_ref.shape[1]
-        stamps = stamps_ref[:, pl.ds(pl.multiple_of(index_ref[j] * m, LANES), m)]
+        stamps = stamps_ref[:, pl.ds(pl.multiple_of(index_ref[PLACE + j] * m, LANES), m)]
         total += dot(ref[:, at : at + m], stamps, NT)
     o_ref[...] = total.astype(BF16)
 
@@ -209,16 +211,16 @@
         out_ref[to : to + bs, width:] = jnp.concatenate(side, axis=0).T.astype(BF16)
 
 
-def form_kernel(at_ref, own_ref, other_ref, q_ref, out_ref, left, right, *wins):
+def form_kernel(slot, at_ref, own_ref, other_ref, q_ref, out_ref, left, right, *wins):
     split_off(own_ref, other_ref, q_ref, left, right)
-    form_rows(q_ref.shape[0], at_ref[0], own_ref, other_ref, left, right, out_ref, *wins)
-
-
-def add_kernel(at_ref, a_ref, b_ref, *o_refs):
+    form_rows(q_ref.shape[0], at_ref[slot], own_ref, other_ref, left, right, out_ref, *wins)
+
+
+def add_kernel(slots, at_ref, a_ref, b_ref, *o_refs):
     width = a_ref.shape[1] - LANES
-    for i, o_ref in enumerate(o_refs):
+    for slot, o_ref in zip(slots, o_refs):
         h = o_ref.shape[0]
-        at = pl.multiple_of(at_ref[i] * h, h)
+        at = 0 if slot is None else pl.multiple_of(at_ref[slot] * h, h)
         a, b = a_ref[pl.ds(at, h), :], b_ref[pl.ds(at, h), :]
         o_ref[:, :width] = (a[:, :width].astype(F32) + b[:, :width].astype(F32)).astype(BF16)
         x = lane_sum3(a[:, width:].astype(F32), GROUP) + lane_sum3(b[:, width:].astype(F32), GROUP)
@@ -229,51 +231,55 @@
         o_ref[:, width:] = jnp.where(lane < 3 * GROUP, packed, 0.0).astype(BF16)
 
 
-def add_shares(a, b, pieces, of=2):
-    shape = jax.ShapeDtypeStruct((a.shape[0] // of, a.shape[1]), BF16)
+def add_shares(a, b, index, *slots):
+    shape = jax.ShapeDtypeStruct((a.shape[0] // (2 if slots else 1), a.shape[1]), BF16)
+    slots = slots or (None,)
     return kernel_call(
-        add_kernel,
-        (shape,) * len(pieces),
+        functools.partial(add_kernel, slots),
+        (shape,) * len(slots),
         in_specs=[smem()] + vmem(2),
-        out_specs=tuple(vmem(len(pieces))),
-    )(jnp.stack(pieces).astype(jnp.int32), a, b)
-
-
-def iterate_kernel(index_ref, near_ref, far_ref, q_ref, p0_ref, p_ref, inv_ref, full, u, v, diag):
+        out_specs=tuple(vmem(len(slots))),
+    )(index, a, b)
+
+
+def unpack(offset, index_ref, share_ref, q_ref, full, u, v, diag):
     k, n = q_ref.shape
-    width = near_ref.shape[1] - LANES
+    width = share_ref.shape[1] - LANES
     bs = width - n // 2
     nb = n // bs
 
-    def unpack(share_ref, offset):
-        def one(r, _):
-            i = index_ref[r + offset]
-            frm = pl.multiple_of(r * bs, bs)
-            to = pl.multiple_of(i * bs, bs)
-            for d in range(nb // 2 + 1):
-                part = share_ref[pl.ds(frm, bs), d * bs : (d + 1) * bs]
-                at = pl.multiple_of(lax.rem(i + d, nb) * bs, bs)
-                full[pl.ds(to, bs), pl.ds(at, bs)] = part
-                if 0 < d < nb // 2:
-                    full[pl.ds(at, bs), pl.ds(to, bs)] = part.T
-            side = share_ref[pl.ds(frm, bs), width:].astype(F32).T
-            side = side[:GROUP] + side[GROUP : 2 * GROUP] + side[2 * GROUP : 3 * GROUP]
-            w = side[:k]
-            diag[:, pl.ds(to, bs)] = side[k : k + 8]
-            q = q_ref[:, pl.ds(to, bs)]
-            us = [part.astype(F32) for part in split3(jnp.concatenate([w, q], axis=0))]
-            v1, v2, v3 = split3(jnp.concatenate([q, w], axis=0))
-            u[pl.ds(to, bs), :LANES] = jnp.concatenate(us[:2], axis=0).T.astype(BF16)
-            tail = jnp.concatenate([us[2], jnp.zeros((2 * k, bs), F32)], axis=0)
-            u[pl.ds(to, bs), LANES:] = tail.T.astype(BF16)
-            v[:, pl.ds(to, bs)] = jnp.concatenate([v1, v2, v3, v1, v2, v1], axis=0)
-            return 0
-
-        lax.fori_loop(0, nb // 2, one, 0)
-
-    unpack(near_ref, 0)
-    unpack(far_ref, nb // 2)
-
+    def one(r, _):
+        i = index_ref[r + offset]
+        frm = pl.multiple_of(r * bs, bs)
+        to = pl.multiple_of(i * bs, bs)
+        for d in range(nb // 2 + 1):
+            part = share_ref[pl.ds(frm, bs), d * bs : (d + 1) * bs]
+            at = pl.multiple_of(lax.rem(i + d, nb) * bs, bs)
+            full[pl.ds(to, bs), pl.ds(at, bs)] = part
+            if 0 < d < nb // 2:
+                full[pl.ds(at, bs), pl.ds(to, bs)] = part.T
+        side = share_ref[pl.ds(frm, bs), width:].astype(F32).T
+        side = side[:GROUP] + side[GROUP : 2 * GROUP] + side[2 * GROUP : 3 * GROUP]
+        w = side[:k]
+        diag[:, pl.ds(to, bs)] = side[k : k + 8]
+        q = q_ref[:, pl.ds(to, bs)]
+        us = [part.astype(F32) for part in split3(jnp.concatenate([w, q], axis=0))]
+        v1, v2, v3 = split3(jnp.concatenate([q, w], axis=0))
+        u[pl.ds(to, bs), :LANES] = jnp.concatenate(us[:2], axis=0).T.astype(BF16)
+        tail = jnp.concatenate([us[2], jnp.zeros((2 * k, bs), F32)], axis=0)
+        u[pl.ds(to, bs), LANES:] = tail.T.astype(BF16)
+        v[:, pl.ds(to, bs)] = jnp.concatenate([v1, v2, v3, v1, v2, v1], axis=0)
+        return 0
+
+    lax.fori_loop(0, nb // 2, one, 0)
+
+
+def iterate_kernel(
+    offset, index_ref, far_ref, q_ref, p0_ref, *refs
+):
+    p_ref, inv_ref, full, u, v, diag = refs[4:]
+    k, _ = q_ref.shape
+    unpack(offset, index_ref, far_ref, q_ref, full, u, v, diag)
     lane = lax.broadcasted_iota(jnp.int32, (k, LANES), 1)
 
     def product(p):
@@ -331,8 +337,22 @@
     for b in (2, 4):
         low = jnp.concatenate([low, flip(low, "pix", xor_pix(b))], axis=1)
     far = flip(low, "pix", xor_pix(1))
+    bit_a = jnp.where(core == 0, x, y)
+    bit_b = jnp.where(core == 0, y, x)
+    bs = 2 * stamps.shape[0]
+    nb = n // bs
     at = jnp.arange(pix, dtype=jnp.int32)
-    index = p ^ (((at & 1) << 1) | ((at & 2) << 1) | (at >> 2))
+    place = p ^ (((at & 1) << 1) | ((at & 2) << 1) | (at >> 2))
+    at = jnp.arange(nb, dtype=jnp.int32)
+    c_of = core ^ ((at >> 3) & 1)
+    a_of = jnp.where(c_of == 0, x, y) ^ ((at >> 2) & 1)
+    b_of = jnp.where(c_of == 0, y, x) ^ ((at >> 1) & 1)
+    order = c_of * 8 + a_of * 4 + b_of * 2 + (z0 ^ (at & 1))
+    quarter = nb // 4
+    pairs = [core * 2 * quarter + (1 - bit_a) * quarter, core * 2 * quarter + bit_a * quarter]
+    for bit in (bit_b, z0, z1):
+        pairs += [1 - bit, bit]
+    index = jnp.concatenate([jnp.stack(pairs), place, order]).astype(jnp.int32)
 
     block = lax.all_to_all(stamps, ("pix", "samp"), split_axis=1, concat_axis=0, tiled=True)
 
@@ -355,66 +375,64 @@
 
     first = [(i, i ^ (2 if i % 2 == 0 else 4)) for i in range(pix)]
     second = [(i, i ^ (4 if i % 2 == 0 else 2)) for i in range(pix)]
-    bit_a = jnp.where(core == 0, x, y)
-    bit_b = jnp.where(core == 0, y, x)
-
     other = flip(block, "pix", xor_pix(1))
-    bs = 2 * stamps.shape[0]
-    nb = n // bs
     px = block.shape[1]
     width = n // 2 + bs
     rows = n // 4
     window = rows - bs + width
     piece = jax.ShapeDtypeStruct((rows, width + LANES), BF16)
-    form = kernel_call(
-        form_kernel,
-        piece,
-        in_specs=[smem()] + vmem(3),
-        out_specs=vmem()[0],
-        scratch_mib=20,
-        scratch_shapes=[
-            pltpu.VMEM((12 * k, n), BF16),
-            pltpu.VMEM((12 * k, n), BF16),
-            pltpu.VMEM((window, 2 * px), BF16),
-            pltpu.VMEM((12 * k, window), BF16),
-        ],
-    )
-    blocks = rows // bs
-    at = core * 2 * blocks
-    send = form((at + (1 - bit_a) * blocks)[None], block, other, q)
+
+    def form(slot):
+        return kernel_call(
+            functools.partial(form_kernel, slot),
+            piece,
+            in_specs=[smem()] + vmem(3),
+            out_specs=vmem()[0],
+            scratch_mib=20,
+            scratch_shapes=[
+                pltpu.VMEM((12 * k, n), BF16),
+                pltpu.VMEM((12 * k, n), BF16),
+                pltpu.VMEM((window, 2 * px), BF16),
+                pltpu.VMEM((12 * k, window), BF16),
+            ],
+        )(index, block, other, q)
+
+    send = form(SEND)
     recv = flip(send, "pix", first)
-    keep = form((at + bit_a * blocks)[None], block, other, q)
-    (send,) = add_shares(keep, recv, [1 - bit_b])
-    (keep,) = add_shares(keep, recv, [bit_b])
+    keep = form(KEEP)
+    (send,) = add_shares(keep, recv, index, SEND + 2)
+    (keep,) = add_shares(keep, recv, index, KEEP + 2)
     recv = flip(send, "pix", second)
-    for b, bit in ((1, z0), (2, z1)):
-        send, keep = add_shares(keep, recv, [1 - bit, bit])
+    for b, slot in ((1, 4), (2, 6)):
+        send, keep = add_shares(keep, recv, index, SEND + slot, KEEP + slot)
         recv = flip(send, "samp", xor_samp(b))
-    (share,) = add_shares(keep, recv, [jnp.int32(0)], of=1)
+    (share,) = add_shares(keep, recv, index)
 
     share = ordered(share, flip(share, "samp", xor_samp(2)), z1)
     for axis, perm in (("samp", xor_samp(1)), ("pix", second), ("pix", first)):
         share = jnp.concatenate([share, flip(share, axis, perm)], axis=0)
     far = flip(share, "pix", xor_pix(1))
-    at = jnp.arange(nb, dtype=jnp.int32)
-    c_of = core ^ ((at >> 3) & 1)
-    a_of = jnp.where(c_of == 0, x, y) ^ ((at >> 2) & 1)
-    b_of = jnp.where(c_of == 0, y, x) ^ ((at >> 1) & 1)
-    index = c_of * 8 + a_of * 4 + b_of * 2 + (z0 ^ (at & 1))
-
+    parts = (
+        jax.ShapeDtypeStruct((n, n), BF16),
+        jax.ShapeDtypeStruct((n, 8 * k), BF16),
+        jax.ShapeDtypeStruct((12 * k, n), BF16),
+        jax.ShapeDtypeStruct((8, n), F32),
+    )
+    parts_now = kernel_call(
+        functools.partial(unpack, BLOCKS),
+        parts,
+        in_specs=[smem()] + vmem(2),
+        out_specs=tuple(vmem(4)),
+        scratch_mib=4,
+    )(index, share, q)
     proj, inv = kernel_call(
-        iterate_kernel,
-        (jax.ShapeDtypeStruct((k, n), BF16), jax.ShapeDtypeStruct((k, LANES), F32)),
-        in_specs=[smem()] + vmem(4),
-        out_specs=tuple(vmem(2)),
-        scratch_mib=24,
-        scratch_shapes=[
-            pltpu.VMEM((n, n), BF16),
-            pltpu.VMEM((n, 8 * k), BF16),
-            pltpu.VMEM((12 * k, n), BF16),
-            pltpu.VMEM((8, n), F32),
-        ],
-    )(index, share, far, q, proj)
+        functools.partial(iterate_kernel, BLOCKS + nb // 2),
+        (jax.ShapeDtypeStruct((k, n), BF16), jax.ShapeDtypeStruct((k, LANES), F32)) + parts,
+        in_specs=[smem()] + vmem(7),
+        out_specs=tuple(vmem(6)),
+        input_output_aliases={4 + i: 2 + i for i in range(4)},
+        scratch_mib=12,
+    )(index, far, q, proj, *parts_now)[:2]
 
     mine = kernel_call(
         functools.partial(finish_kernel, scale),

time: 251 us -> 247 us (0.984)
  waiting for transfers between devices: 145 us -> 148 us
  Pallas kernels: 64.8 us -> 61.9 us
    pallas_call x11 -> x12, Pallas kernels: 64.8 us -> 61.9 us  [kernel_call(): return lambda *args: call(*map(place, args, in_specs))]
  transfers between devices with their start and end apart: 21 -> 21, of which waited for: 19 -> 19; matrix products, arithmetic and copies ran while one was open for 0% -> 0% of each run, Pallas kernels for 5% -> 6%
where the time goes in v6:
time: 247 us
  waiting for transfers between devices  148 us (60%)
  Pallas kernels  61.9 us (25%)
  starting transfers between devices  30.9 us (13%)
  local copies, waits for them, and re-layouts  4.89 us (2%)
    ppermute x20, waiting for transfers between devices, flip(): return lax.ppermute(x, axes, perm)  122 us
    pallas_call x12, Pallas kernels, kernel_call(): return lambda *args: call(*map(place, args, in_specs))  61.9 us
    all_to_all x1, waiting for transfers between devices, sample_space(): lax.all_to_all(stamps, ('pix', 'samp'), split_axis=1, concat_axis=0, tile...  26 us
    ppermute x20, starting transfers between devices, flip(): return lax.ppermute(x, axes, perm)  23.6 us
    all_to_all x1, starting transfers between devices, sample_space(): lax.all_to_all(stamps, ('pix', 'samp'), split_axis=1, concat_axis=0, tile...  7.33 us
  transfers between devices with their start and end apart: 21, of which 19 were waited for; matrix products, arithmetic and copies ran while one was open for 0% of the time, Pallas kernels for 6%

profile of v6, /device:TPU:0, one launch (start us, length us, event | category | flops | bytes accessed | tf_op | source)
XLA Modules:
  0.0 247.1 jit_solution(18016480516675954462)
XLA Ops:
  0.0 3.2 %copy.10 = bf16[8,32,8,512]{3,2,0,1:T(8,128)(2,1)} copy(bf16[8,32,8,512]{3,2,1,0:T(8,128)(2,1)} %bitcast.23) | data formatting | bytes 4194304 | tf_op jit(solution)/shard_map/all_to_all | solution.py:357
  3.2 7.3 %all-to-all-start = ((bf16[64,32,512]{2,0,1:T(8,128)(2,1)}), bf16[64,32,512]{2,0,1:T(8,128)(2,1)S(1)}, u32[]{:S(2)}, u32[]{:S(2)}) async-start(bf16[64,32,512]{2,0,1:T(8,128)(2,1)} %bitcast.24), calls=%async_computation | async-start | bytes 4194304 | tf_op jit(solution)/shard_map/all_to_all | solution.py:357
  10.6 1.8 collective-permute-start.1
  12.4 17.3 %collective-permute-done.1 = bf16[32,2048]{1,0:T(8,128)(2,1)S(1)} collective-permute-done((bf16[32,2048]{1,0:T(8,128)(2,1)S(1)}, bf16[32,2048]{1,0:T(8,128)(2,1)S(1)}, u32[]{:S(2)}, u32[]{:S(2)}) %collective-permute-start.1) | collective-permute-done | bytes 131104 | tf_op jit(solution)/shard_map/ppermute | solution.py:310
  29.7 1.5 collective-permute-start.2
  31.3 26.0 %all-to-all-done = bf16[64,32,512]{2,0,1:T(8,128)(2,1)S(1)} async-done(((bf16[64,32,512]{2,0,1:T(8,128)(2,1)}), bf16[64,32,512]{2,0,1:T(8,128)(2,1)S(1)}, u32[]{:S(2)}, u32[]{:S(2)}) %all-to-all-start) | async-done | bytes 2097184 | tf_op jit(solution)/shard_map/all_to_all | solution.py:357
  57.3 1.8 collective-permute-start
  59.4 4.3 %collective-permute-done.3.far_ref = bf16[32,8192]{1,0:T(8,128)(2,1)S(1)} collective-permute-done((bf16[32,8192]{1,0:T(8,128)(2,1)S(1)}, bf16[32,8192]{1,0:T(8,128)(2,1)S(1)}, u32[]{:S(2)}, u32[]{:S(2)}) %collective-permute-start.3) | collective-permute-done | bytes 524320 | tf_op jit(solution)/shard_map/ppermute | solution.py:310
  63.6 1.6 copy-done
  65.2 1.2 shard_map.28
  66.9 0.8 collective-permute-done.4
  67.8 1.5 collective-permute-start.5
  69.3 2.1 collective-permute-done.5
  71.4 1.5 collective-permute-start.6
  72.9 2.2 collective-permute-done.6
  75.2 2.3 collective-permute-start.7
  77.5 1.9 collective-permute-done.7
  79.4 1.2 collective-permute-start.8
  80.6 4.0 %collective-permute-done.8 = bf16[32,1024]{1,0:T(8,128)(2,1)S(1)} collective-permute-done((bf16[32,1024]{1,0:T(8,128)(2,1)S(1)}, bf16[32,1024]{1,0:T(8,128)(2,1)S(1)}, u32[]{:S(2)}, u32[]{:S(2)}) %collective-permute-start.8) | collective-permute-done | bytes 65568 | tf_op jit(solution)/shard_map/ppermute | solution.py:310
  84.7 1.4 shard_map.29
  86.1 7.5 %shard_map.31 = bf16[512,1280]{1,0:T(8,128)(2,1)S(1)} custom-call(s32[32]{0:T(128)S(1)} %concatenate.63.index_ref.at_ref, bf16[2048,512]{1,0:T(8,128)(2,1)S(1)} %bitcast.20, bf16[2048,512]{1,0:T(8,128)(2,1)} %collective-permute-done.other_ref, f32[32,2048]{1,0:T(8,128)S(1)} %get-tuple-element.17.q_ref), custom_call_target="tpu_custom_call" | custom-call | tf_op jit(solution)/shard_map/pallas_call | solution.py:75
  93.5 2.0 collective-permute-start.9
  95.6 7.4 %shard_map.30.a_ref = bf16[512,1280]{1,0:T(8,128)(2,1)S(1)} custom-call(s32[32]{0:T(128)S(1)} %concatenate.63.index_ref.at_ref, bf16[2048,512]{1,0:T(8,128)(2,1)S(1)} %bitcast.21, bf16[2048,512]{1,0:T(8,128)(2,1)} %collective-permute-done.other_ref, f32[32,2048]{1,0:T(8,128)S(1)} %get-tuple-element.17.q_ref), custom_call_target="tpu_custom_call" | custom-call | tf_op jit(solution)/shard_map/pallas_call | solution.py:75
  103.0 9.4 %collective-permute-done.9.b_ref = bf16[512,1280]{1,0:T(8,128)(2,1)S(1)} collective-permute-done((bf16[512,1280]{1,0:T(8,128)(2,1)S(1)}, bf16[512,1280]{1,0:T(8,128)(2,1)S(1)}, u32[]{:S(2)}, u32[]{:S(2)}) %collective-permute-start.9) | collective-permute-done | bytes 1310752 | tf_op jit(solution)/shard_map/ppermute | solution.py:310
  112.4 1.0 shard_map.33
  113.4 0.8 collective-permute-start.10
  114.2 1.0 shard_map.32.a_ref
  115.3 8.8 %collective-permute-done.10.b_ref = bf16[256,1280]{1,0:T(8,128)(2,1)S(1)} collective-permute-done((bf16[256,1280]{1,0:T(8,128)(2,1)S(1)}, bf16[256,1280]{1,0:T(8,128)(2,1)S(1)}, u32[]{:S(2)}, u32[]{:S(2)}) %collective-permute-start.10) | collective-permute-done | bytes 655392 | tf_op jit(solution)/shard_map/ppermute | solution.py:310
  124.1 1.0 shard_map.34
  125.1 2.5 %collective-permute-start.11 = (bf16[128,1280]{1,0:T(8,128)(2,1)S(1)}, bf16[128,1280]{1,0:T(8,128)(2,1)S(1)}, u32[]{:S(2)}, u32[]{:S(2)}) collective-permute-start(bf16[128,1280]{1,0:T(8,128)(2,1)S(1)} %get-tuple-element.19), channel_id=1, source_target_pairs={{0,8},{8,0},{16,24},{24,16},{1,9},{9,1},{17,25},{25,17},{2,10},{10... | collective-permute-start | bytes 983048 | tf_op jit(solution)/shard_map/ppermute | solution.py:310
  127.5 6.8 %collective-permute-done.11.b_ref = bf16[128,1280]{1,0:T(8,128)(2,1)S(1)} collective-permute-done((bf16[128,1280]{1,0:T(8,128)(2,1)S(1)}, bf16[128,1280]{1,0:T(8,128)(2,1)S(1)}, u32[]{:S(2)}, u32[]{:S(2)}) %collective-permute-start.11) | collective-permute-done | bytes 327712 | tf_op jit(solution)/shard_map/ppermute | solution.py:310
  134.4 0.8 shard_map.35
  135.2 1.1 collective-permute-start.12
  136.3 8.0 %collective-permute-done.12.b_ref = bf16[64,1280]{1,0:T(8,128)(2,1)S(1)} collective-permute-done((bf16[64,1280]{1,0:T(8,128)(2,1)S(1)}, bf16[64,1280]{1,0:T(8,128)(2,1)S(1)}, u32[]{:S(2)}, u32[]{:S(2)}) %collective-permute-start.12) | collective-permute-done | bytes 163872 | tf_op jit(solution)/shard_map/ppermute | solution.py:310
  144.3 0.9 shard_map.36
  145.3 6.9 %collective-permute-done.13 = bf16[64,1280]{1,0:T(8,128)(2,1)S(1)} collective-permute-done((bf16[64,1280]{1,0:T(8,128)(2,1)S(1)}, bf16[64,1280]{1,0:T(8,128)(2,1)S(1)}, u32[]{:S(2)}, u32[]{:S(2)}) %collective-permute-start.13) | collective-permute-done | bytes 163872 | tf_op jit(solution)/shard_map/ppermute | solution.py:310
  152.3 7.1 %collective-permute-done.14 = bf16[128,1280]{1,0:T(8,128)(2,1)S(1)} collective-permute-done((bf16[128,1280]{1,0:T(8,128)(2,1)S(1)}, bf16[128,1280]{1,0:T(8,128)(2,1)S(1)}, u32[]{:S(2)}, u32[]{:S(2)}) %collective-permute-start.14) | collective-permute-done | bytes 327712 | tf_op jit(solution)/shard_map/ppermute | solution.py:310
  159.4 1.6 collective-permute-start.15
  161.0 15.2 %collective-permute-done.15 = bf16[256,1280]{1,0:T(8,128)(2,1)S(1)} collective-permute-done((bf16[256,1280]{1,0:T(8,128)(2,1)S(1)}, bf16[256,1280]{1,0:T(8,128)(2,1)S(1)}, u32[]{:S(2)}, u32[]{:S(2)}) %collective-permute-start.15) | collective-permute-done | bytes 655392 | tf_op jit(solution)/shard_map/ppermute | solution.py:310
  176.4 3.1 %collective-permute-start.16 = (bf16[512,1280]{1,0:T(8,128)(2,1)S(1)}, bf16[512,1280]{1,0:T(8,128)(2,1)S(1)}, u32[]{:S(2)}, u32[]{:S(2)}) collective-permute-start(bf16[512,1280]{1,0:T(8,128)(2,1)S(1)} %pad_maximum_fusion.1), channel_id=1, source_target_pairs={{0,2},{1,5},{2,0},{3,7},{4,6},{5,1},{6,4},{7,3},{8,10},{9,13},{10,... | collective-permute-start | bytes 3932168 | tf_op jit(solution)/shard_map/ppermute | solution.py:310
  179.5 15.6 %collective-permute-done.16 = bf16[512,1280]{1,0:T(8,128)(2,1)S(1)} collective-permute-done((bf16[512,1280]{1,0:T(8,128)(2,1)S(1)}, bf16[512,1280]{1,0:T(8,128)(2,1)S(1)}, u32[]{:S(2)}, u32[]{:S(2)}) %collective-permute-start.16) | collective-permute-done | bytes 1310752 | tf_op jit(solution)/shard_map/ppermute | solution.py:310
  195.4 2.9 %shard_map.37 = (bf16[2048,2048]{1,0:T(8,128)(2,1)S(1)}, bf16[2048,256]{1,0:T(8,128)(2,1)S(1)}, bf16[384,2048]{1,0:T(8,128)(2,1)S(1)}, f32[8,2048]{1,0:T(8,128)S(1)}) custom-call(s32[32]{0:T(128)S(1)} %concatenate.63.index_ref.at_ref, bf16[1024,1280]{1,0:T(8,128)(2,1)S(1)} %pad_maximum_fusion.share_ref, f32[32,2048]{1,0:T(8,128)S(1)} %get-tuple-element.17.q_ref), custom_call_target="tpu_custom_call" | custom-call | tf_op jit(solution)/shard_map/pallas_call | solution.py:75
  198.3 2.0 collective-permute-done.17.far_ref
  200.3 36.3 %shard_map.38 = (bf16[32,2048]{1,0:T(8,128)(2,1)S(1)}, f32[32,128]{1,0:T(8,128)S(1)}, bf16[2048,2048]{1,0:T(8,128)(2,1)S(1)}, bf16[2048,256]{1,0:T(8,128)(2,1)S(...) custom-call(s32[32]{0:T(128)S(1)} %concatenate.63.index_ref.at_ref, ...), custom_call_target="tpu_custom_call", output_to_operand_aliasing={{2}: (4, {}), {3}: (5, {}), {4}: (6, {}), {5}: (7, {})} | custom-call | tf_op jit(solution)/shard_map/pallas_call | solution.py:75
  236.6 0.6 shard_map.39
  237.2 4.8 %collective-permute-done.18 = bf16[32,512]{1,0:T(8,128)(2,1)S(1)} collective-permute-done((bf16[32,512]{1,0:T(8,128)(2,1)S(1)}, bf16[32,512]{1,0:T(8,128)(2,1)S(1)}, u32[]{:S(2)}, u32[]{:S(2)}) %collective-permute-start.18) | collective-permute-done | bytes 32800 | tf_op jit(solution)/shard_map/ppermute | solution.py:310
  242.1 4.3 %collective-permute-done.19 = bf16[32,1024]{1,0:T(8,128)(2,1)S(1)} collective-permute-done((bf16[32,1024]{1,0:T(8,128)(2,1)S(1)}, bf16[32,1024]{1,0:T(8,128)(2,1)S(1)}, u32[]{:S(2)}, u32[]{:S(2)}) %collective-permute-start.19) | collective-permute-done | bytes 65568 | tf_op jit(solution)/shard_map/ppermute | solution.py:310
  246.3 0.7 convert_bitcast_fusion
  (29 shorter events, 1.5 us)
Async XLA Ops:
  3.2 7.3 %copy-start.1 = (f32[2048,32]{0,1:T(8,128)S(1)}, f32[2048,32]{0,1:T(8,128)}, u32[]{:S(2)}) copy-start(f32[2048,32]{0,1:T(8,128)} %param.3) | copy-start | bytes 786436
  3.2 54.1 %all-to-all-start = ((bf16[64,32,512]{2,0,1:T(8,128)(2,1)}), bf16[64,32,512]{2,0,1:T(8,128)(2,1)S(1)}, u32[]{:S(2)}, u32[]{:S(2)}) async-start(bf16[64,32,512]{2,0,1:T(8,128)(2,1)} %bitcast.24), calls=%async_computation | async-start | bytes 4194304 | tf_op jit(solution)/shard_map/all_to_all | solution.py:357
  10.6 19.1 %collective-permute-start.1 = (bf16[32,2048]{1,0:T(8,128)(2,1)S(1)}, bf16[32,2048]{1,0:T(8,128)(2,1)S(1)}, u32[]{:S(2)}, u32[]{:S(2)}) collective-permute-start(bf16[32,2048]{1,0:T(8,128)(2,1)S(1)} %convert_bitcast_fusion.1), channel_id=1, source_target_pairs={{0,2},{1,3},{2,0},{3,1},{4,6},{5,7},{6,4},{7,5},{8,10},{9,11},{10,... | collective-permute-start | bytes 393224 | tf_op jit(solution)/shard_map/ppermute | solution.py:310
  29.7 29.4 %collective-permute-start.2 = (bf16[32,4096]{1,0:T(8,128)(2,1)S(1)}, bf16[32,4096]{1,0:T(8,128)(2,1)S(1)}, u32[]{:S(2)}, u32[]{:S(2)}) collective-permute-start(bf16[32,4096]{1,0:T(8,128)(2,1)S(1)} %pad_maximum_fusion.4), channel_id=1, source_target_pairs={{0,4},{1,5},{2,6},{3,7},{4,0},{5,1},{6,2},{7,3},{8,12},{9,13},{10,... | collective-permute-start | bytes 786440 | tf_op jit(solution)/shard_map/ppermute | solution.py:310
  57.3 28.8 %collective-permute-start = (bf16[2048,512]{1,0:T(8,128)(2,1)S(1)}, bf16[2048,512]{1,0:T(8,128)(2,1)}, u32[]{:S(2)}, u32[]{:S(2)}) collective-permute-start(bf16[2048,512]{1,0:T(8,128)(2,1)S(1)} %bitcast.19), channel_id=1, source_target_pairs={{0,1},{1,0},{2,3},{3,2},{4,5},{5,4},{6,7},{7,6},{8,9},{9,8},{10,11... | collective-permute-start | bytes 6291464 | tf_op jit(solution)/shard_map/ppermute | solution.py:310
  59.2 4.5 %collective-permute-start.3 = (bf16[32,8192]{1,0:T(8,128)(2,1)S(1)}, bf16[32,8192]{1,0:T(8,128)(2,1)S(1)}, u32[]{:S(2)}, u32[]{:S(2)}) collective-permute-start(bf16[32,8192]{1,0:T(8,128)(2,1)S(1)} %pad_maximum_fusion.3.near_ref), channel_id=1, source_target_pairs={{0,1},{1,0},{2,3},{3,2},{4,5},{5,4},{6,7},{7,6},{8,9},{9,8},{10,11... | collective-permute-start | bytes 1572872 | tf_op jit(solution)/shard_map/ppermute | solution.py:310
  63.6 1.6 copy-start
  66.5 1.2 collective-permute-start.4
  67.8 3.7 %collective-permute-start.5 = (bf16[32,128]{1,0:T(8,128)(2,1)S(1)}, bf16[32,128]{1,0:T(8,128)(2,1)S(1)}, u32[]{:S(2)}, u32[]{:S(2)}) collective-permute-start(bf16[32,128]{1,0:T(8,128)(2,1)S(1)} %maximum_select_fusion.5), channel_id=1, source_target_pairs={{0,2},{1,3},{2,0},{3,1},{4,6},{5,7},{6,4},{7,5},{8,10},{9,11},{10,... | collective-permute-start | bytes 24584 | tf_op jit(solution)/shard_map/ppermute | solution.py:310
  71.4 3.7 %collective-permute-start.6 = (bf16[32,256]{1,0:T(8,128)(2,1)S(1)}, bf16[32,256]{1,0:T(8,128)(2,1)S(1)}, u32[]{:S(2)}, u32[]{:S(2)}) collective-permute-start(bf16[32,256]{1,0:T(8,128)(2,1)S(1)} %maximum_select_fusion.4), channel_id=1, source_target_pairs={{0,4},{1,5},{2,6},{3,7},{4,0},{5,1},{6,2},{7,3},{8,12},{9,13},{10,... | collective-permute-start | bytes 49160 | tf_op jit(solution)/shard_map/ppermute | solution.py:310
  75.2 4.2 %collective-permute-start.7 = (bf16[32,512]{1,0:T(8,128)(2,1)S(1)}, bf16[32,512]{1,0:T(8,128)(2,1)S(1)}, u32[]{:S(2)}, u32[]{:S(2)}) collective-permute-start(bf16[32,512]{1,0:T(8,128)(2,1)S(1)} %maximum_select_fusion.3), channel_id=1, source_target_pairs={{0,8},{8,0},{16,24},{24,16},{1,9},{9,1},{17,25},{25,17},{2,10},{10... | collective-permute-start | bytes 98312 | tf_op jit(solution)/shard_map/ppermute | solution.py:310
  79.4 5.2 %collective-permute-start.8 = (bf16[32,1024]{1,0:T(8,128)(2,1)S(1)}, bf16[32,1024]{1,0:T(8,128)(2,1)S(1)}, u32[]{:S(2)}, u32[]{:S(2)}) collective-permute-start(bf16[32,1024]{1,0:T(8,128)(2,1)S(1)} %maximum_select_fusion.2), channel_id=1, source_target_pairs={{0,16},{8,24},{16,0},{24,8},{1,17},{9,25},{17,1},{25,9},{2,18},{10... | collective-permute-start | bytes 196616 | tf_op jit(solution)/shard_map/ppermute | solution.py:310
  93.5 18.9 %collective-permute-start.9 = (bf16[512,1280]{1,0:T(8,128)(2,1)S(1)}, bf16[512,1280]{1,0:T(8,128)(2,1)S(1)}, u32[]{:S(2)}, u32[]{:S(2)}) collective-permute-start(bf16[512,1280]{1,0:T(8,128)(2,1)S(1)} %shard_map.31), channel_id=1, source_target_pairs={{0,2},{1,5},{2,0},{3,7},{4,6},{5,1},{6,4},{7,3},{8,10},{9,13},{10,... | collective-permute-start | bytes 3932168 | tf_op jit(solution)/shard_map/ppermute | solution.py:310
  113.4 10.7 %collective-permute-start.10 = (bf16[256,1280]{1,0:T(8,128)(2,1)S(1)}, bf16[256,1280]{1,0:T(8,128)(2,1)S(1)}, u32[]{:S(2)}, u32[]{:S(2)}) collective-permute-start(bf16[256,1280]{1,0:T(8,128)(2,1)S(1)} %shard_map.33), channel_id=1, source_target_pairs={{0,4},{1,3},{2,6},{3,1},{4,0},{5,7},{6,2},{7,5},{8,12},{9,11},{10,... | collective-permute-start | bytes 1966088 | tf_op jit(solution)/shard_map/ppermute | solution.py:310
  125.1 9.3 %collective-permute-start.11 = (bf16[128,1280]{1,0:T(8,128)(2,1)S(1)}, bf16[128,1280]{1,0:T(8,128)(2,1)S(1)}, u32[]{:S(2)}, u32[]{:S(2)}) collective-permute-start(bf16[128,1280]{1,0:T(8,128)(2,1)S(1)} %get-tuple-element.19), channel_id=1, source_target_pairs={{0,8},{8,0},{16,24},{24,16},{1,9},{9,1},{17,25},{25,17},{2,10},{10... | collective-permute-start | bytes 983048 | tf_op jit(solution)/shard_map/ppermute | solution.py:310
  135.2 9.1 %collective-permute-start.12 = (bf16[64,1280]{1,0:T(8,128)(2,1)S(1)}, bf16[64,1280]{1,0:T(8,128)(2,1)S(1)}, u32[]{:S(2)}, u32[]{:S(2)}) collective-permute-start(bf16[64,1280]{1,0:T(8,128)(2,1)S(1)} %get-tuple-element.21), channel_id=1, source_target_pairs={{0,16},{8,24},{16,0},{24,8},{1,17},{9,25},{17,1},{25,9},{2,18},{10... | collective-permute-start | bytes 491528 | tf_op jit(solution)/shard_map/ppermute | solution.py:310
  145.2 7.0 %collective-permute-start.13 = (bf16[64,1280]{1,0:T(8,128)(2,1)S(1)}, bf16[64,1280]{1,0:T(8,128)(2,1)S(1)}, u32[]{:S(2)}, u32[]{:S(2)}) collective-permute-start(bf16[64,1280]{1,0:T(8,128)(2,1)S(1)} %shard_map.36), channel_id=1, source_target_pairs={{0,16},{8,24},{16,0},{24,8},{1,17},{9,25},{17,1},{25,9},{2,18},{10... | collective-permute-start | bytes 491528 | tf_op jit(solution)/shard_map/ppermute | solution.py:310
  152.3 7.1 %collective-permute-start.14 = (bf16[128,1280]{1,0:T(8,128)(2,1)S(1)}, bf16[128,1280]{1,0:T(8,128)(2,1)S(1)}, u32[]{:S(2)}, u32[]{:S(2)}) collective-permute-start(bf16[128,1280]{1,0:T(8,128)(2,1)S(1)} %maximum_select_fusion), channel_id=1, source_target_pairs={{0,8},{8,0},{16,24},{24,16},{1,9},{9,1},{17,25},{25,17},{2,10},{10... | collective-permute-start | bytes 983048 | tf_op jit(solution)/shard_map/ppermute | solution.py:310
  159.4 16.8 %collective-permute-start.15 = (bf16[256,1280]{1,0:T(8,128)(2,1)S(1)}, bf16[256,1280]{1,0:T(8,128)(2,1)S(1)}, u32[]{:S(2)}, u32[]{:S(2)}) collective-permute-start(bf16[256,1280]{1,0:T(8,128)(2,1)S(1)} %pad_maximum_fusion.2), channel_id=1, source_target_pairs={{0,4},{1,3},{2,6},{3,1},{4,0},{5,7},{6,2},{7,5},{8,12},{9,11},{10,... | collective-permute-start | bytes 1966088 | tf_op jit(solution)/shard_map/ppermute | solution.py:310
  176.4 18.7 %collective-permute-start.16 = (bf16[512,1280]{1,0:T(8,128)(2,1)S(1)}, bf16[512,1280]{1,0:T(8,128)(2,1)S(1)}, u32[]{:S(2)}, u32[]{:S(2)}) collective-permute-start(bf16[512,1280]{1,0:T(8,128)(2,1)S(1)} %pad_maximum_fusion.1), channel_id=1, source_target_pairs={{0,2},{1,5},{2,0},{3,7},{4,6},{5,1},{6,4},{7,3},{8,10},{9,13},{10,... | collective-permute-start | bytes 3932168 | tf_op jit(solution)/shard_map/ppermute | solution.py:310
  195.3 5.0 %collective-permute-start.17 = (bf16[1024,1280]{1,0:T(8,128)(2,1)S(1)}, bf16[1024,1280]{1,0:T(8,128)(2,1)S(1)}, u32[]{:S(2)}, u32[]{:S(2)}) collective-permute-start(bf16[1024,1280]{1,0:T(8,128)(2,1)S(1)} %pad_maximum_fusion.share_ref), channel_id=1, source_target_pairs={{0,1},{1,0},{2,3},{3,2},{4,5},{5,4},{6,7},{7,6},{8,9},{9,8},{10,11... | collective-permute-start | bytes 7864328 | tf_op jit(solution)/shard_map/ppermute | solution.py:310
  237.2 4.8 %collective-permute-start.18 = (bf16[32,512]{1,0:T(8,128)(2,1)S(1)}, bf16[32,512]{1,0:T(8,128)(2,1)S(1)}, u32[]{:S(2)}, u32[]{:S(2)}) collective-permute-start(bf16[32,512]{1,0:T(8,128)(2,1)S(1)} %shard_map.39), channel_id=1, source_target_pairs={{0,16},{8,24},{16,0},{24,8},{1,17},{9,25},{17,1},{25,9},{2,18},{10... | collective-permute-start | bytes 98312 | tf_op jit(solution)/shard_map/ppermute | solution.py:310
  242.1 4.3 %collective-permute-start.19 = (bf16[32,1024]{1,0:T(8,128)(2,1)S(1)}, bf16[32,1024]{1,0:T(8,128)(2,1)S(1)}, u32[]{:S(2)}, u32[]{:S(2)}) collective-permute-start(bf16[32,1024]{1,0:T(8,128)(2,1)S(1)} %pad_maximum_fusion.5), channel_id=1, source_target_pairs={{0,8},{8,0},{16,24},{24,16},{1,9},{9,1},{17,25},{25,17},{2,10},{10... | collective-permute-start | bytes 196616 | tf_op jit(solution)/shard_map/ppermute | solution.py:310

commit v7 on v6

--- a/solution.py
+++ b/solution.py
@@ -14,7 +14,7 @@
 PANEL = 16
 GROUP = 40
 STEP = 2
-SEND, KEEP, PLACE, BLOCKS = 0, 1, 8, 16
+QUARTERS, HALVES, PLACE, BLOCKS = 0, 4, 8, 16
 SAMPLE_SPACE_LIMIT = 4096
 F32 = jnp.float32
 BF16 = jnp.bfloat16
@@ -156,7 +156,7 @@
     q_ref[...] = apply_lower(inverse_lower(gram_of(parts, p0)), parts)
 
 
-def split_off(own_ref, other_ref, q_ref, left, right):
+def factors_kernel(own_ref, other_ref, q_ref, left, right):
     k = q_ref.shape[0]
     q = q_ref[...]
     zeros = jnp.zeros(q.shape, BF16)
@@ -211,9 +211,8 @@
         out_ref[to : to + bs, width:] = jnp.concatenate(side, axis=0).T.astype(BF16)
 
 
-def form_kernel(slot, at_ref, own_ref, other_ref, q_ref, out_ref, left, right, *wins):
-    split_off(own_ref, other_ref, q_ref, left, right)
-    form_rows(q_ref.shape[0], at_ref[slot], own_ref, other_ref, left, right, out_ref, *wins)
+def form_kernel(k, slot, at_ref, own_ref, other_ref, left, right, out_ref, *wins):
+    form_rows(k, at_ref[slot], own_ref, other_ref, left, right, out_ref, *wins)
 
 
 def add_kernel(slots, at_ref, a_ref, b_ref, *o_refs):
@@ -232,7 +231,7 @@
 
 
 def add_shares(a, b, index, *slots):
-    shape = jax.ShapeDtypeStruct((a.shape[0] // (2 if slots else 1), a.shape[1]), BF16)
+    shape = jax.ShapeDtypeStruct((a.shape[0] // max(len(slots), 1), a.shape[1]), BF16)
     slots = slots or (None,)
     return kernel_call(
         functools.partial(add_kernel, slots),
@@ -271,12 +270,16 @@
         v[:, pl.ds(to, bs)] = jnp.concatenate([v1, v2, v3, v1, v2, v1], axis=0)
         return 0
 
-    lax.fori_loop(0, nb // 2, one, 0)
-
-
-def iterate_kernel(
-    offset, index_ref, far_ref, q_ref, p0_ref, *refs
-):
+    lax.fori_loop(0, share_ref.shape[0] // bs, one, 0)
+
+
+def unpack_kernel(offsets, index_ref, *refs):
+    shares, q_ref = refs[: len(offsets)], refs[len(offsets)]
+    for offset, share_ref in zip(offsets, shares):
+        unpack(offset, index_ref, share_ref, q_ref, *refs[-4:])
+
+
+def iterate_kernel(offset, index_ref, far_ref, q_ref, p0_ref, *refs):
     p_ref, inv_ref, full, u, v, diag = refs[4:]
     k, _ = q_ref.shape
     unpack(offset, index_ref, far_ref, q_ref, full, u, v, diag)
@@ -348,9 +351,12 @@
     a_of = jnp.where(c_of == 0, x, y) ^ ((at >> 2) & 1)
     b_of = jnp.where(c_of == 0, y, x) ^ ((at >> 1) & 1)
     order = c_of * 8 + a_of * 4 + b_of * 2 + (z0 ^ (at & 1))
-    quarter = nb // 4
-    pairs = [core * 2 * quarter + (1 - bit_a) * quarter, core * 2 * quarter + bit_a * quarter]
-    for bit in (bit_b, z0, z1):
+    pairs = [
+        (core * 4 + half * 2 + quarter) * (nb // 8)
+        for half in (1 - bit_a, bit_a)
+        for quarter in (1 - bit_b, bit_b)
+    ]
+    for bit in (z0, z1):
         pairs += [1 - bit, bit]
     index = jnp.concatenate([jnp.stack(pairs), place, order]).astype(jnp.int32)
 
@@ -378,61 +384,77 @@
     other = flip(block, "pix", xor_pix(1))
     px = block.shape[1]
     width = n // 2 + bs
-    rows = n // 4
+    rows = n // 8
     window = rows - bs + width
     piece = jax.ShapeDtypeStruct((rows, width + LANES), BF16)
-
-    def form(slot):
+    stack = jax.ShapeDtypeStruct((12 * k, n), BF16)
+    left, right = kernel_call(
+        factors_kernel,
+        (stack, stack),
+        in_specs=vmem(3),
+        out_specs=tuple(vmem(2)),
+        scratch_mib=12,
+    )(block, other, q)
+
+    def form(quarter):
         return kernel_call(
-            functools.partial(form_kernel, slot),
+            functools.partial(form_kernel, k, QUARTERS + quarter),
             piece,
-            in_specs=[smem()] + vmem(3),
+            in_specs=[smem()] + vmem(4),
             out_specs=vmem()[0],
-            scratch_mib=20,
-            scratch_shapes=[
-                pltpu.VMEM((12 * k, n), BF16),
-                pltpu.VMEM((12 * k, n), BF16),
-                pltpu.VMEM((window, 2 * px), BF16),
-                pltpu.VMEM((12 * k, window), BF16),
-            ],
-        )(index, block, other, q)
-
-    send = form(SEND)
-    recv = flip(send, "pix", first)
-    keep = form(KEEP)
-    (send,) = add_shares(keep, recv, index, SEND + 2)
-    (keep,) = add_shares(keep, recv, index, KEEP + 2)
+            scratch_mib=12,
+            scratch_shapes=[pltpu.VMEM((window, 2 * px), BF16), pltpu.VMEM((12 * k, window), BF16)],
+        )(index, block, other, left, right)
+
+    passed = flip(form(0), "pix", first)
+    kept = flip(form(1), "pix", first)
+    (send,) = add_shares(form(2), passed, index)
     recv = flip(send, "pix", second)
-    for b, slot in ((1, 4), (2, 6)):
-        send, keep = add_shares(keep, recv, index, SEND + slot, KEEP + slot)
+    (keep,) = add_shares(form(3), kept, index)
+    for b, slot in ((1, HALVES), (2, HALVES + 2)):
+        send, keep = add_shares(keep, recv, index, slot, slot + 1)
         recv = flip(send, "samp", xor_samp(b))
     (share,) = add_shares(keep, recv, index)
 
     share = ordered(share, flip(share, "samp", xor_samp(2)), z1)
-    for axis, perm in (("samp", xor_samp(1)), ("pix", second), ("pix", first)):
-        share = jnp.concatenate([share, flip(share, axis, perm)], axis=0)
-    far = flip(share, "pix", xor_pix(1))
+    share = jnp.concatenate([share, flip(share, "samp", xor_samp(1))], axis=0)
+    swap = xor_pix(1)
+    over_a = flip(share, "pix", first)
+    over_b = flip(share, "pix", second)
+    over_ab = flip(over_b, "pix", first)
+    near = jnp.concatenate([share, over_b], axis=0)
+    far, far_a, far_ab = [flip(t, "pix", swap) for t in (near, over_a, over_ab)]
     parts = (
         jax.ShapeDtypeStruct((n, n), BF16),
         jax.ShapeDtypeStruct((n, 8 * k), BF16),
         jax.ShapeDtypeStruct((12 * k, n), BF16),
         jax.ShapeDtypeStruct((8, n), F32),
     )
-    parts_now = kernel_call(
-        functools.partial(unpack, BLOCKS),
+    eighth = nb // 8
+    now = kernel_call(
+        functools.partial(unpack_kernel, (BLOCKS, BLOCKS + 4 * eighth)),
         parts,
-        in_specs=[smem()] + vmem(2),
+        in_specs=[smem()] + vmem(3),
         out_specs=tuple(vmem(4)),
         scratch_mib=4,
-    )(index, share, q)
+    )(index, near, far, q)
+    offsets = [BLOCKS + i * eighth for i in (2, 6, 3)]
+    now = kernel_call(
+        functools.partial(unpack_kernel, offsets),
+        parts,
+        in_specs=[smem()] + vmem(8),
+        out_specs=tuple(vmem(4)),
+        input_output_aliases={5 + i: i for i in range(4)},
+        scratch_mib=4,
+    )(index, over_a, far_a, over_ab, q, *now)
     proj, inv = kernel_call(
-        functools.partial(iterate_kernel, BLOCKS + nb // 2),
+        functools.partial(iterate_kernel, BLOCKS + 7 * eighth),
         (jax.ShapeDtypeStruct((k, n), BF16), jax.ShapeDtypeStruct((k, LANES), F32)) + parts,
         in_specs=[smem()] + vmem(7),
         out_specs=tuple(vmem(6)),
         input_output_aliases={4 + i: 2 + i for i in range(4)},
         scratch_mib=12,
-    )(index, far, q, proj, *parts_now)[:2]
+    )(index, far_ab, q, proj, *now)[:2]
 
     mine = kernel_call(
         functools.partial(finish_kernel, scale),

time: 247 us -> 234 us (0.947)
  waiting for transfers between devices: 148 us -> 133 us
    ppermute x20 -> x24, waiting for transfers between devices: 122 us -> 107 us  [flip(): return lax.ppermute(x, axes, perm)]
    pallas_call x12 -> x16, Pallas kernels: 61.9 us -> 64.1 us  [kernel_call(): return lambda *args: call(*map(place, args, in_specs))]
    ppermute x20 -> x24, starting transfers between devices: 23.6 us -> 23.7 us  [flip(): return lax.ppermute(x, axes, perm)]
  transfers between devices with their start and end apart: 21 -> 25, of which waited for: 19 -> 19; matrix products, arithmetic and copies ran while one was open for 0% -> 0% of each run, Pallas kernels for 6% -> 8%
where the time goes in v7:
time: 234 us
  waiting for transfers between devices  133 us (57%)
  Pallas kernels  64.1 us (27%)
  starting transfers between devices  31 us (13%)
  local copies, waits for them, and re-layouts  4.9 us (2%)
    ppermute x24, waiting for transfers between devices, flip(): return lax.ppermute(x, axes, perm)  107 us
    pallas_call x16, Pallas kernels, kernel_call(): return lambda *args: call(*map(place, args, in_specs))  64.1 us
    all_to_all x1, waiting for transfers between devices, sample_space(): lax.all_to_all(stamps, ('pix', 'samp'), split_axis=1, concat_axis=0, tile...  26 us
    ppermute x24, starting transfers between devices, flip(): return lax.ppermute(x, axes, perm)  23.7 us
    all_to_all x1, starting transfers between devices, sample_space(): lax.all_to_all(stamps, ('pix', 'samp'), split_axis=1, concat_axis=0, tile...  7.33 us
  transfers between devices with their start and end apart: 25, of which 19 were waited for; matrix products, arithmetic and copies ran while one was open for 0% of the time, Pallas kernels for 8%

profile of v7, /device:TPU:0, one launch (start us, length us, event | category | flops | bytes accessed | tf_op | source)
XLA Modules:
  0.0 234.0 jit_solution(13322268947205776924)
XLA Ops:
  0.0 3.2 %copy.14 = bf16[8,32,8,512]{3,2,0,1:T(8,128)(2,1)} copy(bf16[8,32,8,512]{3,2,1,0:T(8,128)(2,1)} %bitcast.26) | data formatting | bytes 4194304 | tf_op jit(solution)/shard_map/all_to_all | solution.py:363
  3.2 7.3 %all-to-all-start = ((bf16[64,32,512]{2,0,1:T(8,128)(2,1)}), bf16[64,32,512]{2,0,1:T(8,128)(2,1)S(1)}, u32[]{:S(2)}, u32[]{:S(2)}) async-start(bf16[64,32,512]{2,0,1:T(8,128)(2,1)} %bitcast.27), calls=%async_computation | async-start | bytes 4194304 | tf_op jit(solution)/shard_map/all_to_all | solution.py:363
  10.6 1.8 collective-permute-start.1
  12.4 17.3 %collective-permute-done.1 = bf16[32,2048]{1,0:T(8,128)(2,1)S(1)} collective-permute-done((bf16[32,2048]{1,0:T(8,128)(2,1)S(1)}, bf16[32,2048]{1,0:T(8,128)(2,1)S(1)}, u32[]{:S(2)}, u32[]{:S(2)}) %collective-permute-start.1) | collective-permute-done | bytes 131104 | tf_op jit(solution)/shard_map/ppermute | solution.py:313
  29.8 1.5 collective-permute-start.2
  31.3 26.0 %all-to-all-done = bf16[64,32,512]{2,0,1:T(8,128)(2,1)S(1)} async-done(((bf16[64,32,512]{2,0,1:T(8,128)(2,1)}), bf16[64,32,512]{2,0,1:T(8,128)(2,1)S(1)}, u32[]{:S(2)}, u32[]{:S(2)}) %all-to-all-start) | async-done | bytes 2097184 | tf_op jit(solution)/shard_map/all_to_all | solution.py:363
  57.3 1.8 collective-permute-start
  59.4 4.3 %collective-permute-done.3.far_ref = bf16[32,8192]{1,0:T(8,128)(2,1)S(1)} collective-permute-done((bf16[32,8192]{1,0:T(8,128)(2,1)S(1)}, bf16[32,8192]{1,0:T(8,128)(2,1)S(1)}, u32[]{:S(2)}, u32[]{:S(2)}) %collective-permute-start.3) | collective-permute-done | bytes 524320 | tf_op jit(solution)/shard_map/ppermute | solution.py:313
  63.7 1.6 copy-done
  65.2 1.2 shard_map.28
  66.8 0.8 collective-permute-done.4
  67.8 1.5 collective-permute-start.5
  69.3 2.1 collective-permute-done.5
  71.4 1.5 collective-permute-start.6
  72.9 2.2 collective-permute-done.6
  75.2 2.3 %collective-permute-start.7 = (bf16[32,512]{1,0:T(8,128)(2,1)S(1)}, bf16[32,512]{1,0:T(8,128)(2,1)S(1)}, u32[]{:S(2)}, u32[]{:S(2)}) collective-permute-start(bf16[32,512]{1,0:T(8,128)(2,1)S(1)} %maximum_select_fusion.3), channel_id=1, source_target_pairs={{0,8},{8,0},{16,24},{24,16},{1,9},{9,1},{17,25},{25,17},{2,10},{10... | collective-permute-start | bytes 98312 | tf_op jit(solution)/shard_map/ppermute | solution.py:313
  77.5 1.9 collective-permute-done.7
  79.4 1.2 collective-permute-start.8
  80.6 4.0 %collective-permute-done.8 = bf16[32,1024]{1,0:T(8,128)(2,1)S(1)} collective-permute-done((bf16[32,1024]{1,0:T(8,128)(2,1)S(1)}, bf16[32,1024]{1,0:T(8,128)(2,1)S(1)}, u32[]{:S(2)}, u32[]{:S(2)}) %collective-permute-start.8) | collective-permute-done | bytes 65568 | tf_op jit(solution)/shard_map/ppermute | solution.py:313
  84.7 1.4 shard_map.29
  86.1 5.0 %shard_map.30 = (bf16[384,2048]{1,0:T(8,128)(2,1)S(1)}, bf16[384,2048]{1,0:T(8,128)(2,1)S(1)}) custom-call(bf16[2048,512]{1,0:T(8,128)(2,1)S(1)} %bitcast.20, bf16[2048,512]{1,0:T(8,128)(2,1)} %collective-permute-done.other_ref, f32[32,2048]{1,0:T(8,128)S(1)} %get-tuple-element.23.q_ref.refs_2_.refs_3_), custom_call_target="tpu_custom_call" | custom-call | tf_op jit(solution)/shard_map/pallas_call | solution.py:75
  91.1 2.9 %shard_map.35 = bf16[256,1280]{1,0:T(8,128)(2,1)S(1)} custom-call(s32[32]{0:T(128)S(1)} %concatenate.59.index_ref.at_ref, bf16[2048,512]{1,0:T(8,128)(2,1)S(1)} %bitcast.21, bf16[2048,512]{1,0:T(8,128)(2,1)} %collective-permute-done.other_ref, bf16[384,2048]{1,0:T(8,128)(2,1)S(1)} %get-tuple-element.24.left, bf16[384,2048]{1,0:T(8,128)(2,1)S(1)} %get-tuple-element.25.right), custom_call_target="tpu_custom_call" | custom-call | tf_op jit(solution)/shard_map/pallas_call | solution.py:75
  94.0 2.0 collective-permute-start.10
  96.0 2.9 %shard_map.32 = bf16[256,1280]{1,0:T(8,128)(2,1)S(1)} custom-call(s32[32]{0:T(128)S(1)} %concatenate.59.index_ref.at_ref, bf16[2048,512]{1,0:T(8,128)(2,1)S(1)} %bitcast.22, bf16[2048,512]{1,0:T(8,128)(2,1)} %collective-permute-done.other_ref, bf16[384,2048]{1,0:T(8,128)(2,1)S(1)} %get-tuple-element.24.left, bf16[384,2048]{1,0:T(8,128)(2,1)S(1)} %get-tuple-element.25.right), custom_call_target="tpu_custom_call" | custom-call | tf_op jit(solution)/shard_map/pallas_call | solution.py:75
  99.0 2.9 %shard_map.34.a_ref = bf16[256,1280]{1,0:T(8,128)(2,1)S(1)} custom-call(s32[32]{0:T(128)S(1)} %concatenate.59.index_ref.at_ref, bf16[2048,512]{1,0:T(8,128)(2,1)S(1)} %bitcast.23, bf16[2048,512]{1,0:T(8,128)(2,1)} %collective-permute-done.other_ref, bf16[384,2048]{1,0:T(8,128)(2,1)S(1)} %get-tuple-element.24.left, bf16[384,2048]{1,0:T(8,128)(2,1)S(1)} %get-tuple-element.25.right), custom_call_target="tpu_custom_call" | custom-call | tf_op jit(solution)/shard_map/pallas_call | solution.py:75
  101.9 4.0 %collective-permute-done.10.b_ref = bf16[256,1280]{1,0:T(8,128)(2,1)S(1)} collective-permute-done((bf16[256,1280]{1,0:T(8,128)(2,1)S(1)}, bf16[256,1280]{1,0:T(8,128)(2,1)S(1)}, u32[]{:S(2)}, u32[]{:S(2)}) %collective-permute-start.10) | collective-permute-done | bytes 655392 | tf_op jit(solution)/shard_map/ppermute | solution.py:313
  105.8 1.0 shard_map.36
  107.6 2.9 %shard_map.31.a_ref = bf16[256,1280]{1,0:T(8,128)(2,1)S(1)} custom-call(s32[32]{0:T(128)S(1)} %concatenate.59.index_ref.at_ref, bf16[2048,512]{1,0:T(8,128)(2,1)S(1)} %bitcast.24, bf16[2048,512]{1,0:T(8,128)(2,1)} %collective-permute-done.other_ref, bf16[384,2048]{1,0:T(8,128)(2,1)S(1)} %get-tuple-element.24.left, bf16[384,2048]{1,0:T(8,128)(2,1)S(1)} %get-tuple-element.25.right), custom_call_target="tpu_custom_call" | custom-call | tf_op jit(solution)/shard_map/pallas_call | solution.py:75
  110.5 8.1 %collective-permute-done.9.b_ref = bf16[256,1280]{1,0:T(8,128)(2,1)S(1)} collective-permute-done((bf16[256,1280]{1,0:T(8,128)(2,1)S(1)}, bf16[256,1280]{1,0:T(8,128)(2,1)S(1)}, u32[]{:S(2)}, u32[]{:S(2)}) %collective-permute-start.9) | collective-permute-done | bytes 655392 | tf_op jit(solution)/shard_map/ppermute | solution.py:313
  118.7 1.0 shard_map.33.a_ref
  119.7 1.0 shard_map.37
  120.7 2.1 collective-permute-start.12
  122.8 5.4 %collective-permute-done.12.b_ref = bf16[128,1280]{1,0:T(8,128)(2,1)S(1)} collective-permute-done((bf16[128,1280]{1,0:T(8,128)(2,1)S(1)}, bf16[128,1280]{1,0:T(8,128)(2,1)S(1)}, u32[]{:S(2)}, u32[]{:S(2)}) %collective-permute-start.12) | collective-permute-done | bytes 327712 | tf_op jit(solution)/shard_map/ppermute | solution.py:313
  128.2 0.8 shard_map.38
  129.0 1.1 collective-permute-start.13
  130.1 9.0 %collective-permute-done.13.b_ref = bf16[64,1280]{1,0:T(8,128)(2,1)S(1)} collective-permute-done((bf16[64,1280]{1,0:T(8,128)(2,1)S(1)}, bf16[64,1280]{1,0:T(8,128)(2,1)S(1)}, u32[]{:S(2)}, u32[]{:S(2)}) %collective-permute-start.13) | collective-permute-done | bytes 163872 | tf_op jit(solution)/shard_map/ppermute | solution.py:313
  139.9 7.7 %collective-permute-done.14 = bf16[64,1280]{1,0:T(8,128)(2,1)S(1)} collective-permute-done((bf16[64,1280]{1,0:T(8,128)(2,1)S(1)}, bf16[64,1280]{1,0:T(8,128)(2,1)S(1)}, u32[]{:S(2)}, u32[]{:S(2)}) %collective-permute-start.14) | collective-permute-done | bytes 163872 | tf_op jit(solution)/shard_map/ppermute | solution.py:313
  147.8 7.0 %collective-permute-done.15 = bf16[128,1280]{1,0:T(8,128)(2,1)S(1)} collective-permute-done((bf16[128,1280]{1,0:T(8,128)(2,1)S(1)}, bf16[128,1280]{1,0:T(8,128)(2,1)S(1)}, u32[]{:S(2)}, u32[]{:S(2)}) %collective-permute-start.15) | collective-permute-done | bytes 327712 | tf_op jit(solution)/shard_map/ppermute | solution.py:313
  154.8 2.3 collective-permute-start.16
  157.1 8.6 %collective-permute-done.16 = bf16[256,1280]{1,0:T(8,128)(2,1)S(1)} collective-permute-done((bf16[256,1280]{1,0:T(8,128)(2,1)S(1)}, bf16[256,1280]{1,0:T(8,128)(2,1)S(1)}, u32[]{:S(2)}, u32[]{:S(2)}) %collective-permute-start.16) | collective-permute-done | bytes 655392 | tf_op jit(solution)/shard_map/ppermute | solution.py:313
  165.8 1.8 collective-permute-start.19
  167.9 8.6 %collective-permute-done.19.refs_0_ = bf16[256,1280]{1,0:T(8,128)(2,1)S(1)} collective-permute-done((bf16[256,1280]{1,0:T(8,128)(2,1)S(1)}, bf16[256,1280]{1,0:T(8,128)(2,1)S(1)}, u32[]{:S(2)}, u32[]{:S(2)}) %collective-permute-start.19) | collective-permute-done | bytes 655392 | tf_op jit(solution)/shard_map/ppermute | solution.py:313
  176.4 7.0 %collective-permute-done.17.refs_2_ = bf16[256,1280]{1,0:T(8,128)(2,1)S(1)} collective-permute-done((bf16[256,1280]{1,0:T(8,128)(2,1)S(1)}, bf16[256,1280]{1,0:T(8,128)(2,1)S(1)}, u32[]{:S(2)}, u32[]{:S(2)}) %collective-permute-start.17) | collective-permute-done | bytes 655392 | tf_op jit(solution)/shard_map/ppermute | solution.py:313
  183.5 2.9 %shard_map.40 = (bf16[2048,2048]{1,0:T(8,128)(2,1)S(1)}, bf16[2048,256]{1,0:T(8,128)(2,1)S(1)}, bf16[384,2048]{1,0:T(8,128)(2,1)S(1)}, f32[8,2048]{1,0:T(8,128)S(1)}) custom-call(s32[32]{0:T(128)S(1)} %concatenate.59.index_ref.at_ref, bf16[512,1280]{1,0:T(8,128)(2,1)S(1)} %pad_maximum_fusion.refs_0_, bf16[512,1280]{1,0:T(8,128)(2,1)S(1)} %collective-permute-done.21.refs_1_, ...), custom_call_target="tpu_custom_call" | custom-call | tf_op jit(solution)/shard_map/pallas_call | solution.py:75
  186.3 2.5 %shard_map.41 = (bf16[2048,2048]{1,0:T(8,128)(2,1)S(1)}, bf16[2048,256]{1,0:T(8,128)(2,1)S(1)}, bf16[384,2048]{1,0:T(8,128)(2,1)S(1)}, f32[8,2048]{1,0:T(8,128)S(1)}) custom-call(s32[32]{0:T(128)S(1)} %concatenate.59.index_ref.at_ref, ...), custom_call_target="tpu_custom_call", output_to_operand_aliasing={{0}: (5, {}), {1}: (6, {}), {2}: (7, {}), {3}: (8, {})} | custom-call | tf_op jit(solution)/shard_map/pallas_call | solution.py:75
  188.8 34.6 %shard_map.42 = (bf16[32,2048]{1,0:T(8,128)(2,1)S(1)}, f32[32,128]{1,0:T(8,128)S(1)}, bf16[2048,2048]{1,0:T(8,128)(2,1)S(1)}, bf16[2048,256]{1,0:T(8,128)(2,1)S(...) custom-call(s32[32]{0:T(128)S(1)} %concatenate.59.index_ref.at_ref, ...), custom_call_target="tpu_custom_call", output_to_operand_aliasing={{2}: (4, {}), {3}: (5, {}), {4}: (6, {}), {5}: (7, {})} | custom-call | tf_op jit(solution)/shard_map/pallas_call | solution.py:75
  224.7 4.3 %collective-permute-done.22 = bf16[32,512]{1,0:T(8,128)(2,1)S(1)} collective-permute-done((bf16[32,512]{1,0:T(8,128)(2,1)S(1)}, bf16[32,512]{1,0:T(8,128)(2,1)S(1)}, u32[]{:S(2)}, u32[]{:S(2)}) %collective-permute-start.22) | collective-permute-done | bytes 32800 | tf_op jit(solution)/shard_map/ppermute | solution.py:313
  229.0 4.3 %collective-permute-done.23 = bf16[32,1024]{1,0:T(8,128)(2,1)S(1)} collective-permute-done((bf16[32,1024]{1,0:T(8,128)(2,1)S(1)}, bf16[32,1024]{1,0:T(8,128)(2,1)S(1)}, u32[]{:S(2)}, u32[]{:S(2)}) %collective-permute-start.23) | collective-permute-done | bytes 65568 | tf_op jit(solution)/shard_map/ppermute | solution.py:313
  (40 shorter events, 5.2 us)
Async XLA Ops:
  3.2 7.3 %copy-start.1 = (f32[2048,32]{0,1:T(8,128)S(1)}, f32[2048,32]{0,1:T(8,128)}, u32[]{:S(2)}) copy-start(f32[2048,32]{0,1:T(8,128)} %param.3) | copy-start | bytes 786436
  3.2 54.1 %all-to-all-start = ((bf16[64,32,512]{2,0,1:T(8,128)(2,1)}), bf16[64,32,512]{2,0,1:T(8,128)(2,1)S(1)}, u32[]{:S(2)}, u32[]{:S(2)}) async-start(bf16[64,32,512]{2,0,1:T(8,128)(2,1)} %bitcast.27), calls=%async_computation | async-start | bytes 4194304 | tf_op jit(solution)/shard_map/all_to_all | solution.py:363
  10.6 19.1 %collective-permute-start.1 = (bf16[32,2048]{1,0:T(8,128)(2,1)S(1)}, bf16[32,2048]{1,0:T(8,128)(2,1)S(1)}, u32[]{:S(2)}, u32[]{:S(2)}) collective-permute-start(bf16[32,2048]{1,0:T(8,128)(2,1)S(1)} %convert_bitcast_fusion.1), channel_id=1, source_target_pairs={{0,2},{1,3},{2,0},{3,1},{4,6},{5,7},{6,4},{7,5},{8,10},{9,11},{10,... | collective-permute-start | bytes 393224 | tf_op jit(solution)/shard_map/ppermute | solution.py:313
  29.8 29.4 %collective-permute-start.2 = (bf16[32,4096]{1,0:T(8,128)(2,1)S(1)}, bf16[32,4096]{1,0:T(8,128)(2,1)S(1)}, u32[]{:S(2)}, u32[]{:S(2)}) collective-permute-start(bf16[32,4096]{1,0:T(8,128)(2,1)S(1)} %pad_maximum_fusion.3), channel_id=1, source_target_pairs={{0,4},{1,5},{2,6},{3,7},{4,0},{5,1},{6,2},{7,3},{8,12},{9,13},{10,... | collective-permute-start | bytes 786440 | tf_op jit(solution)/shard_map/ppermute | solution.py:313
  57.3 28.8 %collective-permute-start = (bf16[2048,512]{1,0:T(8,128)(2,1)S(1)}, bf16[2048,512]{1,0:T(8,128)(2,1)}, u32[]{:S(2)}, u32[]{:S(2)}) collective-permute-start(bf16[2048,512]{1,0:T(8,128)(2,1)S(1)} %bitcast.19), channel_id=1, source_target_pairs={{0,1},{1,0},{2,3},{3,2},{4,5},{5,4},{6,7},{7,6},{8,9},{9,8},{10,11... | collective-permute-start | bytes 6291464 | tf_op jit(solution)/shard_map/ppermute | solution.py:313
  59.2 4.5 %collective-permute-start.3 = (bf16[32,8192]{1,0:T(8,128)(2,1)S(1)}, bf16[32,8192]{1,0:T(8,128)(2,1)S(1)}, u32[]{:S(2)}, u32[]{:S(2)}) collective-permute-start(bf16[32,8192]{1,0:T(8,128)(2,1)S(1)} %pad_maximum_fusion.2.near_ref), channel_id=1, source_target_pairs={{0,1},{1,0},{2,3},{3,2},{4,5},{5,4},{6,7},{7,6},{8,9},{9,8},{10,11... | collective-permute-start | bytes 1572872 | tf_op jit(solution)/shard_map/ppermute | solution.py:313
  63.7 1.6 copy-start
  66.4 1.2 collective-permute-start.4
  67.8 3.7 %collective-permute-start.5 = (bf16[32,128]{1,0:T(8,128)(2,1)S(1)}, bf16[32,128]{1,0:T(8,128)(2,1)S(1)}, u32[]{:S(2)}, u32[]{:S(2)}) collective-permute-start(bf16[32,128]{1,0:T(8,128)(2,1)S(1)} %maximum_select_fusion.5), channel_id=1, source_target_pairs={{0,2},{1,3},{2,0},{3,1},{4,6},{5,7},{6,4},{7,5},{8,10},{9,11},{10,... | collective-permute-start | bytes 24584 | tf_op jit(solution)/shard_map/ppermute | solution.py:313
  71.4 3.7 %collective-permute-start.6 = (bf16[32,256]{1,0:T(8,128)(2,1)S(1)}, bf16[32,256]{1,0:T(8,128)(2,1)S(1)}, u32[]{:S(2)}, u32[]{:S(2)}) collective-permute-start(bf16[32,256]{1,0:T(8,128)(2,1)S(1)} %maximum_select_fusion.4), channel_id=1, source_target_pairs={{0,4},{1,5},{2,6},{3,7},{4,0},{5,1},{6,2},{7,3},{8,12},{9,13},{10,... | collective-permute-start | bytes 49160 | tf_op jit(solution)/shard_map/ppermute | solution.py:313
  75.2 4.2 %collective-permute-start.7 = (bf16[32,512]{1,0:T(8,128)(2,1)S(1)}, bf16[32,512]{1,0:T(8,128)(2,1)S(1)}, u32[]{:S(2)}, u32[]{:S(2)}) collective-permute-start(bf16[32,512]{1,0:T(8,128)(2,1)S(1)} %maximum_select_fusion.3), channel_id=1, source_target_pairs={{0,8},{8,0},{16,24},{24,16},{1,9},{9,1},{17,25},{25,17},{2,10},{10... | collective-permute-start | bytes 98312 | tf_op jit(solution)/shard_map/ppermute | solution.py:313
  79.4 5.2 %collective-permute-start.8 = (bf16[32,1024]{1,0:T(8,128)(2,1)S(1)}, bf16[32,1024]{1,0:T(8,128)(2,1)S(1)}, u32[]{:S(2)}, u32[]{:S(2)}) collective-permute-start(bf16[32,1024]{1,0:T(8,128)(2,1)S(1)} %maximum_select_fusion.2), channel_id=1, source_target_pairs={{0,16},{8,24},{16,0},{24,8},{1,17},{9,25},{17,1},{25,9},{2,18},{10... | collective-permute-start | bytes 196616 | tf_op jit(solution)/shard_map/ppermute | solution.py:313
  94.0 11.9 %collective-permute-start.10 = (bf16[256,1280]{1,0:T(8,128)(2,1)S(1)}, bf16[256,1280]{1,0:T(8,128)(2,1)S(1)}, u32[]{:S(2)}, u32[]{:S(2)}) collective-permute-start(bf16[256,1280]{1,0:T(8,128)(2,1)S(1)} %shard_map.35), channel_id=1, source_target_pairs={{0,2},{1,5},{2,0},{3,7},{4,6},{5,1},{6,4},{7,3},{8,10},{9,13},{10,... | collective-permute-start | bytes 1966088 | tf_op jit(solution)/shard_map/ppermute | solution.py:313
  98.9 19.8 %collective-permute-start.9 = (bf16[256,1280]{1,0:T(8,128)(2,1)S(1)}, bf16[256,1280]{1,0:T(8,128)(2,1)S(1)}, u32[]{:S(2)}, u32[]{:S(2)}) collective-permute-start(bf16[256,1280]{1,0:T(8,128)(2,1)S(1)} %shard_map.32), channel_id=1, source_target_pairs={{0,2},{1,5},{2,0},{3,7},{4,6},{5,1},{6,4},{7,3},{8,10},{9,13},{10,... | collective-permute-start | bytes 1966088 | tf_op jit(solution)/shard_map/ppermute | solution.py:313
  106.8 12.8 %collective-permute-start.11 = (bf16[256,1280]{1,0:T(8,128)(2,1)S(1)}, bf16[256,1280]{1,0:T(8,128)(2,1)S(1)}, u32[]{:S(2)}, u32[]{:S(2)}) collective-permute-start(bf16[256,1280]{1,0:T(8,128)(2,1)S(1)} %shard_map.36), channel_id=1, source_target_pairs={{0,4},{1,3},{2,6},{3,1},{4,0},{5,7},{6,2},{7,5},{8,12},{9,11},{10,... | collective-permute-start | bytes 1966088 | tf_op jit(solution)/shard_map/ppermute | solution.py:313
  120.7 7.5 %collective-permute-start.12 = (bf16[128,1280]{1,0:T(8,128)(2,1)S(1)}, bf16[128,1280]{1,0:T(8,128)(2,1)S(1)}, u32[]{:S(2)}, u32[]{:S(2)}) collective-permute-start(bf16[128,1280]{1,0:T(8,128)(2,1)S(1)} %get-tuple-element.27), channel_id=1, source_target_pairs={{0,8},{8,0},{16,24},{24,16},{1,9},{9,1},{17,25},{25,17},{2,10},{10... | collective-permute-start | bytes 983048 | tf_op jit(solution)/shard_map/ppermute | solution.py:313
  129.0 10.0 %collective-permute-start.13 = (bf16[64,1280]{1,0:T(8,128)(2,1)S(1)}, bf16[64,1280]{1,0:T(8,128)(2,1)S(1)}, u32[]{:S(2)}, u32[]{:S(2)}) collective-permute-start(bf16[64,1280]{1,0:T(8,128)(2,1)S(1)} %get-tuple-element.29), channel_id=1, source_target_pairs={{0,16},{8,24},{16,0},{24,8},{1,17},{9,25},{17,1},{25,9},{2,18},{10... | collective-permute-start | bytes 491528 | tf_op jit(solution)/shard_map/ppermute | solution.py:313
  139.8 7.8 %collective-permute-start.14 = (bf16[64,1280]{1,0:T(8,128)(2,1)S(1)}, bf16[64,1280]{1,0:T(8,128)(2,1)S(1)}, u32[]{:S(2)}, u32[]{:S(2)}) collective-permute-start(bf16[64,1280]{1,0:T(8,128)(2,1)S(1)} %shard_map.39), channel_id=1, source_target_pairs={{0,16},{8,24},{16,0},{24,8},{1,17},{9,25},{17,1},{25,9},{2,18},{10... | collective-permute-start | bytes 491528 | tf_op jit(solution)/shard_map/ppermute | solution.py:313
  147.6 7.1 %collective-permute-start.15 = (bf16[128,1280]{1,0:T(8,128)(2,1)S(1)}, bf16[128,1280]{1,0:T(8,128)(2,1)S(1)}, u32[]{:S(2)}, u32[]{:S(2)}) collective-permute-start(bf16[128,1280]{1,0:T(8,128)(2,1)S(1)} %maximum_select_fusion), channel_id=1, source_target_pairs={{0,8},{8,0},{16,24},{24,16},{1,9},{9,1},{17,25},{25,17},{2,10},{10... | collective-permute-start | bytes 983048 | tf_op jit(solution)/shard_map/ppermute | solution.py:313
  154.8 10.8 %collective-permute-start.16 = (bf16[256,1280]{1,0:T(8,128)(2,1)S(1)}, bf16[256,1280]{1,0:T(8,128)(2,1)S(1)}, u32[]{:S(2)}, u32[]{:S(2)}) collective-permute-start(bf16[256,1280]{1,0:T(8,128)(2,1)S(1)} %pad_maximum_fusion.1), channel_id=1, source_target_pairs={{0,4},{1,3},{2,6},{3,1},{4,0},{5,7},{6,2},{7,5},{8,12},{9,11},{10,... | collective-permute-start | bytes 1966088 | tf_op jit(solution)/shard_map/ppermute | solution.py:313
  165.7 17.8 %collective-permute-start.21 = (bf16[512,1280]{1,0:T(8,128)(2,1)S(1)}, bf16[512,1280]{1,0:T(8,128)(2,1)S(1)}, u32[]{:S(2)}, u32[]{:S(2)}) collective-permute-start(bf16[512,1280]{1,0:T(8,128)(2,1)S(1)} %pad_maximum_fusion.refs_0_), channel_id=1, source_target_pairs={{0,1},{1,0},{2,3},{3,2},{4,5},{5,4},{6,7},{7,6},{8,9},{9,8},{10,11... | collective-permute-start | bytes 3932168 | tf_op jit(solution)/shard_map/ppermute | solution.py:313
  165.8 10.7 %collective-permute-start.19 = (bf16[256,1280]{1,0:T(8,128)(2,1)S(1)}, bf16[256,1280]{1,0:T(8,128)(2,1)S(1)}, u32[]{:S(2)}, u32[]{:S(2)}) collective-permute-start(bf16[256,1280]{1,0:T(8,128)(2,1)S(1)} %pad_maximum_fusion.1), channel_id=1, source_target_pairs={{0,2},{1,5},{2,0},{3,7},{4,6},{5,1},{6,4},{7,3},{8,10},{9,13},{10,... | collective-permute-start | bytes 1966088 | tf_op jit(solution)/shard_map/ppermute | solution.py:313
  167.6 15.9 %collective-permute-start.17 = (bf16[256,1280]{1,0:T(8,128)(2,1)S(1)}, bf16[256,1280]{1,0:T(8,128)(2,1)S(1)}, u32[]{:S(2)}, u32[]{:S(2)}) collective-permute-start(bf16[256,1280]{1,0:T(8,128)(2,1)S(1)} %collective-permute-done.16), channel_id=1, source_target_pairs={{0,2},{1,5},{2,0},{3,7},{4,6},{5,1},{6,4},{7,3},{8,10},{9,13},{10,... | collective-permute-start | bytes 1966088 | tf_op jit(solution)/shard_map/ppermute | solution.py:313
  176.4 9.9 %collective-permute-start.20 = (bf16[256,1280]{1,0:T(8,128)(2,1)S(1)}, bf16[256,1280]{1,0:T(8,128)(2,1)S(1)}, u32[]{:S(2)}, u32[]{:S(2)}) collective-permute-start(bf16[256,1280]{1,0:T(8,128)(2,1)S(1)} %collective-permute-done.19.refs_0_), channel_id=1, source_target_pairs={{0,1},{1,0},{2,3},{3,2},{4,5},{5,4},{6,7},{7,6},{8,9},{9,8},{10,11... | collective-permute-start | bytes 1966088 | tf_op jit(solution)/shard_map/ppermute | solution.py:313
  183.5 5.4 %collective-permute-start.18 = (bf16[256,1280]{1,0:T(8,128)(2,1)S(1)}, bf16[256,1280]{1,0:T(8,128)(2,1)S(1)}, u32[]{:S(2)}, u32[]{:S(2)}) collective-permute-start(bf16[256,1280]{1,0:T(8,128)(2,1)S(1)} %collective-permute-done.17.refs_2_), channel_id=1, source_target_pairs={{0,1},{1,0},{2,3},{3,2},{4,5},{5,4},{6,7},{7,6},{8,9},{9,8},{10,11... | collective-permute-start | bytes 1966088 | tf_op jit(solution)/shard_map/ppermute | solution.py:313
  224.0 5.0 %collective-permute-start.22 = (bf16[32,512]{1,0:T(8,128)(2,1)S(1)}, bf16[32,512]{1,0:T(8,128)(2,1)S(1)}, u32[]{:S(2)}, u32[]{:S(2)}) collective-permute-start(bf16[32,512]{1,0:T(8,128)(2,1)S(1)} %shard_map.43), channel_id=1, source_target_pairs={{0,16},{8,24},{16,0},{24,8},{1,17},{9,25},{17,1},{25,9},{2,18},{10... | collective-permute-start | bytes 98312 | tf_op jit(solution)/shard_map/ppermute | solution.py:313
  229.0 4.3 %collective-permute-start.23 = (bf16[32,1024]{1,0:T(8,128)(2,1)S(1)}, bf16[32,1024]{1,0:T(8,128)(2,1)S(1)}, u32[]{:S(2)}, u32[]{:S(2)}) collective-permute-start(bf16[32,1024]{1,0:T(8,128)(2,1)S(1)} %pad_maximum_fusion.4), channel_id=1, source_target_pairs={{0,8},{8,0},{16,24},{24,16},{1,9},{9,1},{17,25},{25,17},{2,10},{10... | collective-permute-start | bytes 196616 | tf_op jit(solution)/shard_map/ppermute | solution.py:313

commit v8 on v7

--- a/solution.py
+++ b/solution.py
@@ -215,14 +215,15 @@
     form_rows(k, at_ref[slot], own_ref, other_ref, left, right, out_ref, *wins)
 
 
-def add_kernel(slots, at_ref, a_ref, b_ref, *o_refs):
-    width = a_ref.shape[1] - LANES
+def add_kernel(slots, at_ref, *refs):
+    shares, o_refs = refs[: -len(slots)], refs[-len(slots) :]
+    width = shares[0].shape[1] - LANES
     for slot, o_ref in zip(slots, o_refs):
         h = o_ref.shape[0]
         at = 0 if slot is None else pl.multiple_of(at_ref[slot] * h, h)
-        a, b = a_ref[pl.ds(at, h), :], b_ref[pl.ds(at, h), :]
-        o_ref[:, :width] = (a[:, :width].astype(F32) + b[:, :width].astype(F32)).astype(BF16)
-        x = lane_sum3(a[:, width:].astype(F32), GROUP) + lane_sum3(b[:, width:].astype(F32), GROUP)
+        parts = [ref[pl.ds(at, h), :].astype(F32) for ref in shares]
+        o_ref[:, :width] = sum(part[:, :width] for part in parts).astype(BF16)
+        x = sum(lane_sum3(part[:, width:], GROUP) for part in parts)
         lane = lax.broadcasted_iota(jnp.int32, x.shape, 1)
         h1, h2, h3 = [part.astype(F32) for part in split3(x)]
         packed = jnp.where(lane < 2 * GROUP, pltpu.roll(h2, GROUP, 1), pltpu.roll(h3, 2 * GROUP, 1))
@@ -230,15 +231,16 @@
         o_ref[:, width:] = jnp.where(lane < 3 * GROUP, packed, 0.0).astype(BF16)
 
 
-def add_shares(a, b, index, *slots):
-    shape = jax.ShapeDtypeStruct((a.shape[0] // max(len(slots), 1), a.shape[1]), BF16)
+def add_shares(index, shares, slots=()):
+    rows, lanes = shares[0].shape
+    shape = jax.ShapeDtypeStruct((rows // max(len(slots), 1), lanes), BF16)
     slots = slots or (None,)
     return kernel_call(
         functools.partial(add_kernel, slots),
         (shape,) * len(slots),
-        in_specs=[smem()] + vmem(2),
+        in_specs=[smem()] + vmem(len(shares)),
         out_specs=tuple(vmem(len(slots))),
-    )(index, a, b)
+    )(index, *shares)
 
 
 def unpack(offset, index_ref, share_ref, q_ref, full, u, v, diag):
@@ -356,9 +358,8 @@
         for half in (1 - bit_a, bit_a)
         for quarter in (1 - bit_b, bit_b)
     ]
-    for bit in (z0, z1):
-        pairs += [1 - bit, bit]
-    index = jnp.concatenate([jnp.stack(pairs), place, order]).astype(jnp.int32)
+    pairs += [1 - z0, z0, 0, 0]
+    index = jnp.concatenate([jnp.stack([jnp.int32(i) for i in pairs]), place, order]).astype(jnp.int32)
 
     block = lax.all_to_all(stamps, ("pix", "samp"), split_axis=1, concat_axis=0, tiled=True)
 
@@ -408,15 +409,12 @@
 
     passed = flip(form(0), "pix", first)
     kept = flip(form(1), "pix", first)
-    (send,) = add_shares(form(2), passed, index)
+    (send,) = add_shares(index, (form(2), passed))
     recv = flip(send, "pix", second)
-    (keep,) = add_shares(form(3), kept, index)
-    for b, slot in ((1, HALVES), (2, HALVES + 2)):
-        send, keep = add_shares(keep, recv, index, slot, slot + 1)
-        recv = flip(send, "samp", xor_samp(b))
-    (share,) = add_shares(keep, recv, index)
-
-    share = ordered(share, flip(share, "samp", xor_samp(2)), z1)
+    send, keep = add_shares(index, (form(3), kept, recv), (HALVES, HALVES + 1))
+    (share,) = add_shares(index, (keep, flip(send, "samp", xor_samp(1))))
+    (share,) = add_shares(index, (share, flip(share, "samp", xor_samp(2))))
+
     share = jnp.concatenate([share, flip(share, "samp", xor_samp(1))], axis=0)
     swap = xor_pix(1)
     over_a = flip(share, "pix", first)

time: 234 us -> 234 us (level)
    pallas_call x16 -> x15, Pallas kernels: 64.1 us -> 63.2 us  [kernel_call(): return lambda *args: call(*map(place, args, in_specs))]
    ppermute x24 -> x23, waiting for transfers between devices: 107 us -> 107 us  [flip(): return lax.ppermute(x, axes, perm)]
    ppermute x24 -> x23, starting transfers between devices: 23.7 us -> 23.7 us  [flip(): return lax.ppermute(x, axes, perm)]
  transfers between devices with their start and end apart: 25 -> 24, of which waited for: 19 -> 18; matrix products, arithmetic and copies ran while one was open for 0% -> 0% of each run, Pallas kernels for 8% -> 7%
where the time goes in v8:
time: 234 us
  waiting for transfers between devices  133 us (57%)
  Pallas kernels  63.2 us (27%)
  starting transfers between devices  31 us (13%)
  local copies, waits for them, and re-layouts  4.9 us (2%)
    ppermute x23, waiting for transfers between devices, flip(): return lax.ppermute(x, axes, perm)  107 us
    pallas_call x15, Pallas kernels, kernel_call(): return lambda *args: call(*map(place, args, in_specs))  63.2 us
    all_to_all x1, waiting for transfers between devices, sample_space(): lax.all_to_all(stamps, ('pix', 'samp'), split_axis=1, concat_axis=0, tile...  26 us
    ppermute x23, starting transfers between devices, flip(): return lax.ppermute(x, axes, perm)  23.7 us
    all_to_all x1, starting transfers between devices, sample_space(): lax.all_to_all(stamps, ('pix', 'samp'), split_axis=1, concat_axis=0, tile...  7.33 us
  transfers between devices with their start and end apart: 24, of which 18 were waited for; matrix products, arithmetic and copies ran while one was open for 0% of the time, Pallas kernels for 7%

profile of v8, /device:TPU:0, one launch (start us, length us, event | category | flops | bytes accessed | tf_op | source)
XLA Modules:
  0.0 233.8 jit_solution(1779562456765385577)
XLA Ops:
  0.0 3.2 %copy.14 = bf16[8,32,8,512]{3,2,0,1:T(8,128)(2,1)} copy(bf16[8,32,8,512]{3,2,1,0:T(8,128)(2,1)} %bitcast.24) | data formatting | bytes 4194304 | tf_op jit(solution)/shard_map/all_to_all | solution.py:364
  3.2 7.3 %all-to-all-start = ((bf16[64,32,512]{2,0,1:T(8,128)(2,1)}), bf16[64,32,512]{2,0,1:T(8,128)(2,1)S(1)}, u32[]{:S(2)}, u32[]{:S(2)}) async-start(bf16[64,32,512]{2,0,1:T(8,128)(2,1)} %bitcast.25), calls=%async_computation | async-start | bytes 4194304 | tf_op jit(solution)/shard_map/all_to_all | solution.py:364
  10.6 1.8 collective-permute-start.1
  12.4 17.3 %collective-permute-done.1 = bf16[32,2048]{1,0:T(8,128)(2,1)S(1)} collective-permute-done((bf16[32,2048]{1,0:T(8,128)(2,1)S(1)}, bf16[32,2048]{1,0:T(8,128)(2,1)S(1)}, u32[]{:S(2)}, u32[]{:S(2)}) %collective-permute-start.1) | collective-permute-done | bytes 131104 | tf_op jit(solution)/shard_map/ppermute | solution.py:315
  29.8 1.5 collective-permute-start.2
  31.3 26.0 %all-to-all-done = bf16[64,32,512]{2,0,1:T(8,128)(2,1)S(1)} async-done(((bf16[64,32,512]{2,0,1:T(8,128)(2,1)}), bf16[64,32,512]{2,0,1:T(8,128)(2,1)S(1)}, u32[]{:S(2)}, u32[]{:S(2)}) %all-to-all-start) | async-done | bytes 2097184 | tf_op jit(solution)/shard_map/all_to_all | solution.py:364
  57.3 1.8 collective-permute-start
  59.4 4.3 %collective-permute-done.3.far_ref = bf16[32,8192]{1,0:T(8,128)(2,1)S(1)} collective-permute-done((bf16[32,8192]{1,0:T(8,128)(2,1)S(1)}, bf16[32,8192]{1,0:T(8,128)(2,1)S(1)}, u32[]{:S(2)}, u32[]{:S(2)}) %collective-permute-start.3) | collective-permute-done | bytes 524320 | tf_op jit(solution)/shard_map/ppermute | solution.py:315
  63.7 1.6 copy-done
  65.3 1.2 shard_map.28
  66.9 0.8 collective-permute-done.4
  67.8 1.5 collective-permute-start.5
  69.3 2.1 collective-permute-done.5
  71.4 1.5 collective-permute-start.6
  72.9 2.2 collective-permute-done.6
  75.2 2.3 %collective-permute-start.7 = (bf16[32,512]{1,0:T(8,128)(2,1)S(1)}, bf16[32,512]{1,0:T(8,128)(2,1)S(1)}, u32[]{:S(2)}, u32[]{:S(2)}) collective-permute-start(bf16[32,512]{1,0:T(8,128)(2,1)S(1)} %maximum_select_fusion.2), channel_id=1, source_target_pairs={{0,8},{8,0},{16,24},{24,16},{1,9},{9,1},{17,25},{25,17},{2,10},{10... | collective-permute-start | bytes 98312 | tf_op jit(solution)/shard_map/ppermute | solution.py:315
  77.5 1.9 collective-permute-done.7
  79.5 1.2 collective-permute-start.8
  80.7 4.0 %collective-permute-done.8 = bf16[32,1024]{1,0:T(8,128)(2,1)S(1)} collective-permute-done((bf16[32,1024]{1,0:T(8,128)(2,1)S(1)}, bf16[32,1024]{1,0:T(8,128)(2,1)S(1)}, u32[]{:S(2)}, u32[]{:S(2)}) %collective-permute-start.8) | collective-permute-done | bytes 65568 | tf_op jit(solution)/shard_map/ppermute | solution.py:315
  84.7 1.4 shard_map.29
  86.1 5.0 %shard_map.30 = (bf16[384,2048]{1,0:T(8,128)(2,1)S(1)}, bf16[384,2048]{1,0:T(8,128)(2,1)S(1)}) custom-call(bf16[2048,512]{1,0:T(8,128)(2,1)S(1)} %bitcast.18, bf16[2048,512]{1,0:T(8,128)(2,1)} %collective-permute-done.other_ref, f32[32,2048]{1,0:T(8,128)S(1)} %get-tuple-element.21.q_ref.refs_2_.refs_3_), custom_call_target="tpu_custom_call" | custom-call | tf_op jit(solution)/shard_map/pallas_call | solution.py:75
  91.1 2.9 %shard_map.34 = bf16[256,1280]{1,0:T(8,128)(2,1)S(1)} custom-call(s32[32]{0:T(128)S(1)} %concatenate.53.index_ref.at_ref, bf16[2048,512]{1,0:T(8,128)(2,1)S(1)} %bitcast.19, bf16[2048,512]{1,0:T(8,128)(2,1)} %collective-permute-done.other_ref, bf16[384,2048]{1,0:T(8,128)(2,1)S(1)} %get-tuple-element.22.left, bf16[384,2048]{1,0:T(8,128)(2,1)S(1)} %get-tuple-element.23.right), custom_call_target="tpu_custom_call" | custom-call | tf_op jit(solution)/shard_map/pallas_call | solution.py:75
  94.0 2.0 collective-permute-start.10
  96.0 2.9 %shard_map.32 = bf16[256,1280]{1,0:T(8,128)(2,1)S(1)} custom-call(s32[32]{0:T(128)S(1)} %concatenate.53.index_ref.at_ref, bf16[2048,512]{1,0:T(8,128)(2,1)S(1)} %bitcast.20, bf16[2048,512]{1,0:T(8,128)(2,1)} %collective-permute-done.other_ref, bf16[384,2048]{1,0:T(8,128)(2,1)S(1)} %get-tuple-element.22.left, bf16[384,2048]{1,0:T(8,128)(2,1)S(1)} %get-tuple-element.23.right), custom_call_target="tpu_custom_call" | custom-call | tf_op jit(solution)/shard_map/pallas_call | solution.py:75
  99.0 2.9 %shard_map.33.refs_0_ = bf16[256,1280]{1,0:T(8,128)(2,1)S(1)} custom-call(s32[32]{0:T(128)S(1)} %concatenate.53.index_ref.at_ref, bf16[2048,512]{1,0:T(8,128)(2,1)S(1)} %bitcast.21, bf16[2048,512]{1,0:T(8,128)(2,1)} %collective-permute-done.other_ref, bf16[384,2048]{1,0:T(8,128)(2,1)S(1)} %get-tuple-element.22.left, ...), custom_call_target="tpu_custom_call" | custom-call | tf_op jit(solution)/shard_map/pallas_call | solution.py:75
  101.9 4.0 %collective-permute-done.10.refs_1_ = bf16[256,1280]{1,0:T(8,128)(2,1)S(1)} collective-permute-done((bf16[256,1280]{1,0:T(8,128)(2,1)S(1)}, bf16[256,1280]{1,0:T(8,128)(2,1)S(1)}, u32[]{:S(2)}, u32[]{:S(2)}) %collective-permute-start.10) | collective-permute-done | bytes 655392 | tf_op jit(solution)/shard_map/ppermute | solution.py:315
  105.8 1.0 shard_map.35
  106.9 0.8 collective-permute-start.11
  107.6 2.8 %shard_map.31.refs_0_ = bf16[256,1280]{1,0:T(8,128)(2,1)S(1)} custom-call(s32[32]{0:T(128)S(1)} %concatenate.53.index_ref.at_ref, bf16[2048,512]{1,0:T(8,128)(2,1)S(1)} %bitcast.22, bf16[2048,512]{1,0:T(8,128)(2,1)} %collective-permute-done.other_ref, bf16[384,2048]{1,0:T(8,128)(2,1)S(1)} %get-tuple-element.22.left, ...), custom_call_target="tpu_custom_call" | custom-call | tf_op jit(solution)/shard_map/pallas_call | solution.py:75
  110.5 8.2 %collective-permute-done.9.refs_1_ = bf16[256,1280]{1,0:T(8,128)(2,1)S(1)} collective-permute-done((bf16[256,1280]{1,0:T(8,128)(2,1)S(1)}, bf16[256,1280]{1,0:T(8,128)(2,1)S(1)}, u32[]{:S(2)}, u32[]{:S(2)}) %collective-permute-start.9) | collective-permute-done | bytes 655392 | tf_op jit(solution)/shard_map/ppermute | solution.py:315
  118.7 1.1 shard_map.36
  119.8 2.1 collective-permute-start.12
  121.9 6.5 %collective-permute-done.12.refs_1_ = bf16[128,1280]{1,0:T(8,128)(2,1)S(1)} collective-permute-done((bf16[128,1280]{1,0:T(8,128)(2,1)S(1)}, bf16[128,1280]{1,0:T(8,128)(2,1)S(1)}, u32[]{:S(2)}, u32[]{:S(2)}) %collective-permute-start.12) | collective-permute-done | bytes 327712 | tf_op jit(solution)/shard_map/ppermute | solution.py:315
  128.4 0.8 shard_map.37.refs_0_
  129.2 1.1 collective-permute-start.13
  130.2 14.5 %collective-permute-done.13.refs_1_ = bf16[128,1280]{1,0:T(8,128)(2,1)S(1)} collective-permute-done((bf16[128,1280]{1,0:T(8,128)(2,1)S(1)}, bf16[128,1280]{1,0:T(8,128)(2,1)S(1)}, u32[]{:S(2)}, u32[]{:S(2)}) %collective-permute-start.13) | collective-permute-done | bytes 327712 | tf_op jit(solution)/shard_map/ppermute | solution.py:315
  145.6 9.0 %collective-permute-done.14 = bf16[128,1280]{1,0:T(8,128)(2,1)S(1)} collective-permute-done((bf16[128,1280]{1,0:T(8,128)(2,1)S(1)}, bf16[128,1280]{1,0:T(8,128)(2,1)S(1)}, u32[]{:S(2)}, u32[]{:S(2)}) %collective-permute-start.14) | collective-permute-done | bytes 327712 | tf_op jit(solution)/shard_map/ppermute | solution.py:315
  154.6 1.9 collective-permute-start.15
  156.6 8.7 %collective-permute-done.15 = bf16[256,1280]{1,0:T(8,128)(2,1)S(1)} collective-permute-done((bf16[256,1280]{1,0:T(8,128)(2,1)S(1)}, bf16[256,1280]{1,0:T(8,128)(2,1)S(1)}, u32[]{:S(2)}, u32[]{:S(2)}) %collective-permute-start.15) | collective-permute-done | bytes 655392 | tf_op jit(solution)/shard_map/ppermute | solution.py:315
  165.4 2.1 collective-permute-start.18
  167.6 8.5 %collective-permute-done.18.refs_0_ = bf16[256,1280]{1,0:T(8,128)(2,1)S(1)} collective-permute-done((bf16[256,1280]{1,0:T(8,128)(2,1)S(1)}, bf16[256,1280]{1,0:T(8,128)(2,1)S(1)}, u32[]{:S(2)}, u32[]{:S(2)}) %collective-permute-start.18) | collective-permute-done | bytes 655392 | tf_op jit(solution)/shard_map/ppermute | solution.py:315
  176.1 7.0 %collective-permute-done.16.refs_2_ = bf16[256,1280]{1,0:T(8,128)(2,1)S(1)} collective-permute-done((bf16[256,1280]{1,0:T(8,128)(2,1)S(1)}, bf16[256,1280]{1,0:T(8,128)(2,1)S(1)}, u32[]{:S(2)}, u32[]{:S(2)}) %collective-permute-start.16) | collective-permute-done | bytes 655392 | tf_op jit(solution)/shard_map/ppermute | solution.py:315
  183.1 2.8 %shard_map.39 = (bf16[2048,2048]{1,0:T(8,128)(2,1)S(1)}, bf16[2048,256]{1,0:T(8,128)(2,1)S(1)}, bf16[384,2048]{1,0:T(8,128)(2,1)S(1)}, f32[8,2048]{1,0:T(8,128)S(1)}) custom-call(s32[32]{0:T(128)S(1)} %concatenate.53.index_ref.at_ref, bf16[512,1280]{1,0:T(8,128)(2,1)S(1)} %pad_maximum_fusion.refs_0_, bf16[512,1280]{1,0:T(8,128)(2,1)S(1)} %collective-permute-done.20.refs_1_, ...), custom_call_target="tpu_custom_call" | custom-call | tf_op jit(solution)/shard_map/pallas_call | solution.py:75
  186.0 2.2 shard_map.40
  188.2 34.8 %shard_map.41 = (bf16[32,2048]{1,0:T(8,128)(2,1)S(1)}, f32[32,128]{1,0:T(8,128)S(1)}, bf16[2048,2048]{1,0:T(8,128)(2,1)S(1)}, bf16[2048,256]{1,0:T(8,128)(2,1)S(...) custom-call(s32[32]{0:T(128)S(1)} %concatenate.53.index_ref.at_ref, ...), custom_call_target="tpu_custom_call", output_to_operand_aliasing={{2}: (4, {}), {3}: (5, {}), {4}: (6, {}), {5}: (7, {})} | custom-call | tf_op jit(solution)/shard_map/pallas_call | solution.py:75
  223.6 1.1 collective-permute-start.21
  224.8 4.0 %collective-permute-done.21 = bf16[32,512]{1,0:T(8,128)(2,1)S(1)} collective-permute-done((bf16[32,512]{1,0:T(8,128)(2,1)S(1)}, bf16[32,512]{1,0:T(8,128)(2,1)S(1)}, u32[]{:S(2)}, u32[]{:S(2)}) %collective-permute-start.21) | collective-permute-done | bytes 32800 | tf_op jit(solution)/shard_map/ppermute | solution.py:315
  228.8 4.3 %collective-permute-done.22 = bf16[32,1024]{1,0:T(8,128)(2,1)S(1)} collective-permute-done((bf16[32,1024]{1,0:T(8,128)(2,1)S(1)}, bf16[32,1024]{1,0:T(8,128)(2,1)S(1)}, u32[]{:S(2)}, u32[]{:S(2)}) %collective-permute-start.22) | collective-permute-done | bytes 65568 | tf_op jit(solution)/shard_map/ppermute | solution.py:315
  (37 shorter events, 3.4 us)
Async XLA Ops:
  3.2 7.3 %copy-start.1 = (f32[2048,32]{0,1:T(8,128)S(1)}, f32[2048,32]{0,1:T(8,128)}, u32[]{:S(2)}) copy-start(f32[2048,32]{0,1:T(8,128)} %param.3) | copy-start | bytes 786436
  3.2 54.1 %all-to-all-start = ((bf16[64,32,512]{2,0,1:T(8,128)(2,1)}), bf16[64,32,512]{2,0,1:T(8,128)(2,1)S(1)}, u32[]{:S(2)}, u32[]{:S(2)}) async-start(bf16[64,32,512]{2,0,1:T(8,128)(2,1)} %bitcast.25), calls=%async_computation | async-start | bytes 4194304 | tf_op jit(solution)/shard_map/all_to_all | solution.py:364
  10.6 19.1 %collective-permute-start.1 = (bf16[32,2048]{1,0:T(8,128)(2,1)S(1)}, bf16[32,2048]{1,0:T(8,128)(2,1)S(1)}, u32[]{:S(2)}, u32[]{:S(2)}) collective-permute-start(bf16[32,2048]{1,0:T(8,128)(2,1)S(1)} %convert_bitcast_fusion.1), channel_id=1, source_target_pairs={{0,2},{1,3},{2,0},{3,1},{4,6},{5,7},{6,4},{7,5},{8,10},{9,11},{10,... | collective-permute-start | bytes 393224 | tf_op jit(solution)/shard_map/ppermute | solution.py:315
  29.8 29.4 %collective-permute-start.2 = (bf16[32,4096]{1,0:T(8,128)(2,1)S(1)}, bf16[32,4096]{1,0:T(8,128)(2,1)S(1)}, u32[]{:S(2)}, u32[]{:S(2)}) collective-permute-start(bf16[32,4096]{1,0:T(8,128)(2,1)S(1)} %pad_maximum_fusion.3), channel_id=1, source_target_pairs={{0,4},{1,5},{2,6},{3,7},{4,0},{5,1},{6,2},{7,3},{8,12},{9,13},{10,... | collective-permute-start | bytes 786440 | tf_op jit(solution)/shard_map/ppermute | solution.py:315
  57.3 28.8 %collective-permute-start = (bf16[2048,512]{1,0:T(8,128)(2,1)S(1)}, bf16[2048,512]{1,0:T(8,128)(2,1)}, u32[]{:S(2)}, u32[]{:S(2)}) collective-permute-start(bf16[2048,512]{1,0:T(8,128)(2,1)S(1)} %bitcast.17), channel_id=1, source_target_pairs={{0,1},{1,0},{2,3},{3,2},{4,5},{5,4},{6,7},{7,6},{8,9},{9,8},{10,11... | collective-permute-start | bytes 6291464 | tf_op jit(solution)/shard_map/ppermute | solution.py:315
  59.2 4.5 %collective-permute-start.3 = (bf16[32,8192]{1,0:T(8,128)(2,1)S(1)}, bf16[32,8192]{1,0:T(8,128)(2,1)S(1)}, u32[]{:S(2)}, u32[]{:S(2)}) collective-permute-start(bf16[32,8192]{1,0:T(8,128)(2,1)S(1)} %pad_maximum_fusion.2.near_ref), channel_id=1, source_target_pairs={{0,1},{1,0},{2,3},{3,2},{4,5},{5,4},{6,7},{7,6},{8,9},{9,8},{10,11... | collective-permute-start | bytes 1572872 | tf_op jit(solution)/shard_map/ppermute | solution.py:315
  63.7 1.6 copy-start
  66.5 1.2 collective-permute-start.4
  67.8 3.7 %collective-permute-start.5 = (bf16[32,128]{1,0:T(8,128)(2,1)S(1)}, bf16[32,128]{1,0:T(8,128)(2,1)S(1)}, u32[]{:S(2)}, u32[]{:S(2)}) collective-permute-start(bf16[32,128]{1,0:T(8,128)(2,1)S(1)} %maximum_select_fusion.4), channel_id=1, source_target_pairs={{0,2},{1,3},{2,0},{3,1},{4,6},{5,7},{6,4},{7,5},{8,10},{9,11},{10,... | collective-permute-start | bytes 24584 | tf_op jit(solution)/shard_map/ppermute | solution.py:315
  71.4 3.7 %collective-permute-start.6 = (bf16[32,256]{1,0:T(8,128)(2,1)S(1)}, bf16[32,256]{1,0:T(8,128)(2,1)S(1)}, u32[]{:S(2)}, u32[]{:S(2)}) collective-permute-start(bf16[32,256]{1,0:T(8,128)(2,1)S(1)} %maximum_select_fusion.3), channel_id=1, source_target_pairs={{0,4},{1,5},{2,6},{3,7},{4,0},{5,1},{6,2},{7,3},{8,12},{9,13},{10,... | collective-permute-start | bytes 49160 | tf_op jit(solution)/shard_map/ppermute | solution.py:315
  75.2 4.2 %collective-permute-start.7 = (bf16[32,512]{1,0:T(8,128)(2,1)S(1)}, bf16[32,512]{1,0:T(8,128)(2,1)S(1)}, u32[]{:S(2)}, u32[]{:S(2)}) collective-permute-start(bf16[32,512]{1,0:T(8,128)(2,1)S(1)} %maximum_select_fusion.2), channel_id=1, source_target_pairs={{0,8},{8,0},{16,24},{24,16},{1,9},{9,1},{17,25},{25,17},{2,10},{10... | collective-permute-start | bytes 98312 | tf_op jit(solution)/shard_map/ppermute | solution.py:315
  79.5 5.2 %collective-permute-start.8 = (bf16[32,1024]{1,0:T(8,128)(2,1)S(1)}, bf16[32,1024]{1,0:T(8,128)(2,1)S(1)}, u32[]{:S(2)}, u32[]{:S(2)}) collective-permute-start(bf16[32,1024]{1,0:T(8,128)(2,1)S(1)} %maximum_select_fusion.1), channel_id=1, source_target_pairs={{0,16},{8,24},{16,0},{24,8},{1,17},{9,25},{17,1},{25,9},{2,18},{10... | collective-permute-start | bytes 196616 | tf_op jit(solution)/shard_map/ppermute | solution.py:315
  94.0 11.9 %collective-permute-start.10 = (bf16[256,1280]{1,0:T(8,128)(2,1)S(1)}, bf16[256,1280]{1,0:T(8,128)(2,1)S(1)}, u32[]{:S(2)}, u32[]{:S(2)}) collective-permute-start(bf16[256,1280]{1,0:T(8,128)(2,1)S(1)} %shard_map.34), channel_id=1, source_target_pairs={{0,2},{1,5},{2,0},{3,7},{4,6},{5,1},{6,4},{7,3},{8,10},{9,13},{10,... | collective-permute-start | bytes 1966088 | tf_op jit(solution)/shard_map/ppermute | solution.py:315
  98.9 19.8 %collective-permute-start.9 = (bf16[256,1280]{1,0:T(8,128)(2,1)S(1)}, bf16[256,1280]{1,0:T(8,128)(2,1)S(1)}, u32[]{:S(2)}, u32[]{:S(2)}) collective-permute-start(bf16[256,1280]{1,0:T(8,128)(2,1)S(1)} %shard_map.32), channel_id=1, source_target_pairs={{0,2},{1,5},{2,0},{3,7},{4,6},{5,1},{6,4},{7,3},{8,10},{9,13},{10,... | collective-permute-start | bytes 1966088 | tf_op jit(solution)/shard_map/ppermute | solution.py:315
  106.9 11.8 %collective-permute-start.11 = (bf16[256,1280]{1,0:T(8,128)(2,1)S(1)}, bf16[256,1280]{1,0:T(8,128)(2,1)S(1)}, u32[]{:S(2)}, u32[]{:S(2)}) collective-permute-start(bf16[256,1280]{1,0:T(8,128)(2,1)S(1)} %shard_map.35), channel_id=1, source_target_pairs={{0,4},{1,3},{2,6},{3,1},{4,0},{5,7},{6,2},{7,5},{8,12},{9,11},{10,... | collective-permute-start | bytes 1966088 | tf_op jit(solution)/shard_map/ppermute | solution.py:315
  119.8 8.6 %collective-permute-start.12 = (bf16[128,1280]{1,0:T(8,128)(2,1)S(1)}, bf16[128,1280]{1,0:T(8,128)(2,1)S(1)}, u32[]{:S(2)}, u32[]{:S(2)}) collective-permute-start(bf16[128,1280]{1,0:T(8,128)(2,1)S(1)} %get-tuple-element.25), channel_id=1, source_target_pairs={{0,8},{8,0},{16,24},{24,16},{1,9},{9,1},{17,25},{25,17},{2,10},{10... | collective-permute-start | bytes 983048 | tf_op jit(solution)/shard_map/ppermute | solution.py:315
  129.2 15.6 %collective-permute-start.13 = (bf16[128,1280]{1,0:T(8,128)(2,1)S(1)}, bf16[128,1280]{1,0:T(8,128)(2,1)S(1)}, u32[]{:S(2)}, u32[]{:S(2)}) collective-permute-start(bf16[128,1280]{1,0:T(8,128)(2,1)S(1)} %shard_map.37.refs_0_), channel_id=1, source_target_pairs={{0,16},{8,24},{16,0},{24,8},{1,17},{9,25},{17,1},{25,9},{2,18},{10... | collective-permute-start | bytes 983048 | tf_op jit(solution)/shard_map/ppermute | solution.py:315
  145.5 9.0 %collective-permute-start.14 = (bf16[128,1280]{1,0:T(8,128)(2,1)S(1)}, bf16[128,1280]{1,0:T(8,128)(2,1)S(1)}, u32[]{:S(2)}, u32[]{:S(2)}) collective-permute-start(bf16[128,1280]{1,0:T(8,128)(2,1)S(1)} %shard_map.38), channel_id=1, source_target_pairs={{0,8},{8,0},{16,24},{24,16},{1,9},{9,1},{17,25},{25,17},{2,10},{10... | collective-permute-start | bytes 983048 | tf_op jit(solution)/shard_map/ppermute | solution.py:315
  154.6 10.7 %collective-permute-start.15 = (bf16[256,1280]{1,0:T(8,128)(2,1)S(1)}, bf16[256,1280]{1,0:T(8,128)(2,1)S(1)}, u32[]{:S(2)}, u32[]{:S(2)}) collective-permute-start(bf16[256,1280]{1,0:T(8,128)(2,1)S(1)} %pad_maximum_fusion.1), channel_id=1, source_target_pairs={{0,4},{1,3},{2,6},{3,1},{4,0},{5,7},{6,2},{7,5},{8,12},{9,11},{10,... | collective-permute-start | bytes 1966088 | tf_op jit(solution)/shard_map/ppermute | solution.py:315
  165.4 17.8 %collective-permute-start.20 = (bf16[512,1280]{1,0:T(8,128)(2,1)S(1)}, bf16[512,1280]{1,0:T(8,128)(2,1)S(1)}, u32[]{:S(2)}, u32[]{:S(2)}) collective-permute-start(bf16[512,1280]{1,0:T(8,128)(2,1)S(1)} %pad_maximum_fusion.refs_0_), channel_id=1, source_target_pairs={{0,1},{1,0},{2,3},{3,2},{4,5},{5,4},{6,7},{7,6},{8,9},{9,8},{10,11... | collective-permute-start | bytes 3932168 | tf_op jit(solution)/shard_map/ppermute | solution.py:315
  165.4 10.7 %collective-permute-start.18 = (bf16[256,1280]{1,0:T(8,128)(2,1)S(1)}, bf16[256,1280]{1,0:T(8,128)(2,1)S(1)}, u32[]{:S(2)}, u32[]{:S(2)}) collective-permute-start(bf16[256,1280]{1,0:T(8,128)(2,1)S(1)} %pad_maximum_fusion.1), channel_id=1, source_target_pairs={{0,2},{1,5},{2,0},{3,7},{4,6},{5,1},{6,4},{7,3},{8,10},{9,13},{10,... | collective-permute-start | bytes 1966088 | tf_op jit(solution)/shard_map/ppermute | solution.py:315
  167.5 15.6 %collective-permute-start.16 = (bf16[256,1280]{1,0:T(8,128)(2,1)S(1)}, bf16[256,1280]{1,0:T(8,128)(2,1)S(1)}, u32[]{:S(2)}, u32[]{:S(2)}) collective-permute-start(bf16[256,1280]{1,0:T(8,128)(2,1)S(1)} %collective-permute-done.15), channel_id=1, source_target_pairs={{0,2},{1,5},{2,0},{3,7},{4,6},{5,1},{6,4},{7,3},{8,10},{9,13},{10,... | collective-permute-start | bytes 1966088 | tf_op jit(solution)/shard_map/ppermute | solution.py:315
  176.1 9.8 %collective-permute-start.19 = (bf16[256,1280]{1,0:T(8,128)(2,1)S(1)}, bf16[256,1280]{1,0:T(8,128)(2,1)S(1)}, u32[]{:S(2)}, u32[]{:S(2)}) collective-permute-start(bf16[256,1280]{1,0:T(8,128)(2,1)S(1)} %collective-permute-done.18.refs_0_), channel_id=1, source_target_pairs={{0,1},{1,0},{2,3},{3,2},{4,5},{5,4},{6,7},{7,6},{8,9},{9,8},{10,11... | collective-permute-start | bytes 1966088 | tf_op jit(solution)/shard_map/ppermute | solution.py:315
  183.1 5.1 %collective-permute-start.17 = (bf16[256,1280]{1,0:T(8,128)(2,1)S(1)}, bf16[256,1280]{1,0:T(8,128)(2,1)S(1)}, u32[]{:S(2)}, u32[]{:S(2)}) collective-permute-start(bf16[256,1280]{1,0:T(8,128)(2,1)S(1)} %collective-permute-done.16.refs_2_), channel_id=1, source_target_pairs={{0,1},{1,0},{2,3},{3,2},{4,5},{5,4},{6,7},{7,6},{8,9},{9,8},{10,11... | collective-permute-start | bytes 1966088 | tf_op jit(solution)/shard_map/ppermute | solution.py:315
  223.6 5.1 %collective-permute-start.21 = (bf16[32,512]{1,0:T(8,128)(2,1)S(1)}, bf16[32,512]{1,0:T(8,128)(2,1)S(1)}, u32[]{:S(2)}, u32[]{:S(2)}) collective-permute-start(bf16[32,512]{1,0:T(8,128)(2,1)S(1)} %shard_map.42), channel_id=1, source_target_pairs={{0,16},{8,24},{16,0},{24,8},{1,17},{9,25},{17,1},{25,9},{2,18},{10... | collective-permute-start | bytes 98312 | tf_op jit(solution)/shard_map/ppermute | solution.py:315
  228.8 4.3 %collective-permute-start.22 = (bf16[32,1024]{1,0:T(8,128)(2,1)S(1)}, bf16[32,1024]{1,0:T(8,128)(2,1)S(1)}, u32[]{:S(2)}, u32[]{:S(2)}) collective-permute-start(bf16[32,1024]{1,0:T(8,128)(2,1)S(1)} %pad_maximum_fusion.4), channel_id=1, source_target_pairs={{0,8},{8,0},{16,24},{24,16},{1,9},{9,1},{17,25},{25,17},{2,10},{10... | collective-permute-start | bytes 196616 | tf_op jit(solution)/shard_map/ppermute | solution.py:315

commit v9 on v8

--- a/solution.py
+++ b/solution.py
@@ -12,9 +12,11 @@
 ITERS = 10
 LANES = 128
 PANEL = 16
-GROUP = 40
+RANK = 16
+GROUP = 20
+HALF = 64
 STEP = 2
-QUARTERS, HALVES, PLACE, BLOCKS = 0, 4, 8, 16
+QUARTERS, HALVES, CORE, PLACE, BLOCKS = 0, 4, 6, 8, 16
 SAMPLE_SPACE_LIMIT = 4096
 F32 = jnp.float32
 BF16 = jnp.bfloat16
@@ -153,7 +155,8 @@
         p_ref[:, to * LANES : (to + 1) * LANES] = block.astype(BF16)
     p0 = p_ref[...]
     parts = (p0, jnp.zeros_like(p0), jnp.zeros_like(p0))
-    q_ref[...] = apply_lower(inverse_lower(gram_of(parts, p0)), parts)
+    q = apply_lower(inverse_lower(gram_of(parts, p0)), parts)
+    q_ref[...] = jnp.where(lax.broadcasted_iota(jnp.int32, q.shape, 0) < RANK, q, 0.0)
 
 
 def factors_kernel(own_ref, other_ref, q_ref, left, right):
@@ -173,46 +176,53 @@
     m = jnp.where(lax.broadcasted_iota(jnp.int32, m.shape, 1) < k, m, 0.0)
     m = pltpu.roll(m, k, 1) + pltpu.roll(m, 2 * k, 1) + pltpu.roll(m, 3 * k, 1)
     w1, w2, w3 = split3(w - 0.5 * apply_lower(m, (q1, q2, q3)))
+    q1, q2, q3, w1, w2, w3 = [part[:RANK] for part in (q1, q2, q3, w1, w2, w3)]
     left[...] = jnp.concatenate([q1, w1, q1, w1, q1, w1, q2, w2, q2, w2, q3, w3], axis=0)
     right[...] = jnp.concatenate([w1, q1, w2, q2, w3, q3, w1, q1, w2, q2, w1, q1], axis=0)
 
 
-def form_rows(k, first, own_ref, other_ref, left, right, out_ref, window, right_win):
+def form_rows(first, core, own_ref, other_ref, left, right, out_ref, window, right_win):
     n, px = own_ref.shape
-    rows, width = out_ref.shape
-    width -= LANES
-    bs = width - n // 2
+    rows = out_ref.shape[0]
+    width = n // 2
+    bs = out_ref.shape[1] - width
     nb = n // bs
     for b in range(window.shape[0] // bs):
         at = pl.multiple_of(lax.rem(first + b, nb) * bs, bs)
         window[b * bs : (b + 1) * bs, :px] = own_ref[pl.ds(at, bs), :]
         window[b * bs : (b + 1) * bs, px:] = other_ref[pl.ds(at, bs), :]
         right_win[:, b * bs : (b + 1) * bs] = right[:, pl.ds(at, bs)]
-    eye = lax.broadcasted_iota(jnp.int32, (bs, bs), 0) == lax.broadcasted_iota(jnp.int32, (bs, bs), 1)
+    lane = lax.broadcasted_iota(jnp.int32, (bs, bs), 1)
+    eye = lax.broadcasted_iota(jnp.int32, (bs, bs), 0) == lane
     step = STEP * bs
     for i in range(rows // bs):
         if i % STEP == 0:
             at = pl.multiple_of((first + i) * bs, bs)
-            lo, end = i * bs, i * bs + step - bs + width
+            lo, end = i * bs, i * bs + step + width
             wide = dot(window[lo : lo + step, :], window[lo:end, :], NT)
             wide -= dot(left[:, pl.ds(at, step)], right_win[:, lo:end], TN)
         off = i % STEP * bs
         to = i * bs
-        s = wide[off : off + bs, off : off + width]
+        s = wide[off : off + bs, off : off + width + bs]
         corner = s[:, :bs]
         diagonal = jnp.sum(jnp.where(eye, corner, 0.0), axis=0, keepdims=True)
         out_ref[to : to + bs, :bs] = jnp.where(eye, 0.0, corner).astype(BF16)
-        out_ref[to : to + bs, bs:width] = s[:, bs:].astype(BF16)
-        side = []
+        out_ref[to : to + bs, bs:width] = s[:, bs:width].astype(BF16)
+        last = s[:, width:]
+        low = last[HALF:]
+        last = jnp.where(core == 0, last, jnp.concatenate([low, pltpu.roll(low, HALF, 1)], axis=0))
+        side = [jnp.zeros((HALF, bs), F32)]
         for g, d in enumerate(split3(diagonal)):
-            side.append(right_win[2 * g * k : (2 * g + 1) * k, to : to + bs].astype(F32))
-            side.append(jnp.broadcast_to(d.astype(F32), (GROUP - k, bs)))
-        side.append(jnp.zeros((LANES - 3 * GROUP, bs), F32))
-        out_ref[to : to + bs, width:] = jnp.concatenate(side, axis=0).T.astype(BF16)
-
-
-def form_kernel(k, slot, at_ref, own_ref, other_ref, left, right, out_ref, *wins):
-    form_rows(k, at_ref[slot], own_ref, other_ref, left, right, out_ref, *wins)
+            w = right_win[2 * g * RANK : (2 * g + 1) * RANK, to : to + bs]
+            side.append(w.astype(F32))
+            side.append(jnp.broadcast_to(d.astype(F32), (GROUP - RANK, bs)))
+        side.append(jnp.zeros((bs - HALF - 3 * GROUP, bs), F32))
+        side = jnp.concatenate(side, axis=0).T
+        out_ref[to : to + bs, width:] = jnp.where(lane < HALF, last, side).astype(BF16)
+
+
+def form_kernel(slot, at_ref, own_ref, other_ref, left, right, out_ref, *wins):
+    form_rows(at_ref[slot], at_ref[CORE], own_ref, other_ref, left, right, out_ref, *wins)
 
 
 def add_kernel(slots, at_ref, *refs):
@@ -223,12 +233,14 @@
         at = 0 if slot is None else pl.multiple_of(at_ref[slot] * h, h)
         parts = [ref[pl.ds(at, h), :].astype(F32) for ref in shares]
         o_ref[:, :width] = sum(part[:, :width] for part in parts).astype(BF16)
-        x = sum(lane_sum3(part[:, width:], GROUP) for part in parts)
-        lane = lax.broadcasted_iota(jnp.int32, x.shape, 1)
+        last = [part[:, width:] for part in parts]
+        x = sum(lane_sum3(part, GROUP) for part in last)
+        lane = lax.broadcasted_iota(jnp.int32, x.shape, 1) - HALF
         h1, h2, h3 = [part.astype(F32) for part in split3(x)]
         packed = jnp.where(lane < 2 * GROUP, pltpu.roll(h2, GROUP, 1), pltpu.roll(h3, 2 * GROUP, 1))
         packed = jnp.where(lane < GROUP, h1, packed)
-        o_ref[:, width:] = jnp.where(lane < 3 * GROUP, packed, 0.0).astype(BF16)
+        packed = jnp.where(lane < 3 * GROUP, packed, 0.0)
+        o_ref[:, width:] = jnp.where(lane < 0, sum(last), packed).astype(BF16)
 
 
 def add_shares(index, shares, slots=()):
@@ -244,31 +256,50 @@
 
 
 def unpack(offset, index_ref, share_ref, q_ref, full, u, v, diag):
-    k, n = q_ref.shape
-    width = share_ref.shape[1] - LANES
-    bs = width - n // 2
+    n = q_ref.shape[1]
+    width = n // 2
+    bs = share_ref.shape[1] - width
     nb = n // bs
+    lane = lax.broadcasted_iota(jnp.int32, (bs, bs), 1)
 
     def one(r, _):
         i = index_ref[r + offset]
         frm = pl.multiple_of(r * bs, bs)
         to = pl.multiple_of(i * bs, bs)
-        for d in range(nb // 2 + 1):
+        for d in range(nb // 2):
             part = share_ref[pl.ds(frm, bs), d * bs : (d + 1) * bs]
             at = pl.multiple_of(lax.rem(i + d, nb) * bs, bs)
             full[pl.ds(to, bs), pl.ds(at, bs)] = part
-            if 0 < d < nb // 2:
+            if d:
                 full[pl.ds(at, bs), pl.ds(to, bs)] = part.T
-        side = share_ref[pl.ds(frm, bs), width:].astype(F32).T
-        side = side[:GROUP] + side[GROUP : 2 * GROUP] + side[2 * GROUP : 3 * GROUP]
-        w = side[:k]
-        diag[:, pl.ds(to, bs)] = side[k : k + 8]
-        q = q_ref[:, pl.ds(to, bs)]
+        at = pl.multiple_of(lax.rem(i + nb // 2, nb) * bs, bs)
+        last = share_ref[pl.ds(frm, bs), width:].astype(F32)
+
+        @pl.when(i < nb // 2)
+        def _():
+            old = full[pl.ds(to, bs), pl.ds(at, bs)].astype(F32)
+            full[pl.ds(to, bs), pl.ds(at, bs)] = jnp.where(lane < HALF, last, old).astype(BF16)
+            full[pl.ds(at, HALF), pl.ds(to, bs)] = last.T[:HALF].astype(BF16)
+
+        @pl.when(i >= nb // 2)
+        def _():
+            low = jnp.where(lane[:HALF] < HALF, last[:HALF], pltpu.roll(last[HALF:], HALF, 1))
+            full[pl.ds(pl.multiple_of(to + HALF, HALF), HALF), pl.ds(at, bs)] = low.astype(BF16)
+            old = full[pl.ds(at, bs), pl.ds(to, bs)].astype(F32)
+            new = jnp.concatenate([low, low], axis=0).T
+            full[pl.ds(at, bs), pl.ds(to, bs)] = jnp.where(lane < HALF, old, new).astype(BF16)
+
+        side = last.T[HALF:]
+        w, d = side[:RANK], side[RANK : RANK + 1]
+        for g in (1, 2):
+            w = w + pltpu.roll(side, HALF - g * GROUP, 0)[:RANK]
+            d = d + side[g * GROUP + RANK : g * GROUP + RANK + 1]
+        diag[:, pl.ds(to, bs)] = jnp.broadcast_to(d, (diag.shape[0], bs))
+        q = q_ref[:RANK, pl.ds(to, bs)]
         us = [part.astype(F32) for part in split3(jnp.concatenate([w, q], axis=0))]
+        us.append(jnp.zeros((bs - 6 * RANK, bs), F32))
+        u[pl.ds(to, bs), :] = jnp.concatenate(us, axis=0).T.astype(BF16)
         v1, v2, v3 = split3(jnp.concatenate([q, w], axis=0))
-        u[pl.ds(to, bs), :LANES] = jnp.concatenate(us[:2], axis=0).T.astype(BF16)
-        tail = jnp.concatenate([us[2], jnp.zeros((2 * k, bs), F32)], axis=0)
-        u[pl.ds(to, bs), LANES:] = tail.T.astype(BF16)
         v[:, pl.ds(to, bs)] = jnp.concatenate([v1, v2, v3, v1, v2, v1], axis=0)
         return 0
 
@@ -289,11 +320,12 @@
 
     def product(p):
         t = dot(p, u[...], NN)
-        t = t[:, :LANES] + t[:, LANES:]
-        t = t + pltpu.roll(t, 2 * k, 1)
+        t = t + pltpu.roll(t, 4 * RANK, 1)
+        t = t + pltpu.roll(t, 2 * RANK, 1)
         h1, h2, h3 = [h.astype(F32) for h in split3(t)]
-        low = lane < 2 * k
-        ts = jnp.concatenate([h1, jnp.where(low, h1, h2), jnp.where(low, h2, h3)], axis=1).astype(BF16)
+        ts = jnp.concatenate(
+            [jnp.where(lane < 6 * RANK, h1, h2), jnp.where(lane < 2 * RANK, h2, h3)[:, :HALF]], axis=1
+        ).astype(BF16)
         y = dot(p, full[...], NN) + dot(ts, v[...], NN) + p.astype(F32) * diag[0:1, :]
         return split3(y)
 
@@ -358,7 +390,7 @@
         for half in (1 - bit_a, bit_a)
         for quarter in (1 - bit_b, bit_b)
     ]
-    pairs += [1 - z0, z0, 0, 0]
+    pairs += [1 - z0, z0, core, 0]
     index = jnp.concatenate([jnp.stack([jnp.int32(i) for i in pairs]), place, order]).astype(jnp.int32)
 
     block = lax.all_to_all(stamps, ("pix", "samp"), split_axis=1, concat_axis=0, tiled=True)
@@ -387,8 +419,8 @@
     width = n // 2 + bs
     rows = n // 8
     window = rows - bs + width
-    piece = jax.ShapeDtypeStruct((rows, width + LANES), BF16)
-    stack = jax.ShapeDtypeStruct((12 * k, n), BF16)
+    piece = jax.ShapeDtypeStruct((rows, width), BF16)
+    stack = jax.ShapeDtypeStruct((12 * RANK, n), BF16)
     left, right = kernel_call(
         factors_kernel,
         (stack, stack),
@@ -399,12 +431,12 @@
 
     def form(quarter):
         return kernel_call(
-            functools.partial(form_kernel, k, QUARTERS + quarter),
+            functools.partial(form_kernel, QUARTERS + quarter),
             piece,
             in_specs=[smem()] + vmem(4),
             out_specs=vmem()[0],
             scratch_mib=12,
-            scratch_shapes=[pltpu.VMEM((window, 2 * px), BF16), pltpu.VMEM((12 * k, window), BF16)],
+            scratch_shapes=[pltpu.VMEM((window, 2 * px), BF16), pltpu.VMEM((12 * RANK, window), BF16)],
         )(index, block, other, left, right)
 
     passed = flip(form(0), "pix", first)
@@ -424,8 +456,8 @@
     far, far_a, far_ab = [flip(t, "pix", swap) for t in (near, over_a, over_ab)]
     parts = (
         jax.ShapeDtypeStruct((n, n), BF16),
-        jax.ShapeDtypeStruct((n, 8 * k), BF16),
-        jax.ShapeDtypeStruct((12 * k, n), BF16),
+        jax.ShapeDtypeStruct((n, bs), BF16),
+        jax.ShapeDtypeStruct((12 * RANK, n), BF16),
         jax.ShapeDtypeStruct((8, n), F32),
     )
     eighth = nb // 8

time: 234 us -> 228 us (0.974)
  waiting for transfers between devices: 133 us -> 127 us
    ppermute x23, waiting for transfers between devices: 107 us -> 101 us  [flip(): return lax.ppermute(x, axes, perm)]
  transfers between devices with their start and end apart: 24 -> 24, of which waited for: 18 -> 18; matrix products, arithmetic and copies ran while one was open for 0% -> 0% of each run, Pallas kernels for 7% -> 9%
where the time goes in v9:
time: 228 us
  waiting for transfers between devices  127 us (56%)
  Pallas kernels  64 us (28%)
  starting transfers between devices  30.9 us (14%)
  local copies, waits for them, and re-layouts  4.91 us (2%)
    ppermute x23, waiting for transfers between devices, flip(): return lax.ppermute(x, axes, perm)  101 us
    pallas_call x15, Pallas kernels, kernel_call(): return lambda *args: call(*map(place, args, in_specs))  64 us
    all_to_all x1, waiting for transfers between devices, sample_space(): lax.all_to_all(stamps, ('pix', 'samp'), split_axis=1, concat_axis=0, tile...  26 us
    ppermute x23, starting transfers between devices, flip(): return lax.ppermute(x, axes, perm)  23.5 us
    all_to_all x1, starting transfers between devices, sample_space(): lax.all_to_all(stamps, ('pix', 'samp'), split_axis=1, concat_axis=0, tile...  7.33 us
  transfers between devices with their start and end apart: 24, of which 18 were waited for; matrix products, arithmetic and copies ran while one was open for 0% of the time, Pallas kernels for 9%

profile of v9, /device:TPU:0, one launch (start us, length us, event | category | flops | bytes accessed | tf_op | source)
XLA Modules:
  0.0 227.9 jit_solution(6952105230300362072)
XLA Ops:
  0.0 3.2 %copy.14 = bf16[8,32,8,512]{3,2,0,1:T(8,128)(2,1)} copy(bf16[8,32,8,512]{3,2,1,0:T(8,128)(2,1)} %bitcast.25) | data formatting | bytes 4194304 | tf_op jit(solution)/shard_map/all_to_all | solution.py:396
  3.2 7.3 %all-to-all-start = ((bf16[64,32,512]{2,0,1:T(8,128)(2,1)}), bf16[64,32,512]{2,0,1:T(8,128)(2,1)S(1)}, u32[]{:S(2)}, u32[]{:S(2)}) async-start(bf16[64,32,512]{2,0,1:T(8,128)(2,1)} %bitcast.26), calls=%async_computation | async-start | bytes 4194304 | tf_op jit(solution)/shard_map/all_to_all | solution.py:396
  10.6 1.8 collective-permute-start.1
  12.4 17.3 %collective-permute-done.1 = bf16[32,2048]{1,0:T(8,128)(2,1)S(1)} collective-permute-done((bf16[32,2048]{1,0:T(8,128)(2,1)S(1)}, bf16[32,2048]{1,0:T(8,128)(2,1)S(1)}, u32[]{:S(2)}, u32[]{:S(2)}) %collective-permute-start.1) | collective-permute-done | bytes 131104 | tf_op jit(solution)/shard_map/ppermute | solution.py:347
  29.8 1.5 collective-permute-start.2
  31.3 26.0 %all-to-all-done = bf16[64,32,512]{2,0,1:T(8,128)(2,1)S(1)} async-done(((bf16[64,32,512]{2,0,1:T(8,128)(2,1)}), bf16[64,32,512]{2,0,1:T(8,128)(2,1)S(1)}, u32[]{:S(2)}, u32[]{:S(2)}) %all-to-all-start) | async-done | bytes 2097184 | tf_op jit(solution)/shard_map/all_to_all | solution.py:396
  57.3 1.8 collective-permute-start
  59.4 4.3 %collective-permute-done.3.far_ref = bf16[32,8192]{1,0:T(8,128)(2,1)S(1)} collective-permute-done((bf16[32,8192]{1,0:T(8,128)(2,1)S(1)}, bf16[32,8192]{1,0:T(8,128)(2,1)S(1)}, u32[]{:S(2)}, u32[]{:S(2)}) %collective-permute-start.3) | collective-permute-done | bytes 524320 | tf_op jit(solution)/shard_map/ppermute | solution.py:347
  63.7 1.6 copy-done
  65.3 1.2 shard_map.28
  66.9 0.8 collective-permute-done.4
  67.8 1.5 collective-permute-start.5
  69.3 2.1 collective-permute-done.5
  71.4 1.5 collective-permute-start.6
  72.9 2.2 collective-permute-done.6
  75.2 2.3 %collective-permute-start.7 = (bf16[32,512]{1,0:T(8,128)(2,1)S(1)}, bf16[32,512]{1,0:T(8,128)(2,1)S(1)}, u32[]{:S(2)}, u32[]{:S(2)}) collective-permute-start(bf16[32,512]{1,0:T(8,128)(2,1)S(1)} %maximum_select_fusion.2), channel_id=1, source_target_pairs={{0,8},{8,0},{16,24},{24,16},{1,9},{9,1},{17,25},{25,17},{2,10},{10... | collective-permute-start | bytes 98312 | tf_op jit(solution)/shard_map/ppermute | solution.py:347
  77.5 1.9 collective-permute-done.7
  79.5 1.2 collective-permute-start.8
  80.7 4.0 %collective-permute-done.8 = bf16[32,1024]{1,0:T(8,128)(2,1)S(1)} collective-permute-done((bf16[32,1024]{1,0:T(8,128)(2,1)S(1)}, bf16[32,1024]{1,0:T(8,128)(2,1)S(1)}, u32[]{:S(2)}, u32[]{:S(2)}) %collective-permute-start.8) | collective-permute-done | bytes 65568 | tf_op jit(solution)/shard_map/ppermute | solution.py:347
  84.7 1.4 shard_map.29
  86.1 4.9 %shard_map.30 = (bf16[192,2048]{1,0:T(8,128)(2,1)S(1)}, bf16[192,2048]{1,0:T(8,128)(2,1)S(1)}) custom-call(bf16[2048,512]{1,0:T(8,128)(2,1)S(1)} %bitcast.19, bf16[2048,512]{1,0:T(8,128)(2,1)} %collective-permute-done.other_ref, f32[32,2048]{1,0:T(8,128)S(1)} %get-tuple-element.21.q_ref.refs_2_.refs_3_), custom_call_target="tpu_custom_call" | custom-call | tf_op jit(solution)/shard_map/pallas_call | solution.py:77
  91.0 2.8 %shard_map.34 = bf16[256,1152]{1,0:T(8,128)(2,1)S(1)} custom-call(s32[32]{0:T(128)S(1)} %concatenate.53.index_ref.at_ref, bf16[2048,512]{1,0:T(8,128)(2,1)S(1)} %bitcast.20, bf16[2048,512]{1,0:T(8,128)(2,1)} %collective-permute-done.other_ref, bf16[192,2048]{1,0:T(8,128)(2,1)S(1)} %get-tuple-element.22.left, bf16[192,2048]{1,0:T(8,128)(2,1)S(1)} %get-tuple-element.23.right), custom_call_target="tpu_custom_call" | custom-call | tf_op jit(solution)/shard_map/pallas_call | solution.py:77
  93.8 2.0 collective-permute-start.10
  95.8 2.8 %shard_map.32 = bf16[256,1152]{1,0:T(8,128)(2,1)S(1)} custom-call(s32[32]{0:T(128)S(1)} %concatenate.53.index_ref.at_ref, bf16[2048,512]{1,0:T(8,128)(2,1)S(1)} %bitcast.21, bf16[2048,512]{1,0:T(8,128)(2,1)} %collective-permute-done.other_ref, bf16[192,2048]{1,0:T(8,128)(2,1)S(1)} %get-tuple-element.22.left, bf16[192,2048]{1,0:T(8,128)(2,1)S(1)} %get-tuple-element.23.right), custom_call_target="tpu_custom_call" | custom-call | tf_op jit(solution)/shard_map/pallas_call | solution.py:77
  98.7 2.8 %shard_map.33.refs_0_ = bf16[256,1152]{1,0:T(8,128)(2,1)S(1)} custom-call(s32[32]{0:T(128)S(1)} %concatenate.53.index_ref.at_ref, bf16[2048,512]{1,0:T(8,128)(2,1)S(1)} %bitcast.22, bf16[2048,512]{1,0:T(8,128)(2,1)} %collective-permute-done.other_ref, bf16[192,2048]{1,0:T(8,128)(2,1)S(1)} %get-tuple-element.22.left, ...), custom_call_target="tpu_custom_call" | custom-call | tf_op jit(solution)/shard_map/pallas_call | solution.py:77
  101.5 3.5 %collective-permute-done.10.refs_1_ = bf16[256,1152]{1,0:T(8,128)(2,1)S(1)} collective-permute-done((bf16[256,1152]{1,0:T(8,128)(2,1)S(1)}, bf16[256,1152]{1,0:T(8,128)(2,1)S(1)}, u32[]{:S(2)}, u32[]{:S(2)}) %collective-permute-start.10) | collective-permute-done | bytes 589856 | tf_op jit(solution)/shard_map/ppermute | solution.py:347
  105.0 1.0 shard_map.35
  106.0 0.8 collective-permute-start.11
  106.8 2.8 %shard_map.31.refs_0_ = bf16[256,1152]{1,0:T(8,128)(2,1)S(1)} custom-call(s32[32]{0:T(128)S(1)} %concatenate.53.index_ref.at_ref, bf16[2048,512]{1,0:T(8,128)(2,1)S(1)} %bitcast.23, bf16[2048,512]{1,0:T(8,128)(2,1)} %collective-permute-done.other_ref, bf16[192,2048]{1,0:T(8,128)(2,1)S(1)} %get-tuple-element.22.left, ...), custom_call_target="tpu_custom_call" | custom-call | tf_op jit(solution)/shard_map/pallas_call | solution.py:77
  109.5 6.8 %collective-permute-done.9.refs_1_ = bf16[256,1152]{1,0:T(8,128)(2,1)S(1)} collective-permute-done((bf16[256,1152]{1,0:T(8,128)(2,1)S(1)}, bf16[256,1152]{1,0:T(8,128)(2,1)S(1)}, u32[]{:S(2)}, u32[]{:S(2)}) %collective-permute-start.9) | collective-permute-done | bytes 589856 | tf_op jit(solution)/shard_map/ppermute | solution.py:347
  116.4 1.1 shard_map.36
  117.5 2.1 collective-permute-start.12
  119.6 5.8 %collective-permute-done.12.refs_1_ = bf16[128,1152]{1,0:T(8,128)(2,1)S(1)} collective-permute-done((bf16[128,1152]{1,0:T(8,128)(2,1)S(1)}, bf16[128,1152]{1,0:T(8,128)(2,1)S(1)}, u32[]{:S(2)}, u32[]{:S(2)}) %collective-permute-start.12) | collective-permute-done | bytes 294944 | tf_op jit(solution)/shard_map/ppermute | solution.py:347
  125.4 0.8 shard_map.37.refs_0_
  126.1 1.1 collective-permute-start.13
  127.2 13.2 %collective-permute-done.13.refs_1_ = bf16[128,1152]{1,0:T(8,128)(2,1)S(1)} collective-permute-done((bf16[128,1152]{1,0:T(8,128)(2,1)S(1)}, bf16[128,1152]{1,0:T(8,128)(2,1)S(1)}, u32[]{:S(2)}, u32[]{:S(2)}) %collective-permute-start.13) | collective-permute-done | bytes 294944 | tf_op jit(solution)/shard_map/ppermute | solution.py:347
  141.2 8.3 %collective-permute-done.14 = bf16[128,1152]{1,0:T(8,128)(2,1)S(1)} collective-permute-done((bf16[128,1152]{1,0:T(8,128)(2,1)S(1)}, bf16[128,1152]{1,0:T(8,128)(2,1)S(1)}, u32[]{:S(2)}, u32[]{:S(2)}) %collective-permute-start.14) | collective-permute-done | bytes 294944 | tf_op jit(solution)/shard_map/ppermute | solution.py:347
  149.5 1.7 collective-permute-start.15
  151.3 8.2 %collective-permute-done.15 = bf16[256,1152]{1,0:T(8,128)(2,1)S(1)} collective-permute-done((bf16[256,1152]{1,0:T(8,128)(2,1)S(1)}, bf16[256,1152]{1,0:T(8,128)(2,1)S(1)}, u32[]{:S(2)}, u32[]{:S(2)}) %collective-permute-start.15) | collective-permute-done | bytes 589856 | tf_op jit(solution)/shard_map/ppermute | solution.py:347
  159.7 2.1 collective-permute-start.18
  161.8 7.8 %collective-permute-done.18.refs_0_ = bf16[256,1152]{1,0:T(8,128)(2,1)S(1)} collective-permute-done((bf16[256,1152]{1,0:T(8,128)(2,1)S(1)}, bf16[256,1152]{1,0:T(8,128)(2,1)S(1)}, u32[]{:S(2)}, u32[]{:S(2)}) %collective-permute-start.18) | collective-permute-done | bytes 589856 | tf_op jit(solution)/shard_map/ppermute | solution.py:347
  169.6 6.3 %collective-permute-done.16.refs_2_ = bf16[256,1152]{1,0:T(8,128)(2,1)S(1)} collective-permute-done((bf16[256,1152]{1,0:T(8,128)(2,1)S(1)}, bf16[256,1152]{1,0:T(8,128)(2,1)S(1)}, u32[]{:S(2)}, u32[]{:S(2)}) %collective-permute-start.16) | collective-permute-done | bytes 589856 | tf_op jit(solution)/shard_map/ppermute | solution.py:347
  175.9 4.4 %shard_map.39 = (bf16[2048,2048]{1,0:T(8,128)(2,1)S(1)}, bf16[2048,128]{1,0:T(8,128)(2,1)S(1)}, bf16[192,2048]{1,0:T(8,128)(2,1)S(1)}, f32[8,2048]{1,0:T(8,128)S(1)}) custom-call(s32[32]{0:T(128)S(1)} %concatenate.53.index_ref.at_ref, bf16[512,1152]{1,0:T(8,128)(2,1)S(1)} %pad_maximum_fusion.refs_0_, bf16[512,1152]{1,0:T(8,128)(2,1)S(1)} %collective-permute-done.20.refs_1_, ...), custom_call_target="tpu_custom_call" | custom-call | tf_op jit(solution)/shard_map/pallas_call | solution.py:77
  180.3 3.3 %shard_map.40 = (bf16[2048,2048]{1,0:T(8,128)(2,1)S(1)}, bf16[2048,128]{1,0:T(8,128)(2,1)S(1)}, bf16[192,2048]{1,0:T(8,128)(2,1)S(1)}, f32[8,2048]{1,0:T(8,128)S(1)}) custom-call(s32[32]{0:T(128)S(1)} %concatenate.53.index_ref.at_ref, ...), custom_call_target="tpu_custom_call", output_to_operand_aliasing={{0}: (5, {}), {1}: (6, {}), {2}: (7, {}), {3}: (8, {})} | custom-call | tf_op jit(solution)/shard_map/pallas_call | solution.py:77
  183.7 33.5 %shard_map.41 = (bf16[32,2048]{1,0:T(8,128)(2,1)S(1)}, f32[32,128]{1,0:T(8,128)S(1)}, bf16[2048,2048]{1,0:T(8,128)(2,1)S(1)}, bf16[2048,128]{1,0:T(8,128)(2,1)S(...) custom-call(s32[32]{0:T(128)S(1)} %concatenate.53.index_ref.at_ref, ...), custom_call_target="tpu_custom_call", output_to_operand_aliasing={{2}: (4, {}), {3}: (5, {}), {4}: (6, {}), {5}: (7, {})} | custom-call | tf_op jit(solution)/shard_map/pallas_call | solution.py:77
  217.8 1.2 collective-permute-start.21
  218.9 4.0 %collective-permute-done.21 = bf16[32,512]{1,0:T(8,128)(2,1)S(1)} collective-permute-done((bf16[32,512]{1,0:T(8,128)(2,1)S(1)}, bf16[32,512]{1,0:T(8,128)(2,1)S(1)}, u32[]{:S(2)}, u32[]{:S(2)}) %collective-permute-start.21) | collective-permute-done | bytes 32800 | tf_op jit(solution)/shard_map/ppermute | solution.py:347
  222.9 4.3 %collective-permute-done.22 = bf16[32,1024]{1,0:T(8,128)(2,1)S(1)} collective-permute-done((bf16[32,1024]{1,0:T(8,128)(2,1)S(1)}, bf16[32,1024]{1,0:T(8,128)(2,1)S(1)}, u32[]{:S(2)}, u32[]{:S(2)}) %collective-permute-start.22) | collective-permute-done | bytes 65568 | tf_op jit(solution)/shard_map/ppermute | solution.py:347
  (36 shorter events, 3.4 us)
Async XLA Ops:
  3.2 7.3 %copy-start.1 = (f32[2048,32]{0,1:T(8,128)S(1)}, f32[2048,32]{0,1:T(8,128)}, u32[]{:S(2)}) copy-start(f32[2048,32]{0,1:T(8,128)} %param.3) | copy-start | bytes 786436
  3.2 54.1 %all-to-all-start = ((bf16[64,32,512]{2,0,1:T(8,128)(2,1)}), bf16[64,32,512]{2,0,1:T(8,128)(2,1)S(1)}, u32[]{:S(2)}, u32[]{:S(2)}) async-start(bf16[64,32,512]{2,0,1:T(8,128)(2,1)} %bitcast.26), calls=%async_computation | async-start | bytes 4194304 | tf_op jit(solution)/shard_map/all_to_all | solution.py:396
  10.6 19.1 %collective-permute-start.1 = (bf16[32,2048]{1,0:T(8,128)(2,1)S(1)}, bf16[32,2048]{1,0:T(8,128)(2,1)S(1)}, u32[]{:S(2)}, u32[]{:S(2)}) collective-permute-start(bf16[32,2048]{1,0:T(8,128)(2,1)S(1)} %convert_bitcast_fusion.1), channel_id=1, source_target_pairs={{0,2},{1,3},{2,0},{3,1},{4,6},{5,7},{6,4},{7,5},{8,10},{9,11},{10,... | collective-permute-start | bytes 393224 | tf_op jit(solution)/shard_map/ppermute | solution.py:347
  29.8 29.4 %collective-permute-start.2 = (bf16[32,4096]{1,0:T(8,128)(2,1)S(1)}, bf16[32,4096]{1,0:T(8,128)(2,1)S(1)}, u32[]{:S(2)}, u32[]{:S(2)}) collective-permute-start(bf16[32,4096]{1,0:T(8,128)(2,1)S(1)} %pad_maximum_fusion.3), channel_id=1, source_target_pairs={{0,4},{1,5},{2,6},{3,7},{4,0},{5,1},{6,2},{7,3},{8,12},{9,13},{10,... | collective-permute-start | bytes 786440 | tf_op jit(solution)/shard_map/ppermute | solution.py:347
  57.3 28.8 %collective-permute-start = (bf16[2048,512]{1,0:T(8,128)(2,1)S(1)}, bf16[2048,512]{1,0:T(8,128)(2,1)}, u32[]{:S(2)}, u32[]{:S(2)}) collective-permute-start(bf16[2048,512]{1,0:T(8,128)(2,1)S(1)} %bitcast.18), channel_id=1, source_target_pairs={{0,1},{1,0},{2,3},{3,2},{4,5},{5,4},{6,7},{7,6},{8,9},{9,8},{10,11... | collective-permute-start | bytes 6291464 | tf_op jit(solution)/shard_map/ppermute | solution.py:347
  59.2 4.5 %collective-permute-start.3 = (bf16[32,8192]{1,0:T(8,128)(2,1)S(1)}, bf16[32,8192]{1,0:T(8,128)(2,1)S(1)}, u32[]{:S(2)}, u32[]{:S(2)}) collective-permute-start(bf16[32,8192]{1,0:T(8,128)(2,1)S(1)} %pad_maximum_fusion.2.near_ref), channel_id=1, source_target_pairs={{0,1},{1,0},{2,3},{3,2},{4,5},{5,4},{6,7},{7,6},{8,9},{9,8},{10,11... | collective-permute-start | bytes 1572872 | tf_op jit(solution)/shard_map/ppermute | solution.py:347
  63.7 1.6 copy-start
  66.5 1.2 collective-permute-start.4
  67.8 3.7 %collective-permute-start.5 = (bf16[32,128]{1,0:T(8,128)(2,1)S(1)}, bf16[32,128]{1,0:T(8,128)(2,1)S(1)}, u32[]{:S(2)}, u32[]{:S(2)}) collective-permute-start(bf16[32,128]{1,0:T(8,128)(2,1)S(1)} %maximum_select_fusion.4), channel_id=1, source_target_pairs={{0,2},{1,3},{2,0},{3,1},{4,6},{5,7},{6,4},{7,5},{8,10},{9,11},{10,... | collective-permute-start | bytes 24584 | tf_op jit(solution)/shard_map/ppermute | solution.py:347
  71.4 3.7 %collective-permute-start.6 = (bf16[32,256]{1,0:T(8,128)(2,1)S(1)}, bf16[32,256]{1,0:T(8,128)(2,1)S(1)}, u32[]{:S(2)}, u32[]{:S(2)}) collective-permute-start(bf16[32,256]{1,0:T(8,128)(2,1)S(1)} %maximum_select_fusion.3), channel_id=1, source_target_pairs={{0,4},{1,5},{2,6},{3,7},{4,0},{5,1},{6,2},{7,3},{8,12},{9,13},{10,... | collective-permute-start | bytes 49160 | tf_op jit(solution)/shard_map/ppermute | solution.py:347
  75.2 4.2 %collective-permute-start.7 = (bf16[32,512]{1,0:T(8,128)(2,1)S(1)}, bf16[32,512]{1,0:T(8,128)(2,1)S(1)}, u32[]{:S(2)}, u32[]{:S(2)}) collective-permute-start(bf16[32,512]{1,0:T(8,128)(2,1)S(1)} %maximum_select_fusion.2), channel_id=1, source_target_pairs={{0,8},{8,0},{16,24},{24,16},{1,9},{9,1},{17,25},{25,17},{2,10},{10... | collective-permute-start | bytes 98312 | tf_op jit(solution)/shard_map/ppermute | solution.py:347
  79.5 5.2 %collective-permute-start.8 = (bf16[32,1024]{1,0:T(8,128)(2,1)S(1)}, bf16[32,1024]{1,0:T(8,128)(2,1)S(1)}, u32[]{:S(2)}, u32[]{:S(2)}) collective-permute-start(bf16[32,1024]{1,0:T(8,128)(2,1)S(1)} %maximum_select_fusion.1), channel_id=1, source_target_pairs={{0,16},{8,24},{16,0},{24,8},{1,17},{9,25},{17,1},{25,9},{2,18},{10... | collective-permute-start | bytes 196616 | tf_op jit(solution)/shard_map/ppermute | solution.py:347
  93.8 11.2 %collective-permute-start.10 = (bf16[256,1152]{1,0:T(8,128)(2,1)S(1)}, bf16[256,1152]{1,0:T(8,128)(2,1)S(1)}, u32[]{:S(2)}, u32[]{:S(2)}) collective-permute-start(bf16[256,1152]{1,0:T(8,128)(2,1)S(1)} %shard_map.34), channel_id=1, source_target_pairs={{0,2},{1,5},{2,0},{3,7},{4,6},{5,1},{6,4},{7,3},{8,10},{9,13},{10,... | collective-permute-start | bytes 1769480 | tf_op jit(solution)/shard_map/ppermute | solution.py:347
  98.6 17.8 %collective-permute-start.9 = (bf16[256,1152]{1,0:T(8,128)(2,1)S(1)}, bf16[256,1152]{1,0:T(8,128)(2,1)S(1)}, u32[]{:S(2)}, u32[]{:S(2)}) collective-permute-start(bf16[256,1152]{1,0:T(8,128)(2,1)S(1)} %shard_map.32), channel_id=1, source_target_pairs={{0,2},{1,5},{2,0},{3,7},{4,6},{5,1},{6,4},{7,3},{8,10},{9,13},{10,... | collective-permute-start | bytes 1769480 | tf_op jit(solution)/shard_map/ppermute | solution.py:347
  106.0 10.4 %collective-permute-start.11 = (bf16[256,1152]{1,0:T(8,128)(2,1)S(1)}, bf16[256,1152]{1,0:T(8,128)(2,1)S(1)}, u32[]{:S(2)}, u32[]{:S(2)}) collective-permute-start(bf16[256,1152]{1,0:T(8,128)(2,1)S(1)} %shard_map.35), channel_id=1, source_target_pairs={{0,4},{1,3},{2,6},{3,1},{4,0},{5,7},{6,2},{7,5},{8,12},{9,11},{10,... | collective-permute-start | bytes 1769480 | tf_op jit(solution)/shard_map/ppermute | solution.py:347
  117.5 7.9 %collective-permute-start.12 = (bf16[128,1152]{1,0:T(8,128)(2,1)S(1)}, bf16[128,1152]{1,0:T(8,128)(2,1)S(1)}, u32[]{:S(2)}, u32[]{:S(2)}) collective-permute-start(bf16[128,1152]{1,0:T(8,128)(2,1)S(1)} %get-tuple-element.25), channel_id=1, source_target_pairs={{0,8},{8,0},{16,24},{24,16},{1,9},{9,1},{17,25},{25,17},{2,10},{10... | collective-permute-start | bytes 884744 | tf_op jit(solution)/shard_map/ppermute | solution.py:347
  126.1 14.2 %collective-permute-start.13 = (bf16[128,1152]{1,0:T(8,128)(2,1)S(1)}, bf16[128,1152]{1,0:T(8,128)(2,1)S(1)}, u32[]{:S(2)}, u32[]{:S(2)}) collective-permute-start(bf16[128,1152]{1,0:T(8,128)(2,1)S(1)} %shard_map.37.refs_0_), channel_id=1, source_target_pairs={{0,16},{8,24},{16,0},{24,8},{1,17},{9,25},{17,1},{25,9},{2,18},{10... | collective-permute-start | bytes 884744 | tf_op jit(solution)/shard_map/ppermute | solution.py:347
  141.2 8.3 %collective-permute-start.14 = (bf16[128,1152]{1,0:T(8,128)(2,1)S(1)}, bf16[128,1152]{1,0:T(8,128)(2,1)S(1)}, u32[]{:S(2)}, u32[]{:S(2)}) collective-permute-start(bf16[128,1152]{1,0:T(8,128)(2,1)S(1)} %shard_map.38), channel_id=1, source_target_pairs={{0,8},{8,0},{16,24},{24,16},{1,9},{9,1},{17,25},{25,17},{2,10},{10... | collective-permute-start | bytes 884744 | tf_op jit(solution)/shard_map/ppermute | solution.py:347
  149.5 9.9 %collective-permute-start.15 = (bf16[256,1152]{1,0:T(8,128)(2,1)S(1)}, bf16[256,1152]{1,0:T(8,128)(2,1)S(1)}, u32[]{:S(2)}, u32[]{:S(2)}) collective-permute-start(bf16[256,1152]{1,0:T(8,128)(2,1)S(1)} %pad_maximum_fusion.1), channel_id=1, source_target_pairs={{0,4},{1,3},{2,6},{3,1},{4,0},{5,7},{6,2},{7,5},{8,12},{9,11},{10,... | collective-permute-start | bytes 1769480 | tf_op jit(solution)/shard_map/ppermute | solution.py:347
  159.6 16.4 %collective-permute-start.20 = (bf16[512,1152]{1,0:T(8,128)(2,1)S(1)}, bf16[512,1152]{1,0:T(8,128)(2,1)S(1)}, u32[]{:S(2)}, u32[]{:S(2)}) collective-permute-start(bf16[512,1152]{1,0:T(8,128)(2,1)S(1)} %pad_maximum_fusion.refs_0_), channel_id=1, source_target_pairs={{0,1},{1,0},{2,3},{3,2},{4,5},{5,4},{6,7},{7,6},{8,9},{9,8},{10,11... | collective-permute-start | bytes 3538952 | tf_op jit(solution)/shard_map/ppermute | solution.py:347
  159.7 10.0 %collective-permute-start.18 = (bf16[256,1152]{1,0:T(8,128)(2,1)S(1)}, bf16[256,1152]{1,0:T(8,128)(2,1)S(1)}, u32[]{:S(2)}, u32[]{:S(2)}) collective-permute-start(bf16[256,1152]{1,0:T(8,128)(2,1)S(1)} %pad_maximum_fusion.1), channel_id=1, source_target_pairs={{0,2},{1,5},{2,0},{3,7},{4,6},{5,1},{6,4},{7,3},{8,10},{9,13},{10,... | collective-permute-start | bytes 1769480 | tf_op jit(solution)/shard_map/ppermute | solution.py:347
  161.8 14.2 %collective-permute-start.16 = (bf16[256,1152]{1,0:T(8,128)(2,1)S(1)}, bf16[256,1152]{1,0:T(8,128)(2,1)S(1)}, u32[]{:S(2)}, u32[]{:S(2)}) collective-permute-start(bf16[256,1152]{1,0:T(8,128)(2,1)S(1)} %collective-permute-done.15), channel_id=1, source_target_pairs={{0,2},{1,5},{2,0},{3,7},{4,6},{5,1},{6,4},{7,3},{8,10},{9,13},{10,... | collective-permute-start | bytes 1769480 | tf_op jit(solution)/shard_map/ppermute | solution.py:347
  169.6 10.7 %collective-permute-start.19 = (bf16[256,1152]{1,0:T(8,128)(2,1)S(1)}, bf16[256,1152]{1,0:T(8,128)(2,1)S(1)}, u32[]{:S(2)}, u32[]{:S(2)}) collective-permute-start(bf16[256,1152]{1,0:T(8,128)(2,1)S(1)} %collective-permute-done.18.refs_0_), channel_id=1, source_target_pairs={{0,1},{1,0},{2,3},{3,2},{4,5},{5,4},{6,7},{7,6},{8,9},{9,8},{10,11... | collective-permute-start | bytes 1769480 | tf_op jit(solution)/shard_map/ppermute | solution.py:347
  175.9 7.7 %collective-permute-start.17 = (bf16[256,1152]{1,0:T(8,128)(2,1)S(1)}, bf16[256,1152]{1,0:T(8,128)(2,1)S(1)}, u32[]{:S(2)}, u32[]{:S(2)}) collective-permute-start(bf16[256,1152]{1,0:T(8,128)(2,1)S(1)} %collective-permute-done.16.refs_2_), channel_id=1, source_target_pairs={{0,1},{1,0},{2,3},{3,2},{4,5},{5,4},{6,7},{7,6},{8,9},{9,8},{10,11... | collective-permute-start | bytes 1769480 | tf_op jit(solution)/shard_map/ppermute | solution.py:347
  217.8 5.1 %collective-permute-start.21 = (bf16[32,512]{1,0:T(8,128)(2,1)S(1)}, bf16[32,512]{1,0:T(8,128)(2,1)S(1)}, u32[]{:S(2)}, u32[]{:S(2)}) collective-permute-start(bf16[32,512]{1,0:T(8,128)(2,1)S(1)} %shard_map.42), channel_id=1, source_target_pairs={{0,16},{8,24},{16,0},{24,8},{1,17},{9,25},{17,1},{25,9},{2,18},{10... | collective-permute-start | bytes 98312 | tf_op jit(solution)/shard_map/ppermute | solution.py:347
  222.9 4.3 %collective-permute-start.22 = (bf16[32,1024]{1,0:T(8,128)(2,1)S(1)}, bf16[32,1024]{1,0:T(8,128)(2,1)S(1)}, u32[]{:S(2)}, u32[]{:S(2)}) collective-permute-start(bf16[32,1024]{1,0:T(8,128)(2,1)S(1)} %pad_maximum_fusion.4), channel_id=1, source_target_pairs={{0,8},{8,0},{16,24},{24,16},{1,9},{9,1},{17,25},{25,17},{2,10},{10... | collective-permute-start | bytes 196616 | tf_op jit(solution)/shard_map/ppermute | solution.py:347

commit v10 on v9

--- a/solution.py
+++ b/solution.py
@@ -181,11 +181,11 @@
     right[...] = jnp.concatenate([w1, q1, w2, q2, w3, q3, w1, q1, w2, q2, w1, q1], axis=0)
 
 
-def form_rows(first, core, own_ref, other_ref, left, right, out_ref, window, right_win):
+def form_rows(first, core, own_ref, other_ref, left, right, out_refs, window, right_win):
     n, px = own_ref.shape
-    rows = out_ref.shape[0]
+    rows, cut = out_refs[0].shape
     width = n // 2
-    bs = out_ref.shape[1] - width
+    bs = cut + out_refs[1].shape[1] - width
     nb = n // bs
     for b in range(window.shape[0] // bs):
         at = pl.multiple_of(lax.rem(first + b, nb) * bs, bs)
@@ -206,8 +206,9 @@
         s = wide[off : off + bs, off : off + width + bs]
         corner = s[:, :bs]
         diagonal = jnp.sum(jnp.where(eye, corner, 0.0), axis=0, keepdims=True)
-        out_ref[to : to + bs, :bs] = jnp.where(eye, 0.0, corner).astype(BF16)
-        out_ref[to : to + bs, bs:width] = s[:, bs:width].astype(BF16)
+        out_refs[0][to : to + bs, :bs] = jnp.where(eye, 0.0, corner).astype(BF16)
+        out_refs[0][to : to + bs, bs:] = s[:, bs:cut].astype(BF16)
+        out_refs[1][to : to + bs, : width - cut] = s[:, cut:width].astype(BF16)
         last = s[:, width:]
         low = last[HALF:]
         last = jnp.where(core == 0, last, jnp.concatenate([low, pltpu.roll(low, HALF, 1)], axis=0))
@@ -218,21 +219,25 @@
             side.append(jnp.broadcast_to(d.astype(F32), (GROUP - RANK, bs)))
         side.append(jnp.zeros((bs - HALF - 3 * GROUP, bs), F32))
         side = jnp.concatenate(side, axis=0).T
-        out_ref[to : to + bs, width:] = jnp.where(lane < HALF, last, side).astype(BF16)
-
-
-def form_kernel(slot, at_ref, own_ref, other_ref, left, right, out_ref, *wins):
-    form_rows(at_ref[slot], at_ref[CORE], own_ref, other_ref, left, right, out_ref, *wins)
-
-
-def add_kernel(slots, at_ref, *refs):
+        last = jnp.where(lane < HALF, last, side)
+        out_refs[1][to : to + bs, width - cut :] = last.astype(BF16)
+
+
+def form_kernel(slot, at_ref, own_ref, other_ref, left, right, out_0, out_1, *wins):
+    outs = (out_0, out_1)
+    form_rows(at_ref[slot], at_ref[CORE], own_ref, other_ref, left, right, outs, *wins)
+
+
+def add_kernel(slots, special, at_ref, *refs):
     shares, o_refs = refs[: -len(slots)], refs[-len(slots) :]
-    width = shares[0].shape[1] - LANES
+    width = shares[0].shape[1] - (LANES if special else 0)
     for slot, o_ref in zip(slots, o_refs):
         h = o_ref.shape[0]
         at = 0 if slot is None else pl.multiple_of(at_ref[slot] * h, h)
         parts = [ref[pl.ds(at, h), :].astype(F32) for ref in shares]
         o_ref[:, :width] = sum(part[:, :width] for part in parts).astype(BF16)
+        if not special:
+            continue
         last = [part[:, width:] for part in parts]
         x = sum(lane_sum3(part, GROUP) for part in last)
         lane = lax.broadcasted_iota(jnp.int32, x.shape, 1) - HALF
@@ -243,22 +248,23 @@
         o_ref[:, width:] = jnp.where(lane < 0, sum(last), packed).astype(BF16)
 
 
-def add_shares(index, shares, slots=()):
+def add_shares(index, special, shares, slots=()):
     rows, lanes = shares[0].shape
     shape = jax.ShapeDtypeStruct((rows // max(len(slots), 1), lanes), BF16)
     slots = slots or (None,)
     return kernel_call(
-        functools.partial(add_kernel, slots),
+        functools.partial(add_kernel, slots, special),
         (shape,) * len(slots),
         in_specs=[smem()] + vmem(len(shares)),
         out_specs=tuple(vmem(len(slots))),
     )(index, *shares)
 
 
-def unpack(offset, index_ref, share_ref, q_ref, full, u, v, diag):
+def unpack(offset, index_ref, share_refs, q_ref, full, u, v, diag):
     n = q_ref.shape[1]
     width = n // 2
-    bs = share_ref.shape[1] - width
+    cut = share_refs[0].shape[1]
+    bs = cut + share_refs[1].shape[1] - width
     nb = n // bs
     lane = lax.broadcasted_iota(jnp.int32, (bs, bs), 1)
 
@@ -267,13 +273,14 @@
         frm = pl.multiple_of(r * bs, bs)
         to = pl.multiple_of(i * bs, bs)
         for d in range(nb // 2):
-            part = share_ref[pl.ds(frm, bs), d * bs : (d + 1) * bs]
+            ref, col = (share_refs[0], d * bs) if d * bs < cut else (share_refs[1], d * bs - cut)
+            part = ref[pl.ds(frm, bs), col : col + bs]
             at = pl.multiple_of(lax.rem(i + d, nb) * bs, bs)
             full[pl.ds(to, bs), pl.ds(at, bs)] = part
             if d:
                 full[pl.ds(at, bs), pl.ds(to, bs)] = part.T
         at = pl.multiple_of(lax.rem(i + nb // 2, nb) * bs, bs)
-        last = share_ref[pl.ds(frm, bs), width:].astype(F32)
+        last = share_refs[1][pl.ds(frm, bs), width - cut :].astype(F32)
 
         @pl.when(i < nb // 2)
         def _():
@@ -303,19 +310,19 @@
         v[:, pl.ds(to, bs)] = jnp.concatenate([v1, v2, v3, v1, v2, v1], axis=0)
         return 0
 
-    lax.fori_loop(0, share_ref.shape[0] // bs, one, 0)
+    lax.fori_loop(0, share_refs[0].shape[0] // bs, one, 0)
 
 
 def unpack_kernel(offsets, index_ref, *refs):
-    shares, q_ref = refs[: len(offsets)], refs[len(offsets)]
-    for offset, share_ref in zip(offsets, shares):
-        unpack(offset, index_ref, share_ref, q_ref, *refs[-4:])
-
-
-def iterate_kernel(offset, index_ref, far_ref, q_ref, p0_ref, *refs):
+    q_ref = refs[2 * len(offsets)]
+    for i, offset in enumerate(offsets):
+        unpack(offset, index_ref, refs[2 * i : 2 * i + 2], q_ref, *refs[-4:])
+
+
+def iterate_kernel(offset, index_ref, far_0, far_1, q_ref, p0_ref, *refs):
     p_ref, inv_ref, full, u, v, diag = refs[4:]
     k, _ = q_ref.shape
-    unpack(offset, index_ref, far_ref, q_ref, full, u, v, diag)
+    unpack(offset, index_ref, (far_0, far_1), q_ref, full, u, v, diag)
     lane = lax.broadcasted_iota(jnp.int32, (k, LANES), 1)
 
     def product(p):
@@ -419,7 +426,8 @@
     width = n // 2 + bs
     rows = n // 8
     window = rows - bs + width
-    piece = jax.ShapeDtypeStruct((rows, width), BF16)
+    cut = (nb // 4 + 1) * bs
+    pieces = tuple(jax.ShapeDtypeStruct((rows, c), BF16) for c in (cut, width - cut))
     stack = jax.ShapeDtypeStruct((12 * RANK, n), BF16)
     left, right = kernel_call(
         factors_kernel,
@@ -432,28 +440,32 @@
     def form(quarter):
         return kernel_call(
             functools.partial(form_kernel, QUARTERS + quarter),
-            piece,
+            pieces,
             in_specs=[smem()] + vmem(4),
-            out_specs=vmem()[0],
+            out_specs=tuple(vmem(2)),
             scratch_mib=12,
             scratch_shapes=[pltpu.VMEM((window, 2 * px), BF16), pltpu.VMEM((12 * RANK, window), BF16)],
         )(index, block, other, left, right)
 
-    passed = flip(form(0), "pix", first)
-    kept = flip(form(1), "pix", first)
-    (send,) = add_shares(index, (form(2), passed))
-    recv = flip(send, "pix", second)
-    send, keep = add_shares(index, (form(3), kept, recv), (HALVES, HALVES + 1))
-    (share,) = add_shares(index, (keep, flip(send, "samp", xor_samp(1))))
-    (share,) = add_shares(index, (share, flip(share, "samp", xor_samp(2))))
-
-    share = jnp.concatenate([share, flip(share, "samp", xor_samp(1))], axis=0)
+    sent = [form(0), form(1)]
+    held = [form(2), form(3)]
     swap = xor_pix(1)
-    over_a = flip(share, "pix", first)
-    over_b = flip(share, "pix", second)
-    over_ab = flip(over_b, "pix", first)
-    near = jnp.concatenate([share, over_b], axis=0)
-    far, far_a, far_ab = [flip(t, "pix", swap) for t in (near, over_a, over_ab)]
+    near, far, over_a, far_a, over_ab, far_ab = ([None, None] for _ in range(6))
+    for e in (0, 1):
+        add = functools.partial(add_shares, index, e == 1)
+        passed, kept = [flip(sent[i][e], "pix", first) for i in (0, 1)]
+        (send,) = add((held[0][e], passed))
+        recv = flip(send, "pix", second)
+        send, keep = add((held[1][e], kept, recv), (HALVES, HALVES + 1))
+        (share,) = add((keep, flip(send, "samp", xor_samp(1))))
+        (share,) = add((share, flip(share, "samp", xor_samp(2))))
+
+        share = jnp.concatenate([share, flip(share, "samp", xor_samp(1))], axis=0)
+        over_a[e] = flip(share, "pix", first)
+        over_b = flip(share, "pix", second)
+        over_ab[e] = flip(over_b, "pix", first)
+        near[e] = jnp.concatenate([share, over_b], axis=0)
+        far[e], far_a[e], far_ab[e] = [flip(t[e], "pix", swap) for t in (near, over_a, over_ab)]
     parts = (
         jax.ShapeDtypeStruct((n, n), BF16),
         jax.ShapeDtypeStruct((n, bs), BF16),
@@ -464,27 +476,27 @@
     now = kernel_call(
         functools.partial(unpack_kernel, (BLOCKS, BLOCKS + 4 * eighth)),
         parts,
-        in_specs=[smem()] + vmem(3),
+        in_specs=[smem()] + vmem(5),
         out_specs=tuple(vmem(4)),
         scratch_mib=4,
-    )(index, near, far, q)
+    )(index, *near, *far, q)
     offsets = [BLOCKS + i * eighth for i in (2, 6, 3)]
     now = kernel_call(
         functools.partial(unpack_kernel, offsets),
         parts,
-        in_specs=[smem()] + vmem(8),
+        in_specs=[smem()] + vmem(11),
         out_specs=tuple(vmem(4)),
-        input_output_aliases={5 + i: i for i in range(4)},
+        input_output_aliases={8 + i: i for i in range(4)},
         scratch_mib=4,
-    )(index, over_a, far_a, over_ab, q, *now)
+    )(index, *over_a, *far_a, *over_ab, q, *now)
     proj, inv = kernel_call(
         functools.partial(iterate_kernel, BLOCKS + 7 * eighth),
         (jax.ShapeDtypeStruct((k, n), BF16), jax.ShapeDtypeStruct((k, LANES), F32)) + parts,
-        in_specs=[smem()] + vmem(7),
+        in_specs=[smem()] + vmem(8),
         out_specs=tuple(vmem(6)),
-        input_output_aliases={4 + i: 2 + i for i in range(4)},
+        input_output_aliases={5 + i: 2 + i for i in range(4)},
         scratch_mib=12,
-    )(index, far_ab, q, proj, *now)[:2]
+    )(index, *far_ab, q, proj, *now)[:2]
 
     mine = kernel_call(
         functools.partial(finish_kernel, scale),

time: 228 us -> 218 us (0.956)
  waiting for transfers between devices: 127 us -> 108 us
  starting transfers between devices: 30.9 us -> 37.7 us
    ppermute x23 -> x35, waiting for transfers between devices: 101 us -> 81.8 us  [flip(): return lax.ppermute(x, axes, perm)]
    ppermute x23 -> x35, starting transfers between devices: 23.5 us -> 30.4 us  [flip(): return lax.ppermute(x, axes, perm)]
    pallas_call x15 -> x19, Pallas kernels: 64 us -> 66 us  [kernel_call(): return lambda *args: call(*map(place, args, in_specs))]
  transfers between devices with their start and end apart: 24 -> 36, of which waited for: 18 -> 23; matrix products, arithmetic and copies ran while one was open for 0% -> 0% of each run, Pallas kernels for 9% -> 11%
where the time goes in v10:
time: 218 us
  waiting for transfers between devices  108 us (50%)
  Pallas kernels  66 us (30%)
  starting transfers between devices  37.7 us (17%)
  local copies, waits for them, and re-layouts  4.9 us (2%)
    ppermute x35, waiting for transfers between devices, flip(): return lax.ppermute(x, axes, perm)  81.8 us
    pallas_call x19, Pallas kernels, kernel_call(): return lambda *args: call(*map(place, args, in_specs))  66 us
    ppermute x35, starting transfers between devices, flip(): return lax.ppermute(x, axes, perm)  30.4 us
    all_to_all x1, waiting for transfers between devices, sample_space(): lax.all_to_all(stamps, ('pix', 'samp'), split_axis=1, concat_axis=0, tile...  26 us
    all_to_all x1, starting transfers between devices, sample_space(): lax.all_to_all(stamps, ('pix', 'samp'), split_axis=1, concat_axis=0, tile...  7.33 us
  transfers between devices with their start and end apart: 36, of which 23 were waited for; matrix products, arithmetic and copies ran while one was open for 0% of the time, Pallas kernels for 11%

profile of v10, /device:TPU:0, one launch (start us, length us, event | category | flops | bytes accessed | tf_op | source)
XLA Modules:
  0.0 217.9 jit_solution(7380942419174703652)
XLA Ops:
  0.0 3.2 %copy.14 = bf16[8,32,8,512]{3,2,0,1:T(8,128)(2,1)} copy(bf16[8,32,8,512]{3,2,1,0:T(8,128)(2,1)} %bitcast.25) | data formatting | bytes 4194304 | tf_op jit(solution)/shard_map/all_to_all | solution.py:403
  3.2 7.3 %all-to-all-start = ((bf16[64,32,512]{2,0,1:T(8,128)(2,1)}), bf16[64,32,512]{2,0,1:T(8,128)(2,1)S(1)}, u32[]{:S(2)}, u32[]{:S(2)}) async-start(bf16[64,32,512]{2,0,1:T(8,128)(2,1)} %bitcast.26), calls=%async_computation | async-start | bytes 4194304 | tf_op jit(solution)/shard_map/all_to_all | solution.py:403
  10.6 1.8 collective-permute-start.1
  12.4 17.3 %collective-permute-done.1 = bf16[32,2048]{1,0:T(8,128)(2,1)S(1)} collective-permute-done((bf16[32,2048]{1,0:T(8,128)(2,1)S(1)}, bf16[32,2048]{1,0:T(8,128)(2,1)S(1)}, u32[]{:S(2)}, u32[]{:S(2)}) %collective-permute-start.1) | collective-permute-done | bytes 131104 | tf_op jit(solution)/shard_map/ppermute | solution.py:354
  29.8 1.5 collective-permute-start.2
  31.3 26.0 %all-to-all-done = bf16[64,32,512]{2,0,1:T(8,128)(2,1)S(1)} async-done(((bf16[64,32,512]{2,0,1:T(8,128)(2,1)}), bf16[64,32,512]{2,0,1:T(8,128)(2,1)S(1)}, u32[]{:S(2)}, u32[]{:S(2)}) %all-to-all-start) | async-done | bytes 2097184 | tf_op jit(solution)/shard_map/all_to_all | solution.py:403
  57.3 1.8 collective-permute-start
  59.4 4.3 %collective-permute-done.3.far_ref = bf16[32,8192]{1,0:T(8,128)(2,1)S(1)} collective-permute-done((bf16[32,8192]{1,0:T(8,128)(2,1)S(1)}, bf16[32,8192]{1,0:T(8,128)(2,1)S(1)}, u32[]{:S(2)}, u32[]{:S(2)}) %collective-permute-start.3) | collective-permute-done | bytes 524320 | tf_op jit(solution)/shard_map/ppermute | solution.py:354
  63.7 1.6 copy-done
  65.2 1.2 shard_map.28
  67.8 1.5 collective-permute-start.5
  69.3 2.1 collective-permute-done.5
  71.4 1.5 collective-permute-start.6
  72.9 2.2 %collective-permute-done.6 = bf16[32,256]{1,0:T(8,128)(2,1)S(1)} collective-permute-done((bf16[32,256]{1,0:T(8,128)(2,1)S(1)}, bf16[32,256]{1,0:T(8,128)(2,1)S(1)}, u32[]{:S(2)}, u32[]{:S(2)}) %collective-permute-start.6) | collective-permute-done | bytes 16416 | tf_op jit(solution)/shard_map/ppermute | solution.py:354
  75.2 2.3 %collective-permute-start.7 = (bf16[32,512]{1,0:T(8,128)(2,1)S(1)}, bf16[32,512]{1,0:T(8,128)(2,1)S(1)}, u32[]{:S(2)}, u32[]{:S(2)}) collective-permute-start(bf16[32,512]{1,0:T(8,128)(2,1)S(1)} %maximum_select_fusion.2), channel_id=1, source_target_pairs={{0,8},{8,0},{16,24},{24,16},{1,9},{9,1},{17,25},{25,17},{2,10},{10... | collective-permute-start | bytes 98312 | tf_op jit(solution)/shard_map/ppermute | solution.py:354
  77.5 1.9 collective-permute-done.7
  80.6 4.0 %collective-permute-done.8 = bf16[32,1024]{1,0:T(8,128)(2,1)S(1)} collective-permute-done((bf16[32,1024]{1,0:T(8,128)(2,1)S(1)}, bf16[32,1024]{1,0:T(8,128)(2,1)S(1)}, u32[]{:S(2)}, u32[]{:S(2)}) %collective-permute-start.8) | collective-permute-done | bytes 65568 | tf_op jit(solution)/shard_map/ppermute | solution.py:354
  84.7 1.4 shard_map.29
  86.1 4.9 %shard_map.30 = (bf16[192,2048]{1,0:T(8,128)(2,1)S(1)}, bf16[192,2048]{1,0:T(8,128)(2,1)S(1)}) custom-call(bf16[2048,512]{1,0:T(8,128)(2,1)S(1)} %bitcast.19, bf16[2048,512]{1,0:T(8,128)(2,1)} %collective-permute-done.other_ref, f32[32,2048]{1,0:T(8,128)S(1)} %get-tuple-element.31.q_ref.refs_4_.refs_6_), custom_call_target="tpu_custom_call" | custom-call | tf_op jit(solution)/shard_map/pallas_call | solution.py:77
  91.0 2.8 %shard_map.34 = (bf16[256,640]{1,0:T(8,128)(2,1)S(1)}, bf16[256,512]{1,0:T(8,128)(2,1)S(1)}) custom-call(s32[32]{0:T(128)S(1)} %concatenate.60.index_ref.at_ref, bf16[2048,512]{1,0:T(8,128)(2,1)S(1)} %bitcast.20, bf16[2048,512]{1,0:T(8,128)(2,1)} %collective-permute-done.other_ref, bf16[192,2048]{1,0:T(8,128)(2,1)S(1)} %get-tuple-element.32.left, ...), custom_call_target="tpu_custom_call" | custom-call | tf_op jit(solution)/shard_map/pallas_call | solution.py:77
  93.8 2.0 collective-permute-start.10
  95.9 2.8 %shard_map.32 = (bf16[256,640]{1,0:T(8,128)(2,1)S(1)}, bf16[256,512]{1,0:T(8,128)(2,1)S(1)}) custom-call(s32[32]{0:T(128)S(1)} %concatenate.60.index_ref.at_ref, bf16[2048,512]{1,0:T(8,128)(2,1)S(1)} %bitcast.21, bf16[2048,512]{1,0:T(8,128)(2,1)} %collective-permute-done.other_ref, bf16[192,2048]{1,0:T(8,128)(2,1)S(1)} %get-tuple-element.32.left, ...), custom_call_target="tpu_custom_call" | custom-call | tf_op jit(solution)/shard_map/pallas_call | solution.py:77
  98.7 2.0 collective-permute-start.9
  100.7 2.8 %shard_map.33 = (bf16[256,640]{1,0:T(8,128)(2,1)S(1)}, bf16[256,512]{1,0:T(8,128)(2,1)S(1)}) custom-call(s32[32]{0:T(128)S(1)} %concatenate.60.index_ref.at_ref, bf16[2048,512]{1,0:T(8,128)(2,1)S(1)} %bitcast.22, bf16[2048,512]{1,0:T(8,128)(2,1)} %collective-permute-done.other_ref, bf16[192,2048]{1,0:T(8,128)(2,1)S(1)} %get-tuple-element.32.left, ...), custom_call_target="tpu_custom_call" | custom-call | tf_op jit(solution)/shard_map/pallas_call | solution.py:77
  104.2 1.3 collective-permute-start.18
  105.5 1.4 collective-permute-done.19.refs_1_
  108.8 2.8 %shard_map.31 = (bf16[256,640]{1,0:T(8,128)(2,1)S(1)}, bf16[256,512]{1,0:T(8,128)(2,1)S(1)}) custom-call(s32[32]{0:T(128)S(1)} %concatenate.60.index_ref.at_ref, bf16[2048,512]{1,0:T(8,128)(2,1)S(1)} %bitcast.23, bf16[2048,512]{1,0:T(8,128)(2,1)} %collective-permute-done.other_ref, bf16[192,2048]{1,0:T(8,128)(2,1)S(1)} %get-tuple-element.32.left, ...), custom_call_target="tpu_custom_call" | custom-call | tf_op jit(solution)/shard_map/pallas_call | solution.py:77
  111.6 4.8 %collective-permute-done.18.refs_1_ = bf16[256,512]{1,0:T(8,128)(2,1)S(1)} collective-permute-done((bf16[256,512]{1,0:T(8,128)(2,1)S(1)}, bf16[256,512]{1,0:T(8,128)(2,1)S(1)}, u32[]{:S(2)}, u32[]{:S(2)}) %collective-permute-start.18) | collective-permute-done | bytes 262176 | tf_op jit(solution)/shard_map/ppermute | solution.py:354
  117.3 2.1 collective-permute-start.21
  120.2 2.7 %collective-permute-done.21.refs_1_ = bf16[128,512]{1,0:T(8,128)(2,1)S(1)} collective-permute-done((bf16[128,512]{1,0:T(8,128)(2,1)S(1)}, bf16[128,512]{1,0:T(8,128)(2,1)S(1)}, u32[]{:S(2)}, u32[]{:S(2)}) %collective-permute-start.21) | collective-permute-done | bytes 131104 | tf_op jit(solution)/shard_map/ppermute | solution.py:354
  124.8 2.0 collective-permute-done.12.refs_1_
  127.4 1.5 collective-permute-start.13
  128.8 3.7 %collective-permute-done.22.refs_1_ = bf16[128,512]{1,0:T(8,128)(2,1)S(1)} collective-permute-done((bf16[128,512]{1,0:T(8,128)(2,1)S(1)}, bf16[128,512]{1,0:T(8,128)(2,1)S(1)}, u32[]{:S(2)}, u32[]{:S(2)}) %collective-permute-start.22) | collective-permute-done | bytes 131104 | tf_op jit(solution)/shard_map/ppermute | solution.py:354
  134.0 2.1 collective-permute-done.13.refs_1_
  136.8 2.5 %collective-permute-done.23 = bf16[128,512]{1,0:T(8,128)(2,1)S(1)} collective-permute-done((bf16[128,512]{1,0:T(8,128)(2,1)S(1)}, bf16[128,512]{1,0:T(8,128)(2,1)S(1)}, u32[]{:S(2)}, u32[]{:S(2)}) %collective-permute-start.23) | collective-permute-done | bytes 131104 | tf_op jit(solution)/shard_map/ppermute | solution.py:354
  139.4 2.8 %collective-permute-done.14 = bf16[128,640]{1,0:T(8,128)(2,1)S(1)} collective-permute-done((bf16[128,640]{1,0:T(8,128)(2,1)S(1)}, bf16[128,640]{1,0:T(8,128)(2,1)S(1)}, u32[]{:S(2)}, u32[]{:S(2)}) %collective-permute-start.14) | collective-permute-done | bytes 163872 | tf_op jit(solution)/shard_map/ppermute | solution.py:354
  142.2 2.5 %collective-permute-start.28 = (bf16[256,512]{1,0:T(8,128)(2,1)S(1)}, bf16[256,512]{1,0:T(8,128)(2,1)S(1)}, u32[]{:S(2)}, u32[]{:S(2)}) collective-permute-start(bf16[256,512]{1,0:T(8,128)(2,1)S(1)} %pad_maximum_fusion.5), channel_id=1, source_target_pairs={{0,2},{1,5},{2,0},{3,7},{4,6},{5,1},{6,4},{7,3},{8,10},{9,13},{10,... | collective-permute-start | bytes 786440 | tf_op jit(solution)/shard_map/ppermute | solution.py:354
  144.7 3.8 %collective-permute-done.24 = bf16[256,512]{1,0:T(8,128)(2,1)S(1)} collective-permute-done((bf16[256,512]{1,0:T(8,128)(2,1)S(1)}, bf16[256,512]{1,0:T(8,128)(2,1)S(1)}, u32[]{:S(2)}, u32[]{:S(2)}) %collective-permute-start.24) | collective-permute-done | bytes 262176 | tf_op jit(solution)/shard_map/ppermute | solution.py:354
  148.6 3.4 %collective-permute-done.15 = bf16[256,640]{1,0:T(8,128)(2,1)S(1)} collective-permute-done((bf16[256,640]{1,0:T(8,128)(2,1)S(1)}, bf16[256,640]{1,0:T(8,128)(2,1)S(1)}, u32[]{:S(2)}, u32[]{:S(2)}) %collective-permute-start.15) | collective-permute-done | bytes 327712 | tf_op jit(solution)/shard_map/ppermute | solution.py:354
  152.8 1.5 collective-permute-start.16
  154.8 4.5 %collective-permute-done.27.refs_0_ = bf16[256,640]{1,0:T(8,128)(2,1)S(1)} collective-permute-done((bf16[256,640]{1,0:T(8,128)(2,1)S(1)}, bf16[256,640]{1,0:T(8,128)(2,1)S(1)}, u32[]{:S(2)}, u32[]{:S(2)}) %collective-permute-start.27) | collective-permute-done | bytes 327712 | tf_op jit(solution)/shard_map/ppermute | solution.py:354
  159.3 3.5 %collective-permute-done.16.refs_4_ = bf16[256,640]{1,0:T(8,128)(2,1)S(1)} collective-permute-done((bf16[256,640]{1,0:T(8,128)(2,1)S(1)}, bf16[256,640]{1,0:T(8,128)(2,1)S(1)}, u32[]{:S(2)}, u32[]{:S(2)}) %collective-permute-start.16) | collective-permute-done | bytes 327712 | tf_op jit(solution)/shard_map/ppermute | solution.py:354
  162.9 2.8 %collective-permute-done.25.refs_5_ = bf16[256,512]{1,0:T(8,128)(2,1)S(1)} collective-permute-done((bf16[256,512]{1,0:T(8,128)(2,1)S(1)}, bf16[256,512]{1,0:T(8,128)(2,1)S(1)}, u32[]{:S(2)}, u32[]{:S(2)}) %collective-permute-start.25) | collective-permute-done | bytes 262176 | tf_op jit(solution)/shard_map/ppermute | solution.py:354
  166.2 4.4 %shard_map.43 = (bf16[2048,2048]{1,0:T(8,128)(2,1)S(1)}, bf16[2048,128]{1,0:T(8,128)(2,1)S(1)}, bf16[192,2048]{1,0:T(8,128)(2,1)S(1)}, f32[8,2048]{1,0:T(8,128)S(1)}) custom-call(s32[32]{0:T(128)S(1)} %concatenate.60.index_ref.at_ref, bf16[512,640]{1,0:T(8,128)(2,1)S(1)} %pad_maximum_fusion.refs_0_, bf16[512,512]{1,0:T(8,128)(2,1)S(1)} %pad_maximum_fusion.2.refs_1_, ...), custom_call_target="tpu_custom_call" | custom-call | tf_op jit(solution)/shard_map/pallas_call | solution.py:77
  170.6 3.5 %shard_map.44 = (bf16[2048,2048]{1,0:T(8,128)(2,1)S(1)}, bf16[2048,128]{1,0:T(8,128)(2,1)S(1)}, bf16[192,2048]{1,0:T(8,128)(2,1)S(1)}, f32[8,2048]{1,0:T(8,128)S(1)}) custom-call(s32[32]{0:T(128)S(1)} %concatenate.60.index_ref.at_ref, ...), custom_call_target="tpu_custom_call", output_to_operand_aliasing={{0}: (8, {}), {1}: (9, {}), {2}: (10, {}), {3}: (11, {})} | custom-call | tf_op jit(solution)/shard_map/pallas_call | solution.py:77
  174.1 33.3 %shard_map.45 = (bf16[32,2048]{1,0:T(8,128)(2,1)S(1)}, f32[32,128]{1,0:T(8,128)S(1)}, bf16[2048,2048]{1,0:T(8,128)(2,1)S(1)}, bf16[2048,128]{1,0:T(8,128)(2,1)S(...) custom-call(s32[32]{0:T(128)S(1)} %concatenate.60.index_ref.at_ref, ...), custom_call_target="tpu_custom_call", output_to_operand_aliasing={{2}: (5, {}), {3}: (6, {}), {4}: (7, {}), {5}: (8, {})} | custom-call | tf_op jit(solution)/shard_map/pallas_call | solution.py:77
  208.0 4.8 %collective-permute-done.33 = bf16[32,512]{1,0:T(8,128)(2,1)S(1)} collective-permute-done((bf16[32,512]{1,0:T(8,128)(2,1)S(1)}, bf16[32,512]{1,0:T(8,128)(2,1)S(1)}, u32[]{:S(2)}, u32[]{:S(2)}) %collective-permute-start.33) | collective-permute-done | bytes 32800 | tf_op jit(solution)/shard_map/ppermute | solution.py:354
  212.9 4.3 %collective-permute-done.34 = bf16[32,1024]{1,0:T(8,128)(2,1)S(1)} collective-permute-done((bf16[32,1024]{1,0:T(8,128)(2,1)S(1)}, bf16[32,1024]{1,0:T(8,128)(2,1)S(1)}, u32[]{:S(2)}, u32[]{:S(2)}) %collective-permute-start.34) | collective-permute-done | bytes 65568 | tf_op jit(solution)/shard_map/ppermute | solution.py:354
  (66 shorter events, 15.3 us)
Async XLA Ops:
  3.2 7.3 %copy-start.1 = (f32[2048,32]{0,1:T(8,128)S(1)}, f32[2048,32]{0,1:T(8,128)}, u32[]{:S(2)}) copy-start(f32[2048,32]{0,1:T(8,128)} %param.3) | copy-start | bytes 786436
  3.2 54.1 %all-to-all-start = ((bf16[64,32,512]{2,0,1:T(8,128)(2,1)}), bf16[64,32,512]{2,0,1:T(8,128)(2,1)S(1)}, u32[]{:S(2)}, u32[]{:S(2)}) async-start(bf16[64,32,512]{2,0,1:T(8,128)(2,1)} %bitcast.26), calls=%async_computation | async-start | bytes 4194304 | tf_op jit(solution)/shard_map/all_to_all | solution.py:403
  10.6 19.1 %collective-permute-start.1 = (bf16[32,2048]{1,0:T(8,128)(2,1)S(1)}, bf16[32,2048]{1,0:T(8,128)(2,1)S(1)}, u32[]{:S(2)}, u32[]{:S(2)}) collective-permute-start(bf16[32,2048]{1,0:T(8,128)(2,1)S(1)} %convert_bitcast_fusion.1), channel_id=1, source_target_pairs={{0,2},{1,3},{2,0},{3,1},{4,6},{5,7},{6,4},{7,5},{8,10},{9,11},{10,... | collective-permute-start | bytes 393224 | tf_op jit(solution)/shard_map/ppermute | solution.py:354
  29.8 29.4 %collective-permute-start.2 = (bf16[32,4096]{1,0:T(8,128)(2,1)S(1)}, bf16[32,4096]{1,0:T(8,128)(2,1)S(1)}, u32[]{:S(2)}, u32[]{:S(2)}) collective-permute-start(bf16[32,4096]{1,0:T(8,128)(2,1)S(1)} %pad_maximum_fusion.4), channel_id=1, source_target_pairs={{0,4},{1,5},{2,6},{3,7},{4,0},{5,1},{6,2},{7,3},{8,12},{9,13},{10,... | collective-permute-start | bytes 786440 | tf_op jit(solution)/shard_map/ppermute | solution.py:354
  57.3 28.8 %collective-permute-start = (bf16[2048,512]{1,0:T(8,128)(2,1)S(1)}, bf16[2048,512]{1,0:T(8,128)(2,1)}, u32[]{:S(2)}, u32[]{:S(2)}) collective-permute-start(bf16[2048,512]{1,0:T(8,128)(2,1)S(1)} %bitcast.18), channel_id=1, source_target_pairs={{0,1},{1,0},{2,3},{3,2},{4,5},{5,4},{6,7},{7,6},{8,9},{9,8},{10,11... | collective-permute-start | bytes 6291464 | tf_op jit(solution)/shard_map/ppermute | solution.py:354
  59.2 4.5 %collective-permute-start.3 = (bf16[32,8192]{1,0:T(8,128)(2,1)S(1)}, bf16[32,8192]{1,0:T(8,128)(2,1)S(1)}, u32[]{:S(2)}, u32[]{:S(2)}) collective-permute-start(bf16[32,8192]{1,0:T(8,128)(2,1)S(1)} %pad_maximum_fusion.1.near_ref), channel_id=1, source_target_pairs={{0,1},{1,0},{2,3},{3,2},{4,5},{5,4},{6,7},{7,6},{8,9},{9,8},{10,11... | collective-permute-start | bytes 1572872 | tf_op jit(solution)/shard_map/ppermute | solution.py:354
  63.7 1.6 copy-start
  66.4 1.2 collective-permute-start.4
  67.8 3.7 %collective-permute-start.5 = (bf16[32,128]{1,0:T(8,128)(2,1)S(1)}, bf16[32,128]{1,0:T(8,128)(2,1)S(1)}, u32[]{:S(2)}, u32[]{:S(2)}) collective-permute-start(bf16[32,128]{1,0:T(8,128)(2,1)S(1)} %maximum_select_fusion.4), channel_id=1, source_target_pairs={{0,2},{1,3},{2,0},{3,1},{4,6},{5,7},{6,4},{7,5},{8,10},{9,11},{10,... | collective-permute-start | bytes 24584 | tf_op jit(solution)/shard_map/ppermute | solution.py:354
  71.4 3.7 %collective-permute-start.6 = (bf16[32,256]{1,0:T(8,128)(2,1)S(1)}, bf16[32,256]{1,0:T(8,128)(2,1)S(1)}, u32[]{:S(2)}, u32[]{:S(2)}) collective-permute-start(bf16[32,256]{1,0:T(8,128)(2,1)S(1)} %maximum_select_fusion.3), channel_id=1, source_target_pairs={{0,4},{1,5},{2,6},{3,7},{4,0},{5,1},{6,2},{7,3},{8,12},{9,13},{10,... | collective-permute-start | bytes 49160 | tf_op jit(solution)/shard_map/ppermute | solution.py:354
  75.2 4.2 %collective-permute-start.7 = (bf16[32,512]{1,0:T(8,128)(2,1)S(1)}, bf16[32,512]{1,0:T(8,128)(2,1)S(1)}, u32[]{:S(2)}, u32[]{:S(2)}) collective-permute-start(bf16[32,512]{1,0:T(8,128)(2,1)S(1)} %maximum_select_fusion.2), channel_id=1, source_target_pairs={{0,8},{8,0},{16,24},{24,16},{1,9},{9,1},{17,25},{25,17},{2,10},{10... | collective-permute-start | bytes 98312 | tf_op jit(solution)/shard_map/ppermute | solution.py:354
  79.4 5.2 %collective-permute-start.8 = (bf16[32,1024]{1,0:T(8,128)(2,1)S(1)}, bf16[32,1024]{1,0:T(8,128)(2,1)S(1)}, u32[]{:S(2)}, u32[]{:S(2)}) collective-permute-start(bf16[32,1024]{1,0:T(8,128)(2,1)S(1)} %maximum_select_fusion.1), channel_id=1, source_target_pairs={{0,16},{8,24},{16,0},{24,8},{1,17},{9,25},{17,1},{25,9},{2,18},{10... | collective-permute-start | bytes 196616 | tf_op jit(solution)/shard_map/ppermute | solution.py:354
  93.8 9.7 %collective-permute-start.10 = (bf16[256,640]{1,0:T(8,128)(2,1)S(1)}, bf16[256,640]{1,0:T(8,128)(2,1)S(1)}, u32[]{:S(2)}, u32[]{:S(2)}) collective-permute-start(bf16[256,640]{1,0:T(8,128)(2,1)S(1)} %get-tuple-element.37), channel_id=1, source_target_pairs={{0,2},{1,5},{2,0},{3,7},{4,6},{5,1},{6,4},{7,3},{8,10},{9,13},{10,... | collective-permute-start | bytes 983048 | tf_op jit(solution)/shard_map/ppermute | solution.py:354
  95.8 11.1 %collective-permute-start.19 = (bf16[256,512]{1,0:T(8,128)(2,1)S(1)}, bf16[256,512]{1,0:T(8,128)(2,1)S(1)}, u32[]{:S(2)}, u32[]{:S(2)}) collective-permute-start(bf16[256,512]{1,0:T(8,128)(2,1)S(1)} %get-tuple-element.43), channel_id=1, source_target_pairs={{0,2},{1,5},{2,0},{3,7},{4,6},{5,1},{6,4},{7,3},{8,10},{9,13},{10,... | collective-permute-start | bytes 786440 | tf_op jit(solution)/shard_map/ppermute | solution.py:354
  98.7 20.7 %collective-permute-start.9 = (bf16[256,640]{1,0:T(8,128)(2,1)S(1)}, bf16[256,640]{1,0:T(8,128)(2,1)S(1)}, u32[]{:S(2)}, u32[]{:S(2)}) collective-permute-start(bf16[256,640]{1,0:T(8,128)(2,1)S(1)} %get-tuple-element.35), channel_id=1, source_target_pairs={{0,2},{1,5},{2,0},{3,7},{4,6},{5,1},{6,4},{7,3},{8,10},{9,13},{10,... | collective-permute-start | bytes 983048 | tf_op jit(solution)/shard_map/ppermute | solution.py:354
  104.1 15.3 %collective-permute-start.11 = (bf16[256,640]{1,0:T(8,128)(2,1)S(1)}, bf16[256,640]{1,0:T(8,128)(2,1)S(1)}, u32[]{:S(2)}, u32[]{:S(2)}) collective-permute-start(bf16[256,640]{1,0:T(8,128)(2,1)S(1)} %shard_map.35), channel_id=1, source_target_pairs={{0,4},{1,3},{2,6},{3,1},{4,0},{5,7},{6,2},{7,5},{8,12},{9,11},{10,... | collective-permute-start | bytes 983048 | tf_op jit(solution)/shard_map/ppermute | solution.py:354
  104.2 12.2 %collective-permute-start.18 = (bf16[256,512]{1,0:T(8,128)(2,1)S(1)}, bf16[256,512]{1,0:T(8,128)(2,1)S(1)}, u32[]{:S(2)}, u32[]{:S(2)}) collective-permute-start(bf16[256,512]{1,0:T(8,128)(2,1)S(1)} %get-tuple-element.41), channel_id=1, source_target_pairs={{0,2},{1,5},{2,0},{3,7},{4,6},{5,1},{6,4},{7,3},{8,10},{9,13},{10,... | collective-permute-start | bytes 786440 | tf_op jit(solution)/shard_map/ppermute | solution.py:354
  107.7 8.7 %collective-permute-start.20 = (bf16[256,512]{1,0:T(8,128)(2,1)S(1)}, bf16[256,512]{1,0:T(8,128)(2,1)S(1)}, u32[]{:S(2)}, u32[]{:S(2)}) collective-permute-start(bf16[256,512]{1,0:T(8,128)(2,1)S(1)} %shard_map.39), channel_id=1, source_target_pairs={{0,4},{1,3},{2,6},{3,1},{4,0},{5,7},{6,2},{7,5},{8,12},{9,11},{10,... | collective-permute-start | bytes 786440 | tf_op jit(solution)/shard_map/ppermute | solution.py:354
  117.3 5.5 %collective-permute-start.21 = (bf16[128,512]{1,0:T(8,128)(2,1)S(1)}, bf16[128,512]{1,0:T(8,128)(2,1)S(1)}, u32[]{:S(2)}, u32[]{:S(2)}) collective-permute-start(bf16[128,512]{1,0:T(8,128)(2,1)S(1)} %get-tuple-element.45), channel_id=1, source_target_pairs={{0,8},{8,0},{16,24},{24,16},{1,9},{9,1},{17,25},{25,17},{2,10},{10... | collective-permute-start | bytes 393224 | tf_op jit(solution)/shard_map/ppermute | solution.py:354
  120.1 6.7 %collective-permute-start.12 = (bf16[128,640]{1,0:T(8,128)(2,1)S(1)}, bf16[128,640]{1,0:T(8,128)(2,1)S(1)}, u32[]{:S(2)}, u32[]{:S(2)}) collective-permute-start(bf16[128,640]{1,0:T(8,128)(2,1)S(1)} %get-tuple-element.39), channel_id=1, source_target_pairs={{0,8},{8,0},{16,24},{24,16},{1,9},{9,1},{17,25},{25,17},{2,10},{10... | collective-permute-start | bytes 491528 | tf_op jit(solution)/shard_map/ppermute | solution.py:354
  123.6 8.9 %collective-permute-start.22 = (bf16[128,512]{1,0:T(8,128)(2,1)S(1)}, bf16[128,512]{1,0:T(8,128)(2,1)S(1)}, u32[]{:S(2)}, u32[]{:S(2)}) collective-permute-start(bf16[128,512]{1,0:T(8,128)(2,1)S(1)} %shard_map.41.refs_0_), channel_id=1, source_target_pairs={{0,16},{8,24},{16,0},{24,8},{1,17},{9,25},{17,1},{25,9},{2,18},{10... | collective-permute-start | bytes 393224 | tf_op jit(solution)/shard_map/ppermute | solution.py:354
  127.4 8.8 %collective-permute-start.13 = (bf16[128,640]{1,0:T(8,128)(2,1)S(1)}, bf16[128,640]{1,0:T(8,128)(2,1)S(1)}, u32[]{:S(2)}, u32[]{:S(2)}) collective-permute-start(bf16[128,640]{1,0:T(8,128)(2,1)S(1)} %shard_map.37.refs_0_), channel_id=1, source_target_pairs={{0,16},{8,24},{16,0},{24,8},{1,17},{9,25},{17,1},{25,9},{2,18},{10... | collective-permute-start | bytes 491528 | tf_op jit(solution)/shard_map/ppermute | solution.py:354
  133.2 6.1 %collective-permute-start.23 = (bf16[128,512]{1,0:T(8,128)(2,1)S(1)}, bf16[128,512]{1,0:T(8,128)(2,1)S(1)}, u32[]{:S(2)}, u32[]{:S(2)}) collective-permute-start(bf16[128,512]{1,0:T(8,128)(2,1)S(1)} %shard_map.42), channel_id=1, source_target_pairs={{0,8},{8,0},{16,24},{24,16},{1,9},{9,1},{17,25},{25,17},{2,10},{10... | collective-permute-start | bytes 393224 | tf_op jit(solution)/shard_map/ppermute | solution.py:354
  136.8 5.4 %collective-permute-start.14 = (bf16[128,640]{1,0:T(8,128)(2,1)S(1)}, bf16[128,640]{1,0:T(8,128)(2,1)S(1)}, u32[]{:S(2)}, u32[]{:S(2)}) collective-permute-start(bf16[128,640]{1,0:T(8,128)(2,1)S(1)} %shard_map.38), channel_id=1, source_target_pairs={{0,8},{8,0},{16,24},{24,16},{1,9},{9,1},{17,25},{25,17},{2,10},{10... | collective-permute-start | bytes 491528 | tf_op jit(solution)/shard_map/ppermute | solution.py:354
  139.3 9.2 %collective-permute-start.24 = (bf16[256,512]{1,0:T(8,128)(2,1)S(1)}, bf16[256,512]{1,0:T(8,128)(2,1)S(1)}, u32[]{:S(2)}, u32[]{:S(2)}) collective-permute-start(bf16[256,512]{1,0:T(8,128)(2,1)S(1)} %pad_maximum_fusion.5), channel_id=1, source_target_pairs={{0,4},{1,3},{2,6},{3,1},{4,0},{5,7},{6,2},{7,5},{8,12},{9,11},{10,... | collective-permute-start | bytes 786440 | tf_op jit(solution)/shard_map/ppermute | solution.py:354
  142.2 9.9 %collective-permute-start.15 = (bf16[256,640]{1,0:T(8,128)(2,1)S(1)}, bf16[256,640]{1,0:T(8,128)(2,1)S(1)}, u32[]{:S(2)}, u32[]{:S(2)}) collective-permute-start(bf16[256,640]{1,0:T(8,128)(2,1)S(1)} %pad_maximum_fusion.3), channel_id=1, source_target_pairs={{0,4},{1,3},{2,6},{3,1},{4,0},{5,7},{6,2},{7,5},{8,12},{9,11},{10,... | collective-permute-start | bytes 983048 | tf_op jit(solution)/shard_map/ppermute | solution.py:354
  142.2 12.1 %collective-permute-start.28 = (bf16[256,512]{1,0:T(8,128)(2,1)S(1)}, bf16[256,512]{1,0:T(8,128)(2,1)S(1)}, u32[]{:S(2)}, u32[]{:S(2)}) collective-permute-start(bf16[256,512]{1,0:T(8,128)(2,1)S(1)} %pad_maximum_fusion.5), channel_id=1, source_target_pairs={{0,2},{1,5},{2,0},{3,7},{4,6},{5,1},{6,4},{7,3},{8,10},{9,13},{10,... | collective-permute-start | bytes 786440 | tf_op jit(solution)/shard_map/ppermute | solution.py:354
  148.6 17.1 %collective-permute-start.32 = (bf16[512,512]{1,0:T(8,128)(2,1)S(1)}, bf16[512,512]{1,0:T(8,128)(2,1)S(1)}, u32[]{:S(2)}, u32[]{:S(2)}) collective-permute-start(bf16[512,512]{1,0:T(8,128)(2,1)S(1)} %pad_maximum_fusion.2.refs_1_), channel_id=1, source_target_pairs={{0,1},{1,0},{2,3},{3,2},{4,5},{5,4},{6,7},{7,6},{8,9},{9,8},{10,11... | collective-permute-start | bytes 1572872 | tf_op jit(solution)/shard_map/ppermute | solution.py:354
  152.1 14.1 %collective-permute-start.31 = (bf16[512,640]{1,0:T(8,128)(2,1)S(1)}, bf16[512,640]{1,0:T(8,128)(2,1)S(1)}, u32[]{:S(2)}, u32[]{:S(2)}) collective-permute-start(bf16[512,640]{1,0:T(8,128)(2,1)S(1)} %pad_maximum_fusion.refs_0_), channel_id=1, source_target_pairs={{0,1},{1,0},{2,3},{3,2},{4,5},{5,4},{6,7},{7,6},{8,9},{9,8},{10,11... | collective-permute-start | bytes 1966088 | tf_op jit(solution)/shard_map/ppermute | solution.py:354
  152.2 7.1 %collective-permute-start.27 = (bf16[256,640]{1,0:T(8,128)(2,1)S(1)}, bf16[256,640]{1,0:T(8,128)(2,1)S(1)}, u32[]{:S(2)}, u32[]{:S(2)}) collective-permute-start(bf16[256,640]{1,0:T(8,128)(2,1)S(1)} %pad_maximum_fusion.3), channel_id=1, source_target_pairs={{0,2},{1,5},{2,0},{3,7},{4,6},{5,1},{6,4},{7,3},{8,10},{9,13},{10,... | collective-permute-start | bytes 983048 | tf_op jit(solution)/shard_map/ppermute | solution.py:354
  152.8 10.1 %collective-permute-start.16 = (bf16[256,640]{1,0:T(8,128)(2,1)S(1)}, bf16[256,640]{1,0:T(8,128)(2,1)S(1)}, u32[]{:S(2)}, u32[]{:S(2)}) collective-permute-start(bf16[256,640]{1,0:T(8,128)(2,1)S(1)} %collective-permute-done.15), channel_id=1, source_target_pairs={{0,2},{1,5},{2,0},{3,7},{4,6},{5,1},{6,4},{7,3},{8,10},{9,13},{10,... | collective-permute-start | bytes 983048 | tf_op jit(solution)/shard_map/ppermute | solution.py:354
  154.3 11.4 %collective-permute-start.25 = (bf16[256,512]{1,0:T(8,128)(2,1)S(1)}, bf16[256,512]{1,0:T(8,128)(2,1)S(1)}, u32[]{:S(2)}, u32[]{:S(2)}) collective-permute-start(bf16[256,512]{1,0:T(8,128)(2,1)S(1)} %collective-permute-done.24), channel_id=1, source_target_pairs={{0,2},{1,5},{2,0},{3,7},{4,6},{5,1},{6,4},{7,3},{8,10},{9,13},{10,... | collective-permute-start | bytes 786440 | tf_op jit(solution)/shard_map/ppermute | solution.py:354
  159.3 11.2 %collective-permute-start.29 = (bf16[256,640]{1,0:T(8,128)(2,1)S(1)}, bf16[256,640]{1,0:T(8,128)(2,1)S(1)}, u32[]{:S(2)}, u32[]{:S(2)}) collective-permute-start(bf16[256,640]{1,0:T(8,128)(2,1)S(1)} %collective-permute-done.27.refs_0_), channel_id=1, source_target_pairs={{0,1},{1,0},{2,3},{3,2},{4,5},{5,4},{6,7},{7,6},{8,9},{9,8},{10,11... | collective-permute-start | bytes 983048 | tf_op jit(solution)/shard_map/ppermute | solution.py:354
  162.9 11.2 %collective-permute-start.17 = (bf16[256,640]{1,0:T(8,128)(2,1)S(1)}, bf16[256,640]{1,0:T(8,128)(2,1)S(1)}, u32[]{:S(2)}, u32[]{:S(2)}) collective-permute-start(bf16[256,640]{1,0:T(8,128)(2,1)S(1)} %collective-permute-done.16.refs_4_), channel_id=1, source_target_pairs={{0,1},{1,0},{2,3},{3,2},{4,5},{5,4},{6,7},{7,6},{8,9},{9,8},{10,11... | collective-permute-start | bytes 983048 | tf_op jit(solution)/shard_map/ppermute | solution.py:354
  165.7 4.9 %collective-permute-start.30 = (bf16[256,512]{1,0:T(8,128)(2,1)S(1)}, bf16[256,512]{1,0:T(8,128)(2,1)S(1)}, u32[]{:S(2)}, u32[]{:S(2)}) collective-permute-start(bf16[256,512]{1,0:T(8,128)(2,1)S(1)} %collective-permute-done.28.refs_1_), channel_id=1, source_target_pairs={{0,1},{1,0},{2,3},{3,2},{4,5},{5,4},{6,7},{7,6},{8,9},{9,8},{10,11... | collective-permute-start | bytes 786440 | tf_op jit(solution)/shard_map/ppermute | solution.py:354
  165.7 8.4 %collective-permute-start.26 = (bf16[256,512]{1,0:T(8,128)(2,1)S(1)}, bf16[256,512]{1,0:T(8,128)(2,1)S(1)}, u32[]{:S(2)}, u32[]{:S(2)}) collective-permute-start(bf16[256,512]{1,0:T(8,128)(2,1)S(1)} %collective-permute-done.25.refs_5_), channel_id=1, source_target_pairs={{0,1},{1,0},{2,3},{3,2},{4,5},{5,4},{6,7},{7,6},{8,9},{9,8},{10,11... | collective-permute-start | bytes 786440 | tf_op jit(solution)/shard_map/ppermute | solution.py:354
  208.0 4.8 %collective-permute-start.33 = (bf16[32,512]{1,0:T(8,128)(2,1)S(1)}, bf16[32,512]{1,0:T(8,128)(2,1)S(1)}, u32[]{:S(2)}, u32[]{:S(2)}) collective-permute-start(bf16[32,512]{1,0:T(8,128)(2,1)S(1)} %shard_map.46), channel_id=1, source_target_pairs={{0,16},{8,24},{16,0},{24,8},{1,17},{9,25},{17,1},{25,9},{2,18},{10... | collective-permute-start | bytes 98312 | tf_op jit(solution)/shard_map/ppermute | solution.py:354
  212.9 4.3 %collective-permute-start.34 = (bf16[32,1024]{1,0:T(8,128)(2,1)S(1)}, bf16[32,1024]{1,0:T(8,128)(2,1)S(1)}, u32[]{:S(2)}, u32[]{:S(2)}) collective-permute-start(bf16[32,1024]{1,0:T(8,128)(2,1)S(1)} %pad_maximum_fusion.6), channel_id=1, source_target_pairs={{0,8},{8,0},{16,24},{24,16},{1,9},{9,1},{17,25},{25,17},{2,10},{10... | collective-permute-start | bytes 196616 | tf_op jit(solution)/shard_map/ppermute | solution.py:354

commit v11 on v10

--- a/solution.py
+++ b/solution.py
@@ -448,7 +448,8 @@
         )(index, block, other, left, right)
 
     sent = [form(0), form(1)]
-    held = [form(2), form(3)]
+    held = [form(2)]
+    held.append(form(3))
     swap = xor_pix(1)
     near, far, over_a, far_a, over_ab, far_ab = ([None, None] for _ in range(6))
     for e in (0, 1):
@@ -457,10 +458,13 @@
         (send,) = add((held[0][e], passed))
         recv = flip(send, "pix", second)
         send, keep = add((held[1][e], kept, recv), (HALVES, HALVES + 1))
-        (share,) = add((keep, flip(send, "samp", xor_samp(1))))
-        (share,) = add((share, flip(share, "samp", xor_samp(2))))
-
-        share = jnp.concatenate([share, flip(share, "samp", xor_samp(1))], axis=0)
+        recv = flip(send, "samp", xor_samp(1))
+        (share,) = add((keep, recv))
+        recv = flip(share, "samp", xor_samp(2))
+        (share,) = add((share, recv))
+
+        recv = flip(share, "samp", xor_samp(1))
+        share = jnp.concatenate([share, recv], axis=0)
         over_a[e] = flip(share, "pix", first)
         over_b = flip(share, "pix", second)
         over_ab[e] = flip(over_b, "pix", first)

time: 218 us -> 218 us (level)
  no operation moved by 1% of the time
where the time goes in v11:
time: 218 us
  waiting for transfers between devices  108 us (50%)
  Pallas kernels  66 us (30%)
  starting transfers between devices  37.7 us (17%)
  local copies, waits for them, and re-layouts  4.9 us (2%)
    ppermute x35, waiting for transfers between devices, flip(): return lax.ppermute(x, axes, perm)  81.8 us
    pallas_call x19, Pallas kernels, kernel_call(): return lambda *args: call(*map(place, args, in_specs))  66 us
    ppermute x35, starting transfers between devices, flip(): return lax.ppermute(x, axes, perm)  30.4 us
    all_to_all x1, waiting for transfers between devices, sample_space(): lax.all_to_all(stamps, ('pix', 'samp'), split_axis=1, concat_axis=0, tile...  26 us
    all_to_all x1, starting transfers between devices, sample_space(): lax.all_to_all(stamps, ('pix', 'samp'), split_axis=1, concat_axis=0, tile...  7.33 us
  transfers between devices with their start and end apart: 36, of which 23 were waited for; matrix products, arithmetic and copies ran while one was open for 0% of the time, Pallas kernels for 11%

profile of v11, /device:TPU:0, one launch (start us, length us, event | category | flops | bytes accessed | tf_op | source)
XLA Modules:
  0.0 217.9 jit_solution(7380942419174703652)
XLA Ops:
  0.0 3.2 %copy.14 = bf16[8,32,8,512]{3,2,0,1:T(8,128)(2,1)} copy(bf16[8,32,8,512]{3,2,1,0:T(8,128)(2,1)} %bitcast.25) | data formatting | bytes 4194304 | tf_op jit(solution)/shard_map/all_to_all | solution.py:403
  3.2 7.3 %all-to-all-start = ((bf16[64,32,512]{2,0,1:T(8,128)(2,1)}), bf16[64,32,512]{2,0,1:T(8,128)(2,1)S(1)}, u32[]{:S(2)}, u32[]{:S(2)}) async-start(bf16[64,32,512]{2,0,1:T(8,128)(2,1)} %bitcast.26), calls=%async_computation | async-start | bytes 4194304 | tf_op jit(solution)/shard_map/all_to_all | solution.py:403
  10.6 1.8 collective-permute-start.1
  12.4 17.3 %collective-permute-done.1 = bf16[32,2048]{1,0:T(8,128)(2,1)S(1)} collective-permute-done((bf16[32,2048]{1,0:T(8,128)(2,1)S(1)}, bf16[32,2048]{1,0:T(8,128)(2,1)S(1)}, u32[]{:S(2)}, u32[]{:S(2)}) %collective-permute-start.1) | collective-permute-done | bytes 131104 | tf_op jit(solution)/shard_map/ppermute | solution.py:354
  29.8 1.5 collective-permute-start.2
  31.3 26.0 %all-to-all-done = bf16[64,32,512]{2,0,1:T(8,128)(2,1)S(1)} async-done(((bf16[64,32,512]{2,0,1:T(8,128)(2,1)}), bf16[64,32,512]{2,0,1:T(8,128)(2,1)S(1)}, u32[]{:S(2)}, u32[]{:S(2)}) %all-to-all-start) | async-done | bytes 2097184 | tf_op jit(solution)/shard_map/all_to_all | solution.py:403
  57.3 1.8 collective-permute-start
  59.4 4.3 %collective-permute-done.3.far_ref = bf16[32,8192]{1,0:T(8,128)(2,1)S(1)} collective-permute-done((bf16[32,8192]{1,0:T(8,128)(2,1)S(1)}, bf16[32,8192]{1,0:T(8,128)(2,1)S(1)}, u32[]{:S(2)}, u32[]{:S(2)}) %collective-permute-start.3) | collective-permute-done | bytes 524320 | tf_op jit(solution)/shard_map/ppermute | solution.py:354
  63.7 1.6 copy-done
  65.2 1.2 shard_map.28
  67.8 1.5 collective-permute-start.5
  69.3 2.1 collective-permute-done.5
  71.4 1.5 collective-permute-start.6
  72.9 2.2 %collective-permute-done.6 = bf16[32,256]{1,0:T(8,128)(2,1)S(1)} collective-permute-done((bf16[32,256]{1,0:T(8,128)(2,1)S(1)}, bf16[32,256]{1,0:T(8,128)(2,1)S(1)}, u32[]{:S(2)}, u32[]{:S(2)}) %collective-permute-start.6) | collective-permute-done | bytes 16416 | tf_op jit(solution)/shard_map/ppermute | solution.py:354
  75.2 2.3 %collective-permute-start.7 = (bf16[32,512]{1,0:T(8,128)(2,1)S(1)}, bf16[32,512]{1,0:T(8,128)(2,1)S(1)}, u32[]{:S(2)}, u32[]{:S(2)}) collective-permute-start(bf16[32,512]{1,0:T(8,128)(2,1)S(1)} %maximum_select_fusion.2), channel_id=1, source_target_pairs={{0,8},{8,0},{16,24},{24,16},{1,9},{9,1},{17,25},{25,17},{2,10},{10... | collective-permute-start | bytes 98312 | tf_op jit(solution)/shard_map/ppermute | solution.py:354
  77.5 1.9 collective-permute-done.7
  80.6 4.0 %collective-permute-done.8 = bf16[32,1024]{1,0:T(8,128)(2,1)S(1)} collective-permute-done((bf16[32,1024]{1,0:T(8,128)(2,1)S(1)}, bf16[32,1024]{1,0:T(8,128)(2,1)S(1)}, u32[]{:S(2)}, u32[]{:S(2)}) %collective-permute-start.8) | collective-permute-done | bytes 65568 | tf_op jit(solution)/shard_map/ppermute | solution.py:354
  84.7 1.4 shard_map.29
  86.1 4.9 %shard_map.30 = (bf16[192,2048]{1,0:T(8,128)(2,1)S(1)}, bf16[192,2048]{1,0:T(8,128)(2,1)S(1)}) custom-call(bf16[2048,512]{1,0:T(8,128)(2,1)S(1)} %bitcast.19, bf16[2048,512]{1,0:T(8,128)(2,1)} %collective-permute-done.other_ref, f32[32,2048]{1,0:T(8,128)S(1)} %get-tuple-element.31.q_ref.refs_4_.refs_6_), custom_call_target="tpu_custom_call" | custom-call | tf_op jit(solution)/shard_map/pallas_call | solution.py:77
  91.0 2.8 %shard_map.34 = (bf16[256,640]{1,0:T(8,128)(2,1)S(1)}, bf16[256,512]{1,0:T(8,128)(2,1)S(1)}) custom-call(s32[32]{0:T(128)S(1)} %concatenate.60.index_ref.at_ref, bf16[2048,512]{1,0:T(8,128)(2,1)S(1)} %bitcast.20, bf16[2048,512]{1,0:T(8,128)(2,1)} %collective-permute-done.other_ref, bf16[192,2048]{1,0:T(8,128)(2,1)S(1)} %get-tuple-element.32.left, ...), custom_call_target="tpu_custom_call" | custom-call | tf_op jit(solution)/shard_map/pallas_call | solution.py:77
  93.8 2.0 collective-permute-start.10
  95.9 2.8 %shard_map.32 = (bf16[256,640]{1,0:T(8,128)(2,1)S(1)}, bf16[256,512]{1,0:T(8,128)(2,1)S(1)}) custom-call(s32[32]{0:T(128)S(1)} %concatenate.60.index_ref.at_ref, bf16[2048,512]{1,0:T(8,128)(2,1)S(1)} %bitcast.21, bf16[2048,512]{1,0:T(8,128)(2,1)} %collective-permute-done.other_ref, bf16[192,2048]{1,0:T(8,128)(2,1)S(1)} %get-tuple-element.32.left, ...), custom_call_target="tpu_custom_call" | custom-call | tf_op jit(solution)/shard_map/pallas_call | solution.py:77
  98.7 2.0 collective-permute-start.9
  100.7 2.8 %shard_map.33 = (bf16[256,640]{1,0:T(8,128)(2,1)S(1)}, bf16[256,512]{1,0:T(8,128)(2,1)S(1)}) custom-call(s32[32]{0:T(128)S(1)} %concatenate.60.index_ref.at_ref, bf16[2048,512]{1,0:T(8,128)(2,1)S(1)} %bitcast.22, bf16[2048,512]{1,0:T(8,128)(2,1)} %collective-permute-done.other_ref, bf16[192,2048]{1,0:T(8,128)(2,1)S(1)} %get-tuple-element.32.left, ...), custom_call_target="tpu_custom_call" | custom-call | tf_op jit(solution)/shard_map/pallas_call | solution.py:77
  104.2 1.3 collective-permute-start.18
  105.5 1.4 collective-permute-done.19.refs_1_
  108.8 2.8 %shard_map.31 = (bf16[256,640]{1,0:T(8,128)(2,1)S(1)}, bf16[256,512]{1,0:T(8,128)(2,1)S(1)}) custom-call(s32[32]{0:T(128)S(1)} %concatenate.60.index_ref.at_ref, bf16[2048,512]{1,0:T(8,128)(2,1)S(1)} %bitcast.23, bf16[2048,512]{1,0:T(8,128)(2,1)} %collective-permute-done.other_ref, bf16[192,2048]{1,0:T(8,128)(2,1)S(1)} %get-tuple-element.32.left, ...), custom_call_target="tpu_custom_call" | custom-call | tf_op jit(solution)/shard_map/pallas_call | solution.py:77
  111.6 4.8 %collective-permute-done.18.refs_1_ = bf16[256,512]{1,0:T(8,128)(2,1)S(1)} collective-permute-done((bf16[256,512]{1,0:T(8,128)(2,1)S(1)}, bf16[256,512]{1,0:T(8,128)(2,1)S(1)}, u32[]{:S(2)}, u32[]{:S(2)}) %collective-permute-start.18) | collective-permute-done | bytes 262176 | tf_op jit(solution)/shard_map/ppermute | solution.py:354
  117.3 2.1 collective-permute-start.21
  120.2 2.7 %collective-permute-done.21.refs_1_ = bf16[128,512]{1,0:T(8,128)(2,1)S(1)} collective-permute-done((bf16[128,512]{1,0:T(8,128)(2,1)S(1)}, bf16[128,512]{1,0:T(8,128)(2,1)S(1)}, u32[]{:S(2)}, u32[]{:S(2)}) %collective-permute-start.21) | collective-permute-done | bytes 131104 | tf_op jit(solution)/shard_map/ppermute | solution.py:354
  124.8 2.0 collective-permute-done.12.refs_1_
  127.4 1.5 collective-permute-start.13
  128.8 3.7 %collective-permute-done.22.refs_1_ = bf16[128,512]{1,0:T(8,128)(2,1)S(1)} collective-permute-done((bf16[128,512]{1,0:T(8,128)(2,1)S(1)}, bf16[128,512]{1,0:T(8,128)(2,1)S(1)}, u32[]{:S(2)}, u32[]{:S(2)}) %collective-permute-start.22) | collective-permute-done | bytes 131104 | tf_op jit(solution)/shard_map/ppermute | solution.py:354
  134.0 2.1 collective-permute-done.13.refs_1_
  136.8 2.5 %collective-permute-done.23 = bf16[128,512]{1,0:T(8,128)(2,1)S(1)} collective-permute-done((bf16[128,512]{1,0:T(8,128)(2,1)S(1)}, bf16[128,512]{1,0:T(8,128)(2,1)S(1)}, u32[]{:S(2)}, u32[]{:S(2)}) %collective-permute-start.23) | collective-permute-done | bytes 131104 | tf_op jit(solution)/shard_map/ppermute | solution.py:354
  139.4 2.8 %collective-permute-done.14 = bf16[128,640]{1,0:T(8,128)(2,1)S(1)} collective-permute-done((bf16[128,640]{1,0:T(8,128)(2,1)S(1)}, bf16[128,640]{1,0:T(8,128)(2,1)S(1)}, u32[]{:S(2)}, u32[]{:S(2)}) %collective-permute-start.14) | collective-permute-done | bytes 163872 | tf_op jit(solution)/shard_map/ppermute | solution.py:354
  142.2 2.5 %collective-permute-start.28 = (bf16[256,512]{1,0:T(8,128)(2,1)S(1)}, bf16[256,512]{1,0:T(8,128)(2,1)S(1)}, u32[]{:S(2)}, u32[]{:S(2)}) collective-permute-start(bf16[256,512]{1,0:T(8,128)(2,1)S(1)} %pad_maximum_fusion.5), channel_id=1, source_target_pairs={{0,2},{1,5},{2,0},{3,7},{4,6},{5,1},{6,4},{7,3},{8,10},{9,13},{10,... | collective-permute-start | bytes 786440 | tf_op jit(solution)/shard_map/ppermute | solution.py:354
  144.7 3.8 %collective-permute-done.24 = bf16[256,512]{1,0:T(8,128)(2,1)S(1)} collective-permute-done((bf16[256,512]{1,0:T(8,128)(2,1)S(1)}, bf16[256,512]{1,0:T(8,128)(2,1)S(1)}, u32[]{:S(2)}, u32[]{:S(2)}) %collective-permute-start.24) | collective-permute-done | bytes 262176 | tf_op jit(solution)/shard_map/ppermute | solution.py:354
  148.6 3.4 %collective-permute-done.15 = bf16[256,640]{1,0:T(8,128)(2,1)S(1)} collective-permute-done((bf16[256,640]{1,0:T(8,128)(2,1)S(1)}, bf16[256,640]{1,0:T(8,128)(2,1)S(1)}, u32[]{:S(2)}, u32[]{:S(2)}) %collective-permute-start.15) | collective-permute-done | bytes 327712 | tf_op jit(solution)/shard_map/ppermute | solution.py:354
  152.8 1.5 collective-permute-start.16
  154.8 4.5 %collective-permute-done.27.refs_0_ = bf16[256,640]{1,0:T(8,128)(2,1)S(1)} collective-permute-done((bf16[256,640]{1,0:T(8,128)(2,1)S(1)}, bf16[256,640]{1,0:T(8,128)(2,1)S(1)}, u32[]{:S(2)}, u32[]{:S(2)}) %collective-permute-start.27) | collective-permute-done | bytes 327712 | tf_op jit(solution)/shard_map/ppermute | solution.py:354
  159.3 3.5 %collective-permute-done.16.refs_4_ = bf16[256,640]{1,0:T(8,128)(2,1)S(1)} collective-permute-done((bf16[256,640]{1,0:T(8,128)(2,1)S(1)}, bf16[256,640]{1,0:T(8,128)(2,1)S(1)}, u32[]{:S(2)}, u32[]{:S(2)}) %collective-permute-start.16) | collective-permute-done | bytes 327712 | tf_op jit(solution)/shard_map/ppermute | solution.py:354
  162.9 2.8 %collective-permute-done.25.refs_5_ = bf16[256,512]{1,0:T(8,128)(2,1)S(1)} collective-permute-done((bf16[256,512]{1,0:T(8,128)(2,1)S(1)}, bf16[256,512]{1,0:T(8,128)(2,1)S(1)}, u32[]{:S(2)}, u32[]{:S(2)}) %collective-permute-start.25) | collective-permute-done | bytes 262176 | tf_op jit(solution)/shard_map/ppermute | solution.py:354
  166.2 4.4 %shard_map.43 = (bf16[2048,2048]{1,0:T(8,128)(2,1)S(1)}, bf16[2048,128]{1,0:T(8,128)(2,1)S(1)}, bf16[192,2048]{1,0:T(8,128)(2,1)S(1)}, f32[8,2048]{1,0:T(8,128)S(1)}) custom-call(s32[32]{0:T(128)S(1)} %concatenate.60.index_ref.at_ref, bf16[512,640]{1,0:T(8,128)(2,1)S(1)} %pad_maximum_fusion.refs_0_, bf16[512,512]{1,0:T(8,128)(2,1)S(1)} %pad_maximum_fusion.2.refs_1_, ...), custom_call_target="tpu_custom_call" | custom-call | tf_op jit(solution)/shard_map/pallas_call | solution.py:77
  170.6 3.5 %shard_map.44 = (bf16[2048,2048]{1,0:T(8,128)(2,1)S(1)}, bf16[2048,128]{1,0:T(8,128)(2,1)S(1)}, bf16[192,2048]{1,0:T(8,128)(2,1)S(1)}, f32[8,2048]{1,0:T(8,128)S(1)}) custom-call(s32[32]{0:T(128)S(1)} %concatenate.60.index_ref.at_ref, ...), custom_call_target="tpu_custom_call", output_to_operand_aliasing={{0}: (8, {}), {1}: (9, {}), {2}: (10, {}), {3}: (11, {})} | custom-call | tf_op jit(solution)/shard_map/pallas_call | solution.py:77
  174.1 33.3 %shard_map.45 = (bf16[32,2048]{1,0:T(8,128)(2,1)S(1)}, f32[32,128]{1,0:T(8,128)S(1)}, bf16[2048,2048]{1,0:T(8,128)(2,1)S(1)}, bf16[2048,128]{1,0:T(8,128)(2,1)S(...) custom-call(s32[32]{0:T(128)S(1)} %concatenate.60.index_ref.at_ref, ...), custom_call_target="tpu_custom_call", output_to_operand_aliasing={{2}: (5, {}), {3}: (6, {}), {4}: (7, {}), {5}: (8, {})} | custom-call | tf_op jit(solution)/shard_map/pallas_call | solution.py:77
  208.0 4.8 %collective-permute-done.33 = bf16[32,512]{1,0:T(8,128)(2,1)S(1)} collective-permute-done((bf16[32,512]{1,0:T(8,128)(2,1)S(1)}, bf16[32,512]{1,0:T(8,128)(2,1)S(1)}, u32[]{:S(2)}, u32[]{:S(2)}) %collective-permute-start.33) | collective-permute-done | bytes 32800 | tf_op jit(solution)/shard_map/ppermute | solution.py:354
  212.9 4.3 %collective-permute-done.34 = bf16[32,1024]{1,0:T(8,128)(2,1)S(1)} collective-permute-done((bf16[32,1024]{1,0:T(8,128)(2,1)S(1)}, bf16[32,1024]{1,0:T(8,128)(2,1)S(1)}, u32[]{:S(2)}, u32[]{:S(2)}) %collective-permute-start.34) | collective-permute-done | bytes 65568 | tf_op jit(solution)/shard_map/ppermute | solution.py:354
  (66 shorter events, 15.3 us)
Async XLA Ops:
  3.2 7.3 %copy-start.1 = (f32[2048,32]{0,1:T(8,128)S(1)}, f32[2048,32]{0,1:T(8,128)}, u32[]{:S(2)}) copy-start(f32[2048,32]{0,1:T(8,128)} %param.3) | copy-start | bytes 786436
  3.2 54.1 %all-to-all-start = ((bf16[64,32,512]{2,0,1:T(8,128)(2,1)}), bf16[64,32,512]{2,0,1:T(8,128)(2,1)S(1)}, u32[]{:S(2)}, u32[]{:S(2)}) async-start(bf16[64,32,512]{2,0,1:T(8,128)(2,1)} %bitcast.26), calls=%async_computation | async-start | bytes 4194304 | tf_op jit(solution)/shard_map/all_to_all | solution.py:403
  10.6 19.1 %collective-permute-start.1 = (bf16[32,2048]{1,0:T(8,128)(2,1)S(1)}, bf16[32,2048]{1,0:T(8,128)(2,1)S(1)}, u32[]{:S(2)}, u32[]{:S(2)}) collective-permute-start(bf16[32,2048]{1,0:T(8,128)(2,1)S(1)} %convert_bitcast_fusion.1), channel_id=1, source_target_pairs={{0,2},{1,3},{2,0},{3,1},{4,6},{5,7},{6,4},{7,5},{8,10},{9,11},{10,... | collective-permute-start | bytes 393224 | tf_op jit(solution)/shard_map/ppermute | solution.py:354
  29.8 29.4 %collective-permute-start.2 = (bf16[32,4096]{1,0:T(8,128)(2,1)S(1)}, bf16[32,4096]{1,0:T(8,128)(2,1)S(1)}, u32[]{:S(2)}, u32[]{:S(2)}) collective-permute-start(bf16[32,4096]{1,0:T(8,128)(2,1)S(1)} %pad_maximum_fusion.4), channel_id=1, source_target_pairs={{0,4},{1,5},{2,6},{3,7},{4,0},{5,1},{6,2},{7,3},{8,12},{9,13},{10,... | collective-permute-start | bytes 786440 | tf_op jit(solution)/shard_map/ppermute | solution.py:354
  57.3 28.8 %collective-permute-start = (bf16[2048,512]{1,0:T(8,128)(2,1)S(1)}, bf16[2048,512]{1,0:T(8,128)(2,1)}, u32[]{:S(2)}, u32[]{:S(2)}) collective-permute-start(bf16[2048,512]{1,0:T(8,128)(2,1)S(1)} %bitcast.18), channel_id=1, source_target_pairs={{0,1},{1,0},{2,3},{3,2},{4,5},{5,4},{6,7},{7,6},{8,9},{9,8},{10,11... | collective-permute-start | bytes 6291464 | tf_op jit(solution)/shard_map/ppermute | solution.py:354
  59.2 4.5 %collective-permute-start.3 = (bf16[32,8192]{1,0:T(8,128)(2,1)S(1)}, bf16[32,8192]{1,0:T(8,128)(2,1)S(1)}, u32[]{:S(2)}, u32[]{:S(2)}) collective-permute-start(bf16[32,8192]{1,0:T(8,128)(2,1)S(1)} %pad_maximum_fusion.1.near_ref), channel_id=1, source_target_pairs={{0,1},{1,0},{2,3},{3,2},{4,5},{5,4},{6,7},{7,6},{8,9},{9,8},{10,11... | collective-permute-start | bytes 1572872 | tf_op jit(solution)/shard_map/ppermute | solution.py:354
  63.7 1.6 copy-start
  66.4 1.2 collective-permute-start.4
  67.8 3.7 %collective-permute-start.5 = (bf16[32,128]{1,0:T(8,128)(2,1)S(1)}, bf16[32,128]{1,0:T(8,128)(2,1)S(1)}, u32[]{:S(2)}, u32[]{:S(2)}) collective-permute-start(bf16[32,128]{1,0:T(8,128)(2,1)S(1)} %maximum_select_fusion.4), channel_id=1, source_target_pairs={{0,2},{1,3},{2,0},{3,1},{4,6},{5,7},{6,4},{7,5},{8,10},{9,11},{10,... | collective-permute-start | bytes 24584 | tf_op jit(solution)/shard_map/ppermute | solution.py:354
  71.4 3.7 %collective-permute-start.6 = (bf16[32,256]{1,0:T(8,128)(2,1)S(1)}, bf16[32,256]{1,0:T(8,128)(2,1)S(1)}, u32[]{:S(2)}, u32[]{:S(2)}) collective-permute-start(bf16[32,256]{1,0:T(8,128)(2,1)S(1)} %maximum_select_fusion.3), channel_id=1, source_target_pairs={{0,4},{1,5},{2,6},{3,7},{4,0},{5,1},{6,2},{7,3},{8,12},{9,13},{10,... | collective-permute-start | bytes 49160 | tf_op jit(solution)/shard_map/ppermute | solution.py:354
  75.2 4.2 %collective-permute-start.7 = (bf16[32,512]{1,0:T(8,128)(2,1)S(1)}, bf16[32,512]{1,0:T(8,128)(2,1)S(1)}, u32[]{:S(2)}, u32[]{:S(2)}) collective-permute-start(bf16[32,512]{1,0:T(8,128)(2,1)S(1)} %maximum_select_fusion.2), channel_id=1, source_target_pairs={{0,8},{8,0},{16,24},{24,16},{1,9},{9,1},{17,25},{25,17},{2,10},{10... | collective-permute-start | bytes 98312 | tf_op jit(solution)/shard_map/ppermute | solution.py:354
  79.4 5.2 %collective-permute-start.8 = (bf16[32,1024]{1,0:T(8,128)(2,1)S(1)}, bf16[32,1024]{1,0:T(8,128)(2,1)S(1)}, u32[]{:S(2)}, u32[]{:S(2)}) collective-permute-start(bf16[32,1024]{1,0:T(8,128)(2,1)S(1)} %maximum_select_fusion.1), channel_id=1, source_target_pairs={{0,16},{8,24},{16,0},{24,8},{1,17},{9,25},{17,1},{25,9},{2,18},{10... | collective-permute-start | bytes 196616 | tf_op jit(solution)/shard_map/ppermute | solution.py:354
  93.8 9.7 %collective-permute-start.10 = (bf16[256,640]{1,0:T(8,128)(2,1)S(1)}, bf16[256,640]{1,0:T(8,128)(2,1)S(1)}, u32[]{:S(2)}, u32[]{:S(2)}) collective-permute-start(bf16[256,640]{1,0:T(8,128)(2,1)S(1)} %get-tuple-element.37), channel_id=1, source_target_pairs={{0,2},{1,5},{2,0},{3,7},{4,6},{5,1},{6,4},{7,3},{8,10},{9,13},{10,... | collective-permute-start | bytes 983048 | tf_op jit(solution)/shard_map/ppermute | solution.py:354
  95.8 11.1 %collective-permute-start.19 = (bf16[256,512]{1,0:T(8,128)(2,1)S(1)}, bf16[256,512]{1,0:T(8,128)(2,1)S(1)}, u32[]{:S(2)}, u32[]{:S(2)}) collective-permute-start(bf16[256,512]{1,0:T(8,128)(2,1)S(1)} %get-tuple-element.43), channel_id=1, source_target_pairs={{0,2},{1,5},{2,0},{3,7},{4,6},{5,1},{6,4},{7,3},{8,10},{9,13},{10,... | collective-permute-start | bytes 786440 | tf_op jit(solution)/shard_map/ppermute | solution.py:354
  98.7 20.7 %collective-permute-start.9 = (bf16[256,640]{1,0:T(8,128)(2,1)S(1)}, bf16[256,640]{1,0:T(8,128)(2,1)S(1)}, u32[]{:S(2)}, u32[]{:S(2)}) collective-permute-start(bf16[256,640]{1,0:T(8,128)(2,1)S(1)} %get-tuple-element.35), channel_id=1, source_target_pairs={{0,2},{1,5},{2,0},{3,7},{4,6},{5,1},{6,4},{7,3},{8,10},{9,13},{10,... | collective-permute-start | bytes 983048 | tf_op jit(solution)/shard_map/ppermute | solution.py:354
  104.1 15.3 %collective-permute-start.11 = (bf16[256,640]{1,0:T(8,128)(2,1)S(1)}, bf16[256,640]{1,0:T(8,128)(2,1)S(1)}, u32[]{:S(2)}, u32[]{:S(2)}) collective-permute-start(bf16[256,640]{1,0:T(8,128)(2,1)S(1)} %shard_map.35), channel_id=1, source_target_pairs={{0,4},{1,3},{2,6},{3,1},{4,0},{5,7},{6,2},{7,5},{8,12},{9,11},{10,... | collective-permute-start | bytes 983048 | tf_op jit(solution)/shard_map/ppermute | solution.py:354
  104.2 12.2 %collective-permute-start.18 = (bf16[256,512]{1,0:T(8,128)(2,1)S(1)}, bf16[256,512]{1,0:T(8,128)(2,1)S(1)}, u32[]{:S(2)}, u32[]{:S(2)}) collective-permute-start(bf16[256,512]{1,0:T(8,128)(2,1)S(1)} %get-tuple-element.41), channel_id=1, source_target_pairs={{0,2},{1,5},{2,0},{3,7},{4,6},{5,1},{6,4},{7,3},{8,10},{9,13},{10,... | collective-permute-start | bytes 786440 | tf_op jit(solution)/shard_map/ppermute | solution.py:354
  107.7 8.7 %collective-permute-start.20 = (bf16[256,512]{1,0:T(8,128)(2,1)S(1)}, bf16[256,512]{1,0:T(8,128)(2,1)S(1)}, u32[]{:S(2)}, u32[]{:S(2)}) collective-permute-start(bf16[256,512]{1,0:T(8,128)(2,1)S(1)} %shard_map.39), channel_id=1, source_target_pairs={{0,4},{1,3},{2,6},{3,1},{4,0},{5,7},{6,2},{7,5},{8,12},{9,11},{10,... | collective-permute-start | bytes 786440 | tf_op jit(solution)/shard_map/ppermute | solution.py:354
  117.3 5.5 %collective-permute-start.21 = (bf16[128,512]{1,0:T(8,128)(2,1)S(1)}, bf16[128,512]{1,0:T(8,128)(2,1)S(1)}, u32[]{:S(2)}, u32[]{:S(2)}) collective-permute-start(bf16[128,512]{1,0:T(8,128)(2,1)S(1)} %get-tuple-element.45), channel_id=1, source_target_pairs={{0,8},{8,0},{16,24},{24,16},{1,9},{9,1},{17,25},{25,17},{2,10},{10... | collective-permute-start | bytes 393224 | tf_op jit(solution)/shard_map/ppermute | solution.py:354
  120.1 6.7 %collective-permute-start.12 = (bf16[128,640]{1,0:T(8,128)(2,1)S(1)}, bf16[128,640]{1,0:T(8,128)(2,1)S(1)}, u32[]{:S(2)}, u32[]{:S(2)}) collective-permute-start(bf16[128,640]{1,0:T(8,128)(2,1)S(1)} %get-tuple-element.39), channel_id=1, source_target_pairs={{0,8},{8,0},{16,24},{24,16},{1,9},{9,1},{17,25},{25,17},{2,10},{10... | collective-permute-start | bytes 491528 | tf_op jit(solution)/shard_map/ppermute | solution.py:354
  123.6 8.9 %collective-permute-start.22 = (bf16[128,512]{1,0:T(8,128)(2,1)S(1)}, bf16[128,512]{1,0:T(8,128)(2,1)S(1)}, u32[]{:S(2)}, u32[]{:S(2)}) collective-permute-start(bf16[128,512]{1,0:T(8,128)(2,1)S(1)} %shard_map.41.refs_0_), channel_id=1, source_target_pairs={{0,16},{8,24},{16,0},{24,8},{1,17},{9,25},{17,1},{25,9},{2,18},{10... | collective-permute-start | bytes 393224 | tf_op jit(solution)/shard_map/ppermute | solution.py:354
  127.4 8.8 %collective-permute-start.13 = (bf16[128,640]{1,0:T(8,128)(2,1)S(1)}, bf16[128,640]{1,0:T(8,128)(2,1)S(1)}, u32[]{:S(2)}, u32[]{:S(2)}) collective-permute-start(bf16[128,640]{1,0:T(8,128)(2,1)S(1)} %shard_map.37.refs_0_), channel_id=1, source_target_pairs={{0,16},{8,24},{16,0},{24,8},{1,17},{9,25},{17,1},{25,9},{2,18},{10... | collective-permute-start | bytes 491528 | tf_op jit(solution)/shard_map/ppermute | solution.py:354
  133.2 6.1 %collective-permute-start.23 = (bf16[128,512]{1,0:T(8,128)(2,1)S(1)}, bf16[128,512]{1,0:T(8,128)(2,1)S(1)}, u32[]{:S(2)}, u32[]{:S(2)}) collective-permute-start(bf16[128,512]{1,0:T(8,128)(2,1)S(1)} %shard_map.42), channel_id=1, source_target_pairs={{0,8},{8,0},{16,24},{24,16},{1,9},{9,1},{17,25},{25,17},{2,10},{10... | collective-permute-start | bytes 393224 | tf_op jit(solution)/shard_map/ppermute | solution.py:354
  136.8 5.4 %collective-permute-start.14 = (bf16[128,640]{1,0:T(8,128)(2,1)S(1)}, bf16[128,640]{1,0:T(8,128)(2,1)S(1)}, u32[]{:S(2)}, u32[]{:S(2)}) collective-permute-start(bf16[128,640]{1,0:T(8,128)(2,1)S(1)} %shard_map.38), channel_id=1, source_target_pairs={{0,8},{8,0},{16,24},{24,16},{1,9},{9,1},{17,25},{25,17},{2,10},{10... | collective-permute-start | bytes 491528 | tf_op jit(solution)/shard_map/ppermute | solution.py:354
  139.3 9.2 %collective-permute-start.24 = (bf16[256,512]{1,0:T(8,128)(2,1)S(1)}, bf16[256,512]{1,0:T(8,128)(2,1)S(1)}, u32[]{:S(2)}, u32[]{:S(2)}) collective-permute-start(bf16[256,512]{1,0:T(8,128)(2,1)S(1)} %pad_maximum_fusion.5), channel_id=1, source_target_pairs={{0,4},{1,3},{2,6},{3,1},{4,0},{5,7},{6,2},{7,5},{8,12},{9,11},{10,... | collective-permute-start | bytes 786440 | tf_op jit(solution)/shard_map/ppermute | solution.py:354
  142.2 9.9 %collective-permute-start.15 = (bf16[256,640]{1,0:T(8,128)(2,1)S(1)}, bf16[256,640]{1,0:T(8,128)(2,1)S(1)}, u32[]{:S(2)}, u32[]{:S(2)}) collective-permute-start(bf16[256,640]{1,0:T(8,128)(2,1)S(1)} %pad_maximum_fusion.3), channel_id=1, source_target_pairs={{0,4},{1,3},{2,6},{3,1},{4,0},{5,7},{6,2},{7,5},{8,12},{9,11},{10,... | collective-permute-start | bytes 983048 | tf_op jit(solution)/shard_map/ppermute | solution.py:354
  142.2 12.1 %collective-permute-start.28 = (bf16[256,512]{1,0:T(8,128)(2,1)S(1)}, bf16[256,512]{1,0:T(8,128)(2,1)S(1)}, u32[]{:S(2)}, u32[]{:S(2)}) collective-permute-start(bf16[256,512]{1,0:T(8,128)(2,1)S(1)} %pad_maximum_fusion.5), channel_id=1, source_target_pairs={{0,2},{1,5},{2,0},{3,7},{4,6},{5,1},{6,4},{7,3},{8,10},{9,13},{10,... | collective-permute-start | bytes 786440 | tf_op jit(solution)/shard_map/ppermute | solution.py:354
  148.6 17.1 %collective-permute-start.32 = (bf16[512,512]{1,0:T(8,128)(2,1)S(1)}, bf16[512,512]{1,0:T(8,128)(2,1)S(1)}, u32[]{:S(2)}, u32[]{:S(2)}) collective-permute-start(bf16[512,512]{1,0:T(8,128)(2,1)S(1)} %pad_maximum_fusion.2.refs_1_), channel_id=1, source_target_pairs={{0,1},{1,0},{2,3},{3,2},{4,5},{5,4},{6,7},{7,6},{8,9},{9,8},{10,11... | collective-permute-start | bytes 1572872 | tf_op jit(solution)/shard_map/ppermute | solution.py:354
  152.1 14.1 %collective-permute-start.31 = (bf16[512,640]{1,0:T(8,128)(2,1)S(1)}, bf16[512,640]{1,0:T(8,128)(2,1)S(1)}, u32[]{:S(2)}, u32[]{:S(2)}) collective-permute-start(bf16[512,640]{1,0:T(8,128)(2,1)S(1)} %pad_maximum_fusion.refs_0_), channel_id=1, source_target_pairs={{0,1},{1,0},{2,3},{3,2},{4,5},{5,4},{6,7},{7,6},{8,9},{9,8},{10,11... | collective-permute-start | bytes 1966088 | tf_op jit(solution)/shard_map/ppermute | solution.py:354
  152.2 7.1 %collective-permute-start.27 = (bf16[256,640]{1,0:T(8,128)(2,1)S(1)}, bf16[256,640]{1,0:T(8,128)(2,1)S(1)}, u32[]{:S(2)}, u32[]{:S(2)}) collective-permute-start(bf16[256,640]{1,0:T(8,128)(2,1)S(1)} %pad_maximum_fusion.3), channel_id=1, source_target_pairs={{0,2},{1,5},{2,0},{3,7},{4,6},{5,1},{6,4},{7,3},{8,10},{9,13},{10,... | collective-permute-start | bytes 983048 | tf_op jit(solution)/shard_map/ppermute | solution.py:354
  152.8 10.1 %collective-permute-start.16 = (bf16[256,640]{1,0:T(8,128)(2,1)S(1)}, bf16[256,640]{1,0:T(8,128)(2,1)S(1)}, u32[]{:S(2)}, u32[]{:S(2)}) collective-permute-start(bf16[256,640]{1,0:T(8,128)(2,1)S(1)} %collective-permute-done.15), channel_id=1, source_target_pairs={{0,2},{1,5},{2,0},{3,7},{4,6},{5,1},{6,4},{7,3},{8,10},{9,13},{10,... | collective-permute-start | bytes 983048 | tf_op jit(solution)/shard_map/ppermute | solution.py:354
  154.3 11.4 %collective-permute-start.25 = (bf16[256,512]{1,0:T(8,128)(2,1)S(1)}, bf16[256,512]{1,0:T(8,128)(2,1)S(1)}, u32[]{:S(2)}, u32[]{:S(2)}) collective-permute-start(bf16[256,512]{1,0:T(8,128)(2,1)S(1)} %collective-permute-done.24), channel_id=1, source_target_pairs={{0,2},{1,5},{2,0},{3,7},{4,6},{5,1},{6,4},{7,3},{8,10},{9,13},{10,... | collective-permute-start | bytes 786440 | tf_op jit(solution)/shard_map/ppermute | solution.py:354
  159.3 11.2 %collective-permute-start.29 = (bf16[256,640]{1,0:T(8,128)(2,1)S(1)}, bf16[256,640]{1,0:T(8,128)(2,1)S(1)}, u32[]{:S(2)}, u32[]{:S(2)}) collective-permute-start(bf16[256,640]{1,0:T(8,128)(2,1)S(1)} %collective-permute-done.27.refs_0_), channel_id=1, source_target_pairs={{0,1},{1,0},{2,3},{3,2},{4,5},{5,4},{6,7},{7,6},{8,9},{9,8},{10,11... | collective-permute-start | bytes 983048 | tf_op jit(solution)/shard_map/ppermute | solution.py:354
  162.9 11.2 %collective-permute-start.17 = (bf16[256,640]{1,0:T(8,128)(2,1)S(1)}, bf16[256,640]{1,0:T(8,128)(2,1)S(1)}, u32[]{:S(2)}, u32[]{:S(2)}) collective-permute-start(bf16[256,640]{1,0:T(8,128)(2,1)S(1)} %collective-permute-done.16.refs_4_), channel_id=1, source_target_pairs={{0,1},{1,0},{2,3},{3,2},{4,5},{5,4},{6,7},{7,6},{8,9},{9,8},{10,11... | collective-permute-start | bytes 983048 | tf_op jit(solution)/shard_map/ppermute | solution.py:354
  165.7 4.9 %collective-permute-start.30 = (bf16[256,512]{1,0:T(8,128)(2,1)S(1)}, bf16[256,512]{1,0:T(8,128)(2,1)S(1)}, u32[]{:S(2)}, u32[]{:S(2)}) collective-permute-start(bf16[256,512]{1,0:T(8,128)(2,1)S(1)} %collective-permute-done.28.refs_1_), channel_id=1, source_target_pairs={{0,1},{1,0},{2,3},{3,2},{4,5},{5,4},{6,7},{7,6},{8,9},{9,8},{10,11... | collective-permute-start | bytes 786440 | tf_op jit(solution)/shard_map/ppermute | solution.py:354
  165.7 8.4 %collective-permute-start.26 = (bf16[256,512]{1,0:T(8,128)(2,1)S(1)}, bf16[256,512]{1,0:T(8,128)(2,1)S(1)}, u32[]{:S(2)}, u32[]{:S(2)}) collective-permute-start(bf16[256,512]{1,0:T(8,128)(2,1)S(1)} %collective-permute-done.25.refs_5_), channel_id=1, source_target_pairs={{0,1},{1,0},{2,3},{3,2},{4,5},{5,4},{6,7},{7,6},{8,9},{9,8},{10,11... | collective-permute-start | bytes 786440 | tf_op jit(solution)/shard_map/ppermute | solution.py:354
  208.0 4.8 %collective-permute-start.33 = (bf16[32,512]{1,0:T(8,128)(2,1)S(1)}, bf16[32,512]{1,0:T(8,128)(2,1)S(1)}, u32[]{:S(2)}, u32[]{:S(2)}) collective-permute-start(bf16[32,512]{1,0:T(8,128)(2,1)S(1)} %shard_map.46), channel_id=1, source_target_pairs={{0,16},{8,24},{16,0},{24,8},{1,17},{9,25},{17,1},{25,9},{2,18},{10... | collective-permute-start | bytes 98312 | tf_op jit(solution)/shard_map/ppermute | solution.py:354
  212.9 4.3 %collective-permute-start.34 = (bf16[32,1024]{1,0:T(8,128)(2,1)S(1)}, bf16[32,1024]{1,0:T(8,128)(2,1)S(1)}, u32[]{:S(2)}, u32[]{:S(2)}) collective-permute-start(bf16[32,1024]{1,0:T(8,128)(2,1)S(1)} %pad_maximum_fusion.6), channel_id=1, source_target_pairs={{0,8},{8,0},{16,24},{24,16},{1,9},{9,1},{17,25},{25,17},{2,10},{10... | collective-permute-start | bytes 196616 | tf_op jit(solution)/shard_map/ppermute | solution.py:354

commit v12 on v11

--- a/solution.py
+++ b/solution.py
@@ -469,7 +469,8 @@
         over_b = flip(share, "pix", second)
         over_ab[e] = flip(over_b, "pix", first)
         near[e] = jnp.concatenate([share, over_b], axis=0)
-        far[e], far_a[e], far_ab[e] = [flip(t[e], "pix", swap) for t in (near, over_a, over_ab)]
+        far[e] = flip(near[e], "pix", swap)
+        far_a[e], far_ab[e] = [flip(t[e], "pix", swap) for t in (over_a, over_ab)]
     parts = (
         jax.ShapeDtypeStruct((n, n), BF16),
         jax.ShapeDtypeStruct((n, bs), BF16),
@@ -484,15 +485,19 @@
         out_specs=tuple(vmem(4)),
         scratch_mib=4,
     )(index, *near, *far, q)
-    offsets = [BLOCKS + i * eighth for i in (2, 6, 3)]
-    now = kernel_call(
-        functools.partial(unpack_kernel, offsets),
-        parts,
-        in_specs=[smem()] + vmem(11),
-        out_specs=tuple(vmem(4)),
-        input_output_aliases={8 + i: i for i in range(4)},
-        scratch_mib=4,
-    )(index, *over_a, *far_a, *over_ab, q, *now)
+
+    def unpack_more(now, slots, *shares):
+        return kernel_call(
+            functools.partial(unpack_kernel, [BLOCKS + i * eighth for i in slots]),
+            parts,
+            in_specs=[smem()] + vmem(len(shares) + 5),
+            out_specs=tuple(vmem(4)),
+            input_output_aliases={len(shares) + 2 + i: i for i in range(4)},
+            scratch_mib=4,
+        )(index, *shares, q, *now)
+
+    now = unpack_more(now, (2, 6), *over_a, *far_a)
+    now = unpack_more(now, (3,), *over_ab)
     proj, inv = kernel_call(
         functools.partial(iterate_kernel, BLOCKS + 7 * eighth),
         (jax.ShapeDtypeStruct((k, n), BF16), jax.ShapeDtypeStruct((k, LANES), F32)) + parts,

time: 218 us -> 219 us (level)
    pallas_call x19 -> x20, Pallas kernels: 66 us -> 66.5 us  [kernel_call(): return lambda *args: call(*map(place, args, in_specs))]
where the time goes in v12:
time: 219 us; the launch traced here: 218 us
  waiting for transfers between devices  108 us (49%)
  Pallas kernels  66.5 us (30%)
  starting transfers between devices  37.8 us (17%)
  local copies, waits for them, and re-layouts  4.9 us (2%)
    ppermute x35, waiting for transfers between devices, flip(): return lax.ppermute(x, axes, perm)  81.7 us
    pallas_call x20, Pallas kernels, kernel_call(): return lambda *args: call(*map(place, args, in_specs))  66.5 us
    ppermute x35, starting transfers between devices, flip(): return lax.ppermute(x, axes, perm)  30.4 us
    all_to_all x1, waiting for transfers between devices, sample_space(): lax.all_to_all(stamps, ('pix', 'samp'), split_axis=1, concat_axis=0, tile...  26 us
    all_to_all x1, starting transfers between devices, sample_space(): lax.all_to_all(stamps, ('pix', 'samp'), split_axis=1, concat_axis=0, tile...  7.33 us
  transfers between devices with their start and end apart: 36, of which 23 were waited for; matrix products, arithmetic and copies ran while one was open for 0% of the time, Pallas kernels for 11%

profile of v12, /device:TPU:0, one launch (start us, length us, event | category | flops | bytes accessed | tf_op | source)
XLA Modules:
  0.0 218.3 jit_solution(11751486125159052729)
XLA Ops:
  0.0 3.2 %copy.18 = bf16[8,32,8,512]{3,2,0,1:T(8,128)(2,1)} copy(bf16[8,32,8,512]{3,2,1,0:T(8,128)(2,1)} %bitcast.25) | data formatting | bytes 4194304 | tf_op jit(solution)/shard_map/all_to_all | solution.py:403
  3.2 7.3 %all-to-all-start = ((bf16[64,32,512]{2,0,1:T(8,128)(2,1)}), bf16[64,32,512]{2,0,1:T(8,128)(2,1)S(1)}, u32[]{:S(2)}, u32[]{:S(2)}) async-start(bf16[64,32,512]{2,0,1:T(8,128)(2,1)} %bitcast.26), calls=%async_computation | async-start | bytes 4194304 | tf_op jit(solution)/shard_map/all_to_all | solution.py:403
  10.6 1.8 collective-permute-start.1
  12.4 17.3 %collective-permute-done.1 = bf16[32,2048]{1,0:T(8,128)(2,1)S(1)} collective-permute-done((bf16[32,2048]{1,0:T(8,128)(2,1)S(1)}, bf16[32,2048]{1,0:T(8,128)(2,1)S(1)}, u32[]{:S(2)}, u32[]{:S(2)}) %collective-permute-start.1) | collective-permute-done | bytes 131104 | tf_op jit(solution)/shard_map/ppermute | solution.py:354
  29.8 1.5 collective-permute-start.2
  31.3 26.0 %all-to-all-done = bf16[64,32,512]{2,0,1:T(8,128)(2,1)S(1)} async-done(((bf16[64,32,512]{2,0,1:T(8,128)(2,1)}), bf16[64,32,512]{2,0,1:T(8,128)(2,1)S(1)}, u32[]{:S(2)}, u32[]{:S(2)}) %all-to-all-start) | async-done | bytes 2097184 | tf_op jit(solution)/shard_map/all_to_all | solution.py:403
  57.3 1.8 collective-permute-start
  59.4 4.3 %collective-permute-done.3.far_ref = bf16[32,8192]{1,0:T(8,128)(2,1)S(1)} collective-permute-done((bf16[32,8192]{1,0:T(8,128)(2,1)S(1)}, bf16[32,8192]{1,0:T(8,128)(2,1)S(1)}, u32[]{:S(2)}, u32[]{:S(2)}) %collective-permute-start.3) | collective-permute-done | bytes 524320 | tf_op jit(solution)/shard_map/ppermute | solution.py:354
  63.7 1.6 copy-done
  67.8 1.5 collective-permute-start.5
  69.3 2.1 collective-permute-done.5
  71.4 1.5 collective-permute-start.6
  72.9 2.2 %collective-permute-done.6 = bf16[32,256]{1,0:T(8,128)(2,1)S(1)} collective-permute-done((bf16[32,256]{1,0:T(8,128)(2,1)S(1)}, bf16[32,256]{1,0:T(8,128)(2,1)S(1)}, u32[]{:S(2)}, u32[]{:S(2)}) %collective-permute-start.6) | collective-permute-done | bytes 16416 | tf_op jit(solution)/shard_map/ppermute | solution.py:354
  75.2 2.3 %collective-permute-start.7 = (bf16[32,512]{1,0:T(8,128)(2,1)S(1)}, bf16[32,512]{1,0:T(8,128)(2,1)S(1)}, u32[]{:S(2)}, u32[]{:S(2)}) collective-permute-start(bf16[32,512]{1,0:T(8,128)(2,1)S(1)} %maximum_select_fusion.2), channel_id=1, source_target_pairs={{0,8},{8,0},{16,24},{24,16},{1,9},{9,1},{17,25},{25,17},{2,10},{10... | collective-permute-start | bytes 98312 | tf_op jit(solution)/shard_map/ppermute | solution.py:354
  77.5 1.9 collective-permute-done.7
  80.6 4.0 %collective-permute-done.8 = bf16[32,1024]{1,0:T(8,128)(2,1)S(1)} collective-permute-done((bf16[32,1024]{1,0:T(8,128)(2,1)S(1)}, bf16[32,1024]{1,0:T(8,128)(2,1)S(1)}, u32[]{:S(2)}, u32[]{:S(2)}) %collective-permute-start.8) | collective-permute-done | bytes 65568 | tf_op jit(solution)/shard_map/ppermute | solution.py:354
  84.7 1.4 shard_map.29
  86.1 4.9 %shard_map.30 = (bf16[192,2048]{1,0:T(8,128)(2,1)S(1)}, bf16[192,2048]{1,0:T(8,128)(2,1)S(1)}) custom-call(bf16[2048,512]{1,0:T(8,128)(2,1)S(1)} %bitcast.19, bf16[2048,512]{1,0:T(8,128)(2,1)} %collective-permute-done.other_ref, f32[32,2048]{1,0:T(8,128)S(1)} %get-tuple-element.35.q_ref.refs_4_.refs_2_), custom_call_target="tpu_custom_call" | custom-call | tf_op jit(solution)/shard_map/pallas_call | solution.py:77
  91.0 2.8 %shard_map.34 = (bf16[256,640]{1,0:T(8,128)(2,1)S(1)}, bf16[256,512]{1,0:T(8,128)(2,1)S(1)}) custom-call(s32[32]{0:T(128)S(1)} %concatenate.60.index_ref.at_ref, bf16[2048,512]{1,0:T(8,128)(2,1)S(1)} %bitcast.20, bf16[2048,512]{1,0:T(8,128)(2,1)} %collective-permute-done.other_ref, bf16[192,2048]{1,0:T(8,128)(2,1)S(1)} %get-tuple-element.36.left, ...), custom_call_target="tpu_custom_call" | custom-call | tf_op jit(solution)/shard_map/pallas_call | solution.py:77
  93.8 2.0 collective-permute-start.10
  95.9 2.8 %shard_map.32 = (bf16[256,640]{1,0:T(8,128)(2,1)S(1)}, bf16[256,512]{1,0:T(8,128)(2,1)S(1)}) custom-call(s32[32]{0:T(128)S(1)} %concatenate.60.index_ref.at_ref, bf16[2048,512]{1,0:T(8,128)(2,1)S(1)} %bitcast.21, bf16[2048,512]{1,0:T(8,128)(2,1)} %collective-permute-done.other_ref, bf16[192,2048]{1,0:T(8,128)(2,1)S(1)} %get-tuple-element.36.left, ...), custom_call_target="tpu_custom_call" | custom-call | tf_op jit(solution)/shard_map/pallas_call | solution.py:77
  98.7 2.0 collective-permute-start.9
  100.7 2.8 %shard_map.33 = (bf16[256,640]{1,0:T(8,128)(2,1)S(1)}, bf16[256,512]{1,0:T(8,128)(2,1)S(1)}) custom-call(s32[32]{0:T(128)S(1)} %concatenate.60.index_ref.at_ref, bf16[2048,512]{1,0:T(8,128)(2,1)S(1)} %bitcast.22, bf16[2048,512]{1,0:T(8,128)(2,1)} %collective-permute-done.other_ref, bf16[192,2048]{1,0:T(8,128)(2,1)S(1)} %get-tuple-element.36.left, ...), custom_call_target="tpu_custom_call" | custom-call | tf_op jit(solution)/shard_map/pallas_call | solution.py:77
  104.2 1.3 collective-permute-start.18
  105.4 1.5 collective-permute-done.19.refs_1_
  108.8 2.8 %shard_map.31 = (bf16[256,640]{1,0:T(8,128)(2,1)S(1)}, bf16[256,512]{1,0:T(8,128)(2,1)S(1)}) custom-call(s32[32]{0:T(128)S(1)} %concatenate.60.index_ref.at_ref, bf16[2048,512]{1,0:T(8,128)(2,1)S(1)} %bitcast.23, bf16[2048,512]{1,0:T(8,128)(2,1)} %collective-permute-done.other_ref, bf16[192,2048]{1,0:T(8,128)(2,1)S(1)} %get-tuple-element.36.left, ...), custom_call_target="tpu_custom_call" | custom-call | tf_op jit(solution)/shard_map/pallas_call | solution.py:77
  111.6 4.8 %collective-permute-done.18.refs_1_ = bf16[256,512]{1,0:T(8,128)(2,1)S(1)} collective-permute-done((bf16[256,512]{1,0:T(8,128)(2,1)S(1)}, bf16[256,512]{1,0:T(8,128)(2,1)S(1)}, u32[]{:S(2)}, u32[]{:S(2)}) %collective-permute-start.18) | collective-permute-done | bytes 262176 | tf_op jit(solution)/shard_map/ppermute | solution.py:354
  117.3 2.1 collective-permute-start.21
  120.1 2.7 %collective-permute-done.21.refs_1_ = bf16[128,512]{1,0:T(8,128)(2,1)S(1)} collective-permute-done((bf16[128,512]{1,0:T(8,128)(2,1)S(1)}, bf16[128,512]{1,0:T(8,128)(2,1)S(1)}, u32[]{:S(2)}, u32[]{:S(2)}) %collective-permute-start.21) | collective-permute-done | bytes 131104 | tf_op jit(solution)/shard_map/ppermute | solution.py:354
  124.7 2.0 collective-permute-done.12.refs_1_
  127.3 1.5 collective-permute-start.13
  128.8 3.6 %collective-permute-done.22.refs_1_ = bf16[128,512]{1,0:T(8,128)(2,1)S(1)} collective-permute-done((bf16[128,512]{1,0:T(8,128)(2,1)S(1)}, bf16[128,512]{1,0:T(8,128)(2,1)S(1)}, u32[]{:S(2)}, u32[]{:S(2)}) %collective-permute-start.22) | collective-permute-done | bytes 131104 | tf_op jit(solution)/shard_map/ppermute | solution.py:354
  134.0 2.1 collective-permute-done.13.refs_1_
  136.8 2.4 %collective-permute-done.23 = bf16[128,512]{1,0:T(8,128)(2,1)S(1)} collective-permute-done((bf16[128,512]{1,0:T(8,128)(2,1)S(1)}, bf16[128,512]{1,0:T(8,128)(2,1)S(1)}, u32[]{:S(2)}, u32[]{:S(2)}) %collective-permute-start.23) | collective-permute-done | bytes 131104 | tf_op jit(solution)/shard_map/ppermute | solution.py:354
  139.3 2.8 %collective-permute-done.14 = bf16[128,640]{1,0:T(8,128)(2,1)S(1)} collective-permute-done((bf16[128,640]{1,0:T(8,128)(2,1)S(1)}, bf16[128,640]{1,0:T(8,128)(2,1)S(1)}, u32[]{:S(2)}, u32[]{:S(2)}) %collective-permute-start.14) | collective-permute-done | bytes 163872 | tf_op jit(solution)/shard_map/ppermute | solution.py:354
  142.4 2.3 %collective-permute-start.28 = (bf16[256,512]{1,0:T(8,128)(2,1)S(1)}, bf16[256,512]{1,0:T(8,128)(2,1)S(1)}, u32[]{:S(2)}, u32[]{:S(2)}) collective-permute-start(bf16[256,512]{1,0:T(8,128)(2,1)S(1)} %pad_maximum_fusion.5), channel_id=1, source_target_pairs={{0,2},{1,5},{2,0},{3,7},{4,6},{5,1},{6,4},{7,3},{8,10},{9,13},{10,... | collective-permute-start | bytes 786440 | tf_op jit(solution)/shard_map/ppermute | solution.py:354
  144.7 3.8 %collective-permute-done.24 = bf16[256,512]{1,0:T(8,128)(2,1)S(1)} collective-permute-done((bf16[256,512]{1,0:T(8,128)(2,1)S(1)}, bf16[256,512]{1,0:T(8,128)(2,1)S(1)}, u32[]{:S(2)}, u32[]{:S(2)}) %collective-permute-start.24) | collective-permute-done | bytes 262176 | tf_op jit(solution)/shard_map/ppermute | solution.py:354
  148.6 3.4 %collective-permute-done.15 = bf16[256,640]{1,0:T(8,128)(2,1)S(1)} collective-permute-done((bf16[256,640]{1,0:T(8,128)(2,1)S(1)}, bf16[256,640]{1,0:T(8,128)(2,1)S(1)}, u32[]{:S(2)}, u32[]{:S(2)}) %collective-permute-start.15) | collective-permute-done | bytes 327712 | tf_op jit(solution)/shard_map/ppermute | solution.py:354
  152.8 1.4 collective-permute-start.16
  154.8 4.5 %collective-permute-done.27.refs_0_ = bf16[256,640]{1,0:T(8,128)(2,1)S(1)} collective-permute-done((bf16[256,640]{1,0:T(8,128)(2,1)S(1)}, bf16[256,640]{1,0:T(8,128)(2,1)S(1)}, u32[]{:S(2)}, u32[]{:S(2)}) %collective-permute-start.27) | collective-permute-done | bytes 327712 | tf_op jit(solution)/shard_map/ppermute | solution.py:354
  159.3 3.5 %collective-permute-done.16.refs_0_ = bf16[256,640]{1,0:T(8,128)(2,1)S(1)} collective-permute-done((bf16[256,640]{1,0:T(8,128)(2,1)S(1)}, bf16[256,640]{1,0:T(8,128)(2,1)S(1)}, u32[]{:S(2)}, u32[]{:S(2)}) %collective-permute-start.16) | collective-permute-done | bytes 327712 | tf_op jit(solution)/shard_map/ppermute | solution.py:354
  162.8 2.8 %collective-permute-done.25.refs_1_ = bf16[256,512]{1,0:T(8,128)(2,1)S(1)} collective-permute-done((bf16[256,512]{1,0:T(8,128)(2,1)S(1)}, bf16[256,512]{1,0:T(8,128)(2,1)S(1)}, u32[]{:S(2)}, u32[]{:S(2)}) %collective-permute-start.25) | collective-permute-done | bytes 262176 | tf_op jit(solution)/shard_map/ppermute | solution.py:354
  166.1 4.4 %shard_map.43 = (bf16[2048,2048]{1,0:T(8,128)(2,1)S(1)}, bf16[2048,128]{1,0:T(8,128)(2,1)S(1)}, bf16[192,2048]{1,0:T(8,128)(2,1)S(1)}, f32[8,2048]{1,0:T(8,128)S(1)}) custom-call(s32[32]{0:T(128)S(1)} %concatenate.60.index_ref.at_ref, bf16[512,640]{1,0:T(8,128)(2,1)S(1)} %pad_maximum_fusion.refs_0_, bf16[512,512]{1,0:T(8,128)(2,1)S(1)} %pad_maximum_fusion.2.refs_1_, ...), custom_call_target="tpu_custom_call" | custom-call | tf_op jit(solution)/shard_map/pallas_call | solution.py:77
  170.5 2.6 %shard_map.44 = (bf16[2048,2048]{1,0:T(8,128)(2,1)S(1)}, bf16[2048,128]{1,0:T(8,128)(2,1)S(1)}, bf16[192,2048]{1,0:T(8,128)(2,1)S(1)}, f32[8,2048]{1,0:T(8,128)S(1)}) custom-call(s32[32]{0:T(128)S(1)} %concatenate.60.index_ref.at_ref, ...), custom_call_target="tpu_custom_call", output_to_operand_aliasing={{0}: (6, {}), {1}: (7, {}), {2}: (8, {}), {3}: (9, {})} | custom-call | tf_op jit(solution)/shard_map/pallas_call | solution.py:77
  173.2 1.4 shard_map.45
  174.6 33.3 %shard_map.46 = (bf16[32,2048]{1,0:T(8,128)(2,1)S(1)}, f32[32,128]{1,0:T(8,128)S(1)}, bf16[2048,2048]{1,0:T(8,128)(2,1)S(1)}, bf16[2048,128]{1,0:T(8,128)(2,1)S(...) custom-call(s32[32]{0:T(128)S(1)} %concatenate.60.index_ref.at_ref, ...), custom_call_target="tpu_custom_call", output_to_operand_aliasing={{2}: (5, {}), {3}: (6, {}), {4}: (7, {}), {5}: (8, {})} | custom-call | tf_op jit(solution)/shard_map/pallas_call | solution.py:77
  208.5 4.8 %collective-permute-done.33 = bf16[32,512]{1,0:T(8,128)(2,1)S(1)} collective-permute-done((bf16[32,512]{1,0:T(8,128)(2,1)S(1)}, bf16[32,512]{1,0:T(8,128)(2,1)S(1)}, u32[]{:S(2)}, u32[]{:S(2)}) %collective-permute-start.33) | collective-permute-done | bytes 32800 | tf_op jit(solution)/shard_map/ppermute | solution.py:354
  213.3 4.3 %collective-permute-done.34 = bf16[32,1024]{1,0:T(8,128)(2,1)S(1)} collective-permute-done((bf16[32,1024]{1,0:T(8,128)(2,1)S(1)}, bf16[32,1024]{1,0:T(8,128)(2,1)S(1)}, u32[]{:S(2)}, u32[]{:S(2)}) %collective-permute-start.34) | collective-permute-done | bytes 65568 | tf_op jit(solution)/shard_map/ppermute | solution.py:354
  (67 shorter events, 16.8 us)
Async XLA Ops:
  3.2 7.3 %copy-start.1 = (f32[2048,32]{0,1:T(8,128)S(1)}, f32[2048,32]{0,1:T(8,128)}, u32[]{:S(2)}) copy-start(f32[2048,32]{0,1:T(8,128)} %param.3) | copy-start | bytes 786436
  3.2 54.1 %all-to-all-start = ((bf16[64,32,512]{2,0,1:T(8,128)(2,1)}), bf16[64,32,512]{2,0,1:T(8,128)(2,1)S(1)}, u32[]{:S(2)}, u32[]{:S(2)}) async-start(bf16[64,32,512]{2,0,1:T(8,128)(2,1)} %bitcast.26), calls=%async_computation | async-start | bytes 4194304 | tf_op jit(solution)/shard_map/all_to_all | solution.py:403
  10.6 19.1 %collective-permute-start.1 = (bf16[32,2048]{1,0:T(8,128)(2,1)S(1)}, bf16[32,2048]{1,0:T(8,128)(2,1)S(1)}, u32[]{:S(2)}, u32[]{:S(2)}) collective-permute-start(bf16[32,2048]{1,0:T(8,128)(2,1)S(1)} %convert_bitcast_fusion.1), channel_id=1, source_target_pairs={{0,2},{1,3},{2,0},{3,1},{4,6},{5,7},{6,4},{7,5},{8,10},{9,11},{10,... | collective-permute-start | bytes 393224 | tf_op jit(solution)/shard_map/ppermute | solution.py:354
  29.8 29.4 %collective-permute-start.2 = (bf16[32,4096]{1,0:T(8,128)(2,1)S(1)}, bf16[32,4096]{1,0:T(8,128)(2,1)S(1)}, u32[]{:S(2)}, u32[]{:S(2)}) collective-permute-start(bf16[32,4096]{1,0:T(8,128)(2,1)S(1)} %pad_maximum_fusion.4), channel_id=1, source_target_pairs={{0,4},{1,5},{2,6},{3,7},{4,0},{5,1},{6,2},{7,3},{8,12},{9,13},{10,... | collective-permute-start | bytes 786440 | tf_op jit(solution)/shard_map/ppermute | solution.py:354
  57.3 28.8 %collective-permute-start = (bf16[2048,512]{1,0:T(8,128)(2,1)S(1)}, bf16[2048,512]{1,0:T(8,128)(2,1)}, u32[]{:S(2)}, u32[]{:S(2)}) collective-permute-start(bf16[2048,512]{1,0:T(8,128)(2,1)S(1)} %bitcast.18), channel_id=1, source_target_pairs={{0,1},{1,0},{2,3},{3,2},{4,5},{5,4},{6,7},{7,6},{8,9},{9,8},{10,11... | collective-permute-start | bytes 6291464 | tf_op jit(solution)/shard_map/ppermute | solution.py:354
  59.2 4.5 %collective-permute-start.3 = (bf16[32,8192]{1,0:T(8,128)(2,1)S(1)}, bf16[32,8192]{1,0:T(8,128)(2,1)S(1)}, u32[]{:S(2)}, u32[]{:S(2)}) collective-permute-start(bf16[32,8192]{1,0:T(8,128)(2,1)S(1)} %pad_maximum_fusion.1.near_ref), channel_id=1, source_target_pairs={{0,1},{1,0},{2,3},{3,2},{4,5},{5,4},{6,7},{7,6},{8,9},{9,8},{10,11... | collective-permute-start | bytes 1572872 | tf_op jit(solution)/shard_map/ppermute | solution.py:354
  63.6 1.6 copy-start
  66.5 1.2 collective-permute-start.4
  67.8 3.7 %collective-permute-start.5 = (bf16[32,128]{1,0:T(8,128)(2,1)S(1)}, bf16[32,128]{1,0:T(8,128)(2,1)S(1)}, u32[]{:S(2)}, u32[]{:S(2)}) collective-permute-start(bf16[32,128]{1,0:T(8,128)(2,1)S(1)} %maximum_select_fusion.4), channel_id=1, source_target_pairs={{0,2},{1,3},{2,0},{3,1},{4,6},{5,7},{6,4},{7,5},{8,10},{9,11},{10,... | collective-permute-start | bytes 24584 | tf_op jit(solution)/shard_map/ppermute | solution.py:354
  71.4 3.7 %collective-permute-start.6 = (bf16[32,256]{1,0:T(8,128)(2,1)S(1)}, bf16[32,256]{1,0:T(8,128)(2,1)S(1)}, u32[]{:S(2)}, u32[]{:S(2)}) collective-permute-start(bf16[32,256]{1,0:T(8,128)(2,1)S(1)} %maximum_select_fusion.3), channel_id=1, source_target_pairs={{0,4},{1,5},{2,6},{3,7},{4,0},{5,1},{6,2},{7,3},{8,12},{9,13},{10,... | collective-permute-start | bytes 49160 | tf_op jit(solution)/shard_map/ppermute | solution.py:354
  75.2 4.2 %collective-permute-start.7 = (bf16[32,512]{1,0:T(8,128)(2,1)S(1)}, bf16[32,512]{1,0:T(8,128)(2,1)S(1)}, u32[]{:S(2)}, u32[]{:S(2)}) collective-permute-start(bf16[32,512]{1,0:T(8,128)(2,1)S(1)} %maximum_select_fusion.2), channel_id=1, source_target_pairs={{0,8},{8,0},{16,24},{24,16},{1,9},{9,1},{17,25},{25,17},{2,10},{10... | collective-permute-start | bytes 98312 | tf_op jit(solution)/shard_map/ppermute | solution.py:354
  79.4 5.2 %collective-permute-start.8 = (bf16[32,1024]{1,0:T(8,128)(2,1)S(1)}, bf16[32,1024]{1,0:T(8,128)(2,1)S(1)}, u32[]{:S(2)}, u32[]{:S(2)}) collective-permute-start(bf16[32,1024]{1,0:T(8,128)(2,1)S(1)} %maximum_select_fusion.1), channel_id=1, source_target_pairs={{0,16},{8,24},{16,0},{24,8},{1,17},{9,25},{17,1},{25,9},{2,18},{10... | collective-permute-start | bytes 196616 | tf_op jit(solution)/shard_map/ppermute | solution.py:354
  93.8 9.7 %collective-permute-start.10 = (bf16[256,640]{1,0:T(8,128)(2,1)S(1)}, bf16[256,640]{1,0:T(8,128)(2,1)S(1)}, u32[]{:S(2)}, u32[]{:S(2)}) collective-permute-start(bf16[256,640]{1,0:T(8,128)(2,1)S(1)} %get-tuple-element.41), channel_id=1, source_target_pairs={{0,2},{1,5},{2,0},{3,7},{4,6},{5,1},{6,4},{7,3},{8,10},{9,13},{10,... | collective-permute-start | bytes 983048 | tf_op jit(solution)/shard_map/ppermute | solution.py:354
  95.8 11.1 %collective-permute-start.19 = (bf16[256,512]{1,0:T(8,128)(2,1)S(1)}, bf16[256,512]{1,0:T(8,128)(2,1)S(1)}, u32[]{:S(2)}, u32[]{:S(2)}) collective-permute-start(bf16[256,512]{1,0:T(8,128)(2,1)S(1)} %get-tuple-element.47), channel_id=1, source_target_pairs={{0,2},{1,5},{2,0},{3,7},{4,6},{5,1},{6,4},{7,3},{8,10},{9,13},{10,... | collective-permute-start | bytes 786440 | tf_op jit(solution)/shard_map/ppermute | solution.py:354
  98.7 20.7 %collective-permute-start.9 = (bf16[256,640]{1,0:T(8,128)(2,1)S(1)}, bf16[256,640]{1,0:T(8,128)(2,1)S(1)}, u32[]{:S(2)}, u32[]{:S(2)}) collective-permute-start(bf16[256,640]{1,0:T(8,128)(2,1)S(1)} %get-tuple-element.39), channel_id=1, source_target_pairs={{0,2},{1,5},{2,0},{3,7},{4,6},{5,1},{6,4},{7,3},{8,10},{9,13},{10,... | collective-permute-start | bytes 983048 | tf_op jit(solution)/shard_map/ppermute | solution.py:354
  104.1 15.3 %collective-permute-start.11 = (bf16[256,640]{1,0:T(8,128)(2,1)S(1)}, bf16[256,640]{1,0:T(8,128)(2,1)S(1)}, u32[]{:S(2)}, u32[]{:S(2)}) collective-permute-start(bf16[256,640]{1,0:T(8,128)(2,1)S(1)} %shard_map.35), channel_id=1, source_target_pairs={{0,4},{1,3},{2,6},{3,1},{4,0},{5,7},{6,2},{7,5},{8,12},{9,11},{10,... | collective-permute-start | bytes 983048 | tf_op jit(solution)/shard_map/ppermute | solution.py:354
  104.2 12.2 %collective-permute-start.18 = (bf16[256,512]{1,0:T(8,128)(2,1)S(1)}, bf16[256,512]{1,0:T(8,128)(2,1)S(1)}, u32[]{:S(2)}, u32[]{:S(2)}) collective-permute-start(bf16[256,512]{1,0:T(8,128)(2,1)S(1)} %get-tuple-element.45), channel_id=1, source_target_pairs={{0,2},{1,5},{2,0},{3,7},{4,6},{5,1},{6,4},{7,3},{8,10},{9,13},{10,... | collective-permute-start | bytes 786440 | tf_op jit(solution)/shard_map/ppermute | solution.py:354
  107.7 8.6 %collective-permute-start.20 = (bf16[256,512]{1,0:T(8,128)(2,1)S(1)}, bf16[256,512]{1,0:T(8,128)(2,1)S(1)}, u32[]{:S(2)}, u32[]{:S(2)}) collective-permute-start(bf16[256,512]{1,0:T(8,128)(2,1)S(1)} %shard_map.39), channel_id=1, source_target_pairs={{0,4},{1,3},{2,6},{3,1},{4,0},{5,7},{6,2},{7,5},{8,12},{9,11},{10,... | collective-permute-start | bytes 786440 | tf_op jit(solution)/shard_map/ppermute | solution.py:354
  117.3 5.6 %collective-permute-start.21 = (bf16[128,512]{1,0:T(8,128)(2,1)S(1)}, bf16[128,512]{1,0:T(8,128)(2,1)S(1)}, u32[]{:S(2)}, u32[]{:S(2)}) collective-permute-start(bf16[128,512]{1,0:T(8,128)(2,1)S(1)} %get-tuple-element.49), channel_id=1, source_target_pairs={{0,8},{8,0},{16,24},{24,16},{1,9},{9,1},{17,25},{25,17},{2,10},{10... | collective-permute-start | bytes 393224 | tf_op jit(solution)/shard_map/ppermute | solution.py:354
  120.0 6.7 %collective-permute-start.12 = (bf16[128,640]{1,0:T(8,128)(2,1)S(1)}, bf16[128,640]{1,0:T(8,128)(2,1)S(1)}, u32[]{:S(2)}, u32[]{:S(2)}) collective-permute-start(bf16[128,640]{1,0:T(8,128)(2,1)S(1)} %get-tuple-element.43), channel_id=1, source_target_pairs={{0,8},{8,0},{16,24},{24,16},{1,9},{9,1},{17,25},{25,17},{2,10},{10... | collective-permute-start | bytes 491528 | tf_op jit(solution)/shard_map/ppermute | solution.py:354
  123.6 8.8 %collective-permute-start.22 = (bf16[128,512]{1,0:T(8,128)(2,1)S(1)}, bf16[128,512]{1,0:T(8,128)(2,1)S(1)}, u32[]{:S(2)}, u32[]{:S(2)}) collective-permute-start(bf16[128,512]{1,0:T(8,128)(2,1)S(1)} %shard_map.41.refs_0_), channel_id=1, source_target_pairs={{0,16},{8,24},{16,0},{24,8},{1,17},{9,25},{17,1},{25,9},{2,18},{10... | collective-permute-start | bytes 393224 | tf_op jit(solution)/shard_map/ppermute | solution.py:354
  127.3 8.8 %collective-permute-start.13 = (bf16[128,640]{1,0:T(8,128)(2,1)S(1)}, bf16[128,640]{1,0:T(8,128)(2,1)S(1)}, u32[]{:S(2)}, u32[]{:S(2)}) collective-permute-start(bf16[128,640]{1,0:T(8,128)(2,1)S(1)} %shard_map.37.refs_0_), channel_id=1, source_target_pairs={{0,16},{8,24},{16,0},{24,8},{1,17},{9,25},{17,1},{25,9},{2,18},{10... | collective-permute-start | bytes 491528 | tf_op jit(solution)/shard_map/ppermute | solution.py:354
  133.1 6.1 %collective-permute-start.23 = (bf16[128,512]{1,0:T(8,128)(2,1)S(1)}, bf16[128,512]{1,0:T(8,128)(2,1)S(1)}, u32[]{:S(2)}, u32[]{:S(2)}) collective-permute-start(bf16[128,512]{1,0:T(8,128)(2,1)S(1)} %shard_map.42), channel_id=1, source_target_pairs={{0,8},{8,0},{16,24},{24,16},{1,9},{9,1},{17,25},{25,17},{2,10},{10... | collective-permute-start | bytes 393224 | tf_op jit(solution)/shard_map/ppermute | solution.py:354
  136.7 5.4 %collective-permute-start.14 = (bf16[128,640]{1,0:T(8,128)(2,1)S(1)}, bf16[128,640]{1,0:T(8,128)(2,1)S(1)}, u32[]{:S(2)}, u32[]{:S(2)}) collective-permute-start(bf16[128,640]{1,0:T(8,128)(2,1)S(1)} %shard_map.38), channel_id=1, source_target_pairs={{0,8},{8,0},{16,24},{24,16},{1,9},{9,1},{17,25},{25,17},{2,10},{10... | collective-permute-start | bytes 491528 | tf_op jit(solution)/shard_map/ppermute | solution.py:354
  139.3 9.2 %collective-permute-start.24 = (bf16[256,512]{1,0:T(8,128)(2,1)S(1)}, bf16[256,512]{1,0:T(8,128)(2,1)S(1)}, u32[]{:S(2)}, u32[]{:S(2)}) collective-permute-start(bf16[256,512]{1,0:T(8,128)(2,1)S(1)} %pad_maximum_fusion.5), channel_id=1, source_target_pairs={{0,4},{1,3},{2,6},{3,1},{4,0},{5,7},{6,2},{7,5},{8,12},{9,11},{10,... | collective-permute-start | bytes 786440 | tf_op jit(solution)/shard_map/ppermute | solution.py:354
  142.1 9.9 %collective-permute-start.15 = (bf16[256,640]{1,0:T(8,128)(2,1)S(1)}, bf16[256,640]{1,0:T(8,128)(2,1)S(1)}, u32[]{:S(2)}, u32[]{:S(2)}) collective-permute-start(bf16[256,640]{1,0:T(8,128)(2,1)S(1)} %pad_maximum_fusion.3), channel_id=1, source_target_pairs={{0,4},{1,3},{2,6},{3,1},{4,0},{5,7},{6,2},{7,5},{8,12},{9,11},{10,... | collective-permute-start | bytes 983048 | tf_op jit(solution)/shard_map/ppermute | solution.py:354
  142.4 11.9 %collective-permute-start.28 = (bf16[256,512]{1,0:T(8,128)(2,1)S(1)}, bf16[256,512]{1,0:T(8,128)(2,1)S(1)}, u32[]{:S(2)}, u32[]{:S(2)}) collective-permute-start(bf16[256,512]{1,0:T(8,128)(2,1)S(1)} %pad_maximum_fusion.5), channel_id=1, source_target_pairs={{0,2},{1,5},{2,0},{3,7},{4,6},{5,1},{6,4},{7,3},{8,10},{9,13},{10,... | collective-permute-start | bytes 786440 | tf_op jit(solution)/shard_map/ppermute | solution.py:354
  148.5 17.1 %collective-permute-start.32 = (bf16[512,512]{1,0:T(8,128)(2,1)S(1)}, bf16[512,512]{1,0:T(8,128)(2,1)S(1)}, u32[]{:S(2)}, u32[]{:S(2)}) collective-permute-start(bf16[512,512]{1,0:T(8,128)(2,1)S(1)} %pad_maximum_fusion.2.refs_1_), channel_id=1, source_target_pairs={{0,1},{1,0},{2,3},{3,2},{4,5},{5,4},{6,7},{7,6},{8,9},{9,8},{10,11... | collective-permute-start | bytes 1572872 | tf_op jit(solution)/shard_map/ppermute | solution.py:354
  152.1 14.1 %collective-permute-start.31 = (bf16[512,640]{1,0:T(8,128)(2,1)S(1)}, bf16[512,640]{1,0:T(8,128)(2,1)S(1)}, u32[]{:S(2)}, u32[]{:S(2)}) collective-permute-start(bf16[512,640]{1,0:T(8,128)(2,1)S(1)} %pad_maximum_fusion.refs_0_), channel_id=1, source_target_pairs={{0,1},{1,0},{2,3},{3,2},{4,5},{5,4},{6,7},{7,6},{8,9},{9,8},{10,11... | collective-permute-start | bytes 1966088 | tf_op jit(solution)/shard_map/ppermute | solution.py:354
  152.1 7.1 %collective-permute-start.27 = (bf16[256,640]{1,0:T(8,128)(2,1)S(1)}, bf16[256,640]{1,0:T(8,128)(2,1)S(1)}, u32[]{:S(2)}, u32[]{:S(2)}) collective-permute-start(bf16[256,640]{1,0:T(8,128)(2,1)S(1)} %pad_maximum_fusion.3), channel_id=1, source_target_pairs={{0,2},{1,5},{2,0},{3,7},{4,6},{5,1},{6,4},{7,3},{8,10},{9,13},{10,... | collective-permute-start | bytes 983048 | tf_op jit(solution)/shard_map/ppermute | solution.py:354
  152.8 10.0 %collective-permute-start.16 = (bf16[256,640]{1,0:T(8,128)(2,1)S(1)}, bf16[256,640]{1,0:T(8,128)(2,1)S(1)}, u32[]{:S(2)}, u32[]{:S(2)}) collective-permute-start(bf16[256,640]{1,0:T(8,128)(2,1)S(1)} %collective-permute-done.15), channel_id=1, source_target_pairs={{0,2},{1,5},{2,0},{3,7},{4,6},{5,1},{6,4},{7,3},{8,10},{9,13},{10,... | collective-permute-start | bytes 983048 | tf_op jit(solution)/shard_map/ppermute | solution.py:354
  154.2 11.4 %collective-permute-start.25 = (bf16[256,512]{1,0:T(8,128)(2,1)S(1)}, bf16[256,512]{1,0:T(8,128)(2,1)S(1)}, u32[]{:S(2)}, u32[]{:S(2)}) collective-permute-start(bf16[256,512]{1,0:T(8,128)(2,1)S(1)} %collective-permute-done.24), channel_id=1, source_target_pairs={{0,2},{1,5},{2,0},{3,7},{4,6},{5,1},{6,4},{7,3},{8,10},{9,13},{10,... | collective-permute-start | bytes 786440 | tf_op jit(solution)/shard_map/ppermute | solution.py:354
  159.3 11.2 %collective-permute-start.29 = (bf16[256,640]{1,0:T(8,128)(2,1)S(1)}, bf16[256,640]{1,0:T(8,128)(2,1)S(1)}, u32[]{:S(2)}, u32[]{:S(2)}) collective-permute-start(bf16[256,640]{1,0:T(8,128)(2,1)S(1)} %collective-permute-done.27.refs_0_), channel_id=1, source_target_pairs={{0,1},{1,0},{2,3},{3,2},{4,5},{5,4},{6,7},{7,6},{8,9},{9,8},{10,11... | collective-permute-start | bytes 983048 | tf_op jit(solution)/shard_map/ppermute | solution.py:354
  162.8 11.8 %collective-permute-start.17 = (bf16[256,640]{1,0:T(8,128)(2,1)S(1)}, bf16[256,640]{1,0:T(8,128)(2,1)S(1)}, u32[]{:S(2)}, u32[]{:S(2)}) collective-permute-start(bf16[256,640]{1,0:T(8,128)(2,1)S(1)} %collective-permute-done.16.refs_0_), channel_id=1, source_target_pairs={{0,1},{1,0},{2,3},{3,2},{4,5},{5,4},{6,7},{7,6},{8,9},{9,8},{10,11... | collective-permute-start | bytes 983048 | tf_op jit(solution)/shard_map/ppermute | solution.py:354
  165.6 4.9 %collective-permute-start.30 = (bf16[256,512]{1,0:T(8,128)(2,1)S(1)}, bf16[256,512]{1,0:T(8,128)(2,1)S(1)}, u32[]{:S(2)}, u32[]{:S(2)}) collective-permute-start(bf16[256,512]{1,0:T(8,128)(2,1)S(1)} %collective-permute-done.28.refs_1_), channel_id=1, source_target_pairs={{0,1},{1,0},{2,3},{3,2},{4,5},{5,4},{6,7},{7,6},{8,9},{9,8},{10,11... | collective-permute-start | bytes 786440 | tf_op jit(solution)/shard_map/ppermute | solution.py:354
  165.6 9.0 %collective-permute-start.26 = (bf16[256,512]{1,0:T(8,128)(2,1)S(1)}, bf16[256,512]{1,0:T(8,128)(2,1)S(1)}, u32[]{:S(2)}, u32[]{:S(2)}) collective-permute-start(bf16[256,512]{1,0:T(8,128)(2,1)S(1)} %collective-permute-done.25.refs_1_), channel_id=1, source_target_pairs={{0,1},{1,0},{2,3},{3,2},{4,5},{5,4},{6,7},{7,6},{8,9},{9,8},{10,11... | collective-permute-start | bytes 786440 | tf_op jit(solution)/shard_map/ppermute | solution.py:354
  208.5 4.8 %collective-permute-start.33 = (bf16[32,512]{1,0:T(8,128)(2,1)S(1)}, bf16[32,512]{1,0:T(8,128)(2,1)S(1)}, u32[]{:S(2)}, u32[]{:S(2)}) collective-permute-start(bf16[32,512]{1,0:T(8,128)(2,1)S(1)} %shard_map.47), channel_id=1, source_target_pairs={{0,16},{8,24},{16,0},{24,8},{1,17},{9,25},{17,1},{25,9},{2,18},{10... | collective-permute-start | bytes 98312 | tf_op jit(solution)/shard_map/ppermute | solution.py:354
  213.3 4.3 %collective-permute-start.34 = (bf16[32,1024]{1,0:T(8,128)(2,1)S(1)}, bf16[32,1024]{1,0:T(8,128)(2,1)S(1)}, u32[]{:S(2)}, u32[]{:S(2)}) collective-permute-start(bf16[32,1024]{1,0:T(8,128)(2,1)S(1)} %pad_maximum_fusion.6), channel_id=1, source_target_pairs={{0,8},{8,0},{16,24},{24,16},{1,9},{9,1},{17,25},{25,17},{2,10},{10... | collective-permute-start | bytes 196616 | tf_op jit(solution)/shard_map/ppermute | solution.py:354

commit v13 on v12

--- a/solution.py
+++ b/solution.py
@@ -263,9 +263,10 @@
 def unpack(offset, index_ref, share_refs, q_ref, full, u, v, diag):
     n = q_ref.shape[1]
     width = n // 2
-    cut = share_refs[0].shape[1]
-    bs = cut + share_refs[1].shape[1] - width
+    bs = LANES
     nb = n // bs
+    cut = (nb // 4 + 1) * bs
+    rows = [ref.shape[0] for ref in share_refs if ref is not None][0]
     lane = lax.broadcasted_iota(jnp.int32, (bs, bs), 1)
 
     def one(r, _):
@@ -274,11 +275,15 @@
         to = pl.multiple_of(i * bs, bs)
         for d in range(nb // 2):
             ref, col = (share_refs[0], d * bs) if d * bs < cut else (share_refs[1], d * bs - cut)
+            if ref is None:
+                continue
             part = ref[pl.ds(frm, bs), col : col + bs]
             at = pl.multiple_of(lax.rem(i + d, nb) * bs, bs)
             full[pl.ds(to, bs), pl.ds(at, bs)] = part
             if d:
                 full[pl.ds(at, bs), pl.ds(to, bs)] = part.T
+        if share_refs[1] is None:
+            return 0
         at = pl.multiple_of(lax.rem(i + nb // 2, nb) * bs, bs)
         last = share_refs[1][pl.ds(frm, bs), width - cut :].astype(F32)
 
@@ -310,13 +315,14 @@
         v[:, pl.ds(to, bs)] = jnp.concatenate([v1, v2, v3, v1, v2, v1], axis=0)
         return 0
 
-    lax.fori_loop(0, share_refs[0].shape[0] // bs, one, 0)
-
-
-def unpack_kernel(offsets, index_ref, *refs):
-    q_ref = refs[2 * len(offsets)]
-    for i, offset in enumerate(offsets):
-        unpack(offset, index_ref, refs[2 * i : 2 * i + 2], q_ref, *refs[-4:])
+    lax.fori_loop(0, rows // bs, one, 0)
+
+
+def unpack_kernel(items, count, index_ref, *refs):
+    shares = iter(refs[:count])
+    for offset, given in items:
+        pair = [next(shares) if e in given else None for e in (0, 1)]
+        unpack(offset, index_ref, pair, refs[count], *refs[-4:])
 
 
 def iterate_kernel(offset, index_ref, far_0, far_1, q_ref, p0_ref, *refs):
@@ -410,8 +416,9 @@
     )(index, low, far, stamps)
     for b in (1, 2, 4):
         proj = ordered(proj, flip(proj, "pix", xor_pix(b)), p & b, axis=1)
-    for b in (1, 2):
-        proj = ordered(proj, flip(proj, "samp", xor_samp(b)), s & b, axis=1)
+    other = flip(proj, "samp", xor_samp(1))
+    proj = ordered(proj, other, z0, axis=1)
+    proj = ordered(proj, flip(proj, "samp", xor_samp(2)), z1, axis=1)
     proj, q = kernel_call(
         functools.partial(basis_kernel, pix, samp),
         (jax.ShapeDtypeStruct((k, n), BF16), jax.ShapeDtypeStruct((k, n), F32)),
@@ -478,26 +485,24 @@
         jax.ShapeDtypeStruct((8, n), F32),
     )
     eighth = nb // 8
-    now = kernel_call(
-        functools.partial(unpack_kernel, (BLOCKS, BLOCKS + 4 * eighth)),
-        parts,
-        in_specs=[smem()] + vmem(5),
-        out_specs=tuple(vmem(4)),
-        scratch_mib=4,
-    )(index, *near, *far, q)
-
-    def unpack_more(now, slots, *shares):
+
+    def unpack_into(now, slots, given, *shares):
+        count = len(shares)
+        items = [(BLOCKS + i * eighth, given) for i in slots]
+        aliases = {count + 2 + i: i for i in range(len(now))}
         return kernel_call(
-            functools.partial(unpack_kernel, [BLOCKS + i * eighth for i in slots]),
+            functools.partial(unpack_kernel, items, count),
             parts,
-            in_specs=[smem()] + vmem(len(shares) + 5),
+            in_specs=[smem()] + vmem(count + 1 + len(now)),
             out_specs=tuple(vmem(4)),
-            input_output_aliases={len(shares) + 2 + i: i for i in range(4)},
+            input_output_aliases=aliases,
             scratch_mib=4,
         )(index, *shares, q, *now)
 
-    now = unpack_more(now, (2, 6), *over_a, *far_a)
-    now = unpack_more(now, (3,), *over_ab)
+    now = unpack_into((), (0, 4), (0,), near[0], far[0])
+    now = unpack_into(now, (0, 4), (1,), near[1], far[1])
+    now = unpack_into(now, (2, 6), (0, 1), *over_a, *far_a)
+    now = unpack_into(now, (3,), (0, 1), *over_ab)
     proj, inv = kernel_call(
         functools.partial(iterate_kernel, BLOCKS + 7 * eighth),
         (jax.ShapeDtypeStruct((k, n), BF16), jax.ShapeDtypeStruct((k, LANES), F32)) + parts,
@@ -528,7 +533,7 @@
     def local(stamps, start_panel):
         n = stamps.shape[0] * pix * samp
         k = start_panel.shape[1]
-        if n <= SAMPLE_SPACE_LIMIT and (pix, samp) == (8, 4) and 4 * k == LANES:
+        if n <= SAMPLE_SPACE_LIMIT and (pix, samp) == (8, 4) and 4 * k == 2 * stamps.shape[0] == LANES:
             return sample_space(stamps, start_panel)
         return pixel_space(stamps, start_panel)
 

time: 219 us -> 227 us (1.037)
  starting transfers between devices: 37.8 us -> 42.1 us
    ppermute x35, starting transfers between devices: 30.4 us -> 34.8 us  [flip(): return lax.ppermute(x, axes, perm)]
    ppermute x35, waiting for transfers between devices: 81.7 us -> 84.2 us  [flip(): return lax.ppermute(x, axes, perm)]
    pallas_call x20 -> x21, Pallas kernels: 66.5 us -> 67.5 us  [kernel_call(): return lambda *args: call(*map(place, args, in_specs))]
  transfers between devices with their start and end apart: 36 -> 36, of which waited for: 23 -> 25; matrix products, arithmetic and copies ran while one was open for 0% -> 0% of each run, Pallas kernels for 11% -> 11%
where the time goes in v13:
time: 227 us; the launch traced here: 226 us
  waiting for transfers between devices  110 us (48%)
  Pallas kernels  67.5 us (30%)
  starting transfers between devices  42.1 us (19%)
  local copies, waits for them, and re-layouts  4.89 us (2%)
    ppermute x35, waiting for transfers between devices, flip(): return lax.ppermute(x, axes, perm)  84.2 us
    pallas_call x21, Pallas kernels, kernel_call(): return lambda *args: call(*map(place, args, in_specs))  67.5 us
    ppermute x35, starting transfers between devices, flip(): return lax.ppermute(x, axes, perm)  34.8 us
    all_to_all x1, waiting for transfers between devices, sample_space(): lax.all_to_all(stamps, ('pix', 'samp'), split_axis=1, concat_axis=0, tile...  26 us
    all_to_all x1, starting transfers between devices, sample_space(): lax.all_to_all(stamps, ('pix', 'samp'), split_axis=1, concat_axis=0, tile...  7.33 us
  transfers between devices with their start and end apart: 36, of which 25 were waited for; matrix products, arithmetic and copies ran while one was open for 0% of the time, Pallas kernels for 11%

profile of v13, /device:TPU:0, one launch (start us, length us, event | category | flops | bytes accessed | tf_op | source)
XLA Modules:
  0.0 226.2 jit_solution(6318489890072263628)
XLA Ops:
  0.0 3.2 %copy.22 = bf16[8,32,8,512]{3,2,0,1:T(8,128)(2,1)} copy(bf16[8,32,8,512]{3,2,1,0:T(8,128)(2,1)} %bitcast.25) | data formatting | bytes 4194304 | tf_op jit(solution)/shard_map/all_to_all | solution.py:409
  3.2 7.3 %all-to-all-start = ((bf16[64,32,512]{2,0,1:T(8,128)(2,1)}), bf16[64,32,512]{2,0,1:T(8,128)(2,1)S(1)}, u32[]{:S(2)}, u32[]{:S(2)}) async-start(bf16[64,32,512]{2,0,1:T(8,128)(2,1)} %bitcast.26), calls=%async_computation | async-start | bytes 4194304 | tf_op jit(solution)/shard_map/all_to_all | solution.py:409
  10.6 1.8 collective-permute-start.1
  12.4 17.3 %collective-permute-done.1 = bf16[32,2048]{1,0:T(8,128)(2,1)S(1)} collective-permute-done((bf16[32,2048]{1,0:T(8,128)(2,1)S(1)}, bf16[32,2048]{1,0:T(8,128)(2,1)S(1)}, u32[]{:S(2)}, u32[]{:S(2)}) %collective-permute-start.1) | collective-permute-done | bytes 131104 | tf_op jit(solution)/shard_map/ppermute | solution.py:360
  29.7 1.5 collective-permute-start.2
  31.3 26.0 %all-to-all-done = bf16[64,32,512]{2,0,1:T(8,128)(2,1)S(1)} async-done(((bf16[64,32,512]{2,0,1:T(8,128)(2,1)}), bf16[64,32,512]{2,0,1:T(8,128)(2,1)S(1)}, u32[]{:S(2)}, u32[]{:S(2)}) %all-to-all-start) | async-done | bytes 2097184 | tf_op jit(solution)/shard_map/all_to_all | solution.py:409
  57.3 1.8 collective-permute-start
  59.4 4.3 %collective-permute-done.3.far_ref = bf16[32,8192]{1,0:T(8,128)(2,1)S(1)} collective-permute-done((bf16[32,8192]{1,0:T(8,128)(2,1)S(1)}, bf16[32,8192]{1,0:T(8,128)(2,1)S(1)}, u32[]{:S(2)}, u32[]{:S(2)}) %collective-permute-start.3) | collective-permute-done | bytes 524320 | tf_op jit(solution)/shard_map/ppermute | solution.py:360
  63.6 1.6 copy-done
  67.7 1.5 collective-permute-start.5
  69.3 2.1 collective-permute-done.5
  71.4 1.5 collective-permute-start.6
  72.9 2.2 collective-permute-done.6
  75.2 2.3 %collective-permute-start.7 = (bf16[32,512]{1,0:T(8,128)(2,1)S(1)}, bf16[32,512]{1,0:T(8,128)(2,1)S(1)}, u32[]{:S(2)}, u32[]{:S(2)}) collective-permute-start(bf16[32,512]{1,0:T(8,128)(2,1)S(1)} %maximum_select_fusion.2), channel_id=1, source_target_pairs={{0,8},{8,0},{16,24},{24,16},{1,9},{9,1},{17,25},{25,17},{2,10},{10... | collective-permute-start | bytes 98312 | tf_op jit(solution)/shard_map/ppermute | solution.py:360
  77.5 1.9 collective-permute-done.7
  80.6 4.0 %collective-permute-done.8 = bf16[32,1024]{1,0:T(8,128)(2,1)S(1)} collective-permute-done((bf16[32,1024]{1,0:T(8,128)(2,1)S(1)}, bf16[32,1024]{1,0:T(8,128)(2,1)S(1)}, u32[]{:S(2)}, u32[]{:S(2)}) %collective-permute-start.8) | collective-permute-done | bytes 65568 | tf_op jit(solution)/shard_map/ppermute | solution.py:360
  84.7 1.4 shard_map.29
  86.0 4.9 %shard_map.30 = (bf16[192,2048]{1,0:T(8,128)(2,1)S(1)}, bf16[192,2048]{1,0:T(8,128)(2,1)S(1)}) custom-call(bf16[2048,512]{1,0:T(8,128)(2,1)S(1)} %bitcast.19, bf16[2048,512]{1,0:T(8,128)(2,1)} %collective-permute-done.other_ref, f32[32,2048]{1,0:T(8,128)S(1)} %get-tuple-element.39.q_ref.refs_2_.refs_4_), custom_call_target="tpu_custom_call" | custom-call | tf_op jit(solution)/shard_map/pallas_call | solution.py:77
  91.0 2.8 %shard_map.34 = (bf16[256,640]{1,0:T(8,128)(2,1)S(1)}, bf16[256,512]{1,0:T(8,128)(2,1)S(1)}) custom-call(s32[32]{0:T(128)S(1)} %concatenate.60.index_ref.at_ref, bf16[2048,512]{1,0:T(8,128)(2,1)S(1)} %bitcast.20, bf16[2048,512]{1,0:T(8,128)(2,1)} %collective-permute-done.other_ref, bf16[192,2048]{1,0:T(8,128)(2,1)S(1)} %get-tuple-element.40.left, ...), custom_call_target="tpu_custom_call" | custom-call | tf_op jit(solution)/shard_map/pallas_call | solution.py:77
  93.8 2.0 collective-permute-start.10
  95.8 2.8 %shard_map.32 = (bf16[256,640]{1,0:T(8,128)(2,1)S(1)}, bf16[256,512]{1,0:T(8,128)(2,1)S(1)}) custom-call(s32[32]{0:T(128)S(1)} %concatenate.60.index_ref.at_ref, bf16[2048,512]{1,0:T(8,128)(2,1)S(1)} %bitcast.21, bf16[2048,512]{1,0:T(8,128)(2,1)} %collective-permute-done.other_ref, bf16[192,2048]{1,0:T(8,128)(2,1)S(1)} %get-tuple-element.40.left, ...), custom_call_target="tpu_custom_call" | custom-call | tf_op jit(solution)/shard_map/pallas_call | solution.py:77
  98.7 2.8 %shard_map.33 = (bf16[256,640]{1,0:T(8,128)(2,1)S(1)}, bf16[256,512]{1,0:T(8,128)(2,1)S(1)}) custom-call(s32[32]{0:T(128)S(1)} %concatenate.60.index_ref.at_ref, bf16[2048,512]{1,0:T(8,128)(2,1)S(1)} %bitcast.22, bf16[2048,512]{1,0:T(8,128)(2,1)} %collective-permute-done.other_ref, bf16[192,2048]{1,0:T(8,128)(2,1)S(1)} %get-tuple-element.40.left, ...), custom_call_target="tpu_custom_call" | custom-call | tf_op jit(solution)/shard_map/pallas_call | solution.py:77
  103.5 2.8 %shard_map.31 = (bf16[256,640]{1,0:T(8,128)(2,1)S(1)}, bf16[256,512]{1,0:T(8,128)(2,1)S(1)}) custom-call(s32[32]{0:T(128)S(1)} %concatenate.60.index_ref.at_ref, bf16[2048,512]{1,0:T(8,128)(2,1)S(1)} %bitcast.23, bf16[2048,512]{1,0:T(8,128)(2,1)} %collective-permute-done.other_ref, bf16[192,2048]{1,0:T(8,128)(2,1)S(1)} %get-tuple-element.40.left, ...), custom_call_target="tpu_custom_call" | custom-call | tf_op jit(solution)/shard_map/pallas_call | solution.py:77
  106.3 1.7 collective-permute-done.9.refs_1_
  107.9 1.4 collective-permute-done.11.refs_2_
  110.0 2.5 %collective-permute-start.12 = (bf16[128,640]{1,0:T(8,128)(2,1)S(1)}, bf16[128,640]{1,0:T(8,128)(2,1)S(1)}, u32[]{:S(2)}, u32[]{:S(2)}) collective-permute-start(bf16[128,640]{1,0:T(8,128)(2,1)S(1)} %get-tuple-element.47), channel_id=1, source_target_pairs={{0,8},{8,0},{16,24},{24,16},{1,9},{9,1},{17,25},{25,17},{2,10},{10... | collective-permute-start | bytes 491528 | tf_op jit(solution)/shard_map/ppermute | solution.py:360
  112.5 4.2 %collective-permute-done.12.refs_1_ = bf16[128,640]{1,0:T(8,128)(2,1)S(1)} collective-permute-done((bf16[128,640]{1,0:T(8,128)(2,1)S(1)}, bf16[128,640]{1,0:T(8,128)(2,1)S(1)}, u32[]{:S(2)}, u32[]{:S(2)}) %collective-permute-start.12) | collective-permute-done | bytes 163872 | tf_op jit(solution)/shard_map/ppermute | solution.py:360
  117.5 6.1 %collective-permute-done.13.refs_1_ = bf16[128,640]{1,0:T(8,128)(2,1)S(1)} collective-permute-done((bf16[128,640]{1,0:T(8,128)(2,1)S(1)}, bf16[128,640]{1,0:T(8,128)(2,1)S(1)}, u32[]{:S(2)}, u32[]{:S(2)}) %collective-permute-start.13) | collective-permute-done | bytes 163872 | tf_op jit(solution)/shard_map/ppermute | solution.py:360
  124.2 3.7 %collective-permute-start.14 = (bf16[128,640]{1,0:T(8,128)(2,1)S(1)}, bf16[128,640]{1,0:T(8,128)(2,1)S(1)}, u32[]{:S(2)}, u32[]{:S(2)}) collective-permute-start(bf16[128,640]{1,0:T(8,128)(2,1)S(1)} %shard_map.38), channel_id=1, source_target_pairs={{0,8},{8,0},{16,24},{24,16},{1,9},{9,1},{17,25},{25,17},{2,10},{10... | collective-permute-start | bytes 491528 | tf_op jit(solution)/shard_map/ppermute | solution.py:360
  128.8 1.7 collective-permute-start.20
  131.3 1.8 collective-permute-start.15
  133.1 1.5 collective-permute-done.18.refs_1_
  137.1 4.2 %collective-permute-done.21.refs_1_ = bf16[128,512]{1,0:T(8,128)(2,1)S(1)} collective-permute-done((bf16[128,512]{1,0:T(8,128)(2,1)S(1)}, bf16[128,512]{1,0:T(8,128)(2,1)S(1)}, u32[]{:S(2)}, u32[]{:S(2)}) %collective-permute-start.21) | collective-permute-done | bytes 131104 | tf_op jit(solution)/shard_map/ppermute | solution.py:360
  143.2 6.2 %collective-permute-done.22.refs_1_ = bf16[128,512]{1,0:T(8,128)(2,1)S(1)} collective-permute-done((bf16[128,512]{1,0:T(8,128)(2,1)S(1)}, bf16[128,512]{1,0:T(8,128)(2,1)S(1)}, u32[]{:S(2)}, u32[]{:S(2)}) %collective-permute-start.22) | collective-permute-done | bytes 131104 | tf_op jit(solution)/shard_map/ppermute | solution.py:360
  150.4 4.8 %collective-permute-done.23 = bf16[128,512]{1,0:T(8,128)(2,1)S(1)} collective-permute-done((bf16[128,512]{1,0:T(8,128)(2,1)S(1)}, bf16[128,512]{1,0:T(8,128)(2,1)S(1)}, u32[]{:S(2)}, u32[]{:S(2)}) %collective-permute-start.23) | collective-permute-done | bytes 131104 | tf_op jit(solution)/shard_map/ppermute | solution.py:360
  156.3 1.5 collective-permute-start.28
  158.3 1.5 collective-permute-start.16
  159.8 4.6 %collective-permute-done.24 = bf16[256,512]{1,0:T(8,128)(2,1)S(1)} collective-permute-done((bf16[256,512]{1,0:T(8,128)(2,1)S(1)}, bf16[256,512]{1,0:T(8,128)(2,1)S(1)}, u32[]{:S(2)}, u32[]{:S(2)}) %collective-permute-start.24) | collective-permute-done | bytes 262176 | tf_op jit(solution)/shard_map/ppermute | solution.py:360
  164.6 1.4 collective-permute-start.25
  166.2 3.5 %collective-permute-done.16.refs_0_ = bf16[256,640]{1,0:T(8,128)(2,1)S(1)} collective-permute-done((bf16[256,640]{1,0:T(8,128)(2,1)S(1)}, bf16[256,640]{1,0:T(8,128)(2,1)S(1)}, u32[]{:S(2)}, u32[]{:S(2)}) %collective-permute-start.16) | collective-permute-done | bytes 327712 | tf_op jit(solution)/shard_map/ppermute | solution.py:360
  169.7 2.8 %collective-permute-done.25.refs_1_ = bf16[256,512]{1,0:T(8,128)(2,1)S(1)} collective-permute-done((bf16[256,512]{1,0:T(8,128)(2,1)S(1)}, bf16[256,512]{1,0:T(8,128)(2,1)S(1)}, u32[]{:S(2)}, u32[]{:S(2)}) %collective-permute-start.25) | collective-permute-done | bytes 262176 | tf_op jit(solution)/shard_map/ppermute | solution.py:360
  173.0 1.4 shard_map.43
  174.5 3.9 %shard_map.44 = (bf16[2048,2048]{1,0:T(8,128)(2,1)S(1)}, bf16[2048,128]{1,0:T(8,128)(2,1)S(1)}, bf16[192,2048]{1,0:T(8,128)(2,1)S(1)}, f32[8,2048]{1,0:T(8,128)S(1)}) custom-call(s32[32]{0:T(128)S(1)} %concatenate.60.index_ref.at_ref, ...), custom_call_target="tpu_custom_call", output_to_operand_aliasing={{0}: (4, {}), {1}: (5, {}), {2}: (6, {}), {3}: (7, {})} | custom-call | tf_op jit(solution)/shard_map/pallas_call | solution.py:77
  178.3 2.6 %shard_map.45 = (bf16[2048,2048]{1,0:T(8,128)(2,1)S(1)}, bf16[2048,128]{1,0:T(8,128)(2,1)S(1)}, bf16[192,2048]{1,0:T(8,128)(2,1)S(1)}, f32[8,2048]{1,0:T(8,128)S(1)}) custom-call(s32[32]{0:T(128)S(1)} %concatenate.60.index_ref.at_ref, ...), custom_call_target="tpu_custom_call", output_to_operand_aliasing={{0}: (6, {}), {1}: (7, {}), {2}: (8, {}), {3}: (9, {})} | custom-call | tf_op jit(solution)/shard_map/pallas_call | solution.py:77
  181.0 1.4 shard_map.46
  182.4 33.3 %shard_map.47 = (bf16[32,2048]{1,0:T(8,128)(2,1)S(1)}, f32[32,128]{1,0:T(8,128)S(1)}, bf16[2048,2048]{1,0:T(8,128)(2,1)S(1)}, bf16[2048,128]{1,0:T(8,128)(2,1)S(...) custom-call(s32[32]{0:T(128)S(1)} %concatenate.60.index_ref.at_ref, ...), custom_call_target="tpu_custom_call", output_to_operand_aliasing={{2}: (5, {}), {3}: (6, {}), {4}: (7, {}), {5}: (8, {})} | custom-call | tf_op jit(solution)/shard_map/pallas_call | solution.py:77
  216.5 4.6 %collective-permute-done.33 = bf16[32,512]{1,0:T(8,128)(2,1)S(1)} collective-permute-done((bf16[32,512]{1,0:T(8,128)(2,1)S(1)}, bf16[32,512]{1,0:T(8,128)(2,1)S(1)}, u32[]{:S(2)}, u32[]{:S(2)}) %collective-permute-start.33) | collective-permute-done | bytes 32800 | tf_op jit(solution)/shard_map/ppermute | solution.py:360
  221.2 4.3 %collective-permute-done.34 = bf16[32,1024]{1,0:T(8,128)(2,1)S(1)} collective-permute-done((bf16[32,1024]{1,0:T(8,128)(2,1)S(1)}, bf16[32,1024]{1,0:T(8,128)(2,1)S(1)}, u32[]{:S(2)}, u32[]{:S(2)}) %collective-permute-start.34) | collective-permute-done | bytes 65568 | tf_op jit(solution)/shard_map/ppermute | solution.py:360
  (68 shorter events, 19.0 us)
Async XLA Ops:
  3.2 7.3 %copy-start.1 = (f32[2048,32]{0,1:T(8,128)S(1)}, f32[2048,32]{0,1:T(8,128)}, u32[]{:S(2)}) copy-start(f32[2048,32]{0,1:T(8,128)} %param.3) | copy-start | bytes 786436
  3.2 54.1 %all-to-all-start = ((bf16[64,32,512]{2,0,1:T(8,128)(2,1)}), bf16[64,32,512]{2,0,1:T(8,128)(2,1)S(1)}, u32[]{:S(2)}, u32[]{:S(2)}) async-start(bf16[64,32,512]{2,0,1:T(8,128)(2,1)} %bitcast.26), calls=%async_computation | async-start | bytes 4194304 | tf_op jit(solution)/shard_map/all_to_all | solution.py:409
  10.6 19.1 %collective-permute-start.1 = (bf16[32,2048]{1,0:T(8,128)(2,1)S(1)}, bf16[32,2048]{1,0:T(8,128)(2,1)S(1)}, u32[]{:S(2)}, u32[]{:S(2)}) collective-permute-start(bf16[32,2048]{1,0:T(8,128)(2,1)S(1)} %convert_bitcast_fusion.1), channel_id=1, source_target_pairs={{0,2},{1,3},{2,0},{3,1},{4,6},{5,7},{6,4},{7,5},{8,10},{9,11},{10,... | collective-permute-start | bytes 393224 | tf_op jit(solution)/shard_map/ppermute | solution.py:360
  29.7 29.4 %collective-permute-start.2 = (bf16[32,4096]{1,0:T(8,128)(2,1)S(1)}, bf16[32,4096]{1,0:T(8,128)(2,1)S(1)}, u32[]{:S(2)}, u32[]{:S(2)}) collective-permute-start(bf16[32,4096]{1,0:T(8,128)(2,1)S(1)} %pad_maximum_fusion.4), channel_id=1, source_target_pairs={{0,4},{1,5},{2,6},{3,7},{4,0},{5,1},{6,2},{7,3},{8,12},{9,13},{10,... | collective-permute-start | bytes 786440 | tf_op jit(solution)/shard_map/ppermute | solution.py:360
  57.3 28.8 %collective-permute-start = (bf16[2048,512]{1,0:T(8,128)(2,1)S(1)}, bf16[2048,512]{1,0:T(8,128)(2,1)}, u32[]{:S(2)}, u32[]{:S(2)}) collective-permute-start(bf16[2048,512]{1,0:T(8,128)(2,1)S(1)} %bitcast.18), channel_id=1, source_target_pairs={{0,1},{1,0},{2,3},{3,2},{4,5},{5,4},{6,7},{7,6},{8,9},{9,8},{10,11... | collective-permute-start | bytes 6291464 | tf_op jit(solution)/shard_map/ppermute | solution.py:360
  59.1 4.5 %collective-permute-start.3 = (bf16[32,8192]{1,0:T(8,128)(2,1)S(1)}, bf16[32,8192]{1,0:T(8,128)(2,1)S(1)}, u32[]{:S(2)}, u32[]{:S(2)}) collective-permute-start(bf16[32,8192]{1,0:T(8,128)(2,1)S(1)} %pad_maximum_fusion.1.near_ref), channel_id=1, source_target_pairs={{0,1},{1,0},{2,3},{3,2},{4,5},{5,4},{6,7},{7,6},{8,9},{9,8},{10,11... | collective-permute-start | bytes 1572872 | tf_op jit(solution)/shard_map/ppermute | solution.py:360
  63.6 1.6 copy-start
  66.4 1.2 collective-permute-start.4
  67.7 3.7 %collective-permute-start.5 = (bf16[32,128]{1,0:T(8,128)(2,1)S(1)}, bf16[32,128]{1,0:T(8,128)(2,1)S(1)}, u32[]{:S(2)}, u32[]{:S(2)}) collective-permute-start(bf16[32,128]{1,0:T(8,128)(2,1)S(1)} %maximum_select_fusion.4), channel_id=1, source_target_pairs={{0,2},{1,3},{2,0},{3,1},{4,6},{5,7},{6,4},{7,5},{8,10},{9,11},{10,... | collective-permute-start | bytes 24584 | tf_op jit(solution)/shard_map/ppermute | solution.py:360
  71.4 3.7 %collective-permute-start.6 = (bf16[32,256]{1,0:T(8,128)(2,1)S(1)}, bf16[32,256]{1,0:T(8,128)(2,1)S(1)}, u32[]{:S(2)}, u32[]{:S(2)}) collective-permute-start(bf16[32,256]{1,0:T(8,128)(2,1)S(1)} %maximum_select_fusion.3), channel_id=1, source_target_pairs={{0,4},{1,5},{2,6},{3,7},{4,0},{5,1},{6,2},{7,3},{8,12},{9,13},{10,... | collective-permute-start | bytes 49160 | tf_op jit(solution)/shard_map/ppermute | solution.py:360
  75.2 4.2 %collective-permute-start.7 = (bf16[32,512]{1,0:T(8,128)(2,1)S(1)}, bf16[32,512]{1,0:T(8,128)(2,1)S(1)}, u32[]{:S(2)}, u32[]{:S(2)}) collective-permute-start(bf16[32,512]{1,0:T(8,128)(2,1)S(1)} %maximum_select_fusion.2), channel_id=1, source_target_pairs={{0,8},{8,0},{16,24},{24,16},{1,9},{9,1},{17,25},{25,17},{2,10},{10... | collective-permute-start | bytes 98312 | tf_op jit(solution)/shard_map/ppermute | solution.py:360
  79.4 5.2 %collective-permute-start.8 = (bf16[32,1024]{1,0:T(8,128)(2,1)S(1)}, bf16[32,1024]{1,0:T(8,128)(2,1)S(1)}, u32[]{:S(2)}, u32[]{:S(2)}) collective-permute-start(bf16[32,1024]{1,0:T(8,128)(2,1)S(1)} %maximum_select_fusion.1), channel_id=1, source_target_pairs={{0,16},{8,24},{16,0},{24,8},{1,17},{9,25},{17,1},{25,9},{2,18},{10... | collective-permute-start | bytes 196616 | tf_op jit(solution)/shard_map/ppermute | solution.py:360
  93.8 7.8 %collective-permute-start.10 = (bf16[256,640]{1,0:T(8,128)(2,1)S(1)}, bf16[256,640]{1,0:T(8,128)(2,1)S(1)}, u32[]{:S(2)}, u32[]{:S(2)}) collective-permute-start(bf16[256,640]{1,0:T(8,128)(2,1)S(1)} %get-tuple-element.45), channel_id=1, source_target_pairs={{0,2},{1,5},{2,0},{3,7},{4,6},{5,1},{6,4},{7,3},{8,10},{9,13},{10,... | collective-permute-start | bytes 983048 | tf_op jit(solution)/shard_map/ppermute | solution.py:360
  98.6 9.3 %collective-permute-start.9 = (bf16[256,640]{1,0:T(8,128)(2,1)S(1)}, bf16[256,640]{1,0:T(8,128)(2,1)S(1)}, u32[]{:S(2)}, u32[]{:S(2)}) collective-permute-start(bf16[256,640]{1,0:T(8,128)(2,1)S(1)} %get-tuple-element.43), channel_id=1, source_target_pairs={{0,2},{1,5},{2,0},{3,7},{4,6},{5,1},{6,4},{7,3},{8,10},{9,13},{10,... | collective-permute-start | bytes 983048 | tf_op jit(solution)/shard_map/ppermute | solution.py:360
  102.2 7.1 %collective-permute-start.11 = (bf16[256,640]{1,0:T(8,128)(2,1)S(1)}, bf16[256,640]{1,0:T(8,128)(2,1)S(1)}, u32[]{:S(2)}, u32[]{:S(2)}) collective-permute-start(bf16[256,640]{1,0:T(8,128)(2,1)S(1)} %shard_map.35), channel_id=1, source_target_pairs={{0,4},{1,3},{2,6},{3,1},{4,0},{5,7},{6,2},{7,5},{8,12},{9,11},{10,... | collective-permute-start | bytes 983048 | tf_op jit(solution)/shard_map/ppermute | solution.py:360
  110.0 6.7 %collective-permute-start.12 = (bf16[128,640]{1,0:T(8,128)(2,1)S(1)}, bf16[128,640]{1,0:T(8,128)(2,1)S(1)}, u32[]{:S(2)}, u32[]{:S(2)}) collective-permute-start(bf16[128,640]{1,0:T(8,128)(2,1)S(1)} %get-tuple-element.47), channel_id=1, source_target_pairs={{0,8},{8,0},{16,24},{24,16},{1,9},{9,1},{17,25},{25,17},{2,10},{10... | collective-permute-start | bytes 491528 | tf_op jit(solution)/shard_map/ppermute | solution.py:360
  112.5 15.4 %collective-permute-start.19 = (bf16[256,512]{1,0:T(8,128)(2,1)S(1)}, bf16[256,512]{1,0:T(8,128)(2,1)S(1)}, u32[]{:S(2)}, u32[]{:S(2)}) collective-permute-start(bf16[256,512]{1,0:T(8,128)(2,1)S(1)} %get-tuple-element.51), channel_id=1, source_target_pairs={{0,2},{1,5},{2,0},{3,7},{4,6},{5,1},{6,4},{7,3},{8,10},{9,13},{10,... | collective-permute-start | bytes 786440 | tf_op jit(solution)/shard_map/ppermute | solution.py:360
  117.3 6.4 %collective-permute-start.13 = (bf16[128,640]{1,0:T(8,128)(2,1)S(1)}, bf16[128,640]{1,0:T(8,128)(2,1)S(1)}, u32[]{:S(2)}, u32[]{:S(2)}) collective-permute-start(bf16[128,640]{1,0:T(8,128)(2,1)S(1)} %shard_map.37.refs_0_), channel_id=1, source_target_pairs={{0,16},{8,24},{16,0},{24,8},{1,17},{9,25},{17,1},{25,9},{2,18},{10... | collective-permute-start | bytes 491528 | tf_op jit(solution)/shard_map/ppermute | solution.py:360
  124.2 7.0 %collective-permute-start.14 = (bf16[128,640]{1,0:T(8,128)(2,1)S(1)}, bf16[128,640]{1,0:T(8,128)(2,1)S(1)}, u32[]{:S(2)}, u32[]{:S(2)}) collective-permute-start(bf16[128,640]{1,0:T(8,128)(2,1)S(1)} %shard_map.38), channel_id=1, source_target_pairs={{0,8},{8,0},{16,24},{24,16},{1,9},{9,1},{17,25},{25,17},{2,10},{10... | collective-permute-start | bytes 491528 | tf_op jit(solution)/shard_map/ppermute | solution.py:360
  128.0 6.6 %collective-permute-start.18 = (bf16[256,512]{1,0:T(8,128)(2,1)S(1)}, bf16[256,512]{1,0:T(8,128)(2,1)S(1)}, u32[]{:S(2)}, u32[]{:S(2)}) collective-permute-start(bf16[256,512]{1,0:T(8,128)(2,1)S(1)} %get-tuple-element.49), channel_id=1, source_target_pairs={{0,2},{1,5},{2,0},{3,7},{4,6},{5,1},{6,4},{7,3},{8,10},{9,13},{10,... | collective-permute-start | bytes 786440 | tf_op jit(solution)/shard_map/ppermute | solution.py:360
  128.8 6.4 %collective-permute-start.20 = (bf16[256,512]{1,0:T(8,128)(2,1)S(1)}, bf16[256,512]{1,0:T(8,128)(2,1)S(1)}, u32[]{:S(2)}, u32[]{:S(2)}) collective-permute-start(bf16[256,512]{1,0:T(8,128)(2,1)S(1)} %shard_map.39), channel_id=1, source_target_pairs={{0,4},{1,3},{2,6},{3,1},{4,0},{5,7},{6,2},{7,5},{8,12},{9,11},{10,... | collective-permute-start | bytes 786440 | tf_op jit(solution)/shard_map/ppermute | solution.py:360
  131.3 18.9 %collective-permute-start.15 = (bf16[256,640]{1,0:T(8,128)(2,1)S(1)}, bf16[256,640]{1,0:T(8,128)(2,1)S(1)}, u32[]{:S(2)}, u32[]{:S(2)}) collective-permute-start(bf16[256,640]{1,0:T(8,128)(2,1)S(1)} %pad_maximum_fusion.3), channel_id=1, source_target_pairs={{0,4},{1,3},{2,6},{3,1},{4,0},{5,7},{6,2},{7,5},{8,12},{9,11},{10,... | collective-permute-start | bytes 983048 | tf_op jit(solution)/shard_map/ppermute | solution.py:360
  136.1 5.2 %collective-permute-start.21 = (bf16[128,512]{1,0:T(8,128)(2,1)S(1)}, bf16[128,512]{1,0:T(8,128)(2,1)S(1)}, u32[]{:S(2)}, u32[]{:S(2)}) collective-permute-start(bf16[128,512]{1,0:T(8,128)(2,1)S(1)} %get-tuple-element.53), channel_id=1, source_target_pairs={{0,8},{8,0},{16,24},{24,16},{1,9},{9,1},{17,25},{25,17},{2,10},{10... | collective-permute-start | bytes 393224 | tf_op jit(solution)/shard_map/ppermute | solution.py:360
  142.1 7.3 %collective-permute-start.22 = (bf16[128,512]{1,0:T(8,128)(2,1)S(1)}, bf16[128,512]{1,0:T(8,128)(2,1)S(1)}, u32[]{:S(2)}, u32[]{:S(2)}) collective-permute-start(bf16[128,512]{1,0:T(8,128)(2,1)S(1)} %shard_map.41.refs_0_), channel_id=1, source_target_pairs={{0,16},{8,24},{16,0},{24,8},{1,17},{9,25},{17,1},{25,9},{2,18},{10... | collective-permute-start | bytes 393224 | tf_op jit(solution)/shard_map/ppermute | solution.py:360
  150.1 5.0 %collective-permute-start.23 = (bf16[128,512]{1,0:T(8,128)(2,1)S(1)}, bf16[128,512]{1,0:T(8,128)(2,1)S(1)}, u32[]{:S(2)}, u32[]{:S(2)}) collective-permute-start(bf16[128,512]{1,0:T(8,128)(2,1)S(1)} %shard_map.42), channel_id=1, source_target_pairs={{0,8},{8,0},{16,24},{24,16},{1,9},{9,1},{17,25},{25,17},{2,10},{10... | collective-permute-start | bytes 393224 | tf_op jit(solution)/shard_map/ppermute | solution.py:360
  150.3 22.2 %collective-permute-start.32 = (bf16[512,640]{1,0:T(8,128)(2,1)S(1)}, bf16[512,640]{1,0:T(8,128)(2,1)S(1)}, u32[]{:S(2)}, u32[]{:S(2)}) collective-permute-start(bf16[512,640]{1,0:T(8,128)(2,1)S(1)} %pad_maximum_fusion.refs_0_), channel_id=1, source_target_pairs={{0,1},{1,0},{2,3},{3,2},{4,5},{5,4},{6,7},{7,6},{8,9},{9,8},{10,11... | collective-permute-start | bytes 1966088 | tf_op jit(solution)/shard_map/ppermute | solution.py:360
  155.2 9.2 %collective-permute-start.24 = (bf16[256,512]{1,0:T(8,128)(2,1)S(1)}, bf16[256,512]{1,0:T(8,128)(2,1)S(1)}, u32[]{:S(2)}, u32[]{:S(2)}) collective-permute-start(bf16[256,512]{1,0:T(8,128)(2,1)S(1)} %pad_maximum_fusion.5), channel_id=1, source_target_pairs={{0,4},{1,3},{2,6},{3,1},{4,0},{5,7},{6,2},{7,5},{8,12},{9,11},{10,... | collective-permute-start | bytes 786440 | tf_op jit(solution)/shard_map/ppermute | solution.py:360
  156.3 8.3 %collective-permute-start.28 = (bf16[256,512]{1,0:T(8,128)(2,1)S(1)}, bf16[256,512]{1,0:T(8,128)(2,1)S(1)}, u32[]{:S(2)}, u32[]{:S(2)}) collective-permute-start(bf16[256,512]{1,0:T(8,128)(2,1)S(1)} %pad_maximum_fusion.5), channel_id=1, source_target_pairs={{0,2},{1,5},{2,0},{3,7},{4,6},{5,1},{6,4},{7,3},{8,10},{9,13},{10,... | collective-permute-start | bytes 786440 | tf_op jit(solution)/shard_map/ppermute | solution.py:360
  157.8 8.4 %collective-permute-start.27 = (bf16[256,640]{1,0:T(8,128)(2,1)S(1)}, bf16[256,640]{1,0:T(8,128)(2,1)S(1)}, u32[]{:S(2)}, u32[]{:S(2)}) collective-permute-start(bf16[256,640]{1,0:T(8,128)(2,1)S(1)} %pad_maximum_fusion.3), channel_id=1, source_target_pairs={{0,2},{1,5},{2,0},{3,7},{4,6},{5,1},{6,4},{7,3},{8,10},{9,13},{10,... | collective-permute-start | bytes 983048 | tf_op jit(solution)/shard_map/ppermute | solution.py:360
  158.3 11.4 %collective-permute-start.16 = (bf16[256,640]{1,0:T(8,128)(2,1)S(1)}, bf16[256,640]{1,0:T(8,128)(2,1)S(1)}, u32[]{:S(2)}, u32[]{:S(2)}) collective-permute-start(bf16[256,640]{1,0:T(8,128)(2,1)S(1)} %collective-permute-done.15), channel_id=1, source_target_pairs={{0,2},{1,5},{2,0},{3,7},{4,6},{5,1},{6,4},{7,3},{8,10},{9,13},{10,... | collective-permute-start | bytes 983048 | tf_op jit(solution)/shard_map/ppermute | solution.py:360
  164.5 10.0 %collective-permute-start.31 = (bf16[512,512]{1,0:T(8,128)(2,1)S(1)}, bf16[512,512]{1,0:T(8,128)(2,1)S(1)}, u32[]{:S(2)}, u32[]{:S(2)}) collective-permute-start(bf16[512,512]{1,0:T(8,128)(2,1)S(1)} %pad_maximum_fusion.2.refs_0_), channel_id=1, source_target_pairs={{0,1},{1,0},{2,3},{3,2},{4,5},{5,4},{6,7},{7,6},{8,9},{9,8},{10,11... | collective-permute-start | bytes 1572872 | tf_op jit(solution)/shard_map/ppermute | solution.py:360
  164.6 7.9 %collective-permute-start.25 = (bf16[256,512]{1,0:T(8,128)(2,1)S(1)}, bf16[256,512]{1,0:T(8,128)(2,1)S(1)}, u32[]{:S(2)}, u32[]{:S(2)}) collective-permute-start(bf16[256,512]{1,0:T(8,128)(2,1)S(1)} %collective-permute-done.24), channel_id=1, source_target_pairs={{0,2},{1,5},{2,0},{3,7},{4,6},{5,1},{6,4},{7,3},{8,10},{9,13},{10,... | collective-permute-start | bytes 786440 | tf_op jit(solution)/shard_map/ppermute | solution.py:360
  166.2 12.2 %collective-permute-start.29 = (bf16[256,640]{1,0:T(8,128)(2,1)S(1)}, bf16[256,640]{1,0:T(8,128)(2,1)S(1)}, u32[]{:S(2)}, u32[]{:S(2)}) collective-permute-start(bf16[256,640]{1,0:T(8,128)(2,1)S(1)} %collective-permute-done.27.refs_0_), channel_id=1, source_target_pairs={{0,1},{1,0},{2,3},{3,2},{4,5},{5,4},{6,7},{7,6},{8,9},{9,8},{10,11... | collective-permute-start | bytes 983048 | tf_op jit(solution)/shard_map/ppermute | solution.py:360
  169.7 12.7 %collective-permute-start.17 = (bf16[256,640]{1,0:T(8,128)(2,1)S(1)}, bf16[256,640]{1,0:T(8,128)(2,1)S(1)}, u32[]{:S(2)}, u32[]{:S(2)}) collective-permute-start(bf16[256,640]{1,0:T(8,128)(2,1)S(1)} %collective-permute-done.16.refs_0_), channel_id=1, source_target_pairs={{0,1},{1,0},{2,3},{3,2},{4,5},{5,4},{6,7},{7,6},{8,9},{9,8},{10,11... | collective-permute-start | bytes 983048 | tf_op jit(solution)/shard_map/ppermute | solution.py:360
  172.5 5.9 %collective-permute-start.30 = (bf16[256,512]{1,0:T(8,128)(2,1)S(1)}, bf16[256,512]{1,0:T(8,128)(2,1)S(1)}, u32[]{:S(2)}, u32[]{:S(2)}) collective-permute-start(bf16[256,512]{1,0:T(8,128)(2,1)S(1)} %collective-permute-done.28.refs_1_), channel_id=1, source_target_pairs={{0,1},{1,0},{2,3},{3,2},{4,5},{5,4},{6,7},{7,6},{8,9},{9,8},{10,11... | collective-permute-start | bytes 786440 | tf_op jit(solution)/shard_map/ppermute | solution.py:360
  172.5 9.9 %collective-permute-start.26 = (bf16[256,512]{1,0:T(8,128)(2,1)S(1)}, bf16[256,512]{1,0:T(8,128)(2,1)S(1)}, u32[]{:S(2)}, u32[]{:S(2)}) collective-permute-start(bf16[256,512]{1,0:T(8,128)(2,1)S(1)} %collective-permute-done.25.refs_1_), channel_id=1, source_target_pairs={{0,1},{1,0},{2,3},{3,2},{4,5},{5,4},{6,7},{7,6},{8,9},{9,8},{10,11... | collective-permute-start | bytes 786440 | tf_op jit(solution)/shard_map/ppermute | solution.py:360
  216.3 4.8 %collective-permute-start.33 = (bf16[32,512]{1,0:T(8,128)(2,1)S(1)}, bf16[32,512]{1,0:T(8,128)(2,1)S(1)}, u32[]{:S(2)}, u32[]{:S(2)}) collective-permute-start(bf16[32,512]{1,0:T(8,128)(2,1)S(1)} %shard_map.48), channel_id=1, source_target_pairs={{0,16},{8,24},{16,0},{24,8},{1,17},{9,25},{17,1},{25,9},{2,18},{10... | collective-permute-start | bytes 98312 | tf_op jit(solution)/shard_map/ppermute | solution.py:360
  221.2 4.3 %collective-permute-start.34 = (bf16[32,1024]{1,0:T(8,128)(2,1)S(1)}, bf16[32,1024]{1,0:T(8,128)(2,1)S(1)}, u32[]{:S(2)}, u32[]{:S(2)}) collective-permute-start(bf16[32,1024]{1,0:T(8,128)(2,1)S(1)} %pad_maximum_fusion.6), channel_id=1, source_target_pairs={{0,8},{8,0},{16,24},{24,16},{1,9},{9,1},{17,25},{25,17},{2,10},{10... | collective-permute-start | bytes 196616 | tf_op jit(solution)/shard_map/ppermute | solution.py:360

commit v14 on v13

--- a/solution.py
+++ b/solution.py
@@ -269,7 +269,7 @@
     rows = [ref.shape[0] for ref in share_refs if ref is not None][0]
     lane = lax.broadcasted_iota(jnp.int32, (bs, bs), 1)
 
-    def one(r, _):
+    def one(first_half, r, _):
         i = index_ref[r + offset]
         frm = pl.multiple_of(r * bs, bs)
         to = pl.multiple_of(i * bs, bs)
@@ -287,14 +287,11 @@
         at = pl.multiple_of(lax.rem(i + nb // 2, nb) * bs, bs)
         last = share_refs[1][pl.ds(frm, bs), width - cut :].astype(F32)
 
-        @pl.when(i < nb // 2)
-        def _():
+        if first_half:
             old = full[pl.ds(to, bs), pl.ds(at, bs)].astype(F32)
             full[pl.ds(to, bs), pl.ds(at, bs)] = jnp.where(lane < HALF, last, old).astype(BF16)
             full[pl.ds(at, HALF), pl.ds(to, bs)] = last.T[:HALF].astype(BF16)
-
-        @pl.when(i >= nb // 2)
-        def _():
+        else:
             low = jnp.where(lane[:HALF] < HALF, last[:HALF], pltpu.roll(last[HALF:], HALF, 1))
             full[pl.ds(pl.multiple_of(to + HALF, HALF), HALF), pl.ds(at, bs)] = low.astype(BF16)
             old = full[pl.ds(at, bs), pl.ds(to, bs)].astype(F32)
@@ -315,7 +312,15 @@
         v[:, pl.ds(to, bs)] = jnp.concatenate([v1, v2, v3, v1, v2, v1], axis=0)
         return 0
 
-    lax.fori_loop(0, rows // bs, one, 0)
+    def every(first_half):
+        lax.fori_loop(0, rows // bs, functools.partial(one, first_half), 0, unroll=True)
+
+    if share_refs[1] is None:
+        every(True)
+        return
+    first_half = index_ref[offset] < nb // 2
+    pl.when(first_half)(lambda: every(True))
+    pl.when(jnp.logical_not(first_half))(lambda: every(False))
 
 
 def unpack_kernel(items, count, index_ref, *refs):
@@ -346,7 +351,7 @@
         parts = product(p)
         return apply_lower(inverse_lower(gram_of(parts, p)), parts).astype(BF16)
 
-    p = lax.fori_loop(0, ITERS - 1, sweep, p0_ref[...])
+    p = lax.fori_loop(0, ITERS - 1, sweep, p0_ref[...], unroll=3)
     p_ref[...] = p
     inv_ref[...] = inverse_lower(gram_of(product(p), p))
 
@@ -500,8 +505,9 @@
         )(index, *shares, q, *now)
 
     now = unpack_into((), (0, 4), (0,), near[0], far[0])
+    now = unpack_into(now, (2, 6), (0,), over_a[0], far_a[0])
     now = unpack_into(now, (0, 4), (1,), near[1], far[1])
-    now = unpack_into(now, (2, 6), (0, 1), *over_a, *far_a)
+    now = unpack_into(now, (2, 6), (1,), over_a[1], far_a[1])
     now = unpack_into(now, (3,), (0, 1), *over_ab)
     proj, inv = kernel_call(
         functools.partial(iterate_kernel, BLOCKS + 7 * eighth),

time: 227 us -> 222 us (0.978)
  Pallas kernels: 67.5 us -> 63.4 us
    pallas_call x21 -> x22, Pallas kernels: 67.5 us -> 63.4 us  [kernel_call(): return lambda *args: call(*map(place, args, in_specs))]
  transfers between devices with their start and end apart: 36 -> 36, of which waited for: 25 -> 25; matrix products, arithmetic and copies ran while one was open for 0% -> 0% of each run, Pallas kernels for 11% -> 10%
where the time goes in v14:
time: 222 us
  waiting for transfers between devices  110 us (50%)
  Pallas kernels  63.4 us (29%)
  starting transfers between devices  42.3 us (19%)
  local copies, waits for them, and re-layouts  4.89 us (2%)
    ppermute x35, waiting for transfers between devices, flip(): return lax.ppermute(x, axes, perm)  83.9 us
    pallas_call x22, Pallas kernels, kernel_call(): return lambda *args: call(*map(place, args, in_specs))  63.4 us
    ppermute x35, starting transfers between devices, flip(): return lax.ppermute(x, axes, perm)  35 us
    all_to_all x1, waiting for transfers between devices, sample_space(): lax.all_to_all(stamps, ('pix', 'samp'), split_axis=1, concat_axis=0, tile...  26 us
    all_to_all x1, starting transfers between devices, sample_space(): lax.all_to_all(stamps, ('pix', 'samp'), split_axis=1, concat_axis=0, tile...  7.33 us
  transfers between devices with their start and end apart: 36, of which 25 were waited for; matrix products, arithmetic and copies ran while one was open for 0% of the time, Pallas kernels for 10%

profile of v14, /device:TPU:0, one launch (start us, length us, event | category | flops | bytes accessed | tf_op | source)
XLA Modules:
  0.0 222.0 jit_solution(17995888580107351699)
XLA Ops:
  0.0 3.2 %copy.26 = bf16[8,32,8,512]{3,2,0,1:T(8,128)(2,1)} copy(bf16[8,32,8,512]{3,2,1,0:T(8,128)(2,1)} %bitcast.25) | data formatting | bytes 4194304 | tf_op jit(solution)/shard_map/all_to_all | solution.py:414
  3.2 7.3 %all-to-all-start = ((bf16[64,32,512]{2,0,1:T(8,128)(2,1)}), bf16[64,32,512]{2,0,1:T(8,128)(2,1)S(1)}, u32[]{:S(2)}, u32[]{:S(2)}) async-start(bf16[64,32,512]{2,0,1:T(8,128)(2,1)} %bitcast.26), calls=%async_computation | async-start | bytes 4194304 | tf_op jit(solution)/shard_map/all_to_all | solution.py:414
  10.6 1.8 collective-permute-start.1
  12.4 17.3 %collective-permute-done.1 = bf16[32,2048]{1,0:T(8,128)(2,1)S(1)} collective-permute-done((bf16[32,2048]{1,0:T(8,128)(2,1)S(1)}, bf16[32,2048]{1,0:T(8,128)(2,1)S(1)}, u32[]{:S(2)}, u32[]{:S(2)}) %collective-permute-start.1) | collective-permute-done | bytes 131104 | tf_op jit(solution)/shard_map/ppermute | solution.py:365
  29.7 1.5 collective-permute-start.2
  31.3 26.0 %all-to-all-done = bf16[64,32,512]{2,0,1:T(8,128)(2,1)S(1)} async-done(((bf16[64,32,512]{2,0,1:T(8,128)(2,1)}), bf16[64,32,512]{2,0,1:T(8,128)(2,1)S(1)}, u32[]{:S(2)}, u32[]{:S(2)}) %all-to-all-start) | async-done | bytes 2097184 | tf_op jit(solution)/shard_map/all_to_all | solution.py:414
  57.3 1.8 collective-permute-start
  59.4 4.3 %collective-permute-done.3.far_ref = bf16[32,8192]{1,0:T(8,128)(2,1)S(1)} collective-permute-done((bf16[32,8192]{1,0:T(8,128)(2,1)S(1)}, bf16[32,8192]{1,0:T(8,128)(2,1)S(1)}, u32[]{:S(2)}, u32[]{:S(2)}) %collective-permute-start.3) | collective-permute-done | bytes 524320 | tf_op jit(solution)/shard_map/ppermute | solution.py:365
  63.6 1.6 copy-done
  65.2 1.2 shard_map.28
  67.7 1.5 collective-permute-start.5
  69.3 2.1 collective-permute-done.5
  71.4 1.5 collective-permute-start.6
  72.9 2.2 %collective-permute-done.6 = bf16[32,256]{1,0:T(8,128)(2,1)S(1)} collective-permute-done((bf16[32,256]{1,0:T(8,128)(2,1)S(1)}, bf16[32,256]{1,0:T(8,128)(2,1)S(1)}, u32[]{:S(2)}, u32[]{:S(2)}) %collective-permute-start.6) | collective-permute-done | bytes 16416 | tf_op jit(solution)/shard_map/ppermute | solution.py:365
  75.2 2.4 %collective-permute-start.7 = (bf16[32,512]{1,0:T(8,128)(2,1)S(1)}, bf16[32,512]{1,0:T(8,128)(2,1)S(1)}, u32[]{:S(2)}, u32[]{:S(2)}) collective-permute-start(bf16[32,512]{1,0:T(8,128)(2,1)S(1)} %maximum_select_fusion.2), channel_id=1, source_target_pairs={{0,8},{8,0},{16,24},{24,16},{1,9},{9,1},{17,25},{25,17},{2,10},{10... | collective-permute-start | bytes 98312 | tf_op jit(solution)/shard_map/ppermute | solution.py:365
  77.5 1.9 collective-permute-done.7
  80.6 4.0 %collective-permute-done.8 = bf16[32,1024]{1,0:T(8,128)(2,1)S(1)} collective-permute-done((bf16[32,1024]{1,0:T(8,128)(2,1)S(1)}, bf16[32,1024]{1,0:T(8,128)(2,1)S(1)}, u32[]{:S(2)}, u32[]{:S(2)}) %collective-permute-start.8) | collective-permute-done | bytes 65568 | tf_op jit(solution)/shard_map/ppermute | solution.py:365
  84.7 1.4 shard_map.29
  86.0 4.9 %shard_map.30 = (bf16[192,2048]{1,0:T(8,128)(2,1)S(1)}, bf16[192,2048]{1,0:T(8,128)(2,1)S(1)}) custom-call(bf16[2048,512]{1,0:T(8,128)(2,1)S(1)} %bitcast.19, bf16[2048,512]{1,0:T(8,128)(2,1)} %collective-permute-done.other_ref, f32[32,2048]{1,0:T(8,128)S(1)} %get-tuple-element.43.q_ref.refs_2_), custom_call_target="tpu_custom_call" | custom-call | tf_op jit(solution)/shard_map/pallas_call | solution.py:77
  91.0 2.8 %shard_map.34 = (bf16[256,640]{1,0:T(8,128)(2,1)S(1)}, bf16[256,512]{1,0:T(8,128)(2,1)S(1)}) custom-call(s32[32]{0:T(128)S(1)} %concatenate.60.index_ref.at_ref, bf16[2048,512]{1,0:T(8,128)(2,1)S(1)} %bitcast.20, bf16[2048,512]{1,0:T(8,128)(2,1)} %collective-permute-done.other_ref, bf16[192,2048]{1,0:T(8,128)(2,1)S(1)} %get-tuple-element.44.left, ...), custom_call_target="tpu_custom_call" | custom-call | tf_op jit(solution)/shard_map/pallas_call | solution.py:77
  93.8 2.0 collective-permute-start.10
  95.8 2.8 %shard_map.32 = (bf16[256,640]{1,0:T(8,128)(2,1)S(1)}, bf16[256,512]{1,0:T(8,128)(2,1)S(1)}) custom-call(s32[32]{0:T(128)S(1)} %concatenate.60.index_ref.at_ref, bf16[2048,512]{1,0:T(8,128)(2,1)S(1)} %bitcast.21, bf16[2048,512]{1,0:T(8,128)(2,1)} %collective-permute-done.other_ref, bf16[192,2048]{1,0:T(8,128)(2,1)S(1)} %get-tuple-element.44.left, ...), custom_call_target="tpu_custom_call" | custom-call | tf_op jit(solution)/shard_map/pallas_call | solution.py:77
  98.7 2.8 %shard_map.33 = (bf16[256,640]{1,0:T(8,128)(2,1)S(1)}, bf16[256,512]{1,0:T(8,128)(2,1)S(1)}) custom-call(s32[32]{0:T(128)S(1)} %concatenate.60.index_ref.at_ref, bf16[2048,512]{1,0:T(8,128)(2,1)S(1)} %bitcast.22, bf16[2048,512]{1,0:T(8,128)(2,1)} %collective-permute-done.other_ref, bf16[192,2048]{1,0:T(8,128)(2,1)S(1)} %get-tuple-element.44.left, ...), custom_call_target="tpu_custom_call" | custom-call | tf_op jit(solution)/shard_map/pallas_call | solution.py:77
  102.2 1.2 collective-permute-start.11
  103.5 2.8 %shard_map.31 = (bf16[256,640]{1,0:T(8,128)(2,1)S(1)}, bf16[256,512]{1,0:T(8,128)(2,1)S(1)}) custom-call(s32[32]{0:T(128)S(1)} %concatenate.60.index_ref.at_ref, bf16[2048,512]{1,0:T(8,128)(2,1)S(1)} %bitcast.23, bf16[2048,512]{1,0:T(8,128)(2,1)} %collective-permute-done.other_ref, bf16[192,2048]{1,0:T(8,128)(2,1)S(1)} %get-tuple-element.44.left, ...), custom_call_target="tpu_custom_call" | custom-call | tf_op jit(solution)/shard_map/pallas_call | solution.py:77
  106.3 1.7 collective-permute-done.9.refs_1_
  107.9 1.4 collective-permute-done.11.refs_2_
  110.0 2.5 %collective-permute-start.12 = (bf16[128,640]{1,0:T(8,128)(2,1)S(1)}, bf16[128,640]{1,0:T(8,128)(2,1)S(1)}, u32[]{:S(2)}, u32[]{:S(2)}) collective-permute-start(bf16[128,640]{1,0:T(8,128)(2,1)S(1)} %get-tuple-element.51), channel_id=1, source_target_pairs={{0,8},{8,0},{16,24},{24,16},{1,9},{9,1},{17,25},{25,17},{2,10},{10... | collective-permute-start | bytes 491528 | tf_op jit(solution)/shard_map/ppermute | solution.py:365
  112.5 4.2 %collective-permute-done.12.refs_1_ = bf16[128,640]{1,0:T(8,128)(2,1)S(1)} collective-permute-done((bf16[128,640]{1,0:T(8,128)(2,1)S(1)}, bf16[128,640]{1,0:T(8,128)(2,1)S(1)}, u32[]{:S(2)}, u32[]{:S(2)}) %collective-permute-start.12) | collective-permute-done | bytes 163872 | tf_op jit(solution)/shard_map/ppermute | solution.py:365
  117.5 6.1 %collective-permute-done.13.refs_1_ = bf16[128,640]{1,0:T(8,128)(2,1)S(1)} collective-permute-done((bf16[128,640]{1,0:T(8,128)(2,1)S(1)}, bf16[128,640]{1,0:T(8,128)(2,1)S(1)}, u32[]{:S(2)}, u32[]{:S(2)}) %collective-permute-start.13) | collective-permute-done | bytes 163872 | tf_op jit(solution)/shard_map/ppermute | solution.py:365
  124.2 3.7 %collective-permute-start.14 = (bf16[128,640]{1,0:T(8,128)(2,1)S(1)}, bf16[128,640]{1,0:T(8,128)(2,1)S(1)}, u32[]{:S(2)}, u32[]{:S(2)}) collective-permute-start(bf16[128,640]{1,0:T(8,128)(2,1)S(1)} %shard_map.38), channel_id=1, source_target_pairs={{0,8},{8,0},{16,24},{24,16},{1,9},{9,1},{17,25},{25,17},{2,10},{10... | collective-permute-start | bytes 491528 | tf_op jit(solution)/shard_map/ppermute | solution.py:365
  128.8 1.7 collective-permute-start.20
  131.3 1.9 collective-permute-start.15
  133.2 1.4 collective-permute-done.18.refs_1_
  137.1 4.2 %collective-permute-done.21.refs_1_ = bf16[128,512]{1,0:T(8,128)(2,1)S(1)} collective-permute-done((bf16[128,512]{1,0:T(8,128)(2,1)S(1)}, bf16[128,512]{1,0:T(8,128)(2,1)S(1)}, u32[]{:S(2)}, u32[]{:S(2)}) %collective-permute-start.21) | collective-permute-done | bytes 131104 | tf_op jit(solution)/shard_map/ppermute | solution.py:365
  143.2 6.2 %collective-permute-done.22.refs_1_ = bf16[128,512]{1,0:T(8,128)(2,1)S(1)} collective-permute-done((bf16[128,512]{1,0:T(8,128)(2,1)S(1)}, bf16[128,512]{1,0:T(8,128)(2,1)S(1)}, u32[]{:S(2)}, u32[]{:S(2)}) %collective-permute-start.22) | collective-permute-done | bytes 131104 | tf_op jit(solution)/shard_map/ppermute | solution.py:365
  150.4 4.8 %collective-permute-done.23 = bf16[128,512]{1,0:T(8,128)(2,1)S(1)} collective-permute-done((bf16[128,512]{1,0:T(8,128)(2,1)S(1)}, bf16[128,512]{1,0:T(8,128)(2,1)S(1)}, u32[]{:S(2)}, u32[]{:S(2)}) %collective-permute-start.23) | collective-permute-done | bytes 131104 | tf_op jit(solution)/shard_map/ppermute | solution.py:365
  156.2 1.6 collective-permute-start.27
  158.3 1.6 collective-permute-start.16
  159.9 4.5 %collective-permute-done.24 = bf16[256,512]{1,0:T(8,128)(2,1)S(1)} collective-permute-done((bf16[256,512]{1,0:T(8,128)(2,1)S(1)}, bf16[256,512]{1,0:T(8,128)(2,1)S(1)}, u32[]{:S(2)}, u32[]{:S(2)}) %collective-permute-start.24) | collective-permute-done | bytes 262176 | tf_op jit(solution)/shard_map/ppermute | solution.py:365
  164.6 1.5 collective-permute-start.25
  166.1 3.5 %collective-permute-done.16.refs_0_ = bf16[256,640]{1,0:T(8,128)(2,1)S(1)} collective-permute-done((bf16[256,640]{1,0:T(8,128)(2,1)S(1)}, bf16[256,640]{1,0:T(8,128)(2,1)S(1)}, u32[]{:S(2)}, u32[]{:S(2)}) %collective-permute-start.16) | collective-permute-done | bytes 327712 | tf_op jit(solution)/shard_map/ppermute | solution.py:365
  169.6 2.8 %collective-permute-done.25.refs_1_ = bf16[256,512]{1,0:T(8,128)(2,1)S(1)} collective-permute-done((bf16[256,512]{1,0:T(8,128)(2,1)S(1)}, bf16[256,512]{1,0:T(8,128)(2,1)S(1)}, u32[]{:S(2)}, u32[]{:S(2)}) %collective-permute-start.25) | collective-permute-done | bytes 262176 | tf_op jit(solution)/shard_map/ppermute | solution.py:365
  175.0 2.0 shard_map.45
  177.0 1.3 shard_map.46
  179.3 32.2 %shard_map.48 = (bf16[32,2048]{1,0:T(8,128)(2,1)S(1)}, f32[32,128]{1,0:T(8,128)S(1)}, bf16[2048,2048]{1,0:T(8,128)(2,1)S(1)}, bf16[2048,128]{1,0:T(8,128)(2,1)S(...) custom-call(s32[32]{0:T(128)S(1)} %concatenate.60.index_ref.at_ref, ...), custom_call_target="tpu_custom_call", output_to_operand_aliasing={{2}: (5, {}), {3}: (6, {}), {4}: (7, {}), {5}: (8, {})} | custom-call | tf_op jit(solution)/shard_map/pallas_call | solution.py:77
  212.4 4.5 %collective-permute-done.33 = bf16[32,512]{1,0:T(8,128)(2,1)S(1)} collective-permute-done((bf16[32,512]{1,0:T(8,128)(2,1)S(1)}, bf16[32,512]{1,0:T(8,128)(2,1)S(1)}, u32[]{:S(2)}, u32[]{:S(2)}) %collective-permute-start.33) | collective-permute-done | bytes 32800 | tf_op jit(solution)/shard_map/ppermute | solution.py:365
  217.0 4.3 %collective-permute-done.34 = bf16[32,1024]{1,0:T(8,128)(2,1)S(1)} collective-permute-done((bf16[32,1024]{1,0:T(8,128)(2,1)S(1)}, bf16[32,1024]{1,0:T(8,128)(2,1)S(1)}, u32[]{:S(2)}, u32[]{:S(2)}) %collective-permute-start.34) | collective-permute-done | bytes 65568 | tf_op jit(solution)/shard_map/ppermute | solution.py:365
  (69 shorter events, 19.6 us)
Async XLA Ops:
  3.2 7.3 %copy-start.1 = (f32[2048,32]{0,1:T(8,128)S(1)}, f32[2048,32]{0,1:T(8,128)}, u32[]{:S(2)}) copy-start(f32[2048,32]{0,1:T(8,128)} %param.3) | copy-start | bytes 786436
  3.2 54.1 %all-to-all-start = ((bf16[64,32,512]{2,0,1:T(8,128)(2,1)}), bf16[64,32,512]{2,0,1:T(8,128)(2,1)S(1)}, u32[]{:S(2)}, u32[]{:S(2)}) async-start(bf16[64,32,512]{2,0,1:T(8,128)(2,1)} %bitcast.26), calls=%async_computation | async-start | bytes 4194304 | tf_op jit(solution)/shard_map/all_to_all | solution.py:414
  10.6 19.1 %collective-permute-start.1 = (bf16[32,2048]{1,0:T(8,128)(2,1)S(1)}, bf16[32,2048]{1,0:T(8,128)(2,1)S(1)}, u32[]{:S(2)}, u32[]{:S(2)}) collective-permute-start(bf16[32,2048]{1,0:T(8,128)(2,1)S(1)} %convert_bitcast_fusion.1), channel_id=1, source_target_pairs={{0,2},{1,3},{2,0},{3,1},{4,6},{5,7},{6,4},{7,5},{8,10},{9,11},{10,... | collective-permute-start | bytes 393224 | tf_op jit(solution)/shard_map/ppermute | solution.py:365
  29.7 29.4 %collective-permute-start.2 = (bf16[32,4096]{1,0:T(8,128)(2,1)S(1)}, bf16[32,4096]{1,0:T(8,128)(2,1)S(1)}, u32[]{:S(2)}, u32[]{:S(2)}) collective-permute-start(bf16[32,4096]{1,0:T(8,128)(2,1)S(1)} %pad_maximum_fusion.4), channel_id=1, source_target_pairs={{0,4},{1,5},{2,6},{3,7},{4,0},{5,1},{6,2},{7,3},{8,12},{9,13},{10,... | collective-permute-start | bytes 786440 | tf_op jit(solution)/shard_map/ppermute | solution.py:365
  57.3 28.8 %collective-permute-start = (bf16[2048,512]{1,0:T(8,128)(2,1)S(1)}, bf16[2048,512]{1,0:T(8,128)(2,1)}, u32[]{:S(2)}, u32[]{:S(2)}) collective-permute-start(bf16[2048,512]{1,0:T(8,128)(2,1)S(1)} %bitcast.18), channel_id=1, source_target_pairs={{0,1},{1,0},{2,3},{3,2},{4,5},{5,4},{6,7},{7,6},{8,9},{9,8},{10,11... | collective-permute-start | bytes 6291464 | tf_op jit(solution)/shard_map/ppermute | solution.py:365
  59.1 4.5 %collective-permute-start.3 = (bf16[32,8192]{1,0:T(8,128)(2,1)S(1)}, bf16[32,8192]{1,0:T(8,128)(2,1)S(1)}, u32[]{:S(2)}, u32[]{:S(2)}) collective-permute-start(bf16[32,8192]{1,0:T(8,128)(2,1)S(1)} %pad_maximum_fusion.1.near_ref), channel_id=1, source_target_pairs={{0,1},{1,0},{2,3},{3,2},{4,5},{5,4},{6,7},{7,6},{8,9},{9,8},{10,11... | collective-permute-start | bytes 1572872 | tf_op jit(solution)/shard_map/ppermute | solution.py:365
  63.6 1.6 copy-start
  66.4 1.2 collective-permute-start.4
  67.7 3.7 %collective-permute-start.5 = (bf16[32,128]{1,0:T(8,128)(2,1)S(1)}, bf16[32,128]{1,0:T(8,128)(2,1)S(1)}, u32[]{:S(2)}, u32[]{:S(2)}) collective-permute-start(bf16[32,128]{1,0:T(8,128)(2,1)S(1)} %maximum_select_fusion.4), channel_id=1, source_target_pairs={{0,2},{1,3},{2,0},{3,1},{4,6},{5,7},{6,4},{7,5},{8,10},{9,11},{10,... | collective-permute-start | bytes 24584 | tf_op jit(solution)/shard_map/ppermute | solution.py:365
  71.4 3.7 %collective-permute-start.6 = (bf16[32,256]{1,0:T(8,128)(2,1)S(1)}, bf16[32,256]{1,0:T(8,128)(2,1)S(1)}, u32[]{:S(2)}, u32[]{:S(2)}) collective-permute-start(bf16[32,256]{1,0:T(8,128)(2,1)S(1)} %maximum_select_fusion.3), channel_id=1, source_target_pairs={{0,4},{1,5},{2,6},{3,7},{4,0},{5,1},{6,2},{7,3},{8,12},{9,13},{10,... | collective-permute-start | bytes 49160 | tf_op jit(solution)/shard_map/ppermute | solution.py:365
  75.2 4.2 %collective-permute-start.7 = (bf16[32,512]{1,0:T(8,128)(2,1)S(1)}, bf16[32,512]{1,0:T(8,128)(2,1)S(1)}, u32[]{:S(2)}, u32[]{:S(2)}) collective-permute-start(bf16[32,512]{1,0:T(8,128)(2,1)S(1)} %maximum_select_fusion.2), channel_id=1, source_target_pairs={{0,8},{8,0},{16,24},{24,16},{1,9},{9,1},{17,25},{25,17},{2,10},{10... | collective-permute-start | bytes 98312 | tf_op jit(solution)/shard_map/ppermute | solution.py:365
  79.4 5.2 %collective-permute-start.8 = (bf16[32,1024]{1,0:T(8,128)(2,1)S(1)}, bf16[32,1024]{1,0:T(8,128)(2,1)S(1)}, u32[]{:S(2)}, u32[]{:S(2)}) collective-permute-start(bf16[32,1024]{1,0:T(8,128)(2,1)S(1)} %maximum_select_fusion.1), channel_id=1, source_target_pairs={{0,16},{8,24},{16,0},{24,8},{1,17},{9,25},{17,1},{25,9},{2,18},{10... | collective-permute-start | bytes 196616 | tf_op jit(solution)/shard_map/ppermute | solution.py:365
  93.8 7.8 %collective-permute-start.10 = (bf16[256,640]{1,0:T(8,128)(2,1)S(1)}, bf16[256,640]{1,0:T(8,128)(2,1)S(1)}, u32[]{:S(2)}, u32[]{:S(2)}) collective-permute-start(bf16[256,640]{1,0:T(8,128)(2,1)S(1)} %get-tuple-element.49), channel_id=1, source_target_pairs={{0,2},{1,5},{2,0},{3,7},{4,6},{5,1},{6,4},{7,3},{8,10},{9,13},{10,... | collective-permute-start | bytes 983048 | tf_op jit(solution)/shard_map/ppermute | solution.py:365
  98.6 9.3 %collective-permute-start.9 = (bf16[256,640]{1,0:T(8,128)(2,1)S(1)}, bf16[256,640]{1,0:T(8,128)(2,1)S(1)}, u32[]{:S(2)}, u32[]{:S(2)}) collective-permute-start(bf16[256,640]{1,0:T(8,128)(2,1)S(1)} %get-tuple-element.47), channel_id=1, source_target_pairs={{0,2},{1,5},{2,0},{3,7},{4,6},{5,1},{6,4},{7,3},{8,10},{9,13},{10,... | collective-permute-start | bytes 983048 | tf_op jit(solution)/shard_map/ppermute | solution.py:365
  102.2 7.1 %collective-permute-start.11 = (bf16[256,640]{1,0:T(8,128)(2,1)S(1)}, bf16[256,640]{1,0:T(8,128)(2,1)S(1)}, u32[]{:S(2)}, u32[]{:S(2)}) collective-permute-start(bf16[256,640]{1,0:T(8,128)(2,1)S(1)} %shard_map.35), channel_id=1, source_target_pairs={{0,4},{1,3},{2,6},{3,1},{4,0},{5,7},{6,2},{7,5},{8,12},{9,11},{10,... | collective-permute-start | bytes 983048 | tf_op jit(solution)/shard_map/ppermute | solution.py:365
  110.0 6.7 %collective-permute-start.12 = (bf16[128,640]{1,0:T(8,128)(2,1)S(1)}, bf16[128,640]{1,0:T(8,128)(2,1)S(1)}, u32[]{:S(2)}, u32[]{:S(2)}) collective-permute-start(bf16[128,640]{1,0:T(8,128)(2,1)S(1)} %get-tuple-element.51), channel_id=1, source_target_pairs={{0,8},{8,0},{16,24},{24,16},{1,9},{9,1},{17,25},{25,17},{2,10},{10... | collective-permute-start | bytes 491528 | tf_op jit(solution)/shard_map/ppermute | solution.py:365
  112.5 15.4 %collective-permute-start.19 = (bf16[256,512]{1,0:T(8,128)(2,1)S(1)}, bf16[256,512]{1,0:T(8,128)(2,1)S(1)}, u32[]{:S(2)}, u32[]{:S(2)}) collective-permute-start(bf16[256,512]{1,0:T(8,128)(2,1)S(1)} %get-tuple-element.55), channel_id=1, source_target_pairs={{0,2},{1,5},{2,0},{3,7},{4,6},{5,1},{6,4},{7,3},{8,10},{9,13},{10,... | collective-permute-start | bytes 786440 | tf_op jit(solution)/shard_map/ppermute | solution.py:365
  117.3 6.4 %collective-permute-start.13 = (bf16[128,640]{1,0:T(8,128)(2,1)S(1)}, bf16[128,640]{1,0:T(8,128)(2,1)S(1)}, u32[]{:S(2)}, u32[]{:S(2)}) collective-permute-start(bf16[128,640]{1,0:T(8,128)(2,1)S(1)} %shard_map.37.refs_0_), channel_id=1, source_target_pairs={{0,16},{8,24},{16,0},{24,8},{1,17},{9,25},{17,1},{25,9},{2,18},{10... | collective-permute-start | bytes 491528 | tf_op jit(solution)/shard_map/ppermute | solution.py:365
  124.2 7.0 %collective-permute-start.14 = (bf16[128,640]{1,0:T(8,128)(2,1)S(1)}, bf16[128,640]{1,0:T(8,128)(2,1)S(1)}, u32[]{:S(2)}, u32[]{:S(2)}) collective-permute-start(bf16[128,640]{1,0:T(8,128)(2,1)S(1)} %shard_map.38), channel_id=1, source_target_pairs={{0,8},{8,0},{16,24},{24,16},{1,9},{9,1},{17,25},{25,17},{2,10},{10... | collective-permute-start | bytes 491528 | tf_op jit(solution)/shard_map/ppermute | solution.py:365
  127.9 6.6 %collective-permute-start.18 = (bf16[256,512]{1,0:T(8,128)(2,1)S(1)}, bf16[256,512]{1,0:T(8,128)(2,1)S(1)}, u32[]{:S(2)}, u32[]{:S(2)}) collective-permute-start(bf16[256,512]{1,0:T(8,128)(2,1)S(1)} %get-tuple-element.53), channel_id=1, source_target_pairs={{0,2},{1,5},{2,0},{3,7},{4,6},{5,1},{6,4},{7,3},{8,10},{9,13},{10,... | collective-permute-start | bytes 786440 | tf_op jit(solution)/shard_map/ppermute | solution.py:365
  128.8 6.4 %collective-permute-start.20 = (bf16[256,512]{1,0:T(8,128)(2,1)S(1)}, bf16[256,512]{1,0:T(8,128)(2,1)S(1)}, u32[]{:S(2)}, u32[]{:S(2)}) collective-permute-start(bf16[256,512]{1,0:T(8,128)(2,1)S(1)} %shard_map.39), channel_id=1, source_target_pairs={{0,4},{1,3},{2,6},{3,1},{4,0},{5,7},{6,2},{7,5},{8,12},{9,11},{10,... | collective-permute-start | bytes 786440 | tf_op jit(solution)/shard_map/ppermute | solution.py:365
  131.3 18.9 %collective-permute-start.15 = (bf16[256,640]{1,0:T(8,128)(2,1)S(1)}, bf16[256,640]{1,0:T(8,128)(2,1)S(1)}, u32[]{:S(2)}, u32[]{:S(2)}) collective-permute-start(bf16[256,640]{1,0:T(8,128)(2,1)S(1)} %pad_maximum_fusion.3), channel_id=1, source_target_pairs={{0,4},{1,3},{2,6},{3,1},{4,0},{5,7},{6,2},{7,5},{8,12},{9,11},{10,... | collective-permute-start | bytes 983048 | tf_op jit(solution)/shard_map/ppermute | solution.py:365
  136.1 5.2 %collective-permute-start.21 = (bf16[128,512]{1,0:T(8,128)(2,1)S(1)}, bf16[128,512]{1,0:T(8,128)(2,1)S(1)}, u32[]{:S(2)}, u32[]{:S(2)}) collective-permute-start(bf16[128,512]{1,0:T(8,128)(2,1)S(1)} %get-tuple-element.57), channel_id=1, source_target_pairs={{0,8},{8,0},{16,24},{24,16},{1,9},{9,1},{17,25},{25,17},{2,10},{10... | collective-permute-start | bytes 393224 | tf_op jit(solution)/shard_map/ppermute | solution.py:365
  142.0 7.3 %collective-permute-start.22 = (bf16[128,512]{1,0:T(8,128)(2,1)S(1)}, bf16[128,512]{1,0:T(8,128)(2,1)S(1)}, u32[]{:S(2)}, u32[]{:S(2)}) collective-permute-start(bf16[128,512]{1,0:T(8,128)(2,1)S(1)} %shard_map.41.refs_0_), channel_id=1, source_target_pairs={{0,16},{8,24},{16,0},{24,8},{1,17},{9,25},{17,1},{25,9},{2,18},{10... | collective-permute-start | bytes 393224 | tf_op jit(solution)/shard_map/ppermute | solution.py:365
  150.1 5.0 %collective-permute-start.23 = (bf16[128,512]{1,0:T(8,128)(2,1)S(1)}, bf16[128,512]{1,0:T(8,128)(2,1)S(1)}, u32[]{:S(2)}, u32[]{:S(2)}) collective-permute-start(bf16[128,512]{1,0:T(8,128)(2,1)S(1)} %shard_map.42), channel_id=1, source_target_pairs={{0,8},{8,0},{16,24},{24,16},{1,9},{9,1},{17,25},{25,17},{2,10},{10... | collective-permute-start | bytes 393224 | tf_op jit(solution)/shard_map/ppermute | solution.py:365
  150.3 22.2 %collective-permute-start.32 = (bf16[512,640]{1,0:T(8,128)(2,1)S(1)}, bf16[512,640]{1,0:T(8,128)(2,1)S(1)}, u32[]{:S(2)}, u32[]{:S(2)}) collective-permute-start(bf16[512,640]{1,0:T(8,128)(2,1)S(1)} %pad_maximum_fusion.refs_0_), channel_id=1, source_target_pairs={{0,1},{1,0},{2,3},{3,2},{4,5},{5,4},{6,7},{7,6},{8,9},{9,8},{10,11... | collective-permute-start | bytes 1966088 | tf_op jit(solution)/shard_map/ppermute | solution.py:365
  155.2 9.2 %collective-permute-start.24 = (bf16[256,512]{1,0:T(8,128)(2,1)S(1)}, bf16[256,512]{1,0:T(8,128)(2,1)S(1)}, u32[]{:S(2)}, u32[]{:S(2)}) collective-permute-start(bf16[256,512]{1,0:T(8,128)(2,1)S(1)} %pad_maximum_fusion.5), channel_id=1, source_target_pairs={{0,4},{1,3},{2,6},{3,1},{4,0},{5,7},{6,2},{7,5},{8,12},{9,11},{10,... | collective-permute-start | bytes 786440 | tf_op jit(solution)/shard_map/ppermute | solution.py:365
  156.2 8.3 %collective-permute-start.27 = (bf16[256,512]{1,0:T(8,128)(2,1)S(1)}, bf16[256,512]{1,0:T(8,128)(2,1)S(1)}, u32[]{:S(2)}, u32[]{:S(2)}) collective-permute-start(bf16[256,512]{1,0:T(8,128)(2,1)S(1)} %pad_maximum_fusion.5), channel_id=1, source_target_pairs={{0,2},{1,5},{2,0},{3,7},{4,6},{5,1},{6,4},{7,3},{8,10},{9,13},{10,... | collective-permute-start | bytes 786440 | tf_op jit(solution)/shard_map/ppermute | solution.py:365
  157.9 8.2 %collective-permute-start.30 = (bf16[256,640]{1,0:T(8,128)(2,1)S(1)}, bf16[256,640]{1,0:T(8,128)(2,1)S(1)}, u32[]{:S(2)}, u32[]{:S(2)}) collective-permute-start(bf16[256,640]{1,0:T(8,128)(2,1)S(1)} %pad_maximum_fusion.3), channel_id=1, source_target_pairs={{0,2},{1,5},{2,0},{3,7},{4,6},{5,1},{6,4},{7,3},{8,10},{9,13},{10,... | collective-permute-start | bytes 983048 | tf_op jit(solution)/shard_map/ppermute | solution.py:365
  158.3 11.4 %collective-permute-start.16 = (bf16[256,640]{1,0:T(8,128)(2,1)S(1)}, bf16[256,640]{1,0:T(8,128)(2,1)S(1)}, u32[]{:S(2)}, u32[]{:S(2)}) collective-permute-start(bf16[256,640]{1,0:T(8,128)(2,1)S(1)} %collective-permute-done.15), channel_id=1, source_target_pairs={{0,2},{1,5},{2,0},{3,7},{4,6},{5,1},{6,4},{7,3},{8,10},{9,13},{10,... | collective-permute-start | bytes 983048 | tf_op jit(solution)/shard_map/ppermute | solution.py:365
  164.5 10.5 %collective-permute-start.29 = (bf16[512,512]{1,0:T(8,128)(2,1)S(1)}, bf16[512,512]{1,0:T(8,128)(2,1)S(1)}, u32[]{:S(2)}, u32[]{:S(2)}) collective-permute-start(bf16[512,512]{1,0:T(8,128)(2,1)S(1)} %pad_maximum_fusion.2.refs_0_), channel_id=1, source_target_pairs={{0,1},{1,0},{2,3},{3,2},{4,5},{5,4},{6,7},{7,6},{8,9},{9,8},{10,11... | collective-permute-start | bytes 1572872 | tf_op jit(solution)/shard_map/ppermute | solution.py:365
  164.6 7.9 %collective-permute-start.25 = (bf16[256,512]{1,0:T(8,128)(2,1)S(1)}, bf16[256,512]{1,0:T(8,128)(2,1)S(1)}, u32[]{:S(2)}, u32[]{:S(2)}) collective-permute-start(bf16[256,512]{1,0:T(8,128)(2,1)S(1)} %collective-permute-done.24), channel_id=1, source_target_pairs={{0,2},{1,5},{2,0},{3,7},{4,6},{5,1},{6,4},{7,3},{8,10},{9,13},{10,... | collective-permute-start | bytes 786440 | tf_op jit(solution)/shard_map/ppermute | solution.py:365
  166.1 8.0 %collective-permute-start.31 = (bf16[256,640]{1,0:T(8,128)(2,1)S(1)}, bf16[256,640]{1,0:T(8,128)(2,1)S(1)}, u32[]{:S(2)}, u32[]{:S(2)}) collective-permute-start(bf16[256,640]{1,0:T(8,128)(2,1)S(1)} %collective-permute-done.30.refs_0_), channel_id=1, source_target_pairs={{0,1},{1,0},{2,3},{3,2},{4,5},{5,4},{6,7},{7,6},{8,9},{9,8},{10,11... | collective-permute-start | bytes 983048 | tf_op jit(solution)/shard_map/ppermute | solution.py:365
  169.6 9.7 %collective-permute-start.17 = (bf16[256,640]{1,0:T(8,128)(2,1)S(1)}, bf16[256,640]{1,0:T(8,128)(2,1)S(1)}, u32[]{:S(2)}, u32[]{:S(2)}) collective-permute-start(bf16[256,640]{1,0:T(8,128)(2,1)S(1)} %collective-permute-done.16.refs_0_), channel_id=1, source_target_pairs={{0,1},{1,0},{2,3},{3,2},{4,5},{5,4},{6,7},{7,6},{8,9},{9,8},{10,11... | collective-permute-start | bytes 983048 | tf_op jit(solution)/shard_map/ppermute | solution.py:365
  172.4 4.6 %collective-permute-start.28 = (bf16[256,512]{1,0:T(8,128)(2,1)S(1)}, bf16[256,512]{1,0:T(8,128)(2,1)S(1)}, u32[]{:S(2)}, u32[]{:S(2)}) collective-permute-start(bf16[256,512]{1,0:T(8,128)(2,1)S(1)} %collective-permute-done.27.refs_0_), channel_id=1, source_target_pairs={{0,1},{1,0},{2,3},{3,2},{4,5},{5,4},{6,7},{7,6},{8,9},{9,8},{10,11... | collective-permute-start | bytes 786440 | tf_op jit(solution)/shard_map/ppermute | solution.py:365
  172.4 6.9 %collective-permute-start.26 = (bf16[256,512]{1,0:T(8,128)(2,1)S(1)}, bf16[256,512]{1,0:T(8,128)(2,1)S(1)}, u32[]{:S(2)}, u32[]{:S(2)}) collective-permute-start(bf16[256,512]{1,0:T(8,128)(2,1)S(1)} %collective-permute-done.25.refs_1_), channel_id=1, source_target_pairs={{0,1},{1,0},{2,3},{3,2},{4,5},{5,4},{6,7},{7,6},{8,9},{9,8},{10,11... | collective-permute-start | bytes 786440 | tf_op jit(solution)/shard_map/ppermute | solution.py:365
  212.1 4.8 %collective-permute-start.33 = (bf16[32,512]{1,0:T(8,128)(2,1)S(1)}, bf16[32,512]{1,0:T(8,128)(2,1)S(1)}, u32[]{:S(2)}, u32[]{:S(2)}) collective-permute-start(bf16[32,512]{1,0:T(8,128)(2,1)S(1)} %shard_map.49), channel_id=1, source_target_pairs={{0,16},{8,24},{16,0},{24,8},{1,17},{9,25},{17,1},{25,9},{2,18},{10... | collective-permute-start | bytes 98312 | tf_op jit(solution)/shard_map/ppermute | solution.py:365
  217.0 4.3 %collective-permute-start.34 = (bf16[32,1024]{1,0:T(8,128)(2,1)S(1)}, bf16[32,1024]{1,0:T(8,128)(2,1)S(1)}, u32[]{:S(2)}, u32[]{:S(2)}) collective-permute-start(bf16[32,1024]{1,0:T(8,128)(2,1)S(1)} %pad_maximum_fusion.6), channel_id=1, source_target_pairs={{0,8},{8,0},{16,24},{24,16},{1,9},{9,1},{17,25},{25,17},{2,10},{10... | collective-permute-start | bytes 196616 | tf_op jit(solution)/shard_map/ppermute | solution.py:365

commit v15 on v14

--- a/solution.py
+++ b/solution.py
@@ -110,9 +110,9 @@
 
 def gram_of(parts, right):
     k = right.shape[0]
-    wide = jnp.concatenate([right, jnp.zeros((3 * k, right.shape[1]), right.dtype)], axis=0)
-    g = dot(jnp.concatenate(parts, axis=0), wide, NT)
-    return g[:k] + g[k : 2 * k] + g[2 * k :]
+    g = dot(jnp.concatenate(parts, axis=0), right, NT)
+    g = g[:k] + g[k : 2 * k] + g[2 * k :]
+    return jnp.concatenate([g, jnp.zeros((k, 3 * k), F32)], axis=1)
 
 
 def apply_lower(inv, parts):

time: 222 us -> 222 us (level)
  no operation moved by 1% of the time
where the time goes in v15:
time: 222 us
  waiting for transfers between devices  110 us (50%)
  Pallas kernels  63.4 us (29%)
  starting transfers between devices  42.2 us (19%)
  local copies, waits for them, and re-layouts  4.89 us (2%)
    ppermute x35, waiting for transfers between devices, flip(): return lax.ppermute(x, axes, perm)  84.1 us
    pallas_call x22, Pallas kernels, kernel_call(): return lambda *args: call(*map(place, args, in_specs))  63.4 us
    ppermute x35, starting transfers between devices, flip(): return lax.ppermute(x, axes, perm)  34.9 us
    all_to_all x1, waiting for transfers between devices, sample_space(): lax.all_to_all(stamps, ('pix', 'samp'), split_axis=1, concat_axis=0, tile...  26 us
    all_to_all x1, starting transfers between devices, sample_space(): lax.all_to_all(stamps, ('pix', 'samp'), split_axis=1, concat_axis=0, tile...  7.33 us
  transfers between devices with their start and end apart: 36, of which 25 were waited for; matrix products, arithmetic and copies ran while one was open for 0% of the time, Pallas kernels for 10%

profile of v15, /device:TPU:0, one launch (start us, length us, event | category | flops | bytes accessed | tf_op | source)
XLA Modules:
  0.0 222.0 jit_solution(5192372472612604509)
XLA Ops:
  0.0 3.2 %copy.26 = bf16[8,32,8,512]{3,2,0,1:T(8,128)(2,1)} copy(bf16[8,32,8,512]{3,2,1,0:T(8,128)(2,1)} %bitcast.25) | data formatting | bytes 4194304 | tf_op jit(solution)/shard_map/all_to_all | solution.py:414
  3.2 7.3 %all-to-all-start = ((bf16[64,32,512]{2,0,1:T(8,128)(2,1)}), bf16[64,32,512]{2,0,1:T(8,128)(2,1)S(1)}, u32[]{:S(2)}, u32[]{:S(2)}) async-start(bf16[64,32,512]{2,0,1:T(8,128)(2,1)} %bitcast.26), calls=%async_computation | async-start | bytes 4194304 | tf_op jit(solution)/shard_map/all_to_all | solution.py:414
  10.6 1.8 collective-permute-start.1
  12.4 17.3 %collective-permute-done.1 = bf16[32,2048]{1,0:T(8,128)(2,1)S(1)} collective-permute-done((bf16[32,2048]{1,0:T(8,128)(2,1)S(1)}, bf16[32,2048]{1,0:T(8,128)(2,1)S(1)}, u32[]{:S(2)}, u32[]{:S(2)}) %collective-permute-start.1) | collective-permute-done | bytes 131104 | tf_op jit(solution)/shard_map/ppermute | solution.py:365
  29.7 1.5 collective-permute-start.2
  31.3 26.0 %all-to-all-done = bf16[64,32,512]{2,0,1:T(8,128)(2,1)S(1)} async-done(((bf16[64,32,512]{2,0,1:T(8,128)(2,1)}), bf16[64,32,512]{2,0,1:T(8,128)(2,1)S(1)}, u32[]{:S(2)}, u32[]{:S(2)}) %all-to-all-start) | async-done | bytes 2097184 | tf_op jit(solution)/shard_map/all_to_all | solution.py:414
  57.3 1.8 collective-permute-start
  59.4 4.3 %collective-permute-done.3.far_ref = bf16[32,8192]{1,0:T(8,128)(2,1)S(1)} collective-permute-done((bf16[32,8192]{1,0:T(8,128)(2,1)S(1)}, bf16[32,8192]{1,0:T(8,128)(2,1)S(1)}, u32[]{:S(2)}, u32[]{:S(2)}) %collective-permute-start.3) | collective-permute-done | bytes 524320 | tf_op jit(solution)/shard_map/ppermute | solution.py:365
  63.6 1.6 copy-done
  65.2 1.2 shard_map.28
  67.7 1.5 collective-permute-start.5
  69.3 2.1 collective-permute-done.5
  71.4 1.5 collective-permute-start.6
  72.9 2.2 %collective-permute-done.6 = bf16[32,256]{1,0:T(8,128)(2,1)S(1)} collective-permute-done((bf16[32,256]{1,0:T(8,128)(2,1)S(1)}, bf16[32,256]{1,0:T(8,128)(2,1)S(1)}, u32[]{:S(2)}, u32[]{:S(2)}) %collective-permute-start.6) | collective-permute-done | bytes 16416 | tf_op jit(solution)/shard_map/ppermute | solution.py:365
  75.2 2.4 %collective-permute-start.7 = (bf16[32,512]{1,0:T(8,128)(2,1)S(1)}, bf16[32,512]{1,0:T(8,128)(2,1)S(1)}, u32[]{:S(2)}, u32[]{:S(2)}) collective-permute-start(bf16[32,512]{1,0:T(8,128)(2,1)S(1)} %maximum_select_fusion.2), channel_id=1, source_target_pairs={{0,8},{8,0},{16,24},{24,16},{1,9},{9,1},{17,25},{25,17},{2,10},{10... | collective-permute-start | bytes 98312 | tf_op jit(solution)/shard_map/ppermute | solution.py:365
  77.5 1.9 collective-permute-done.7
  80.6 4.0 %collective-permute-done.8 = bf16[32,1024]{1,0:T(8,128)(2,1)S(1)} collective-permute-done((bf16[32,1024]{1,0:T(8,128)(2,1)S(1)}, bf16[32,1024]{1,0:T(8,128)(2,1)S(1)}, u32[]{:S(2)}, u32[]{:S(2)}) %collective-permute-start.8) | collective-permute-done | bytes 65568 | tf_op jit(solution)/shard_map/ppermute | solution.py:365
  84.7 1.4 shard_map.29
  86.0 4.9 %shard_map.30 = (bf16[192,2048]{1,0:T(8,128)(2,1)S(1)}, bf16[192,2048]{1,0:T(8,128)(2,1)S(1)}) custom-call(bf16[2048,512]{1,0:T(8,128)(2,1)S(1)} %bitcast.19, bf16[2048,512]{1,0:T(8,128)(2,1)} %collective-permute-done.other_ref, f32[32,2048]{1,0:T(8,128)S(1)} %get-tuple-element.43.q_ref.refs_2_), custom_call_target="tpu_custom_call" | custom-call | tf_op jit(solution)/shard_map/pallas_call | solution.py:77
  91.0 2.8 %shard_map.34 = (bf16[256,640]{1,0:T(8,128)(2,1)S(1)}, bf16[256,512]{1,0:T(8,128)(2,1)S(1)}) custom-call(s32[32]{0:T(128)S(1)} %concatenate.60.index_ref.at_ref, bf16[2048,512]{1,0:T(8,128)(2,1)S(1)} %bitcast.20, bf16[2048,512]{1,0:T(8,128)(2,1)} %collective-permute-done.other_ref, bf16[192,2048]{1,0:T(8,128)(2,1)S(1)} %get-tuple-element.44.left, ...), custom_call_target="tpu_custom_call" | custom-call | tf_op jit(solution)/shard_map/pallas_call | solution.py:77
  93.8 2.0 collective-permute-start.10
  95.8 2.8 %shard_map.32 = (bf16[256,640]{1,0:T(8,128)(2,1)S(1)}, bf16[256,512]{1,0:T(8,128)(2,1)S(1)}) custom-call(s32[32]{0:T(128)S(1)} %concatenate.60.index_ref.at_ref, bf16[2048,512]{1,0:T(8,128)(2,1)S(1)} %bitcast.21, bf16[2048,512]{1,0:T(8,128)(2,1)} %collective-permute-done.other_ref, bf16[192,2048]{1,0:T(8,128)(2,1)S(1)} %get-tuple-element.44.left, ...), custom_call_target="tpu_custom_call" | custom-call | tf_op jit(solution)/shard_map/pallas_call | solution.py:77
  98.7 2.8 %shard_map.33 = (bf16[256,640]{1,0:T(8,128)(2,1)S(1)}, bf16[256,512]{1,0:T(8,128)(2,1)S(1)}) custom-call(s32[32]{0:T(128)S(1)} %concatenate.60.index_ref.at_ref, bf16[2048,512]{1,0:T(8,128)(2,1)S(1)} %bitcast.22, bf16[2048,512]{1,0:T(8,128)(2,1)} %collective-permute-done.other_ref, bf16[192,2048]{1,0:T(8,128)(2,1)S(1)} %get-tuple-element.44.left, ...), custom_call_target="tpu_custom_call" | custom-call | tf_op jit(solution)/shard_map/pallas_call | solution.py:77
  102.2 1.2 collective-permute-start.11
  103.5 2.8 %shard_map.31 = (bf16[256,640]{1,0:T(8,128)(2,1)S(1)}, bf16[256,512]{1,0:T(8,128)(2,1)S(1)}) custom-call(s32[32]{0:T(128)S(1)} %concatenate.60.index_ref.at_ref, bf16[2048,512]{1,0:T(8,128)(2,1)S(1)} %bitcast.23, bf16[2048,512]{1,0:T(8,128)(2,1)} %collective-permute-done.other_ref, bf16[192,2048]{1,0:T(8,128)(2,1)S(1)} %get-tuple-element.44.left, ...), custom_call_target="tpu_custom_call" | custom-call | tf_op jit(solution)/shard_map/pallas_call | solution.py:77
  106.3 1.7 collective-permute-done.9.refs_1_
  107.9 1.4 collective-permute-done.11.refs_2_
  110.0 2.5 %collective-permute-start.12 = (bf16[128,640]{1,0:T(8,128)(2,1)S(1)}, bf16[128,640]{1,0:T(8,128)(2,1)S(1)}, u32[]{:S(2)}, u32[]{:S(2)}) collective-permute-start(bf16[128,640]{1,0:T(8,128)(2,1)S(1)} %get-tuple-element.51), channel_id=1, source_target_pairs={{0,8},{8,0},{16,24},{24,16},{1,9},{9,1},{17,25},{25,17},{2,10},{10... | collective-permute-start | bytes 491528 | tf_op jit(solution)/shard_map/ppermute | solution.py:365
  112.5 4.2 %collective-permute-done.12.refs_1_ = bf16[128,640]{1,0:T(8,128)(2,1)S(1)} collective-permute-done((bf16[128,640]{1,0:T(8,128)(2,1)S(1)}, bf16[128,640]{1,0:T(8,128)(2,1)S(1)}, u32[]{:S(2)}, u32[]{:S(2)}) %collective-permute-start.12) | collective-permute-done | bytes 163872 | tf_op jit(solution)/shard_map/ppermute | solution.py:365
  117.5 6.1 %collective-permute-done.13.refs_1_ = bf16[128,640]{1,0:T(8,128)(2,1)S(1)} collective-permute-done((bf16[128,640]{1,0:T(8,128)(2,1)S(1)}, bf16[128,640]{1,0:T(8,128)(2,1)S(1)}, u32[]{:S(2)}, u32[]{:S(2)}) %collective-permute-start.13) | collective-permute-done | bytes 163872 | tf_op jit(solution)/shard_map/ppermute | solution.py:365
  124.2 3.7 %collective-permute-start.14 = (bf16[128,640]{1,0:T(8,128)(2,1)S(1)}, bf16[128,640]{1,0:T(8,128)(2,1)S(1)}, u32[]{:S(2)}, u32[]{:S(2)}) collective-permute-start(bf16[128,640]{1,0:T(8,128)(2,1)S(1)} %shard_map.38), channel_id=1, source_target_pairs={{0,8},{8,0},{16,24},{24,16},{1,9},{9,1},{17,25},{25,17},{2,10},{10... | collective-permute-start | bytes 491528 | tf_op jit(solution)/shard_map/ppermute | solution.py:365
  128.8 1.7 collective-permute-start.20
  131.3 1.8 collective-permute-start.15
  133.1 1.5 collective-permute-done.18.refs_1_
  137.1 4.2 %collective-permute-done.21.refs_1_ = bf16[128,512]{1,0:T(8,128)(2,1)S(1)} collective-permute-done((bf16[128,512]{1,0:T(8,128)(2,1)S(1)}, bf16[128,512]{1,0:T(8,128)(2,1)S(1)}, u32[]{:S(2)}, u32[]{:S(2)}) %collective-permute-start.21) | collective-permute-done | bytes 131104 | tf_op jit(solution)/shard_map/ppermute | solution.py:365
  143.2 6.2 %collective-permute-done.22.refs_1_ = bf16[128,512]{1,0:T(8,128)(2,1)S(1)} collective-permute-done((bf16[128,512]{1,0:T(8,128)(2,1)S(1)}, bf16[128,512]{1,0:T(8,128)(2,1)S(1)}, u32[]{:S(2)}, u32[]{:S(2)}) %collective-permute-start.22) | collective-permute-done | bytes 131104 | tf_op jit(solution)/shard_map/ppermute | solution.py:365
  150.4 4.8 %collective-permute-done.23 = bf16[128,512]{1,0:T(8,128)(2,1)S(1)} collective-permute-done((bf16[128,512]{1,0:T(8,128)(2,1)S(1)}, bf16[128,512]{1,0:T(8,128)(2,1)S(1)}, u32[]{:S(2)}, u32[]{:S(2)}) %collective-permute-start.23) | collective-permute-done | bytes 131104 | tf_op jit(solution)/shard_map/ppermute | solution.py:365
  156.3 1.6 collective-permute-start.27
  158.3 1.6 collective-permute-start.16
  159.9 4.6 %collective-permute-done.24 = bf16[256,512]{1,0:T(8,128)(2,1)S(1)} collective-permute-done((bf16[256,512]{1,0:T(8,128)(2,1)S(1)}, bf16[256,512]{1,0:T(8,128)(2,1)S(1)}, u32[]{:S(2)}, u32[]{:S(2)}) %collective-permute-start.24) | collective-permute-done | bytes 262176 | tf_op jit(solution)/shard_map/ppermute | solution.py:365
  164.6 1.5 collective-permute-start.25
  166.1 3.5 %collective-permute-done.16.refs_0_ = bf16[256,640]{1,0:T(8,128)(2,1)S(1)} collective-permute-done((bf16[256,640]{1,0:T(8,128)(2,1)S(1)}, bf16[256,640]{1,0:T(8,128)(2,1)S(1)}, u32[]{:S(2)}, u32[]{:S(2)}) %collective-permute-start.16) | collective-permute-done | bytes 327712 | tf_op jit(solution)/shard_map/ppermute | solution.py:365
  169.7 2.8 %collective-permute-done.25.refs_1_ = bf16[256,512]{1,0:T(8,128)(2,1)S(1)} collective-permute-done((bf16[256,512]{1,0:T(8,128)(2,1)S(1)}, bf16[256,512]{1,0:T(8,128)(2,1)S(1)}, u32[]{:S(2)}, u32[]{:S(2)}) %collective-permute-start.25) | collective-permute-done | bytes 262176 | tf_op jit(solution)/shard_map/ppermute | solution.py:365
  175.0 2.0 shard_map.45
  177.1 1.3 shard_map.46
  179.3 32.2 %shard_map.48 = (bf16[32,2048]{1,0:T(8,128)(2,1)S(1)}, f32[32,128]{1,0:T(8,128)S(1)}, bf16[2048,2048]{1,0:T(8,128)(2,1)S(1)}, bf16[2048,128]{1,0:T(8,128)(2,1)S(...) custom-call(s32[32]{0:T(128)S(1)} %concatenate.60.index_ref.at_ref, ...), custom_call_target="tpu_custom_call", output_to_operand_aliasing={{2}: (5, {}), {3}: (6, {}), {4}: (7, {}), {5}: (8, {})} | custom-call | tf_op jit(solution)/shard_map/pallas_call | solution.py:77
  212.4 4.6 %collective-permute-done.33 = bf16[32,512]{1,0:T(8,128)(2,1)S(1)} collective-permute-done((bf16[32,512]{1,0:T(8,128)(2,1)S(1)}, bf16[32,512]{1,0:T(8,128)(2,1)S(1)}, u32[]{:S(2)}, u32[]{:S(2)}) %collective-permute-start.33) | collective-permute-done | bytes 32800 | tf_op jit(solution)/shard_map/ppermute | solution.py:365
  217.0 4.3 %collective-permute-done.34 = bf16[32,1024]{1,0:T(8,128)(2,1)S(1)} collective-permute-done((bf16[32,1024]{1,0:T(8,128)(2,1)S(1)}, bf16[32,1024]{1,0:T(8,128)(2,1)S(1)}, u32[]{:S(2)}, u32[]{:S(2)}) %collective-permute-start.34) | collective-permute-done | bytes 65568 | tf_op jit(solution)/shard_map/ppermute | solution.py:365
  (69 shorter events, 19.6 us)
Async XLA Ops:
  3.2 7.3 %copy-start.1 = (f32[2048,32]{0,1:T(8,128)S(1)}, f32[2048,32]{0,1:T(8,128)}, u32[]{:S(2)}) copy-start(f32[2048,32]{0,1:T(8,128)} %param.3) | copy-start | bytes 786436
  3.2 54.1 %all-to-all-start = ((bf16[64,32,512]{2,0,1:T(8,128)(2,1)}), bf16[64,32,512]{2,0,1:T(8,128)(2,1)S(1)}, u32[]{:S(2)}, u32[]{:S(2)}) async-start(bf16[64,32,512]{2,0,1:T(8,128)(2,1)} %bitcast.26), calls=%async_computation | async-start | bytes 4194304 | tf_op jit(solution)/shard_map/all_to_all | solution.py:414
  10.6 19.1 %collective-permute-start.1 = (bf16[32,2048]{1,0:T(8,128)(2,1)S(1)}, bf16[32,2048]{1,0:T(8,128)(2,1)S(1)}, u32[]{:S(2)}, u32[]{:S(2)}) collective-permute-start(bf16[32,2048]{1,0:T(8,128)(2,1)S(1)} %convert_bitcast_fusion.1), channel_id=1, source_target_pairs={{0,2},{1,3},{2,0},{3,1},{4,6},{5,7},{6,4},{7,5},{8,10},{9,11},{10,... | collective-permute-start | bytes 393224 | tf_op jit(solution)/shard_map/ppermute | solution.py:365
  29.7 29.4 %collective-permute-start.2 = (bf16[32,4096]{1,0:T(8,128)(2,1)S(1)}, bf16[32,4096]{1,0:T(8,128)(2,1)S(1)}, u32[]{:S(2)}, u32[]{:S(2)}) collective-permute-start(bf16[32,4096]{1,0:T(8,128)(2,1)S(1)} %pad_maximum_fusion.4), channel_id=1, source_target_pairs={{0,4},{1,5},{2,6},{3,7},{4,0},{5,1},{6,2},{7,3},{8,12},{9,13},{10,... | collective-permute-start | bytes 786440 | tf_op jit(solution)/shard_map/ppermute | solution.py:365
  57.3 28.8 %collective-permute-start = (bf16[2048,512]{1,0:T(8,128)(2,1)S(1)}, bf16[2048,512]{1,0:T(8,128)(2,1)}, u32[]{:S(2)}, u32[]{:S(2)}) collective-permute-start(bf16[2048,512]{1,0:T(8,128)(2,1)S(1)} %bitcast.18), channel_id=1, source_target_pairs={{0,1},{1,0},{2,3},{3,2},{4,5},{5,4},{6,7},{7,6},{8,9},{9,8},{10,11... | collective-permute-start | bytes 6291464 | tf_op jit(solution)/shard_map/ppermute | solution.py:365
  59.1 4.5 %collective-permute-start.3 = (bf16[32,8192]{1,0:T(8,128)(2,1)S(1)}, bf16[32,8192]{1,0:T(8,128)(2,1)S(1)}, u32[]{:S(2)}, u32[]{:S(2)}) collective-permute-start(bf16[32,8192]{1,0:T(8,128)(2,1)S(1)} %pad_maximum_fusion.1.near_ref), channel_id=1, source_target_pairs={{0,1},{1,0},{2,3},{3,2},{4,5},{5,4},{6,7},{7,6},{8,9},{9,8},{10,11... | collective-permute-start | bytes 1572872 | tf_op jit(solution)/shard_map/ppermute | solution.py:365
  63.6 1.6 copy-start
  66.4 1.2 collective-permute-start.4
  67.7 3.7 %collective-permute-start.5 = (bf16[32,128]{1,0:T(8,128)(2,1)S(1)}, bf16[32,128]{1,0:T(8,128)(2,1)S(1)}, u32[]{:S(2)}, u32[]{:S(2)}) collective-permute-start(bf16[32,128]{1,0:T(8,128)(2,1)S(1)} %maximum_select_fusion.4), channel_id=1, source_target_pairs={{0,2},{1,3},{2,0},{3,1},{4,6},{5,7},{6,4},{7,5},{8,10},{9,11},{10,... | collective-permute-start | bytes 24584 | tf_op jit(solution)/shard_map/ppermute | solution.py:365
  71.4 3.7 %collective-permute-start.6 = (bf16[32,256]{1,0:T(8,128)(2,1)S(1)}, bf16[32,256]{1,0:T(8,128)(2,1)S(1)}, u32[]{:S(2)}, u32[]{:S(2)}) collective-permute-start(bf16[32,256]{1,0:T(8,128)(2,1)S(1)} %maximum_select_fusion.3), channel_id=1, source_target_pairs={{0,4},{1,5},{2,6},{3,7},{4,0},{5,1},{6,2},{7,3},{8,12},{9,13},{10,... | collective-permute-start | bytes 49160 | tf_op jit(solution)/shard_map/ppermute | solution.py:365
  75.2 4.2 %collective-permute-start.7 = (bf16[32,512]{1,0:T(8,128)(2,1)S(1)}, bf16[32,512]{1,0:T(8,128)(2,1)S(1)}, u32[]{:S(2)}, u32[]{:S(2)}) collective-permute-start(bf16[32,512]{1,0:T(8,128)(2,1)S(1)} %maximum_select_fusion.2), channel_id=1, source_target_pairs={{0,8},{8,0},{16,24},{24,16},{1,9},{9,1},{17,25},{25,17},{2,10},{10... | collective-permute-start | bytes 98312 | tf_op jit(solution)/shard_map/ppermute | solution.py:365
  79.4 5.2 %collective-permute-start.8 = (bf16[32,1024]{1,0:T(8,128)(2,1)S(1)}, bf16[32,1024]{1,0:T(8,128)(2,1)S(1)}, u32[]{:S(2)}, u32[]{:S(2)}) collective-permute-start(bf16[32,1024]{1,0:T(8,128)(2,1)S(1)} %maximum_select_fusion.1), channel_id=1, source_target_pairs={{0,16},{8,24},{16,0},{24,8},{1,17},{9,25},{17,1},{25,9},{2,18},{10... | collective-permute-start | bytes 196616 | tf_op jit(solution)/shard_map/ppermute | solution.py:365
  93.8 7.8 %collective-permute-start.10 = (bf16[256,640]{1,0:T(8,128)(2,1)S(1)}, bf16[256,640]{1,0:T(8,128)(2,1)S(1)}, u32[]{:S(2)}, u32[]{:S(2)}) collective-permute-start(bf16[256,640]{1,0:T(8,128)(2,1)S(1)} %get-tuple-element.49), channel_id=1, source_target_pairs={{0,2},{1,5},{2,0},{3,7},{4,6},{5,1},{6,4},{7,3},{8,10},{9,13},{10,... | collective-permute-start | bytes 983048 | tf_op jit(solution)/shard_map/ppermute | solution.py:365
  98.6 9.3 %collective-permute-start.9 = (bf16[256,640]{1,0:T(8,128)(2,1)S(1)}, bf16[256,640]{1,0:T(8,128)(2,1)S(1)}, u32[]{:S(2)}, u32[]{:S(2)}) collective-permute-start(bf16[256,640]{1,0:T(8,128)(2,1)S(1)} %get-tuple-element.47), channel_id=1, source_target_pairs={{0,2},{1,5},{2,0},{3,7},{4,6},{5,1},{6,4},{7,3},{8,10},{9,13},{10,... | collective-permute-start | bytes 983048 | tf_op jit(solution)/shard_map/ppermute | solution.py:365
  102.2 7.1 %collective-permute-start.11 = (bf16[256,640]{1,0:T(8,128)(2,1)S(1)}, bf16[256,640]{1,0:T(8,128)(2,1)S(1)}, u32[]{:S(2)}, u32[]{:S(2)}) collective-permute-start(bf16[256,640]{1,0:T(8,128)(2,1)S(1)} %shard_map.35), channel_id=1, source_target_pairs={{0,4},{1,3},{2,6},{3,1},{4,0},{5,7},{6,2},{7,5},{8,12},{9,11},{10,... | collective-permute-start | bytes 983048 | tf_op jit(solution)/shard_map/ppermute | solution.py:365
  110.0 6.7 %collective-permute-start.12 = (bf16[128,640]{1,0:T(8,128)(2,1)S(1)}, bf16[128,640]{1,0:T(8,128)(2,1)S(1)}, u32[]{:S(2)}, u32[]{:S(2)}) collective-permute-start(bf16[128,640]{1,0:T(8,128)(2,1)S(1)} %get-tuple-element.51), channel_id=1, source_target_pairs={{0,8},{8,0},{16,24},{24,16},{1,9},{9,1},{17,25},{25,17},{2,10},{10... | collective-permute-start | bytes 491528 | tf_op jit(solution)/shard_map/ppermute | solution.py:365
  112.5 15.4 %collective-permute-start.19 = (bf16[256,512]{1,0:T(8,128)(2,1)S(1)}, bf16[256,512]{1,0:T(8,128)(2,1)S(1)}, u32[]{:S(2)}, u32[]{:S(2)}) collective-permute-start(bf16[256,512]{1,0:T(8,128)(2,1)S(1)} %get-tuple-element.55), channel_id=1, source_target_pairs={{0,2},{1,5},{2,0},{3,7},{4,6},{5,1},{6,4},{7,3},{8,10},{9,13},{10,... | collective-permute-start | bytes 786440 | tf_op jit(solution)/shard_map/ppermute | solution.py:365
  117.3 6.4 %collective-permute-start.13 = (bf16[128,640]{1,0:T(8,128)(2,1)S(1)}, bf16[128,640]{1,0:T(8,128)(2,1)S(1)}, u32[]{:S(2)}, u32[]{:S(2)}) collective-permute-start(bf16[128,640]{1,0:T(8,128)(2,1)S(1)} %shard_map.37.refs_0_), channel_id=1, source_target_pairs={{0,16},{8,24},{16,0},{24,8},{1,17},{9,25},{17,1},{25,9},{2,18},{10... | collective-permute-start | bytes 491528 | tf_op jit(solution)/shard_map/ppermute | solution.py:365
  124.2 7.0 %collective-permute-start.14 = (bf16[128,640]{1,0:T(8,128)(2,1)S(1)}, bf16[128,640]{1,0:T(8,128)(2,1)S(1)}, u32[]{:S(2)}, u32[]{:S(2)}) collective-permute-start(bf16[128,640]{1,0:T(8,128)(2,1)S(1)} %shard_map.38), channel_id=1, source_target_pairs={{0,8},{8,0},{16,24},{24,16},{1,9},{9,1},{17,25},{25,17},{2,10},{10... | collective-permute-start | bytes 491528 | tf_op jit(solution)/shard_map/ppermute | solution.py:365
  128.0 6.6 %collective-permute-start.18 = (bf16[256,512]{1,0:T(8,128)(2,1)S(1)}, bf16[256,512]{1,0:T(8,128)(2,1)S(1)}, u32[]{:S(2)}, u32[]{:S(2)}) collective-permute-start(bf16[256,512]{1,0:T(8,128)(2,1)S(1)} %get-tuple-element.53), channel_id=1, source_target_pairs={{0,2},{1,5},{2,0},{3,7},{4,6},{5,1},{6,4},{7,3},{8,10},{9,13},{10,... | collective-permute-start | bytes 786440 | tf_op jit(solution)/shard_map/ppermute | solution.py:365
  128.8 6.4 %collective-permute-start.20 = (bf16[256,512]{1,0:T(8,128)(2,1)S(1)}, bf16[256,512]{1,0:T(8,128)(2,1)S(1)}, u32[]{:S(2)}, u32[]{:S(2)}) collective-permute-start(bf16[256,512]{1,0:T(8,128)(2,1)S(1)} %shard_map.39), channel_id=1, source_target_pairs={{0,4},{1,3},{2,6},{3,1},{4,0},{5,7},{6,2},{7,5},{8,12},{9,11},{10,... | collective-permute-start | bytes 786440 | tf_op jit(solution)/shard_map/ppermute | solution.py:365
  131.3 18.9 %collective-permute-start.15 = (bf16[256,640]{1,0:T(8,128)(2,1)S(1)}, bf16[256,640]{1,0:T(8,128)(2,1)S(1)}, u32[]{:S(2)}, u32[]{:S(2)}) collective-permute-start(bf16[256,640]{1,0:T(8,128)(2,1)S(1)} %pad_maximum_fusion.3), channel_id=1, source_target_pairs={{0,4},{1,3},{2,6},{3,1},{4,0},{5,7},{6,2},{7,5},{8,12},{9,11},{10,... | collective-permute-start | bytes 983048 | tf_op jit(solution)/shard_map/ppermute | solution.py:365
  136.1 5.2 %collective-permute-start.21 = (bf16[128,512]{1,0:T(8,128)(2,1)S(1)}, bf16[128,512]{1,0:T(8,128)(2,1)S(1)}, u32[]{:S(2)}, u32[]{:S(2)}) collective-permute-start(bf16[128,512]{1,0:T(8,128)(2,1)S(1)} %get-tuple-element.57), channel_id=1, source_target_pairs={{0,8},{8,0},{16,24},{24,16},{1,9},{9,1},{17,25},{25,17},{2,10},{10... | collective-permute-start | bytes 393224 | tf_op jit(solution)/shard_map/ppermute | solution.py:365
  142.0 7.3 %collective-permute-start.22 = (bf16[128,512]{1,0:T(8,128)(2,1)S(1)}, bf16[128,512]{1,0:T(8,128)(2,1)S(1)}, u32[]{:S(2)}, u32[]{:S(2)}) collective-permute-start(bf16[128,512]{1,0:T(8,128)(2,1)S(1)} %shard_map.41.refs_0_), channel_id=1, source_target_pairs={{0,16},{8,24},{16,0},{24,8},{1,17},{9,25},{17,1},{25,9},{2,18},{10... | collective-permute-start | bytes 393224 | tf_op jit(solution)/shard_map/ppermute | solution.py:365
  150.1 5.0 %collective-permute-start.23 = (bf16[128,512]{1,0:T(8,128)(2,1)S(1)}, bf16[128,512]{1,0:T(8,128)(2,1)S(1)}, u32[]{:S(2)}, u32[]{:S(2)}) collective-permute-start(bf16[128,512]{1,0:T(8,128)(2,1)S(1)} %shard_map.42), channel_id=1, source_target_pairs={{0,8},{8,0},{16,24},{24,16},{1,9},{9,1},{17,25},{25,17},{2,10},{10... | collective-permute-start | bytes 393224 | tf_op jit(solution)/shard_map/ppermute | solution.py:365
  150.3 22.2 %collective-permute-start.32 = (bf16[512,640]{1,0:T(8,128)(2,1)S(1)}, bf16[512,640]{1,0:T(8,128)(2,1)S(1)}, u32[]{:S(2)}, u32[]{:S(2)}) collective-permute-start(bf16[512,640]{1,0:T(8,128)(2,1)S(1)} %pad_maximum_fusion.refs_0_), channel_id=1, source_target_pairs={{0,1},{1,0},{2,3},{3,2},{4,5},{5,4},{6,7},{7,6},{8,9},{9,8},{10,11... | collective-permute-start | bytes 1966088 | tf_op jit(solution)/shard_map/ppermute | solution.py:365
  155.2 9.2 %collective-permute-start.24 = (bf16[256,512]{1,0:T(8,128)(2,1)S(1)}, bf16[256,512]{1,0:T(8,128)(2,1)S(1)}, u32[]{:S(2)}, u32[]{:S(2)}) collective-permute-start(bf16[256,512]{1,0:T(8,128)(2,1)S(1)} %pad_maximum_fusion.5), channel_id=1, source_target_pairs={{0,4},{1,3},{2,6},{3,1},{4,0},{5,7},{6,2},{7,5},{8,12},{9,11},{10,... | collective-permute-start | bytes 786440 | tf_op jit(solution)/shard_map/ppermute | solution.py:365
  156.3 8.3 %collective-permute-start.27 = (bf16[256,512]{1,0:T(8,128)(2,1)S(1)}, bf16[256,512]{1,0:T(8,128)(2,1)S(1)}, u32[]{:S(2)}, u32[]{:S(2)}) collective-permute-start(bf16[256,512]{1,0:T(8,128)(2,1)S(1)} %pad_maximum_fusion.5), channel_id=1, source_target_pairs={{0,2},{1,5},{2,0},{3,7},{4,6},{5,1},{6,4},{7,3},{8,10},{9,13},{10,... | collective-permute-start | bytes 786440 | tf_op jit(solution)/shard_map/ppermute | solution.py:365
  157.8 8.3 %collective-permute-start.30 = (bf16[256,640]{1,0:T(8,128)(2,1)S(1)}, bf16[256,640]{1,0:T(8,128)(2,1)S(1)}, u32[]{:S(2)}, u32[]{:S(2)}) collective-permute-start(bf16[256,640]{1,0:T(8,128)(2,1)S(1)} %pad_maximum_fusion.3), channel_id=1, source_target_pairs={{0,2},{1,5},{2,0},{3,7},{4,6},{5,1},{6,4},{7,3},{8,10},{9,13},{10,... | collective-permute-start | bytes 983048 | tf_op jit(solution)/shard_map/ppermute | solution.py:365
  158.3 11.4 %collective-permute-start.16 = (bf16[256,640]{1,0:T(8,128)(2,1)S(1)}, bf16[256,640]{1,0:T(8,128)(2,1)S(1)}, u32[]{:S(2)}, u32[]{:S(2)}) collective-permute-start(bf16[256,640]{1,0:T(8,128)(2,1)S(1)} %collective-permute-done.15), channel_id=1, source_target_pairs={{0,2},{1,5},{2,0},{3,7},{4,6},{5,1},{6,4},{7,3},{8,10},{9,13},{10,... | collective-permute-start | bytes 983048 | tf_op jit(solution)/shard_map/ppermute | solution.py:365
  164.5 10.6 %collective-permute-start.29 = (bf16[512,512]{1,0:T(8,128)(2,1)S(1)}, bf16[512,512]{1,0:T(8,128)(2,1)S(1)}, u32[]{:S(2)}, u32[]{:S(2)}) collective-permute-start(bf16[512,512]{1,0:T(8,128)(2,1)S(1)} %pad_maximum_fusion.2.refs_0_), channel_id=1, source_target_pairs={{0,1},{1,0},{2,3},{3,2},{4,5},{5,4},{6,7},{7,6},{8,9},{9,8},{10,11... | collective-permute-start | bytes 1572872 | tf_op jit(solution)/shard_map/ppermute | solution.py:365
  164.6 7.9 %collective-permute-start.25 = (bf16[256,512]{1,0:T(8,128)(2,1)S(1)}, bf16[256,512]{1,0:T(8,128)(2,1)S(1)}, u32[]{:S(2)}, u32[]{:S(2)}) collective-permute-start(bf16[256,512]{1,0:T(8,128)(2,1)S(1)} %collective-permute-done.24), channel_id=1, source_target_pairs={{0,2},{1,5},{2,0},{3,7},{4,6},{5,1},{6,4},{7,3},{8,10},{9,13},{10,... | collective-permute-start | bytes 786440 | tf_op jit(solution)/shard_map/ppermute | solution.py:365
  166.1 8.0 %collective-permute-start.31 = (bf16[256,640]{1,0:T(8,128)(2,1)S(1)}, bf16[256,640]{1,0:T(8,128)(2,1)S(1)}, u32[]{:S(2)}, u32[]{:S(2)}) collective-permute-start(bf16[256,640]{1,0:T(8,128)(2,1)S(1)} %collective-permute-done.30.refs_0_), channel_id=1, source_target_pairs={{0,1},{1,0},{2,3},{3,2},{4,5},{5,4},{6,7},{7,6},{8,9},{9,8},{10,11... | collective-permute-start | bytes 983048 | tf_op jit(solution)/shard_map/ppermute | solution.py:365
  169.6 9.7 %collective-permute-start.17 = (bf16[256,640]{1,0:T(8,128)(2,1)S(1)}, bf16[256,640]{1,0:T(8,128)(2,1)S(1)}, u32[]{:S(2)}, u32[]{:S(2)}) collective-permute-start(bf16[256,640]{1,0:T(8,128)(2,1)S(1)} %collective-permute-done.16.refs_0_), channel_id=1, source_target_pairs={{0,1},{1,0},{2,3},{3,2},{4,5},{5,4},{6,7},{7,6},{8,9},{9,8},{10,11... | collective-permute-start | bytes 983048 | tf_op jit(solution)/shard_map/ppermute | solution.py:365
  172.5 4.6 %collective-permute-start.28 = (bf16[256,512]{1,0:T(8,128)(2,1)S(1)}, bf16[256,512]{1,0:T(8,128)(2,1)S(1)}, u32[]{:S(2)}, u32[]{:S(2)}) collective-permute-start(bf16[256,512]{1,0:T(8,128)(2,1)S(1)} %collective-permute-done.27.refs_0_), channel_id=1, source_target_pairs={{0,1},{1,0},{2,3},{3,2},{4,5},{5,4},{6,7},{7,6},{8,9},{9,8},{10,11... | collective-permute-start | bytes 786440 | tf_op jit(solution)/shard_map/ppermute | solution.py:365
  172.5 6.9 %collective-permute-start.26 = (bf16[256,512]{1,0:T(8,128)(2,1)S(1)}, bf16[256,512]{1,0:T(8,128)(2,1)S(1)}, u32[]{:S(2)}, u32[]{:S(2)}) collective-permute-start(bf16[256,512]{1,0:T(8,128)(2,1)S(1)} %collective-permute-done.25.refs_1_), channel_id=1, source_target_pairs={{0,1},{1,0},{2,3},{3,2},{4,5},{5,4},{6,7},{7,6},{8,9},{9,8},{10,11... | collective-permute-start | bytes 786440 | tf_op jit(solution)/shard_map/ppermute | solution.py:365
  212.2 4.8 %collective-permute-start.33 = (bf16[32,512]{1,0:T(8,128)(2,1)S(1)}, bf16[32,512]{1,0:T(8,128)(2,1)S(1)}, u32[]{:S(2)}, u32[]{:S(2)}) collective-permute-start(bf16[32,512]{1,0:T(8,128)(2,1)S(1)} %shard_map.49), channel_id=1, source_target_pairs={{0,16},{8,24},{16,0},{24,8},{1,17},{9,25},{17,1},{25,9},{2,18},{10... | collective-permute-start | bytes 98312 | tf_op jit(solution)/shard_map/ppermute | solution.py:365
  217.0 4.3 %collective-permute-start.34 = (bf16[32,1024]{1,0:T(8,128)(2,1)S(1)}, bf16[32,1024]{1,0:T(8,128)(2,1)S(1)}, u32[]{:S(2)}, u32[]{:S(2)}) collective-permute-start(bf16[32,1024]{1,0:T(8,128)(2,1)S(1)} %pad_maximum_fusion.6), channel_id=1, source_target_pairs={{0,8},{8,0},{16,24},{24,16},{1,9},{9,1},{17,25},{25,17},{2,10},{10... | collective-permute-start | bytes 196616 | tf_op jit(solution)/shard_map/ppermute | solution.py:365
